TPU v7x, 32 devices: a whole 2x2x4 slice. The times are simulated.
32 devices in a mesh: dp: 4 (over z), row: 4 (over y, x), col: 2 (over core).
Axes of the slice: x: 2, y: 2, z: 4, core: 2. Of those that a mesh axis runs over, the one named last changes fastest.
Arguments:
- tokens: bfloat16 [8, 1024, 2048], P(('dp', 'col'), 'row'), may hold values from -6 to 6
- prefix_len: int32 [8], P(('dp', 'col')), may hold values from 102 to 512, as said below
- norm1_gain: bfloat16 [2048], replicated, may hold values from 0.5 to 1.5
- norm1_bias: bfloat16 [2048], replicated, may hold values from -1.1953125 to 1.1953125
- query_key_value_weight: bfloat16 [2048, 3, 2048], P(('dp', 'col'), None, 'row'), may hold values from -0.125 to 0.125
- query_key_value_bias: bfloat16 [3, 2048], P(None, 'row'), may hold values from -2.5 to 2.5
- attention_output_weight: bfloat16 [2048, 2048], P(('dp', 'col'), 'row'), may hold values from -0.75 to 0.75
- norm2_gain: bfloat16 [2048], replicated, may hold values from 0.5 to 1.5
- norm2_bias: bfloat16 [2048], replicated, may hold values from -1.1953125 to 1.1953125
- gate_up_projection_weight: bfloat16 [2048, 2, 5632], P(('dp', 'row'), None, 'col'), may hold values from -0.125 to 0.125
- down_projection_weight: bfloat16 [2048, 5632], P(('dp', 'row'), 'col'), may hold values from -0.078125 to 0.078125
- grad_out: bfloat16 [8, 1024, 2048], P(('dp', 'col'), 'row'), may hold values from -30 to 30
Outputs:
- layer_out: bfloat16 [8, 1024, 2048], P(('dp', 'col'), 'row')
- input_token_gradient: float32 [8, 1024, 2048], P(('dp', 'col'), 'row')
- grad_norm1_gain: float32 [2048], replicated
- grad_norm1_bias: float32 [2048], replicated
- grad_qkv_weight: float32 [2048, 3, 2048], P(('dp', 'col'), None, 'row')
- grad_qkv_bias: float32 [3, 2048], P(None, 'row')
- grad_out_weight: float32 [2048, 2048], P(('dp', 'col'), 'row')
- grad_norm2_gain: float32 [2048], replicated
- grad_norm2_bias: float32 [2048], replicated
- grad_gate_up_weight: float32 [2048, 2, 5632], P(('dp', 'row'), None, 'col')
- grad_down_weight: float32 [2048, 5632], P(('dp', 'row'), 'col')
Inputs may be any that keep to these rules, and one draw needn't show every extreme that they name: `prefix_len`: both ends of the range occur in every draw.
All inputs are finite; a program needn't handle non-finite values.
Results may differ from a plain program's by a relative error of at most 0.02.
Values may be sent and summed in bfloat16 or wider, within the bound.
No kernel may reach another device: no remote copies, remote signals or barrier semaphores. Data moves between devices by JAX's collectives and lax.ppermute only.
A program may use at most 192 MiB of HBM per device.

v0:
```python
import math

import jax
import jax.numpy as jnp
from jax import lax
from jax.sharding import PartitionSpec as P

HD = 64
ROT = 16
LEN = 1024


norm_eps = 1e-05
rope_base = 10000.0
masked_fill = -1e30


def layer_norm_forward(values, norm_gain, norm_shift):
    centre = jnp.mean(values, axis=-1, keepdims=True)
    centred = values - centre
    variance = jnp.mean(centred * centred, axis=-1, keepdims=True)
    inverse = lax.rsqrt(variance + norm_eps)
    normed = centred * inverse
    return (normed * norm_gain + norm_shift, normed, inverse)


def layer_norm_backward(incoming, normed, inverse, norm_gain):
    scaled = incoming * norm_gain
    inner = jnp.mean(scaled, axis=-1, keepdims=True)
    along = jnp.mean(scaled * normed, axis=-1, keepdims=True)
    return inverse * (scaled - inner - normed * along)


def rotary_tables():
    half_rot = ROT // 2
    freqs = rope_base ** (-jnp.arange(half_rot, dtype=jnp.float32) * 2.0 / ROT)
    angles = jnp.arange(LEN, dtype=jnp.float32)[:, None] * freqs[None, :]
    return (jnp.cos(angles)[:, None, :], jnp.sin(angles)[:, None, :])


def rotate(heads, cosine, sines):
    half_rot = ROT // 2
    first = heads[..., :half_rot]
    second = heads[..., half_rot:ROT]
    return jnp.concatenate(
        [first * cosine - second * sines, second * cosine + first * sines, heads[..., ROT:]],
        axis=-1,
    )


def unrotate(grads, cosine, sines):
    half_rot = ROT // 2
    first = grads[..., :half_rot]
    second = grads[..., half_rot:ROT]
    return jnp.concatenate(
        [first * cosine + second * sines, second * cosine - first * sines, grads[..., ROT:]],
        axis=-1,
    )


def visible(row_start, block_size, prefix):
    query_place = row_start + jnp.arange(block_size)
    key_place = jnp.arange(LEN)
    return (key_place[None, :] <= query_place[:, None]) | (key_place[None, :] < prefix)


def attend_forward(seq_item):
    queries, keys_all, values, prefix = seq_item
    block_size = min(512, LEN)
    scale = 1.0 / math.sqrt(HD)

    def one_block(row_start):
        query_rows = lax.dynamic_slice_in_dim(queries, row_start, block_size, 0)
        scores = (
            jnp.einsum("qhd,khd->hqk", query_rows, keys_all, preferred_element_type=jnp.float32)
            * scale
        )
        scores = jnp.where(visible(row_start, block_size, prefix)[None], scores, masked_fill)
        row_top = jnp.max(scores, axis=-1, keepdims=True)
        exp_scores = jnp.exp(scores - row_top)
        row_total = jnp.sum(exp_scores, axis=-1, keepdims=True)
        attn_probs = (exp_scores / row_total).astype(jnp.bfloat16)
        result = jnp.einsum("hqk,khd->qhd", attn_probs, values, preferred_element_type=jnp.float32)
        return (result.astype(jnp.bfloat16), (row_top + jnp.log(row_total))[..., 0])

    starts = jnp.arange(LEN // block_size, dtype=jnp.int32) * block_size
    blocks_out, log_sums = lax.map(one_block, starts)
    return (blocks_out.reshape(queries.shape), log_sums)


def attend_backward(seq_item):
    queries, keys_all, values, prefix, log_sums, heads_gradient = seq_item
    block_size = min(512, LEN)
    scale = 1.0 / math.sqrt(HD)

    def one_block(running, block_idx):
        grad_keys, grad_values = running
        row_start = block_idx * block_size
        query_rows = lax.dynamic_slice_in_dim(queries, row_start, block_size, 0)
        grad_rows = lax.dynamic_slice_in_dim(heads_gradient, row_start, block_size, 0)
        scores = (
            jnp.einsum("qhd,khd->hqk", query_rows, keys_all, preferred_element_type=jnp.float32)
            * scale
        )
        allowed = visible(row_start, block_size, prefix)[None]
        attn_probs = jnp.where(allowed, jnp.exp(scores - log_sums[block_idx][..., None]), 0.0)
        grad_probs = jnp.einsum(
            "qhd,khd->hqk", grad_rows, values, preferred_element_type=jnp.float32
        )
        inner = jnp.sum(attn_probs * grad_probs, axis=-1, keepdims=True)
        grad_scores = (attn_probs * (grad_probs - inner)).astype(jnp.bfloat16)
        grad_query = (
            jnp.einsum("hqk,khd->qhd", grad_scores, keys_all, preferred_element_type=jnp.float32)
            * scale
        )
        grad_keys = (
            grad_keys
            + jnp.einsum(
                "hqk,qhd->khd", grad_scores, query_rows, preferred_element_type=jnp.float32
            )
            * scale
        )
        grad_values = grad_values + jnp.einsum(
            "hqk,qhd->khd",
            attn_probs.astype(jnp.bfloat16),
            grad_rows,
            preferred_element_type=jnp.float32,
        )
        return ((grad_keys, grad_values), grad_query)

    zeros_kv = jnp.zeros(keys_all.shape, jnp.float32)
    block_ids = jnp.arange(LEN // block_size, dtype=jnp.int32)
    (grad_keys, grad_values), grad_queries = lax.scan(one_block, (zeros_kv, zeros_kv), block_ids)
    return (grad_queries.reshape(queries.shape), grad_keys, grad_values)


def gather_attention(query_key_value_weight, attention_output_weight):
    return (
        lax.all_gather(query_key_value_weight, ("dp", "col"), axis=0, tiled=True),
        lax.all_gather(attention_output_weight, ("dp", "col"), axis=0, tiled=True),
    )


def gather_mlp(gate_up_projection_weight, down_projection_weight):
    return (
        lax.all_gather(gate_up_projection_weight, ("dp", "row"), axis=0, tiled=True),
        lax.all_gather(down_projection_weight, ("dp", "row"), axis=0, tiled=True),
    )


def body(
    tokens,
    prefix_len,
    norm1_gain,
    norm1_bias,
    query_key_value_weight,
    query_key_value_bias,
    attention_output_weight,
    norm2_gain,
    norm2_bias,
    gate_up_projection_weight,
    down_projection_weight,
    grad_out,
):
    local_seqs = tokens.shape[0]
    model_width = tokens.shape[2]
    head_cols = query_key_value_weight.shape[2]
    heads_local = head_cols // HD
    cosine, sines = rotary_tables()
    first_norm_gain = norm1_gain.astype(jnp.float32)
    second_norm_gain = norm2_gain.astype(jnp.float32)
    inputs = tokens.astype(jnp.float32)
    first_normalized, first_standardized, first_inverse_deviation = layer_norm_forward(
        inputs, first_norm_gain, norm1_bias.astype(jnp.float32)
    )
    first_norm_input = first_normalized.astype(jnp.bfloat16)
    sequence_input = lax.all_gather(first_norm_input, "row", axis=1, tiled=True)
    query_key_value_gathered, output_weight_gathered = gather_attention(
        query_key_value_weight, attention_output_weight
    )
    projected_values = jnp.einsum(
        "wbv,vtp->wbtp",
        sequence_input,
        query_key_value_gathered,
        preferred_element_type=jnp.float32,
    ) + query_key_value_bias.astype(jnp.float32)
    head_shape = (local_seqs, LEN, heads_local, HD)
    queries = rotate(projected_values[:, :, 0].reshape(head_shape), cosine, sines).astype(
        jnp.bfloat16
    )
    keys_all = rotate(projected_values[:, :, 1].reshape(head_shape), cosine, sines).astype(
        jnp.bfloat16
    )
    values = projected_values[:, :, 2].reshape(head_shape).astype(jnp.bfloat16)
    attention_result, log_sums = lax.map(attend_forward, (queries, keys_all, values, prefix_len))
    flattened_heads = attention_result.reshape(local_seqs, LEN, head_cols)
    partial_out = jnp.einsum(
        "woh,ch->woc", flattened_heads, output_weight_gathered, preferred_element_type=jnp.float32
    )
    residual_branch = lax.psum_scatter(partial_out, "row", scatter_dimension=1, tiled=True)
    middle = inputs + residual_branch
    second_normalized, second_standardized, second_inverse_deviation = layer_norm_forward(
        middle, second_norm_gain, norm2_bias.astype(jnp.float32)
    )
    second_norm_input = second_normalized.astype(jnp.bfloat16)
    group_input = lax.all_gather(second_norm_input, "col", axis=0, tiled=True)
    gate_up_weight_gathered, down_weight_gathered = gather_mlp(
        gate_up_projection_weight, down_projection_weight
    )
    gate_up_values = jnp.einsum(
        "ekx,xzi->ekzi", group_input, gate_up_weight_gathered, preferred_element_type=jnp.float32
    )
    gate_vals = gate_up_values[:, :, 0]
    up_vals = gate_up_values[:, :, 1]
    sigmoid_vals = jax.nn.sigmoid(gate_vals)
    swish_vals = gate_vals * sigmoid_vals
    hidden_state = (swish_vals * up_vals).astype(jnp.bfloat16)
    mixed_state = lax.psum_scatter(
        jnp.einsum(
            "zxq,iq->zxi", hidden_state, down_weight_gathered, preferred_element_type=jnp.float32
        ).astype(jnp.bfloat16),
        "col",
        scatter_dimension=0,
        tiled=True,
    ).astype(jnp.float32)
    layer_out = (middle + mixed_state).astype(jnp.bfloat16)
    group_gradient = lax.all_gather(grad_out, "col", axis=0, tiled=True)
    gate_up_weight_backward, down_weight_backward = (gate_up_weight_gathered, down_weight_gathered)
    grad_down_full = jnp.einsum(
        "vik,viy->ky", group_gradient, hidden_state, preferred_element_type=jnp.float32
    )
    grad_hidden = jnp.einsum(
        "hba,ay->hby", group_gradient, down_weight_backward, preferred_element_type=jnp.float32
    )
    grad_gates = grad_hidden * up_vals * sigmoid_vals * (1.0 + gate_vals * (1.0 - sigmoid_vals))
    grad_ups = grad_hidden * swish_vals
    gate_up_gradient = jnp.stack([grad_gates, grad_ups], axis=2).astype(jnp.bfloat16)
    grad_gu_full = jnp.einsum(
        "gbw,gbvq->wvq", group_input, gate_up_gradient, preferred_element_type=jnp.float32
    )
    second_norm_gradient = lax.psum_scatter(
        jnp.einsum(
            "jbnk,enk->jbe",
            gate_up_gradient,
            gate_up_weight_backward,
            preferred_element_type=jnp.float32,
        ),
        "col",
        scatter_dimension=0,
        tiled=True,
    )
    grad_gu_shard, grad_down_shard = (
        lax.psum_scatter(
            grad_gu_full.astype(jnp.bfloat16), ("dp", "row"), scatter_dimension=0, tiled=True
        ).astype(jnp.float32),
        lax.psum_scatter(
            grad_down_full.astype(jnp.bfloat16), ("dp", "row"), scatter_dimension=0, tiled=True
        ).astype(jnp.float32),
    )
    middle_gradient = grad_out.astype(jnp.float32) + layer_norm_backward(
        second_norm_gradient, second_standardized, second_inverse_deviation, second_norm_gain
    )
    second_gain_gradient = jnp.sum(second_norm_gradient * second_standardized, axis=(0, 1))
    grad_bias_second = jnp.sum(second_norm_gradient, axis=(0, 1))
    sequence_gradient = lax.all_gather(
        middle_gradient.astype(jnp.bfloat16), "row", axis=1, tiled=True
    )
    query_key_value_backward, output_weight_backward = (
        query_key_value_gathered,
        output_weight_gathered,
    )
    grad_out_full = jnp.einsum(
        "ueh,uep->hp", sequence_gradient, flattened_heads, preferred_element_type=jnp.float32
    )
    heads_gradient = jnp.einsum(
        "hcu,uq->hcq", sequence_gradient, output_weight_backward, preferred_element_type=jnp.float32
    )
    heads_gradient = heads_gradient.astype(jnp.bfloat16).reshape(head_shape)
    grad_queries, grad_keys, grad_values = lax.map(
        attend_backward, (queries, keys_all, values, prefix_len, log_sums, heads_gradient)
    )
    grad_queries = unrotate(grad_queries, cosine, sines)
    grad_keys = unrotate(grad_keys, cosine, sines)
    projection_gradient = jnp.stack([grad_queries, grad_keys, grad_values], axis=2)
    projection_gradient = projection_gradient.reshape(local_seqs, LEN, 3, head_cols).astype(
        jnp.bfloat16
    )
    grad_bias_local = jnp.sum(projection_gradient, axis=(0, 1), dtype=jnp.float32)
    grad_qkv_full = jnp.einsum(
        "jam,jafz->mfz", sequence_input, projection_gradient, preferred_element_type=jnp.float32
    )
    grad_first_part = jnp.einsum(
        "zehg,phg->zep",
        projection_gradient,
        query_key_value_backward,
        preferred_element_type=jnp.float32,
    )
    first_norm_gradient = lax.psum_scatter(
        grad_first_part.astype(jnp.bfloat16), "row", scatter_dimension=1, tiled=True
    ).astype(jnp.float32)
    grad_qkv_shard, grad_wout_shard = (
        lax.psum_scatter(
            grad_qkv_full.astype(jnp.bfloat16), ("dp", "col"), scatter_dimension=0, tiled=True
        ).astype(jnp.float32),
        lax.psum_scatter(
            grad_out_full.astype(jnp.bfloat16), ("dp", "col"), scatter_dimension=0, tiled=True
        ).astype(jnp.float32),
    )
    input_token_gradient = middle_gradient + layer_norm_backward(
        first_norm_gradient, first_standardized, first_inverse_deviation, first_norm_gain
    )
    first_gain_gradient = jnp.sum(first_norm_gradient * first_standardized, axis=(0, 1))
    grad_bias_first = jnp.sum(first_norm_gradient, axis=(0, 1))
    col_offset = lax.axis_index("row") * head_cols
    bias_full = lax.dynamic_update_slice(
        jnp.zeros((3, model_width), jnp.float32), grad_bias_local, (jnp.int32(0), col_offset)
    )
    summed = lax.psum(
        (first_gain_gradient, grad_bias_first, second_gain_gradient, grad_bias_second, bias_full),
        ("dp", "row", "col"),
    )
    grad_qkv_bias = lax.dynamic_slice_in_dim(summed[4], col_offset, head_cols, 1)
    return (
        layer_out,
        input_token_gradient,
        summed[0],
        summed[1],
        grad_qkv_shard,
        grad_qkv_bias,
        grad_wout_shard,
        summed[2],
        summed[3],
        grad_gu_shard,
        grad_down_shard,
    )


def solution(mesh):
    in_specs = (
        P(("dp", "col"), "row", None),
        P(("dp", "col")),
        P(),
        P(),
        P(("dp", "col"), None, "row"),
        P(None, "row"),
        P(("dp", "col"), "row"),
        P(),
        P(),
        P(("dp", "row"), None, "col"),
        P(("dp", "row"), "col"),
        P(("dp", "col"), "row", None),
    )
    out_specs = (
        P(("dp", "col"), "row", None),
        P(("dp", "col"), "row", None),
        P(),
        P(),
        P(("dp", "col"), None, "row"),
        P(None, "row"),
        P(("dp", "col"), "row"),
        P(),
        P(),
        P(("dp", "row"), None, "col"),
        P(("dp", "row"), "col"),
    )
    return jax.shard_map(body, mesh=mesh, in_specs=in_specs, out_specs=out_specs, check_vma=False)
```

profile of v0, /device:TPU:10, one launch (start us, length us, event | category | flops | bytes accessed | tf_op | source)
XLA Modules:
  0.0 1744.5 jit_solution(16572784761236038617)
XLA Ops:
  17.4 51.5 %all-gather.9.cloned.1.call-done = bf16[1,1024,2048]{2,1,0:T(8,128)(2,1)} async-done(((bf16[1,256,2048]{2,1,0:T(8,128)(2,1)}), bf16[1,1024,2048]{2,1,0:T(8,128)(2,1)}) %all-gather.9.cloned.1.call-update) | async-done | bytes 4194320 | tf_op jit(solution)/shard_map/all_gather | solution.py:177
  68.9 64.6 %all-gather.11.cloned.1.call-done = bf16[2048,3,512]{0,2,1:T(8,128)(2,1)} async-done(((bf16[256,3,512]{0,2,1:T(8,128)(2,1)}), bf16[2048,3,512]{0,2,1:T(8,128)(2,1)}) %all-gather.11.cloned.1.call-update) | async-done | bytes 6291472 | tf_op jit(solution)/shard_map/all_gather | solution.py:139
  146.9 47.7 %while.47 = (s32[]{:T(128)}, bf16[2,512,8,64]{1,3,2,0:T(8,128)(2,1)S(1)}, f32[2,8,512]{2,1,0:T(8,128)S(1)}, s32[2]{0:T(128)S(1)}, s32[]{:T(128)}, /*index=5*/bf1...) while((s32[]{:T(128)}, ...), condition=%wide.region_5.6_spmd, body=%wide.region_2.5_spmd.sunk | while | flops 1125381632 | bytes 55711928 | solution.py:87
  204.4 86.8 %reduce-scatter.11.cloned.1.call-done = f32[1,256,2048]{2,1,0:T(8,128)} async-done(((f32[1,1024,2048]{2,1,0:T(8,128)}), f32[1,256,2048]{2,1,0:T(8,128)}) %reduce-scatter.11.cloned.1.call-update) | async-done | bytes 2097168 | tf_op jit(solution)/shard_map/reduce_scatter | solution.py:200
  306.1 252.5 %all-gather.17.cloned.1.call-done = bf16[2048,2,2816]{2,0,1:T(8,128)(2,1)} async-done(((bf16[128,2,2816]{2,0,1:T(8,128)(2,1)}), bf16[2048,2,2816]{2,0,1:T(8,128)(2,1)}) %all-gather.17.cloned.1.call-update) | async-done | bytes 23068688 | tf_op jit(solution)/shard_map/all_gather | solution.py:146
  558.6 19.7 %fusion.29 = f32[2,256,2,2816]{3,1,2,0:T(8,128)} fusion(bf16[2048,2,2816]{2,0,1:T(8,128)(2,1)} %all-gather.17.cloned.1.call-done, bf16[2,256,2048]{2,1,0:T(8,128)(2,1)} %all-gather.15.cloned.1.call-done), kind=kOutput, calls=%fused_computation.46 | convolution fusion | flops 11811160064 | bytes 36700160 | tf_op jit(solution)/shard_map/ekx,xzi->ekzi/dot_general | solution.py:210
  578.2 136.4 %all-gather.19.cloned.1.call-done = bf16[2048,2816]{1,0:T(8,128)(2,1)} async-done(((bf16[128,2816]{1,0:T(8,128)(2,1)}), bf16[2048,2816]{1,0:T(8,128)(2,1)}) %all-gather.19.cloned.1.call-update) | async-done | bytes 11534352 | tf_op jit(solution)/shard_map/all_gather | solution.py:147
  714.7 15.6 fusion.58
  730.3 20.0 %fusion.44 = f32[2,256,2048]{2,1,0:T(8,128)} fusion(bf16[2048,2,2816]{2,0,1:T(8,128)(2,1)} %all-gather.17.cloned.1.call-done, bf16[2,256,1,2816]{3,1,0,2:T(8,128)(2,1)} %get-tuple-element.298, bf16[2,256,1,2816]{3,1,0,2:T(8,128)(2,1)} %get-tuple-element.297), kind=kOutput, calls=%fused_computation.73 | convolution fusion | flops 11814043648 | bytes 33030144 | tf_op jit(solution)/shard_map/jbnk,enk->jbe/dot_general | solution.py:242
  781.9 53.6 %all-gather.23.cloned.1.call-done = bf16[1,1024,2048]{2,1,0:T(8,128)(2,1)} async-done(((bf16[1,256,2048]{2,1,0:T(8,128)(2,1)}), bf16[1,1024,2048]{2,1,0:T(8,128)(2,1)}) %all-gather.23.cloned.1.call-update) | async-done | bytes 4194320 | tf_op jit(solution)/shard_map/all_gather | solution.py:265
  852.7 15.3 copy.74
  874.4 157.3 %while.48 = (s32[]{:T(128)}, f32[1024,8,64]{0,2,1:T(8,128)}, f32[1024,8,64]{0,2,1:T(8,128)}, f32[2,512,8,64]{1,0,3,2:T(2,128)}, s32[2]{0:T(128)S(1)}, /*index=5*...) while((s32[]{:T(128)}, f32[1024,8,64]{0,2,1:T(8,128)}, ...), condition=%wide.region_15.16_spmd.clone, body=%wide.region_13.15_spmd.clone.sunk | while | flops 2726032896 | bytes 296835584 | solution.py:133
  888.7 15.2 multiply_reduce_fusion.6
  933.0 19.5 %dynamic_update_slice.38 = f32[2,512,8,64]{1,0,3,2:T(2,128)} dynamic-update-slice(f32[2,512,8,64]{1,0,3,2:T(2,128)} %get-tuple-element.495, f32[1,512,8,64]{1,0,3,2:T(1,128)S(1)} %copy.94, s32[]{:T(128)S(6)} %copy.111, s32[]{:T(128)} %constant.88.clone.1..sunk.1, s32[]{:T(128)} %constant.88.clone.1..sunk.1, s32[]{:T(128)} %constant.88.clone.1..sunk.1) | dynamic-update-slice | bytes 2097156 | tf_op jit(solution)/shard_map/while/body/eval_jaxpr/while/body/jit(dynamic_update_index_in_dim)/dynamic_update_slice | solution.py:133
  966.4 15.2 multiply_reduce_fusion.6
  1012.2 19.5 %dynamic_update_slice.38 = f32[2,512,8,64]{1,0,3,2:T(2,128)} dynamic-update-slice(f32[2,512,8,64]{1,0,3,2:T(2,128)} %get-tuple-element.495, f32[1,512,8,64]{1,0,3,2:T(1,128)S(1)} %copy.94, s32[]{:T(128)S(6)} %copy.111, s32[]{:T(128)} %constant.88.clone.1..sunk.1, s32[]{:T(128)} %constant.88.clone.1..sunk.1, s32[]{:T(128)} %constant.88.clone.1..sunk.1) | dynamic-update-slice | bytes 2097156 | tf_op jit(solution)/shard_map/while/body/eval_jaxpr/while/body/jit(dynamic_update_index_in_dim)/dynamic_update_slice | solution.py:133
  1048.1 11.9 fusion.47
  1060.0 11.7 convolution_convert_fusion
  1071.8 20.0 %bitcast_convert_fusion = bf16[2048,2,2816]{2,0,1:T(8,128)(2,1)} fusion(bf16[2,256,1,2816]{3,1,0,2:T(8,128)(2,1)} %get-tuple-element.298, bf16[2,256,1,2816]{3,1,0,2:T(8,128)(2,1)} %get-tuple-element.297, bf16[2,256,2048]{2,1,0:T(8,128)(2,1)} %all-gather.15.cloned.1.call-done), kind=kOutput, calls=%fused_computation.42 | convolution fusion | flops 11834228736 | bytes 30932992 | tf_op jit(solution)/shard_map/gbw,gbvq->wvq/dot_general | solution.py:238
  1094.3 30.2 %reduce-scatter.25.cloned.1.call-done = bf16[128,2816]{1,0:T(8,128)(2,1)} async-done(((bf16[2048,2816]{1,0:T(8,128)(2,1)}), bf16[128,2816]{1,0:T(8,128)(2,1)}) %reduce-scatter.25.cloned.1.call-update) | async-done | bytes 720912
  1129.2 50.7 %reduce-scatter.17.cloned.1.call-done = bf16[1,256,2048]{2,1,0:T(8,128)(2,1)} async-done(((bf16[1,1024,2048]{2,1,0:T(8,128)(2,1)}), bf16[1,256,2048]{2,1,0:T(8,128)(2,1)}) %reduce-scatter.17.cloned.1.call-update) | async-done | bytes 1048592 | tf_op jit(solution)/shard_map/reduce_scatter | solution.py:298
  1182.3 42.9 %all-reduce = (f32[2048]{0:T(1024)}, f32[2048]{0:T(1024)}, f32[3,2048]{1,0:T(4,128)S(1)}, f32[2048]{0:T(1024)}, f32[2048]{0:T(1024)}) all-reduce(f32[2048]{0:T(1024)S(1)} %get-tuple-element.241, f32[2048]{0:T(1024)S(1)} %get-tuple-element.245, ...), channel_id=1, replica_groups=mesh['dp'=4,'row'=4,'col'=2] {'dp','row','col'}, use_global_device_ids=true, to_apply=%region_20.21 | all-reduce | flops 14336 | bytes 114688 | tf_op jit(solution)/shard_map/psum | solution.py:318
  1229.1 21.0 %reduce-scatter.19.cloned.1.call-done = bf16[256,3,512]{2,0,1:T(8,128)(2,1)} async-done(((bf16[2048,3,512]{2,0,1:T(8,128)(2,1)}), bf16[256,3,512]{2,0,1:T(8,128)(2,1)}) %reduce-scatter.19.cloned.1.call-update) | async-done | bytes 786448 | tf_op jit(solution)/shard_map/reduce_scatter | solution.py:302
  1252.6 480.8 %reduce-scatter.23.cloned.1.call-done = bf16[128,2,2816]{2,0,1:T(8,128)(2,1)} async-done(((bf16[2048,2,2816]{2,0,1:T(8,128)(2,1)}), bf16[128,2,2816]{2,0,1:T(8,128)(2,1)}) %reduce-scatter.23.cloned.1.call-update) | async-done | bytes 1441808 | tf_op jit(solution)/shard_map/reduce_scatter | solution.py:253
  (231 shorter events, 256.4 us)
Async XLA Ops:
  7.2 61.8 %all-gather.9.cloned.1.call-start = ((), (), s32[]{:S(2)}) async-start(), calls=%async_computation.8 | async-start | bytes 5242880 | tf_op jit(solution)/shard_map/all_gather | solution.py:177
  15.1 118.5 %all-gather.11.cloned.1.call-start = ((), (), s32[]{:S(2)}) async-start(), calls=%async_computation.9 | async-start | bytes 7077888 | tf_op jit(solution)/shard_map/all_gather | solution.py:139
  16.3 179.7 %all-gather.13.cloned.1.call-start = ((), (), s32[]{:S(2)}) async-start(), calls=%async_computation.10 | async-start | bytes 2359296 | tf_op jit(solution)/shard_map/all_gather | solution.py:140
  17.1 274.1 %reduce-scatter.11.cloned.1.call-start = ((), (), s32[]{:S(2)}) async-start(), calls=%async_computation.11 | async-start | bytes 10485760 | tf_op jit(solution)/shard_map/reduce_scatter | solution.py:200
  17.4 128.2 %copy-start.9 = (f32[1024,8]{0,1:T(8,128)}, f32[1024,8]{0,1:T(8,128)S(1)}, u32[]{:S(2)}) copy-start(f32[1024,8]{0,1:T(8,128)S(1)} %get-tuple-element.315) | copy-start | bytes 98308
  17.4 128.2 %copy-start.11 = (f32[1024,8]{0,1:T(8,128)}, f32[1024,8]{0,1:T(8,128)S(1)}, u32[]{:S(2)}) copy-start(f32[1024,8]{0,1:T(8,128)S(1)} %get-tuple-element.316) | copy-start | bytes 98308
  203.7 102.4 %all-gather.15.cloned.1.call-start = ((), (), s32[]{:S(2)}) async-start(), calls=%async_computation.12 | async-start | bytes 3145728 | tf_op jit(solution)/shard_map/all_gather | solution.py:206
  295.1 263.5 %all-gather.17.cloned.1.call-start = ((), (), s32[]{:S(2)}) async-start(), calls=%async_computation.13 | async-start | bytes 24510464 | tf_op jit(solution)/shard_map/all_gather | solution.py:146
  297.8 280.5 %all-gather.21.cloned.1.call-start = ((), (), s32[]{:S(2)}) async-start(), calls=%async_computation.16 | async-start | bytes 3145728 | tf_op jit(solution)/shard_map/all_gather | solution.py:227
  298.5 416.2 %all-gather.19.cloned.1.call-start = ((), (), s32[]{:S(2)}) async-start(), calls=%async_computation.14 | async-start | bytes 12255232 | tf_op jit(solution)/shard_map/all_gather | solution.py:147
  299.3 463.6 %reduce-scatter.15.cloned.1.call-start = ((), (), s32[]{:S(2)}) async-start(), calls=%async_computation.17 | async-start | bytes 6291456 | tf_op jit(solution)/shard_map/reduce_scatter | solution.py:241
  750.3 26.3 %reduce-scatter.13.cloned.1.call-start = ((), (), s32[]{:S(2)}) async-start(), calls=%async_computation.15 | async-start | bytes 3145728 | tf_op jit(solution)/shard_map/reduce_scatter | solution.py:218
  761.2 74.3 %all-gather.23.cloned.1.call-start = ((), (), s32[]{:S(2)}) async-start(), calls=%async_computation.18 | async-start | bytes 5242880 | tf_op jit(solution)/shard_map/all_gather | solution.py:265
  781.9 310.5 %reduce-scatter.21.cloned.1.call-start = ((), (), s32[]{:S(2)}) async-start(), calls=%async_computation.21 | async-start | bytes 2359296 | tf_op jit(solution)/shard_map/reduce_scatter | solution.py:305
  841.7 282.7 %reduce-scatter.25.cloned.1.call-start = ((), (), s32[]{:S(2)}) async-start(), calls=%async_computation.23 | async-start | bytes 12255232
  868.1 311.9 %reduce-scatter.17.cloned.1.call-start = ((), (), s32[]{:S(2)}) async-start(), calls=%async_computation.19 | async-start | bytes 5242880 | tf_op jit(solution)/shard_map/reduce_scatter | solution.py:298
  1060.0 190.1 %reduce-scatter.19.cloned.1.call-start = ((), (), s32[]{:S(2)}) async-start(), calls=%async_computation.20 | async-start | bytes 7077888 | tf_op jit(solution)/shard_map/reduce_scatter | solution.py:302
  1071.8 661.6 %reduce-scatter.23.cloned.1.call-start = ((), (), s32[]{:S(2)}) async-start(), calls=%async_computation.22 | async-start | bytes 24510464 | tf_op jit(solution)/shard_map/reduce_scatter | solution.py:253
  1092.3 87.6 %copy-start.4 = (bf16[1,256,2048]{2,1,0:T(8,128)(2,1)S(1)}, bf16[1,256,2048]{2,1,0:T(8,128)(2,1)}, u32[]{:S(2)}) copy-start(bf16[1,256,2048]{2,1,0:T(8,128)(2,1)} %param.16) | copy-start | bytes 3145732
  1092.4 87.6 %copy-start.16 = (f32[2048]{0:T(1024)S(1)}, f32[2048]{0:T(1024)}, u32[]{:S(2)}) copy-start(f32[2048]{0:T(1024)} %copy-done.15) | copy-start | bytes 24580
  1092.4 87.6 %copy-start.20 = (f32[256]{0:T(256)S(1)}, f32[256]{0:T(256)}, u32[]{:S(2)}) copy-start(f32[256]{0:T(256)} %copy-done.19) | copy-start | bytes 3076
  1094.3 87.9 %copy-start.17 = (f32[2048]{0:T(1024)S(1)}, f32[2048]{0:T(1024)}, u32[]{:S(2)}) copy-start(f32[2048]{0:T(1024)} %get-tuple-element.238) | copy-start | bytes 24580
  1094.3 87.9 %copy-start.18 = (f32[2048]{0:T(1024)S(1)}, f32[2048]{0:T(1024)}, u32[]{:S(2)}) copy-start(f32[2048]{0:T(1024)} %get-tuple-element.243) | copy-start | bytes 24580
  1094.3 131.4 %copy-start.5 = (f32[1,256,2048]{2,1,0:T(8,128)S(1)}, f32[1,256,2048]{2,1,0:T(8,128)}, u32[]{:S(2)}) copy-start(f32[1,256,2048]{2,1,0:T(8,128)} %get-tuple-element.290) | copy-start | bytes 6291460
  (34 other events, 455.4 us)
Sparse Core Ops, SparseCore 0:
  15.2 53.6 all-gather.8
  71.1 62.3 all-gather.10
  135.1 30.0 all-gather.12
  203.8 87.2 reduce-scatter.10
  295.2 10.8 all-gather.14
  309.3 249.2 all-gather.16
  560.1 11.2 all-gather.20
  574.1 140.5 all-gather.18
  750.4 12.3 reduce-scatter.14
  765.5 11.0 reduce-scatter.12
  782.0 53.4 all-gather.22
  841.9 32.3 reduce-scatter.20
  876.5 247.9 reduce-scatter.24
  1127.3 52.5 reduce-scatter.16
  1182.1 67.9 reduce-scatter.18
  1252.3 481.0 reduce-scatter.22
where the time goes:
time: 1750 us; the launch traced here: 1740 us
  waiting for transfers between devices  1250 us (71%)
  matrix products  252 us (14%)
  local copies, waits for them, and re-layouts  97.1 us (6%)
  other arithmetic  68.7 us (4%)
  blocking collectives  42.9 us (2%)
  loops' own time  18.9 us (1%)
    reduce_scatter x1, waiting for transfers between devices, body(): lax.psum_scatter(grad_gu_full.astype(jnp.bfloat16), ('dp', 'row'), scatte...  481 us
    all_gather x1, waiting for transfers between devices, gather_mlp(): lax.all_gather(gate_up_projection_weight, ('dp', 'row'), axis=0, tiled=True)  252 us
    all_gather x1, waiting for transfers between devices, gather_mlp(): lax.all_gather(down_projection_weight, ('dp', 'row'), axis=0, tiled=True)  136 us
    reduce_scatter x1, waiting for transfers between devices, body(): lax.psum_scatter(partial_out, 'row', scatter_dimension=1, tiled=True)  86.8 us
    all_gather x1, waiting for transfers between devices, gather_attention(): lax.all_gather(query_key_value_weight, ('dp', 'col'), axis=0, tiled=True)  64.6 us
    all_gather x1, waiting for transfers between devices, body(): lax.all_gather(middle_gradient.astype(jnp.bfloat16), 'row', axis=1, tiled...  53.6 us
    all_gather x1, waiting for transfers between devices, body(): sequence_input = lax.all_gather(first_norm_input, 'row', axis=1, tiled=True)  51.5 us
    reduce_scatter x1, waiting for transfers between devices, body(): lax.psum_scatter(grad_first_part.astype(jnp.bfloat16), 'row', scatter_dim...  50.7 us
  transfers between devices with their start and end apart: 16, of which 13 were waited for; matrix products, arithmetic and copies ran while one was open for 19% of the time, Pallas kernels for 0%

commit v1 on v0

v1 whole, which is shorter than its diff:
```python
import math

import jax
import jax.numpy as jnp
from jax import lax
from jax.sharding import PartitionSpec as P

HD = 64
ROT = 16

norm_eps = 1e-05
rope_base = 10000.0
masked_fill = -1e30

bf16 = jnp.bfloat16
f32 = jnp.float32


def layer_norm_forward(values, norm_gain, norm_shift):
    centre = jnp.mean(values, axis=-1, keepdims=True)
    centred = values - centre
    variance = jnp.mean(centred * centred, axis=-1, keepdims=True)
    inverse = lax.rsqrt(variance + norm_eps)
    normed = centred * inverse
    return (normed * norm_gain + norm_shift, normed, inverse)


def layer_norm_backward(incoming, normed, inverse, norm_gain):
    scaled = incoming * norm_gain
    inner = jnp.mean(scaled, axis=-1, keepdims=True)
    along = jnp.mean(scaled * normed, axis=-1, keepdims=True)
    return inverse * (scaled - inner - normed * along)


def rotary_tables(length):
    half_rot = ROT // 2
    freqs = rope_base ** (-jnp.arange(half_rot, dtype=f32) * 2.0 / ROT)
    angles = jnp.arange(length, dtype=f32)[:, None] * freqs[None, :]
    return (jnp.cos(angles)[:, None, :], jnp.sin(angles)[:, None, :])


def rotate(heads, cosine, sines):
    half_rot = ROT // 2
    first = heads[..., :half_rot]
    second = heads[..., half_rot:ROT]
    return jnp.concatenate(
        [first * cosine - second * sines, second * cosine + first * sines, heads[..., ROT:]],
        axis=-1,
    )


def dot(left, right, dims):
    return lax.dot_general(left, right, (dims, ((), ())), preferred_element_type=f32)


def nn(left, right):
    return dot(left, right, ((1,), (0,)))


def nt(left, right):
    return dot(left, right, ((1,), (1,)))


def tn(left, right):
    return dot(left, right, ((0,), (0,)))


def visible(length, prefix):
    place = jnp.arange(length)
    return (place[None, :] <= place[:, None]) | (place[None, :] < prefix)


def attend_forward(queries, keys_all, values, prefix):
    scale = 1.0 / math.sqrt(HD)
    scores = jnp.einsum("qhd,khd->hqk", queries, keys_all, preferred_element_type=f32) * scale
    scores = jnp.where(visible(queries.shape[0], prefix)[None], scores, masked_fill)
    row_top = jnp.max(scores, axis=-1, keepdims=True)
    exp_scores = jnp.exp(scores - row_top)
    row_total = jnp.sum(exp_scores, axis=-1, keepdims=True)
    attn_probs = (exp_scores / row_total).astype(bf16)
    result = jnp.einsum("hqk,khd->qhd", attn_probs, values, preferred_element_type=f32)
    return result.astype(bf16), (row_top + jnp.log(row_total))


def attend_backward(queries, keys_all, values, prefix, log_sums, grad_rows):
    scale = 1.0 / math.sqrt(HD)
    scores = jnp.einsum("qhd,khd->hqk", queries, keys_all, preferred_element_type=f32) * scale
    allowed = visible(queries.shape[0], prefix)[None]
    attn_probs = jnp.where(allowed, jnp.exp(scores - log_sums), 0.0)
    grad_probs = jnp.einsum("qhd,khd->hqk", grad_rows, values, preferred_element_type=f32)
    inner = jnp.sum(attn_probs * grad_probs, axis=-1, keepdims=True)
    grad_scores = (attn_probs * (grad_probs - inner)).astype(bf16)
    grad_q = jnp.einsum("hqk,khd->qhd", grad_scores, keys_all, preferred_element_type=f32) * scale
    grad_k = jnp.einsum("hqk,qhd->khd", grad_scores, queries, preferred_element_type=f32) * scale
    grad_v = jnp.einsum(
        "hqk,qhd->khd", attn_probs.astype(bf16), grad_rows, preferred_element_type=f32
    )
    return grad_q, grad_k, grad_v


def make_body(mesh):
    R = mesh.shape["row"]
    C = mesh.shape["col"]
    N = max(R, C)

    def row_permute(block, k):
        return lax.ppermute(block, "row", [(i, i ^ k) for i in range(R)])

    def gather_rel(block):
        if R != 4:
            return [block] + [row_permute(block, k) for k in range(1, R)]
        half = block.shape[0] // 2
        one = row_permute(block, 1)
        two = row_permute(block, 2)
        top = row_permute(one[:half], 2)
        low = row_permute(two[half:], 1)
        return [block, one, two, jnp.concatenate([top, low], axis=0)]

    def scatter_rel(blocks):
        if R != 4:
            total = blocks[0]
            for k in range(1, R):
                total = total + row_permute(blocks[k].astype(bf16), k).astype(f32)
            return total
        half = blocks[0].shape[0] // 2
        b = [(x[:half], x[half:]) for x in blocks]
        top0 = row_permute(b[1][0].astype(bf16), 1)
        top2 = row_permute(b[3][0].astype(bf16), 1)
        low0 = row_permute(b[2][1].astype(bf16), 2)
        low1 = row_permute(b[3][1].astype(bf16), 2)
        top2 = row_permute((b[2][0].astype(f32) + top2.astype(f32)).astype(bf16), 2)
        low1 = row_permute((b[1][1].astype(f32) + low1.astype(f32)).astype(bf16), 1)
        top = b[0][0].astype(f32) + top0.astype(f32) + top2.astype(f32)
        low = b[0][1].astype(f32) + low0.astype(f32) + low1.astype(f32)
        return jnp.concatenate([top, low], axis=0)

    def xor_blocks(array, r):
        size = array.shape[0] // R
        return jnp.concatenate(
            [lax.dynamic_slice_in_dim(array, (r ^ k) * size, size, 0) for k in range(R)], axis=0
        )

    def source_place(s, c):
        return (s % (R // C)) * C + c if C <= R else c

    def source_dest(s, c, k):
        slot = source_place(s, c) ^ k
        if C <= R:
            return slot, s // (R // C)
        q = C // R
        return slot // q, s * q + slot % q

    def exchange_pairs(k):
        pairs = []
        for s in range(R):
            for c in range(C):
                dr, dc = source_dest(s, c, k)
                pairs.append((s * C + c, dr * C + dc))
        return pairs

    def spread_weights(pieces, u, v):
        out = jnp.zeros(pieces.shape, pieces.dtype)
        for k in range(N):
            sent = lax.dynamic_index_in_dim(pieces, u ^ k, 0, keepdims=True)
            got = lax.ppermute(sent, ("row", "col"), exchange_pairs(k))
            out = lax.dynamic_update_slice_in_dim(out, got, v ^ k, 0)
        return out

    def return_weights(pieces, u, v):
        out = jnp.zeros(pieces.shape, pieces.dtype)
        for k in range(N):
            sent = lax.dynamic_index_in_dim(pieces, v ^ k, 0, keepdims=True)
            got = lax.ppermute(sent, ("row", "col"), [(b, a) for a, b in exchange_pairs(k)])
            out = lax.dynamic_update_slice_in_dim(out, got, u ^ k, 0)
        return out

    def sum_everywhere(array):
        for name in ("col", "row", "dp"):
            size = mesh.shape[name]
            step = 1
            while step < size:
                array = array + lax.ppermute(array, name, [(i, i ^ step) for i in range(size)])
                step *= 2
        return array

    def body(
        tokens,
        prefix_len,
        norm1_gain,
        norm1_bias,
        query_key_value_weight,
        query_key_value_bias,
        attention_output_weight,
        norm2_gain,
        norm2_bias,
        gate_up_projection_weight,
        down_projection_weight,
        grad_out,
    ):
        r = lax.axis_index("row")
        c = lax.axis_index("col")
        block = tokens.shape[1]
        length = block * R
        width = tokens.shape[2]
        head_cols = query_key_value_weight.shape[2]
        heads = head_cols // HD
        prefix = prefix_len[0]
        w_rows, _, ff_local = gate_up_projection_weight.shape
        ff_slice = ff_local // R
        ff = ff_slice * C
        q_rows = max(1, C // R)
        u = source_place(r, c)
        v = r if C <= R else r * q_rows + c % q_rows

        cosine, sines = rotary_tables(length)
        gain1 = norm1_gain.astype(f32)
        gain2 = norm2_gain.astype(f32)
        inputs = tokens[0].astype(f32)
        first, first_std, first_inv = layer_norm_forward(inputs, gain1, norm1_bias.astype(f32))
        seq_in = jnp.concatenate(gather_rel(first.astype(bf16)), axis=0)

        w_qkv = lax.all_gather(
            query_key_value_weight.reshape(-1, 3 * head_cols), ("dp", "col"), axis=0, tiled=True
        )
        w_out = lax.all_gather(attention_output_weight, ("dp", "col"), axis=0, tiled=True)

        packed = jnp.concatenate(
            [
                gate_up_projection_weight[:, 0].reshape(w_rows, R, ff_slice),
                gate_up_projection_weight[:, 1].reshape(w_rows, R, ff_slice),
                down_projection_weight.reshape(w_rows, R, ff_slice),
            ],
            axis=2,
        )
        packed = packed.transpose(1, 0, 2).reshape(R, q_rows, w_rows // q_rows, 3 * ff_slice)
        packed = packed.reshape(R * q_rows, w_rows // q_rows, 3 * ff_slice)
        arrived = spread_weights(packed, u, v)
        a_rows = N // C
        arrived = arrived.reshape(a_rows, C, w_rows // q_rows, 3, ff_slice)
        arrived = arrived.transpose(3, 0, 2, 1, 4).reshape(3, a_rows * w_rows // q_rows, ff)
        gu_shard = jnp.concatenate([arrived[0], arrived[1]], axis=1)
        w_gu = lax.all_gather(gu_shard, ("dp", "col"), axis=0, tiled=True)
        w_down = lax.all_gather(arrived[2], ("dp", "col"), axis=0, tiled=True)

        dy = grad_out[0]
        dy_rel = jnp.concatenate(gather_rel(dy), axis=0)

        projected = nn(seq_in, w_qkv) + query_key_value_bias.astype(f32).reshape(-1)
        projected = xor_blocks(projected, r).reshape(length, 3, heads, HD)
        queries = rotate(projected[:, 0], cosine, sines).astype(bf16)
        keys_all = rotate(projected[:, 1], cosine, sines).astype(bf16)
        values = projected[:, 2].astype(bf16)
        attended, log_sums = attend_forward(queries, keys_all, values, prefix)
        attended = xor_blocks(attended.reshape(length, head_cols), r)
        own = nt(attended[:block], w_out)
        others = nt(attended[block:], w_out).astype(bf16)
        residual = scatter_rel([own] + [others[k * block : (k + 1) * block] for k in range(R - 1)])
        middle = inputs + residual

        second, second_std, second_inv = layer_norm_forward(
            middle, gain2, norm2_bias.astype(f32)
        )
        second_in = jnp.concatenate(gather_rel(second.astype(bf16)), axis=0)
        gate_up = nn(second_in, w_gu)
        gate_vals = gate_up[:, :ff]
        up_vals = gate_up[:, ff:]
        sig = jax.nn.sigmoid(gate_vals)
        swish = gate_vals * sig
        hidden = (swish * up_vals).astype(bf16)
        grad_down = tn(dy_rel, hidden).astype(bf16)
        grad_down = lax.psum_scatter(grad_down, ("dp", "col"), scatter_dimension=0, tiled=True)
        grad_hidden = nn(dy_rel, w_down)
        grad_gate = grad_hidden * up_vals * sig * (1.0 + gate_vals * (1.0 - sig))
        grad_up = grad_hidden * swish
        grad_gu_vals = jnp.concatenate([grad_gate.astype(bf16), grad_up.astype(bf16)], axis=1)
        own = nt(grad_gu_vals[:block], w_gu)
        others = nt(grad_gu_vals[block:], w_gu).astype(bf16)
        grad_second = scatter_rel(
            [own] + [others[k * block : (k + 1) * block] for k in range(R - 1)]
        )
        grad_gu = tn(second_in, grad_gu_vals).astype(bf16)
        grad_gu = lax.psum_scatter(grad_gu, ("dp", "col"), scatter_dimension=0, tiled=True)
        own = nt(hidden[:block], w_down)
        others = nt(hidden[block:], w_down).astype(bf16)
        mixed = scatter_rel([own] + [others[k * block : (k + 1) * block] for k in range(R - 1)])
        layer_out = (middle + mixed).astype(bf16)

        grad_middle = dy.astype(f32) + layer_norm_backward(
            grad_second, second_std, second_inv, gain2
        )
        gain2_grad = jnp.sum(grad_second * second_std, axis=0)
        bias2_grad = jnp.sum(grad_second, axis=0)

        branch = jnp.concatenate(gather_rel(grad_middle.astype(bf16)), axis=0)
        grad_heads = nn(branch, w_out).astype(bf16)
        grad_wout = tn(branch, attended).astype(bf16)
        grad_wout = lax.psum_scatter(grad_wout, ("dp", "col"), scatter_dimension=0, tiled=True)
        grad_heads = xor_blocks(grad_heads, r).reshape(length, heads, HD)
        grad_q, grad_k, grad_v = attend_backward(
            queries, keys_all, values, prefix, log_sums, grad_heads
        )
        grad_proj = jnp.stack(
            [rotate(grad_q, cosine, -sines), rotate(grad_k, cosine, -sines), grad_v], axis=1
        )
        grad_proj = grad_proj.reshape(length, 3 * head_cols).astype(bf16)
        grad_proj = xor_blocks(grad_proj, r)
        bias_local = jnp.sum(grad_proj, axis=0, dtype=f32).reshape(3, head_cols)
        grad_wqkv = tn(seq_in, grad_proj).astype(bf16)
        grad_wqkv = lax.psum_scatter(grad_wqkv, ("dp", "col"), scatter_dimension=0, tiled=True)
        own = nt(grad_proj[:block], w_qkv)
        others = nt(grad_proj[block:], w_qkv).astype(bf16)
        grad_first = scatter_rel(
            [own] + [others[k * block : (k + 1) * block] for k in range(R - 1)]
        )
        input_grad = grad_middle + layer_norm_backward(grad_first, first_std, first_inv, gain1)
        gain1_grad = jnp.sum(grad_first * first_std, axis=0)
        bias1_grad = jnp.sum(grad_first, axis=0)

        col_offset = r * head_cols
        bias_full = lax.dynamic_update_slice(
            jnp.zeros((3, width), f32), bias_local, (jnp.int32(0), col_offset)
        )
        early = jnp.concatenate([gain2_grad[None], bias2_grad[None], bias_full], axis=0)
        early = sum_everywhere(early)
        late = sum_everywhere(jnp.stack([gain1_grad, bias1_grad]))
        grad_bias = lax.dynamic_slice_in_dim(early[2:], col_offset, head_cols, 1)

        a = a_rows * w_rows // q_rows
        back = jnp.stack([grad_gu[:, :ff], grad_gu[:, ff:], grad_down]).reshape(
            3, a_rows, w_rows // q_rows, C, ff_slice
        )
        back = back.transpose(1, 3, 2, 0, 4).reshape(N, w_rows // q_rows, 3 * ff_slice)
        home = return_weights(back, u, v).reshape(R, w_rows, 3, ff_slice)
        home = home.transpose(1, 2, 0, 3).reshape(w_rows, 3, ff_local).astype(f32)
        return (
            layer_out[None],
            input_grad[None],
            late[0],
            late[1],
            grad_wqkv.astype(f32).reshape(-1, 3, head_cols),
            grad_bias,
            grad_wout.astype(f32),
            early[0],
            early[1],
            home[:, :2],
            home[:, 2],
        )

    return body


def solution(mesh):
    in_specs = (
        P(("dp", "col"), "row", None),
        P(("dp", "col")),
        P(),
        P(),
        P(("dp", "col"), None, "row"),
        P(None, "row"),
        P(("dp", "col"), "row"),
        P(),
        P(),
        P(("dp", "row"), None, "col"),
        P(("dp", "row"), "col"),
        P(("dp", "col"), "row", None),
    )
    out_specs = (
        P(("dp", "col"), "row", None),
        P(("dp", "col"), "row", None),
        P(),
        P(),
        P(("dp", "col"), None, "row"),
        P(None, "row"),
        P(("dp", "col"), "row"),
        P(),
        P(),
        P(("dp", "row"), None, "col"),
        P(("dp", "row"), "col"),
    )
    return jax.shard_map(
        make_body(mesh), mesh=mesh, in_specs=in_specs, out_specs=out_specs, check_vma=False
    )
```

time: 1750 us -> 769 us (0.44)
  waiting for transfers between devices: 1250 us -> 260 us
  starting transfers between devices: 0.65 us -> 63.1 us
  blocking collectives: 42.9 us -> 0 us
  matrix products: 252 us -> 231 us
  loops' own time: 18.9 us -> 0 us
    reduce_scatter x7 -> x4, waiting for transfers between devices: 652 us -> 0.01 us  [the longest x1 0.01 us: body(): lax.psum_scatter(grad_down, ('dp', 'col'), scatter_dimension=0, tiled=True)]
    all_gather x8 -> x4, waiting for transfers between devices: 565 us -> 0.03 us  [the longest x1 0.02 us: body(): lax.all_gather(attention_output_weight, ('dp', 'col'), axis=0, tiled=True)]
    ppermute x0 -> x58, waiting for transfers between devices: none -> 259 us  [the longest x40 195 us: row_permute(): return lax.ppermute(block, 'row', [(i, i ^ k) for i in range(R)])]
    ppermute x0 -> x58, starting transfers between devices: none -> 62.6 us  [the longest x40 35.8 us: row_permute(): return lax.ppermute(block, 'row', [(i, i ^ k) for i in range(R)])]
    psum x1 -> x0, blocking collectives: 42.9 us -> none  [body(): lax.psum((first_gain_gradient, grad_bias_first, second_gain_gradient, gra...]
    dynamic_update_slice x5 -> x9, local copies, waits for them, and re-layouts: 41.3 us -> 1.65 us  [the longest x4 1.34 us: return_weights(): out = lax.dynamic_update_slice_in_dim(out, got, u ^ k, 0)]
    unnamed x17 -> x8, waiting for transfers between devices: 32.4 us -> 0.81 us
    dot_general x26 -> x22, matrix products: 252 us -> 231 us  [the longest x16 140 us: dot(): lax.dot_general(left, right, (dims, ((), ())), preferred_element_type=f32)]
  transfers between devices with their start and end apart: 16 -> 66, of which waited for: 13 -> 42; matrix products, arithmetic and copies ran while one was open for 19% -> 49% of each run, Pallas kernels for 0% -> 0%
where the time goes in v1:
time: 769 us; the launch traced here: 756 us
  waiting for transfers between devices  260 us (34%)
  matrix products  231 us (30%)
  local copies, waits for them, and re-layouts  101 us (13%)
  other arithmetic  84.9 us (11%)
  starting transfers between devices  63.1 us (8%)
  between operations  16.6 us (2%)
    ppermute x40, waiting for transfers between devices, row_permute(): return lax.ppermute(block, 'row', [(i, i ^ k) for i in range(R)])  195 us
    dot_general x16, matrix products, dot(): lax.dot_general(left, right, (dims, ((), ())), preferred_element_type=f32)  140 us
    unnamed x163, local copies, waits for them, and re-layouts  39 us
    ppermute x40, starting transfers between devices, row_permute(): return lax.ppermute(block, 'row', [(i, i ^ k) for i in range(R)])  35.8 us
    convert_element_type x1, other arithmetic, attend_backward(): grad_scores = (attn_probs * (grad_probs - inner)).astype(bf16)  28.8 us
    dot_general x1, matrix products, attend_backward(): jnp.einsum('qhd,khd->hqk', grad_rows, values, preferred_element_type=f32)  24.3 us
    another operation x6, local copies, waits for them, and re-layouts, body(): jnp.stack([grad_gu[:, :ff], grad_gu[:, ff:], grad_down])  24 us
    ppermute x10, waiting for transfers between devices, sum_everywhere(): lax.ppermute(array, name, [(i, i ^ step) for i in range(size)])  22.8 us
  transfers between devices with their start and end apart: 66, of which 42 were waited for; matrix products, arithmetic and copies ran while one was open for 49% of the time, Pallas kernels for 0%

profile of v1, /device:TPU:10, one launch (start us, length us, event | category | flops | bytes accessed | tf_op | source)
XLA Modules:
  0.0 756.3 jit_solution(4899007792306347195)
XLA Ops:
  63.1 21.7 %collective-permute-done = bf16[256,2048]{1,0:T(8,128)(2,1)S(1)} collective-permute-done((bf16[256,2048]{1,0:T(8,128)(2,1)}, bf16[256,2048]{1,0:T(8,128)(2,1)S(1)}, u32[]{:S(2)}, u32[]{:S(2)}) %collective-permute-start) | collective-permute-done | bytes 1048608 | tf_op jit(solution)/shard_map/ppermute | solution.py:107
  105.4 10.1 %convolution_add_fusion = f32[1024,1536]{1,0:T(8,128)S(1)} fusion(bf16[1024,2048]{1,0:T(8,128)(2,1)} %constant_dynamic-update-slice_fusion, bf16[2048,1536]{0,1:T(8,128)(2,1)} %all-gather.5.cloned.1.call-done, f32[1536]{0:T(1024)S(1)} %reshape.463), kind=kOutput, calls=%fused_computation.29 | convolution fusion | flops 6444023808 | bytes 16783360 | tf_op jit(solution)/shard_map/dot_general | solution.py:53
  128.6 14.2 %select_reduce_fusion = (f32[8,1024]{1,0:T(8,128)S(1)}, f32[8,1024,1024]{1,2,0:T(8,128)}) fusion(pred[1024,1024]{0,1:T(8,128)(4,1)S(1)} %fusion.14, bf16[1024,8,48]{0,2,1:T(8,128)(2,1)S(1)} %slice.497, bf16[1024,8,8]{0,2,1:T(8,128)(2,1)S(1)} %get-tuple-element.135, bf16[1024,8,8]{0,2,1:T(8,128)(2,1)S(1)} %get-tuple-element.136, ...), kind=kOutput, calls=%fused_computation.5 | convolution fusion | flops 1105190912 | bytes 36732928 | tf_op jit(solution)/shard_map/qhd,khd->hqk/dot_general | solution.py:75
  142.9 14.4 %fusion = f32[8,1024]{1,0:T(8,128)S(1)} fusion(f32[8,1024,1024]{1,2,0:T(8,128)} %get-tuple-element.143, f32[8,1024]{1,0:T(8,128)S(1)} %get-tuple-element.142, pred[1024,1024]{0,1:T(8,128)(4,1)S(1)} %fusion.14), kind=kLoop, calls=%fused_computation.6 | loop fusion | flops 33546240 | bytes 34668544 | tf_op jit(solution)/shard_map/reduce_sum | solution.py:79
  157.3 16.5 %fusion.50 = bf16[8,64,1024]{2,1,0:T(8,128)(2,1)S(1)} fusion(f32[8,1024,1024]{1,2,0:T(8,128)} %get-tuple-element.143, f32[8,1024]{1,0:T(8,128)S(1)} %fusion, f32[8,1024]{1,0:T(8,128)S(1)} %get-tuple-element.142, pred[1024,1024]{0,1:T(8,128)(4,1)S(1)} %fusion.14, f32[1024,3,8,64]{0,3,2,1:T(8,128)} %bitcast.153), kind=kOutput, calls=%fused_computation.98 | convolution fusion | flops 1116209152 | bytes 36765696 | tf_op jit(solution)/shard_map/hqk,khd->qhd/dot_general | solution.py:81
  182.8 10.1 %collective-permute-done.8 = bf16[128,2048]{1,0:T(8,128)(2,1)S(1)} collective-permute-done((bf16[128,2048]{1,0:T(8,128)(2,1)S(1)}, bf16[128,2048]{1,0:T(8,128)(2,1)S(1)}, u32[]{:S(2)}, u32[]{:S(2)}) %collective-permute-start.8) | collective-permute-done | bytes 524320 | tf_op jit(solution)/shard_map/ppermute | solution.py:107
  195.4 21.6 %collective-permute-done.24 = bf16[256,2048]{1,0:T(8,128)(2,1)S(1)} collective-permute-done((bf16[256,2048]{1,0:T(8,128)(2,1)S(1)}, bf16[256,2048]{1,0:T(8,128)(2,1)S(1)}, u32[]{:S(2)}, u32[]{:S(2)}) %collective-permute-start.24) | collective-permute-done | bytes 1048608 | tf_op jit(solution)/shard_map/ppermute | solution.py:107
  218.2 10.1 %collective-permute-done.4 = bf16[128,2048]{1,0:T(8,128)(2,1)S(1)} collective-permute-done((bf16[128,2048]{1,0:T(8,128)(2,1)S(1)}, bf16[128,2048]{1,0:T(8,128)(2,1)S(1)}, u32[]{:S(2)}, u32[]{:S(2)}) %collective-permute-start.4) | collective-permute-done | bytes 524320 | tf_op jit(solution)/shard_map/ppermute | solution.py:107
  228.6 9.0 %collective-permute-done.9 = bf16[128,2048]{1,0:T(8,128)(2,1)S(1)} collective-permute-done((bf16[128,2048]{1,0:T(8,128)(2,1)S(1)}, bf16[128,2048]{1,0:T(8,128)(2,1)S(1)}, u32[]{:S(2)}, u32[]{:S(2)}) %collective-permute-start.9) | collective-permute-done | bytes 524320 | tf_op jit(solution)/shard_map/ppermute | solution.py:107
  243.7 10.6 %collective-permute-done.26 = bf16[128,2048]{1,0:T(8,128)(2,1)S(1)} collective-permute-done((bf16[128,2048]{1,0:T(8,128)(2,1)S(1)}, bf16[128,2048]{1,0:T(8,128)(2,1)S(1)}, u32[]{:S(2)}, u32[]{:S(2)}) %collective-permute-start.26) | collective-permute-done | bytes 524320 | tf_op jit(solution)/shard_map/ppermute | solution.py:107
  254.3 13.0 %collective-permute-done.10 = bf16[256,2048]{1,0:T(8,128)(2,1)S(1)} collective-permute-done((bf16[256,2048]{1,0:T(8,128)(2,1)S(1)}, bf16[256,2048]{1,0:T(8,128)(2,1)S(1)}, u32[]{:S(2)}, u32[]{:S(2)}) %collective-permute-start.10) | collective-permute-done | bytes 1048608 | tf_op jit(solution)/shard_map/ppermute | solution.py:107
  287.7 19.0 %fusion.127 = f32[1024,2816]{1,0:T(8,128)} fusion(bf16[1024,2048]{1,0:T(8,128)(2,1)} %constant_dynamic-update-slice_fusion.5, bf16[2048,2816]{0,1:T(8,128)(2,1)} %all-gather.9.cloned.1.call-done), kind=kOutput, calls=%fused_computation.267 | convolution fusion | flops 11811160064 | bytes 27262976 | tf_op jit(solution)/shard_map/dot_general | solution.py:53
  306.7 16.8 %multiply_convert_fusion.2 = (bf16[1024,1408]{1,0:T(8,128)(2,1)}, bf16[1024,1408]{1,0:T(8,128)(2,1)}, bf16[1024,1408]{1,0:T(8,128)(2,1)S(1)}) fusion(f32[1024,2816]{1,0:T(8,128)} %fusion.127, bf16[1024,2048]{1,0:T(8,128)(2,1)} %copy-done.50, bf16[2048,1408]{0,1:T(8,128)(2,1)} %all-gather.11.cloned.1.call-done), kind=kOutput, calls=%fused_computation.20 | convolution fusion | flops 5927206912 | bytes 30146560 | tf_op jit(solution)/shard_map/dot_general | solution.py:53
  333.9 18.6 %convolution_convert_fusion = bf16[2048,2816]{1,0:T(8,128)(2,1)} fusion(bf16[1024,2048]{1,0:T(8,128)(2,1)} %constant_dynamic-update-slice_fusion.5, bf16[1024,1408]{1,0:T(8,128)(2,1)} %get-tuple-element.56, bf16[1024,1408]{1,0:T(8,128)(2,1)} %get-tuple-element.55), kind=kOutput, calls=%fused_computation.11 | convolution fusion | flops 11828461568 | bytes 21495808 | tf_op jit(solution)/shard_map/dot_general | solution.py:53
  352.6 13.7 %fusion.15 = bf16[768,2048]{1,0:T(8,128)(2,1)S(1)} fusion(bf16[2048,2816]{0,1:T(8,128)(2,1)} %all-gather.9.cloned.1.call-done, bf16[1024,1408]{1,0:T(8,128)(2,1)} %get-tuple-element.56, bf16[1024,1408]{1,0:T(8,128)(2,1)} %get-tuple-element.55), kind=kOutput, calls=%fused_computation.36 | convolution fusion | flops 8868593664 | bytes 20447232 | tf_op jit(solution)/shard_map/dot_general | solution.py:53
  370.7 10.7 %collective-permute-done.32 = bf16[128,2048]{1,0:T(8,128)(2,1)S(1)} collective-permute-done((bf16[128,2048]{1,0:T(8,128)(2,1)S(1)}, bf16[128,2048]{1,0:T(8,128)(2,1)S(1)}, u32[]{:S(2)}, u32[]{:S(2)}) %collective-permute-start.32) | collective-permute-done | bytes 524320 | tf_op jit(solution)/shard_map/ppermute | solution.py:107
  406.0 21.9 %collective-permute-done.34 = bf16[256,2048]{1,0:T(8,128)(2,1)S(1)} collective-permute-done((bf16[256,2048]{1,0:T(8,128)(2,1)}, bf16[256,2048]{1,0:T(8,128)(2,1)S(1)}, u32[]{:S(2)}, u32[]{:S(2)}) %collective-permute-start.34) | collective-permute-done | bytes 1048608 | tf_op jit(solution)/shard_map/ppermute | solution.py:107
  445.7 24.3 %multiply_reduce_fusion = (f32[8,1024]{1,0:T(8,128)S(1)}, f32[8,1024,1024]{1,2,0:T(8,128)}) fusion(f32[8,1024,1024]{1,2,0:T(8,128)} %get-tuple-element.143, f32[8,1024]{1,0:T(8,128)S(1)} %log_add_fusion, pred[1024,1024]{0,1:T(8,128)(4,1)S(1)} %copy-done.3, bf16[1024,8,64]{0,2,1:T(8,128)(2,1)S(1)} %bitcast.174, f32[1024,3,8,64]{0,3,2,1:T(8,128)} %bitcast.154), kind=kOutput, calls=%fused_computation.1 | convolution fusion | flops 1115676672 | bytes 70320128 | tf_op jit(solution)/shard_map/qhd,khd->hqk/dot_general | solution.py:90
  470.0 28.8 %multiply_convert_fusion = bf16[8,1024,1024]{1,2,0:T(8,128)(2,1)} fusion(f32[8,1024,1024]{1,2,0:T(8,128)} %get-tuple-element.145, f32[8,1024,1024]{1,2,0:T(8,128)} %get-tuple-element.143, f32[8,1024]{1,0:T(8,128)S(1)} %get-tuple-element.144, f32[8,1024]{1,0:T(8,128)S(1)} %log_add_fusion, pred[1024,1024]{0,1:T(8,128)(4,1)S(1)} %copy-done.3), kind=kLoop, calls=%fused_computation | loop fusion | flops 50331648 | bytes 85000192 | tf_op jit(solution)/shard_map/convert_element_type | solution.py:92
  498.8 11.4 %multiply_bitcast_fusion = f32[1024,8,64]{0,2,1:T(8,128)S(1)} fusion(bf16[8,1024,1024]{1,2,0:T(8,128)(2,1)} %multiply_convert_fusion, bf16[1024,8,48]{0,2,1:T(8,128)(2,1)} %copy-done.25, bf16[1024,8,8]{0,2,1:T(8,128)(2,1)} %copy-done.41, bf16[1024,8,8]{0,2,1:T(8,128)(2,1)} %copy-done.40), kind=kOutput, calls=%fused_computation.83 | convolution fusion | flops 1077411840 | bytes 19922944 | tf_op jit(solution)/shard_map/hqk,qhd->khd/dot_general | solution.py:94
  511.3 9.4 %multiply_bitcast_fusion.1 = f32[1024,8,64]{0,2,1:T(8,128)S(1)} fusion(bf16[8,1024,1024]{1,2,0:T(8,128)(2,1)} %multiply_convert_fusion, bf16[1024,8,48]{0,2,1:T(8,128)(2,1)} %copy-done.24, bf16[1024,8,8]{0,2,1:T(8,128)(2,1)S(1)} %copy-done.37, bf16[1024,8,8]{0,2,1:T(8,128)(2,1)S(1)} %copy-done.39), kind=kOutput, calls=%fused_computation.84 | convolution fusion | flops 1077411840 | bytes 19922944 | tf_op jit(solution)/shard_map/hqk,khd->qhd/dot_general | solution.py:93
  530.1 15.9 %fusion.55 = bf16[1024,1,8,64]{0,3,2,1:T(8,128)(2,1)} fusion(bf16[1024,8,64]{0,2,1:T(8,128)(2,1)S(1)} %bitcast.175, f32[8,1024,1024]{1,2,0:T(8,128)} %get-tuple-element.143, f32[8,1024]{1,0:T(8,128)S(1)} %log_add_fusion, pred[1024,1024]{0,1:T(8,128)(4,1)S(1)} %copy-done.3), kind=kOutput, calls=%fused_computation.105 | convolution fusion | flops 1107820544 | bytes 36732928 | tf_op jit(solution)/shard_map/hqk,qhd->khd/dot_general | solution.py:95
  612.6 10.2 %collective-permute-done.51 = f32[5,2048]{1,0:T(8,128)S(1)} collective-permute-done((f32[5,2048]{1,0:T(8,128)S(1)}, f32[5,2048]{1,0:T(8,128)S(1)}, u32[]{:S(2)}, u32[]{:S(2)}) %collective-permute-start.51) | collective-permute-done | bytes 40992 | tf_op jit(solution)/shard_map/ppermute | solution.py:182
  727.4 13.4 %collective-permute-done.56 = bf16[1,128,2112]{1,2,0:T(8,128)(2,1)S(1)} collective-permute-done((bf16[1,128,2112]{1,2,0:T(8,128)(2,1)S(1)}, bf16[1,128,2112]{1,2,0:T(8,128)(2,1)S(1)}, u32[]{:S(2)}, u32[]{:S(2)}) %collective-permute-start.56) | collective-permute-done | bytes 540704 | tf_op jit(solution)/shard_map/ppermute | solution.py:173
  (432 shorter events, 374.3 us)
Async XLA Ops:
  7.2 98.2 %all-gather.5.cloned.1.call-start = ((), (), s32[]{:S(2)}) async-start(), calls=%async_computation.4 | async-start | bytes 7077888 | tf_op jit(solution)/shard_map/all_gather | solution.py:222
  9.7 164.3 %all-gather.7.cloned.1.call-start = ((), (), s32[]{:S(2)}) async-start(), calls=%async_computation.5 | async-start | bytes 2359296 | tf_op jit(solution)/shard_map/all_gather | solution.py:225
  10.4 277.3 %all-gather.9.cloned.1.call-start = ((), (), s32[]{:S(2)}) async-start(), calls=%async_computation.6 | async-start | bytes 12976128 | tf_op jit(solution)/shard_map/all_gather | solution.py:242
  55.0 251.7 %all-gather.11.cloned.1.call-start = ((), (), s32[]{:S(2)}) async-start(), calls=%async_computation.7 | async-start | bytes 6488064 | tf_op jit(solution)/shard_map/all_gather | solution.py:243
  58.0 26.7 %collective-permute-start = (bf16[256,2048]{1,0:T(8,128)(2,1)}, bf16[256,2048]{1,0:T(8,128)(2,1)S(1)}, u32[]{:S(2)}, u32[]{:S(2)}) collective-permute-start(bf16[256,2048]{1,0:T(8,128)(2,1)} %get-tuple-element.54), channel_id=1, source_target_pairs={{0,2},{2,0},{4,6},{6,4},{1,3},{3,1},{5,7},{7,5},{8,10},{10,8},{12,... | collective-permute-start | bytes 3145736 | tf_op jit(solution)/shard_map/ppermute | solution.py:107
  60.6 29.3 %collective-permute-start.1 = (bf16[256,2048]{1,0:T(8,128)(2,1)}, bf16[256,2048]{1,0:T(8,128)(2,1)}, u32[]{:S(2)}, u32[]{:S(2)}) collective-permute-start(bf16[256,2048]{1,0:T(8,128)(2,1)} %get-tuple-element.54), channel_id=1, source_target_pairs={{0,4},{2,6},{4,0},{6,2},{1,5},{3,7},{5,1},{7,3},{8,12},{10,14},{12... | collective-permute-start | bytes 3145736 | tf_op jit(solution)/shard_map/ppermute | solution.py:107
  89.6 577.5 %reduce-scatter.11.cloned.1.call-start = ((), (), s32[]{:S(2)}) async-start(), calls=%async_computation.11 | async-start | bytes 6488064 | tf_op jit(solution)/shard_map/reduce_scatter | solution.py:271
  180.1 36.9 %collective-permute-start.24 = (bf16[256,2048]{1,0:T(8,128)(2,1)S(1)}, bf16[256,2048]{1,0:T(8,128)(2,1)S(1)}, u32[]{:S(2)}, u32[]{:S(2)}) collective-permute-start(bf16[256,2048]{1,0:T(8,128)(2,1)S(1)} %bitcast.166), channel_id=1, source_target_pairs={{0,2},{2,0},{4,6},{6,4},{1,3},{3,1},{5,7},{7,5},{8,10},{10,8},{12,... | collective-permute-start | bytes 3145736 | tf_op jit(solution)/shard_map/ppermute | solution.py:107
  181.8 46.5 %collective-permute-start.4 = (bf16[128,2048]{1,0:T(8,128)(2,1)S(1)}, bf16[128,2048]{1,0:T(8,128)(2,1)S(1)}, u32[]{:S(2)}, u32[]{:S(2)}) collective-permute-start(bf16[128,2048]{1,0:T(8,128)(2,1)S(1)} %get-tuple-element.86), channel_id=1, source_target_pairs={{0,2},{2,0},{4,6},{6,4},{1,3},{3,1},{5,7},{7,5},{8,10},{10,8},{12,... | collective-permute-start | bytes 1572872 | tf_op jit(solution)/shard_map/ppermute | solution.py:107
  182.1 46.5 %collective-permute-start.7 = (bf16[128,2048]{1,0:T(8,128)(2,1)S(1)}, bf16[128,2048]{1,0:T(8,128)(2,1)S(1)}, u32[]{:S(2)}, u32[]{:S(2)}) collective-permute-start(bf16[128,2048]{1,0:T(8,128)(2,1)S(1)} %get-tuple-element.88), channel_id=1, source_target_pairs={{0,4},{2,6},{4,0},{6,2},{1,5},{3,7},{5,1},{7,3},{8,12},{10,14},{12... | collective-permute-start | bytes 1572872 | tf_op jit(solution)/shard_map/ppermute | solution.py:107
  195.0 33.6 %collective-permute-start.6 = (bf16[128,2048]{1,0:T(8,128)(2,1)S(1)}, bf16[128,2048]{1,0:T(8,128)(2,1)S(1)}, u32[]{:S(2)}, u32[]{:S(2)}) collective-permute-start(bf16[128,2048]{1,0:T(8,128)(2,1)S(1)} %get-tuple-element.90), channel_id=1, source_target_pairs={{0,4},{2,6},{4,0},{6,2},{1,5},{3,7},{5,1},{7,3},{8,12},{10,14},{12... | collective-permute-start | bytes 1572872 | tf_op jit(solution)/shard_map/ppermute | solution.py:107
  195.3 42.3 %collective-permute-start.9 = (bf16[128,2048]{1,0:T(8,128)(2,1)S(1)}, bf16[128,2048]{1,0:T(8,128)(2,1)S(1)}, u32[]{:S(2)}, u32[]{:S(2)}) collective-permute-start(bf16[128,2048]{1,0:T(8,128)(2,1)S(1)} %get-tuple-element.91), channel_id=1, source_target_pairs={{0,2},{2,0},{4,6},{6,4},{1,3},{3,1},{5,7},{7,5},{8,10},{10,8},{12,... | collective-permute-start | bytes 1572872 | tf_op jit(solution)/shard_map/ppermute | solution.py:107
  217.0 26.0 %collective-permute-start.25 = (bf16[256,2048]{1,0:T(8,128)(2,1)S(1)}, bf16[256,2048]{1,0:T(8,128)(2,1)S(1)}, u32[]{:S(2)}, u32[]{:S(2)}) collective-permute-start(bf16[256,2048]{1,0:T(8,128)(2,1)S(1)} %bitcast.167), channel_id=1, source_target_pairs={{0,4},{2,6},{4,0},{6,2},{1,5},{3,7},{5,1},{7,3},{8,12},{10,14},{12... | collective-permute-start | bytes 3145736 | tf_op jit(solution)/shard_map/ppermute | solution.py:107
  228.3 26.0 %collective-permute-start.26 = (bf16[128,2048]{1,0:T(8,128)(2,1)S(1)}, bf16[128,2048]{1,0:T(8,128)(2,1)S(1)}, u32[]{:S(2)}, u32[]{:S(2)}) collective-permute-start(bf16[128,2048]{1,0:T(8,128)(2,1)S(1)} %slice.384), channel_id=1, source_target_pairs={{0,4},{2,6},{4,0},{6,2},{1,5},{3,7},{5,1},{7,3},{8,12},{10,14},{12... | collective-permute-start | bytes 1572872 | tf_op jit(solution)/shard_map/ppermute | solution.py:107
  240.9 35.9 %collective-permute-start.11 = (bf16[256,2048]{1,0:T(8,128)(2,1)S(1)}, bf16[256,2048]{1,0:T(8,128)(2,1)S(1)}, u32[]{:S(2)}, u32[]{:S(2)}) collective-permute-start(bf16[256,2048]{1,0:T(8,128)(2,1)S(1)} %get-tuple-element.50), channel_id=1, source_target_pairs={{0,4},{2,6},{4,0},{6,2},{1,5},{3,7},{5,1},{7,3},{8,12},{10,14},{12... | collective-permute-start | bytes 3145736 | tf_op jit(solution)/shard_map/ppermute | solution.py:107
  241.3 26.0 %collective-permute-start.10 = (bf16[256,2048]{1,0:T(8,128)(2,1)S(1)}, bf16[256,2048]{1,0:T(8,128)(2,1)S(1)}, u32[]{:S(2)}, u32[]{:S(2)}) collective-permute-start(bf16[256,2048]{1,0:T(8,128)(2,1)S(1)} %get-tuple-element.50), channel_id=1, source_target_pairs={{0,2},{2,0},{4,6},{6,4},{1,3},{3,1},{5,7},{7,5},{8,10},{10,8},{12,... | collective-permute-start | bytes 3145736 | tf_op jit(solution)/shard_map/ppermute | solution.py:107
  243.1 32.5 %collective-permute-start.27 = (bf16[128,2048]{1,0:T(8,128)(2,1)S(1)}, bf16[128,2048]{1,0:T(8,128)(2,1)S(1)}, u32[]{:S(2)}, u32[]{:S(2)}) collective-permute-start(bf16[128,2048]{1,0:T(8,128)(2,1)S(1)} %slice.385), channel_id=1, source_target_pairs={{0,2},{2,0},{4,6},{6,4},{1,3},{3,1},{5,7},{7,5},{8,10},{10,8},{12,... | collective-permute-start | bytes 1572872 | tf_op jit(solution)/shard_map/ppermute | solution.py:107
  333.9 341.2 %reduce-scatter.9.cloned.1.call-start = ((), (), s32[]{:S(2)}) async-start(), calls=%async_computation.10 | async-start | bytes 12976128 | tf_op jit(solution)/shard_map/reduce_scatter | solution.py:282
  352.6 359.0 %reduce-scatter.7.cloned.1.call-start = ((), (), s32[]{:S(2)}) async-start(), calls=%async_computation.9 | async-start | bytes 2359296 | tf_op jit(solution)/shard_map/reduce_scatter | solution.py:297
  368.5 25.8 %collective-permute-start.28 = (bf16[128,2048]{1,0:T(8,128)(2,1)S(1)}, bf16[128,2048]{1,0:T(8,128)(2,1)S(1)}, u32[]{:S(2)}, u32[]{:S(2)}) collective-permute-start(bf16[128,2048]{1,0:T(8,128)(2,1)S(1)} %get-tuple-element.74), channel_id=1, source_target_pairs={{0,2},{2,0},{4,6},{6,4},{1,3},{3,1},{5,7},{7,5},{8,10},{10,8},{12,... | collective-permute-start | bytes 1572872 | tf_op jit(solution)/shard_map/ppermute | solution.py:107
  526.5 186.9 %reduce-scatter.5.cloned.1.call-start = ((), (), s32[]{:S(2)}) async-start(), calls=%async_computation.8 | async-start | bytes 7077888 | tf_op jit(solution)/shard_map/reduce_scatter | solution.py:309
  568.7 40.8 %collective-permute-start.18 = (bf16[128,2048]{1,0:T(8,128)(2,1)}, bf16[128,2048]{1,0:T(8,128)(2,1)}, u32[]{:S(2)}, u32[]{:S(2)}) collective-permute-start(bf16[128,2048]{1,0:T(8,128)(2,1)} %get-tuple-element.80), channel_id=1, source_target_pairs={{0,2},{2,0},{4,6},{6,4},{1,3},{3,1},{5,7},{7,5},{8,10},{10,8},{12,... | collective-permute-start | bytes 1572872 | tf_op jit(solution)/shard_map/ppermute | solution.py:107
  571.4 38.6 %collective-permute-start.21 = (bf16[128,2048]{1,0:T(8,128)(2,1)}, bf16[128,2048]{1,0:T(8,128)(2,1)}, u32[]{:S(2)}, u32[]{:S(2)}) collective-permute-start(bf16[128,2048]{1,0:T(8,128)(2,1)} %get-tuple-element.82), channel_id=1, source_target_pairs={{0,4},{2,6},{4,0},{6,2},{1,5},{3,7},{5,1},{7,3},{8,12},{10,14},{12... | collective-permute-start | bytes 1572872 | tf_op jit(solution)/shard_map/ppermute | solution.py:107
  664.2 41.6 %collective-permute-start.48 = (f32[2,2048]{1,0:T(2,128)S(1)}, f32[2,2048]{1,0:T(2,128)S(1)}, u32[]{:S(2)}, u32[]{:S(2)}) collective-permute-start(f32[2,2048]{1,0:T(2,128)S(1)} %add.334), channel_id=1, source_target_pairs={{0,16},{8,24},{16,0},{24,8},{1,17},{9,25},{17,1},{25,9},{2,18},{10... | collective-permute-start | bytes 49160 | tf_op jit(solution)/shard_map/ppermute | solution.py:182
  (113 other events, 1442.6 us)
Sparse Core Ops, SparseCore 0:
  10.2 63.5 all-gather.4
  75.3 30.0 all-gather.6
  107.6 105.1 all-gather.8
  214.8 58.9 all-gather.10
  334.0 62.9 reduce-scatter.10
  399.1 117.6 reduce-scatter.8
  526.6 32.7 reduce-scatter.6
  561.7 71.2 reduce-scatter.4

commit v2 on v1

v2 whole, which is shorter than its diff:
```python
import functools
import math

import jax
import jax.numpy as jnp
from jax import lax
from jax.experimental import pallas as pl
from jax.experimental.pallas import tpu as pltpu
from jax.sharding import PartitionSpec as P

HD = 64
ROT = 16

norm_eps = 1e-05
rope_base = 10000.0
masked_fill = -1e30

bf16 = jnp.bfloat16
f32 = jnp.float32


def layer_norm_forward(values, norm_gain, norm_shift):
    centre = jnp.mean(values, axis=-1, keepdims=True)
    centred = values - centre
    variance = jnp.mean(centred * centred, axis=-1, keepdims=True)
    inverse = lax.rsqrt(variance + norm_eps)
    normed = centred * inverse
    return (normed * norm_gain + norm_shift, normed, inverse)


def layer_norm_backward(incoming, normed, inverse, norm_gain):
    scaled = incoming * norm_gain
    inner = jnp.mean(scaled, axis=-1, keepdims=True)
    along = jnp.mean(scaled * normed, axis=-1, keepdims=True)
    return inverse * (scaled - inner - normed * along)


def rotary_tables(places):
    half_rot = ROT // 2
    column = jnp.arange(2 * HD) % HD
    freqs = rope_base ** (-(column % half_rot).astype(f32) * 2.0 / ROT)
    angles = places.astype(f32)[:, None] * freqs[None, :]
    sines = jnp.sin(angles)
    cosine = jnp.where(column < ROT, jnp.cos(angles), 1.0)
    left = jnp.where((column >= half_rot) & (column < ROT), sines, 0.0)
    right = jnp.where(column < half_rot, -sines, 0.0)
    return jnp.stack([cosine, left, right])


def dot(left, right, dims):
    return lax.dot_general(left, right, (dims, ((), ())), preferred_element_type=f32)


def nn(left, right):
    return dot(left, right, ((1,), (0,)))


def nt(left, right):
    return dot(left, right, ((1,), (1,)))


def tn(left, right):
    return dot(left, right, ((0,), (0,)))


def key_blocks(jq, blocks):
    return max(jq + 1, blocks // 2)


def block_mask(qpos, kpos, jq, jk, blocks, prefix):
    if jk < jq:
        return None
    causal = kpos <= qpos
    if jk >= blocks // 2:
        return causal
    early = kpos < prefix
    return (causal | early) if jk == jq else early


def head_lane(head):
    lane = lax.broadcasted_iota(jnp.int32, (1, 2 * HD), 1)
    return (lane < HD) if head == 0 else (lane >= HD)


def forward_kernel(blocks, size, info, proj, table, qkv, out, sums):
    w = 2 * HD
    scale = 1.0 / math.sqrt(HD)
    r, prefix = info[0], info[1]
    for j in range(blocks):
        rows = pl.ds(j * size, size)
        cosine, left, right = table[0, rows], table[1, rows], table[2, rows]
        for part in range(2):
            x = proj[rows, part * w : (part + 1) * w]
            x = x * cosine + pltpu.roll(x, 8, 1) * left + pltpu.roll(x, w - 8, 1) * right
            qkv[rows, part * w : (part + 1) * w] = x.astype(bf16)
        qkv[rows, 2 * w : 3 * w] = proj[rows, 2 * w : 3 * w].astype(bf16)
    places = [pl.ds(pl.multiple_of((j ^ r) * size, size), size) for j in range(blocks)]
    for jq in range(blocks):
        count = key_blocks(jq, blocks)
        q = qkv[places[jq], 0:w].astype(f32) * scale
        qpos = jq * size + lax.broadcasted_iota(jnp.int32, (size, size), 0)
        results = []
        tops = []
        for head in range(2):
            qh = jnp.where(head_lane(head), q, 0.0).astype(bf16)
            scores = []
            for jk in range(count):
                s = nt(qh, qkv[places[jk], w : 2 * w])
                kpos = jk * size + lax.broadcasted_iota(jnp.int32, (size, size), 1)
                mask = block_mask(qpos, kpos, jq, jk, blocks, prefix)
                scores.append(s if mask is None else jnp.where(mask, s, masked_fill))
            top = jnp.max(scores[0], axis=1, keepdims=True)
            for s in scores[1:]:
                top = jnp.maximum(top, jnp.max(s, axis=1, keepdims=True))
            total = 0.0
            result = 0.0
            for jk in range(count):
                e = jnp.exp(scores[jk] - top)
                total = total + jnp.sum(e, axis=1, keepdims=True)
                result = result + nn(e.astype(bf16), qkv[places[jk], 2 * w : 3 * w])
            results.append(result / total)
            tops.append(top + jnp.log(total))
        out[places[jq], :] = jnp.where(head_lane(0), results[0], results[1]).astype(bf16)
        both = jnp.where(head_lane(0), tops[0], tops[1])
        flipped = both.T
        sums[0, jq, 0:8, :] = flipped[0:8]
        sums[0, jq, 8:16, :] = flipped[HD : HD + 8]


def backward_kernel(blocks, size, info, qkv, table, sums, grads, out, bias, qm, km, gm, acc):
    w = 2 * HD
    scale = 1.0 / math.sqrt(HD)
    r, prefix = info[0], info[1]
    for head in range(2):
        lanes = head_lane(head)
        for j in range(blocks):
            rows = pl.ds(j * size, size)
            q = qkv[rows, 0:w].astype(f32) * scale
            k = qkv[rows, w : 2 * w].astype(f32) * scale
            qm[head, rows] = jnp.where(lanes, q, 0.0).astype(bf16)
            km[head, rows] = jnp.where(lanes, k, 0.0).astype(bf16)
            gm[head, rows] = jnp.where(lanes, grads[rows, :].astype(f32), 0.0).astype(bf16)
    acc[...] = jnp.zeros_like(acc)
    places = [pl.ds(pl.multiple_of((j ^ r) * size, size), size) for j in range(blocks)]
    for jq in range(blocks):
        count = key_blocks(jq, blocks)
        rq = places[jq]
        qpos = jq * size + lax.broadcasted_iota(jnp.int32, (size, size), 1)
        grad_q = 0.0
        for head in range(2):
            top = sums[0, jq, 8 * head : 8 * head + 1, :]
            probs = []
            products = []
            inner = 0.0
            for jk in range(count):
                s = nt(qkv[places[jk], w : 2 * w], qm[head, rq])
                p = jnp.exp(s - top)
                kpos = jk * size + lax.broadcasted_iota(jnp.int32, (size, size), 0)
                mask = block_mask(qpos, kpos, jq, jk, blocks, prefix)
                if mask is not None:
                    p = jnp.where(mask, p, 0.0)
                t = p * nt(qkv[places[jk], 2 * w : 3 * w], gm[head, rq])
                inner = inner + jnp.sum(t, axis=0, keepdims=True)
                probs.append(p)
                products.append(t)
            for jk in range(count):
                rk = places[jk]
                d = (products[jk] - probs[jk] * inner).astype(bf16)
                acc[1, rk] += nn(probs[jk].astype(bf16), gm[head, rq])
                acc[0, rk] += nn(d, qm[head, rq])
                grad_q = grad_q + tn(d, km[head, rk])
        cosine, left, right = table[0, rq], table[1, rq], table[2, rq]
        x = grad_q
        x = x * cosine - pltpu.roll(x, 8, 1) * left - pltpu.roll(x, w - 8, 1) * right
        out[rq, 0:w] = x.astype(bf16)
    bias_q = 0.0
    bias_k = 0.0
    bias_v = 0.0
    for j in range(blocks):
        rows = pl.ds(j * size, size)
        x = acc[0, rows]
        x = x * table[0, rows]
        x = x - pltpu.roll(acc[0, rows], 8, 1) * table[1, rows]
        x = x - pltpu.roll(acc[0, rows], w - 8, 1) * table[2, rows]
        x = x.astype(bf16)
        y = acc[1, rows].astype(bf16)
        out[rows, w : 2 * w] = x
        out[rows, 2 * w : 3 * w] = y
        bias_q = bias_q + jnp.sum(out[rows, 0:w].astype(f32), axis=0, keepdims=True)
        bias_k = bias_k + jnp.sum(x.astype(f32), axis=0, keepdims=True)
        bias_v = bias_v + jnp.sum(y.astype(f32), axis=0, keepdims=True)
    row = jnp.concatenate([bias_q, bias_k, bias_v], axis=1)
    bias[0] = jnp.broadcast_to(row, (8, 3 * w))


def attend_forward(info, projected, table, blocks):
    length = projected.shape[0]
    w = 2 * HD
    pairs = projected.shape[1] // (3 * w)
    size = length // blocks
    spec = pltpu.PrefetchScalarGridSpec(
        num_scalar_prefetch=1,
        grid=(pairs,),
        in_specs=[
            pl.BlockSpec((length, 3 * w), lambda p, i: (0, p)),
            pl.BlockSpec((3, length, w), lambda p, i: (0, 0, 0)),
        ],
        out_specs=[
            pl.BlockSpec((length, 3 * w), lambda p, i: (0, p)),
            pl.BlockSpec((length, w), lambda p, i: (0, p)),
            pl.BlockSpec((1, blocks, 16, size), lambda p, i: (p, 0, 0, 0)),
        ],
    )
    return pl.pallas_call(
        lambda *refs: forward_kernel(blocks, size, *refs),
        grid_spec=spec,
        out_shape=[
            jax.ShapeDtypeStruct((length, 3 * w * pairs), bf16),
            jax.ShapeDtypeStruct((length, w * pairs), bf16),
            jax.ShapeDtypeStruct((pairs, blocks, 16, size), f32),
        ],
        name="attend_forward",
        compiler_params=pltpu.CompilerParams(vmem_limit_bytes=48 << 20),
    )(info, projected, table)


def attend_backward(info, qkv, table, sums, grads, blocks):
    length = qkv.shape[0]
    w = 2 * HD
    pairs = qkv.shape[1] // (3 * w)
    size = length // blocks
    spec = pltpu.PrefetchScalarGridSpec(
        num_scalar_prefetch=1,
        grid=(pairs,),
        in_specs=[
            pl.BlockSpec((length, 3 * w), lambda p, i: (0, p)),
            pl.BlockSpec((3, length, w), lambda p, i: (0, 0, 0)),
            pl.BlockSpec((1, blocks, 16, size), lambda p, i: (p, 0, 0, 0)),
            pl.BlockSpec((length, w), lambda p, i: (0, p)),
        ],
        out_specs=[
            pl.BlockSpec((length, 3 * w), lambda p, i: (0, p)),
            pl.BlockSpec((1, 8, 3 * w), lambda p, i: (p, 0, 0)),
        ],
        scratch_shapes=[
            pltpu.VMEM((2, length, w), bf16),
            pltpu.VMEM((2, length, w), bf16),
            pltpu.VMEM((2, length, w), bf16),
            pltpu.VMEM((2, length, w), f32),
        ],
    )
    return pl.pallas_call(
        lambda *refs: backward_kernel(blocks, size, *refs),
        grid_spec=spec,
        out_shape=[
            jax.ShapeDtypeStruct((length, 3 * w * pairs), bf16),
            jax.ShapeDtypeStruct((pairs, 8, 3 * w), f32),
        ],
        name="attend_backward",
        compiler_params=pltpu.CompilerParams(vmem_limit_bytes=48 << 20),
    )(info, qkv, table, sums, grads)


def pack_kernel(R, q, info, gate_up, down, out):
    fs = down.shape[1] // R
    rows = down.shape[0] // q
    for slot in range(R * q):
        span = pl.ds((slot % q) * rows, rows)
        lo = (slot // q) * fs
        k = slot ^ info[2]
        out[k, :, 0:fs] = gate_up[0, span, lo : lo + fs]
        out[k, :, fs : 2 * fs] = gate_up[1, span, lo : lo + fs]
        out[k, :, 2 * fs : 3 * fs] = down[span, lo : lo + fs]


def unpack_kernel(C, info, *refs):
    pieces, (gate_up, down, held) = refs[:-3], refs[-3:]
    rows = held.shape[1]
    ff = down.shape[1]
    fs = ff // C
    for k, piece in enumerate(pieces):
        held[k ^ info[3]] = piece[...]
    for place in range(len(pieces)):
        span = pl.ds((place // C) * rows, rows)
        lo = (place % C) * fs
        gate_up[span, lo : lo + fs] = held[place, :, 0:fs]
        gate_up[span, ff + lo : ff + lo + fs] = held[place, :, fs : 2 * fs]
        down[span, lo : lo + fs] = held[place, :, 2 * fs : 3 * fs]


def pack_back_kernel(C, info, gate_up, down, out):
    rows = out.shape[1]
    ff = down.shape[1]
    fs = ff // C
    for place in range(out.shape[0]):
        span = pl.ds((place // C) * rows, rows)
        lo = (place % C) * fs
        k = place ^ info[3]
        out[k, :, 0:fs] = gate_up[span, lo : lo + fs]
        out[k, :, fs : 2 * fs] = gate_up[span, ff + lo : ff + lo + fs]
        out[k, :, 2 * fs : 3 * fs] = down[span, lo : lo + fs]


def unpack_back_kernel(R, q, info, *refs):
    pieces, (gate_up, down, held) = refs[:-3], refs[-3:]
    rows = held.shape[1]
    fs = down.shape[1] // R
    for k, piece in enumerate(pieces):
        held[k ^ info[2]] = piece[...]
    for slot in range(len(pieces)):
        span = pl.ds((slot % q) * rows, rows)
        lo = (slot // q) * fs
        gate_up[0, span, lo : lo + fs] = held[slot, :, 0:fs].astype(f32)
        gate_up[1, span, lo : lo + fs] = held[slot, :, fs : 2 * fs].astype(f32)
        down[span, lo : lo + fs] = held[slot, :, 2 * fs : 3 * fs].astype(f32)


def prepare_kernel(info, qkv, outer, out):
    w = 2 * HD
    cols = outer.shape[1]
    for pair in range(cols // w):
        for part in range(3):
            lo = (3 * pair + part) * w
            out[:, lo : lo + w] = qkv[part, :, pair * w : (pair + 1) * w]
    out[:, 3 * cols :] = outer[...]


def finish_kernel(info, grads, qkv, outer):
    w = 2 * HD
    cols = outer.shape[1]
    for pair in range(cols // w):
        for part in range(3):
            lo = (3 * pair + part) * w
            qkv[part, :, pair * w : (pair + 1) * w] = grads[:, lo : lo + w].astype(f32)
    outer[...] = grads[:, 3 * cols :].astype(f32)


def whole_call(kernel, info, arrays, shapes, scratch=()):
    def spec(shape):
        return pl.BlockSpec(shape, lambda i, s: (0,) * len(shape))

    return pl.pallas_call(
        kernel,
        grid_spec=pltpu.PrefetchScalarGridSpec(
            num_scalar_prefetch=1,
            grid=(1,),
            in_specs=[spec(a.shape) for a in arrays],
            out_specs=[spec(a.shape) for a in shapes],
            scratch_shapes=list(scratch),
        ),
        out_shape=shapes,
        compiler_params=pltpu.CompilerParams(vmem_limit_bytes=48 << 20),
    )(info, *arrays)


def make_body(mesh):
    R = mesh.shape["row"]
    C = mesh.shape["col"]
    N = max(R, C)

    def row_permute(block, k):
        return lax.ppermute(block, "row", [(i, i ^ k) for i in range(R)])

    def gather_rel(block, after=None):
        if R != 4:
            return [block] + [row_permute(block, k) for k in range(1, R)]
        half = block.shape[0] // 2
        if after is not None:
            block, _ = lax.optimization_barrier((block, after))
        one = row_permute(block, 1)
        two = row_permute(block, 2)
        top = row_permute(one[:half], 2)
        low = row_permute(two[half:], 1)
        return [block, one, two, jnp.concatenate([top, low], axis=0)]

    def scatter_rel(blocks):
        if R != 4:
            total = blocks[0]
            for k in range(1, R):
                total = total + row_permute(blocks[k].astype(bf16), k).astype(f32)
            return total
        half = blocks[0].shape[0] // 2
        b = [(x[:half], x[half:]) for x in blocks]
        top2 = row_permute(b[3][0].astype(bf16), 1)
        low1 = row_permute(b[3][1].astype(bf16), 2)
        top0 = row_permute(b[1][0].astype(bf16), 1)
        low0 = row_permute(b[2][1].astype(bf16), 2)
        top2 = row_permute((b[2][0].astype(f32) + top2.astype(f32)).astype(bf16), 2)
        low1 = row_permute((b[1][1].astype(f32) + low1.astype(f32)).astype(bf16), 1)
        top = b[0][0].astype(f32) + top0.astype(f32) + top2.astype(f32)
        low = b[0][1].astype(f32) + low0.astype(f32) + low1.astype(f32)
        return jnp.concatenate([top, low], axis=0)

    def source_place(s, c):
        return (s % (R // C)) * C + c if C <= R else c

    def source_dest(s, c, k):
        slot = source_place(s, c) ^ k
        if C <= R:
            return slot, s // (R // C)
        q = C // R
        return slot // q, s * q + slot % q

    def exchange_pairs(k):
        pairs = []
        for s in range(R):
            for c in range(C):
                dr, dc = source_dest(s, c, k)
                pairs.append((s * C + c, dr * C + dc))
        return pairs

    def spread(packed):
        return [lax.ppermute(packed[k], ("row", "col"), exchange_pairs(k)) for k in range(N)]

    def bring_back(packed):
        return [
            lax.ppermute(packed[k], ("row", "col"), [(b, a) for a, b in exchange_pairs(k)])
            for k in range(N)
        ]

    def sum_everywhere(array):
        for name in ("col", "row", "dp"):
            size = mesh.shape[name]
            step = 1
            while step < size:
                other = lax.ppermute(array, name, [(i, i ^ step) for i in range(size)])
                step *= 2
                array = array + other
        return array

    def body(
        tokens,
        prefix_len,
        norm1_gain,
        norm1_bias,
        query_key_value_weight,
        query_key_value_bias,
        attention_output_weight,
        norm2_gain,
        norm2_bias,
        gate_up_projection_weight,
        down_projection_weight,
        grad_out,
    ):
        r = lax.axis_index("row")
        c = lax.axis_index("col")
        block = tokens.shape[1]
        width = tokens.shape[2]
        head_cols = query_key_value_weight.shape[2]
        pairs = head_cols // (2 * HD)
        places = (jnp.arange(R)[:, None] ^ r) * block + jnp.arange(block)[None, :]
        table = rotary_tables(places.reshape(-1))
        w_rows, _, ff_local = gate_up_projection_weight.shape
        ff_slice = ff_local // R
        ff = ff_slice * C
        q_rows = max(1, C // R)
        u = source_place(r, c)
        v = r if C <= R else r * q_rows + c % q_rows
        info = jnp.stack([r, prefix_len[0], u, v]).astype(jnp.int32)
        rows = w_rows // q_rows
        a_rows = N // C * rows
        piece = (3 * ff_slice + 127) // 128 * 128

        gain1 = norm1_gain.astype(f32)
        gain2 = norm2_gain.astype(f32)
        inputs = tokens[0].astype(f32)
        first, first_std, first_inv = layer_norm_forward(inputs, gain1, norm1_bias.astype(f32))
        seq_in = jnp.concatenate(gather_rel(first.astype(bf16)), axis=0)

        (attn_shard,) = whole_call(
            prepare_kernel,
            info,
            [query_key_value_weight.transpose(1, 0, 2), attention_output_weight],
            [jax.ShapeDtypeStruct((attention_output_weight.shape[0], 4 * head_cols), bf16)],
        )
        w_attn = lax.all_gather(attn_shard, ("dp", "col"), axis=0, tiled=True)
        (packed,) = whole_call(
            functools.partial(pack_kernel, R, q_rows),
            info,
            [gate_up_projection_weight.transpose(1, 0, 2), down_projection_weight],
            [jax.ShapeDtypeStruct((N, rows, piece), bf16)],
        )
        packed, seq_in = lax.optimization_barrier((packed, seq_in))
        held = pltpu.VMEM((N, rows, piece), bf16)
        gu_shard, down_shard = whole_call(
            functools.partial(unpack_kernel, C),
            info,
            spread(packed),
            [
                jax.ShapeDtypeStruct((a_rows, 2 * ff), bf16),
                jax.ShapeDtypeStruct((a_rows, ff), bf16),
            ],
            [held],
        )
        w_gu = lax.all_gather(gu_shard, ("dp", "col"), axis=0, tiled=True)
        w_down = lax.all_gather(down_shard, ("dp", "col"), axis=0, tiled=True)

        w_attn, _ = lax.optimization_barrier((w_attn, gu_shard))
        w_qkv = w_attn[:, : 3 * head_cols]
        w_out = w_attn[:, 3 * head_cols :]
        dy_rel = jnp.concatenate(gather_rel(grad_out[0], gu_shard), axis=0)
        dy = grad_out[0]
        bias = query_key_value_bias.astype(f32).reshape(3, pairs, 2 * HD).transpose(1, 0, 2)
        projected = nn(seq_in, w_qkv) + bias.reshape(-1)

        qkv, attended, log_sums = attend_forward(info, projected, table, R)
        own = nt(attended[:block], w_out)
        others = nt(attended[block:], w_out).astype(bf16)
        residual = scatter_rel([own] + [others[k * block : (k + 1) * block] for k in range(R - 1)])
        middle = inputs + residual

        second, second_std, second_inv = layer_norm_forward(
            middle, gain2, norm2_bias.astype(f32)
        )
        second_in = jnp.concatenate(gather_rel(second.astype(bf16)), axis=0)
        gate_up = nn(second_in, w_gu)
        gate_vals = gate_up[:, :ff]
        up_vals = gate_up[:, ff:]
        sig = jax.nn.sigmoid(gate_vals)
        swish = gate_vals * sig
        hidden = (swish * up_vals).astype(bf16)
        grad_down = tn(dy_rel, hidden).astype(bf16)
        _, w_down = lax.optimization_barrier((grad_down, w_down))
        grad_down = lax.psum_scatter(grad_down, ("dp", "col"), scatter_dimension=0, tiled=True)
        grad_hidden = nn(dy_rel, w_down)
        grad_gate = grad_hidden * up_vals * sig * (1.0 + gate_vals * (1.0 - sig))
        grad_up = grad_hidden * swish
        grad_gu_vals = jnp.concatenate([grad_gate.astype(bf16), grad_up.astype(bf16)], axis=1)
        own = nt(grad_gu_vals[:block], w_gu)
        others = nt(grad_gu_vals[block:], w_gu).astype(bf16)
        others, second_in = lax.optimization_barrier((others, second_in))
        grad_second = scatter_rel(
            [own] + [others[k * block : (k + 1) * block] for k in range(R - 1)]
        )
        grad_gu = tn(second_in, grad_gu_vals).astype(bf16)
        grad_gu = lax.psum_scatter(grad_gu, ("dp", "col"), scatter_dimension=0, tiled=True)

        grad_middle = dy.astype(f32) + layer_norm_backward(
            grad_second, second_std, second_inv, gain2
        )
        gain2_grad = jnp.sum(grad_second * second_std, axis=0)
        bias2_grad = jnp.sum(grad_second, axis=0)

        branch = jnp.concatenate(gather_rel(grad_middle.astype(bf16)), axis=0)
        branch, hidden = lax.optimization_barrier((branch, hidden))
        own = nt(hidden[:block], w_down)
        others = nt(hidden[block:], w_down).astype(bf16)
        mixed = scatter_rel([own] + [others[k * block : (k + 1) * block] for k in range(R - 1)])
        layer_out = (middle + mixed).astype(bf16)
        grad_heads = nn(branch, w_out).astype(bf16)
        grad_proj, bias_local = attend_backward(info, qkv, table, log_sums, grad_heads, R)
        bias_local = bias_local[:, 0].reshape(pairs, 3, 2 * HD)
        bias_local = bias_local.transpose(1, 0, 2).reshape(3, head_cols)
        grad_attn = jnp.concatenate(
            [tn(seq_in, grad_proj).astype(bf16), tn(branch, attended).astype(bf16)], axis=1
        )
        grad_attn = lax.psum_scatter(grad_attn, ("dp", "col"), scatter_dimension=0, tiled=True)
        own = nt(grad_proj[:block], w_qkv)
        others = nt(grad_proj[block:], w_qkv).astype(bf16)
        others, grad_gu = lax.optimization_barrier((others, grad_gu))
        grad_first = scatter_rel(
            [own] + [others[k * block : (k + 1) * block] for k in range(R - 1)]
        )
        input_grad = grad_middle + layer_norm_backward(grad_first, first_std, first_inv, gain1)
        gain1_grad = jnp.sum(grad_first * first_std, axis=0)
        bias1_grad = jnp.sum(grad_first, axis=0)

        col_offset = r * head_cols
        bias_full = lax.dynamic_update_slice(
            jnp.zeros((3, width), f32), bias_local, (jnp.int32(0), col_offset)
        )
        sums = jnp.stack([gain1_grad, bias1_grad, gain2_grad, bias2_grad])
        sums = sum_everywhere(jnp.concatenate([sums, bias_full], axis=0))
        grad_bias = lax.dynamic_slice_in_dim(sums[4:], col_offset, head_cols, 1)

        (packed,) = whole_call(
            functools.partial(pack_back_kernel, C),
            info,
            [grad_gu, grad_down],
            [jax.ShapeDtypeStruct((N, rows, piece), bf16)],
        )
        home_gu, home_down = whole_call(
            functools.partial(unpack_back_kernel, R, q_rows),
            info,
            bring_back(packed),
            [
                jax.ShapeDtypeStruct((2, w_rows, ff_local), f32),
                jax.ShapeDtypeStruct((w_rows, ff_local), f32),
            ],
            [held],
        )
        home_qkv, home_out = whole_call(
            finish_kernel,
            info,
            [grad_attn],
            [
                jax.ShapeDtypeStruct((3, grad_attn.shape[0], head_cols), f32),
                jax.ShapeDtypeStruct((grad_attn.shape[0], head_cols), f32),
            ],
        )
        return (
            layer_out[None],
            input_grad[None],
            sums[0],
            sums[1],
            home_qkv.transpose(1, 0, 2),
            grad_bias,
            home_out,
            sums[2],
            sums[3],
            home_gu.transpose(1, 0, 2),
            home_down,
        )

    return body


def solution(mesh):
    in_specs = (
        P(("dp", "col"), "row", None),
        P(("dp", "col")),
        P(),
        P(),
        P(("dp", "col"), None, "row"),
        P(None, "row"),
        P(("dp", "col"), "row"),
        P(),
        P(),
        P(("dp", "row"), None, "col"),
        P(("dp", "row"), "col"),
        P(("dp", "col"), "row", None),
    )
    out_specs = (
        P(("dp", "col"), "row", None),
        P(("dp", "col"), "row", None),
        P(),
        P(),
        P(("dp", "col"), None, "row"),
        P(None, "row"),
        P(("dp", "col"), "row"),
        P(),
        P(),
        P(("dp", "row"), None, "col"),
        P(("dp", "row"), "col"),
    )
    body = make_body(mesh)

    return jax.shard_map(body, mesh=mesh, in_specs=in_specs, out_specs=out_specs, check_vma=False)
```

time: 769 us -> 632 us (0.82)
  matrix products: 231 us -> 142 us
  local copies, waits for them, and re-layouts: 101 us -> 38.7 us
  Pallas kernels: 0 us -> 56.9 us
  other arithmetic: 84.9 us -> 40.3 us
  waiting for transfers between devices: 260 us -> 270 us
    dot_general x6 -> x0, matrix products: 91.7 us -> none  [the longest x1 24.3 us: attend_backward(): jnp.einsum('qhd,khd->hqk', grad_rows, values, preferred_element_type=f32)]
    pallas_call x0 -> x8, Pallas kernels: none -> 56.9 us  [the longest x1 28 us: attend_backward(): pl.pallas_call(lambda *refs: backward_kernel(blocks, size, *refs), grid_s...]
    ppermute x18 -> x13, waiting for transfers between devices: 64.3 us -> 27.1 us  [the longest x4 21.7 us: spread(): lax.ppermute(packed[k], ('row', 'col'), exchange_pairs(k))]
    reduce_scatter x2 -> x1, waiting for transfers between devices: 0.01 us -> 31.5 us  [body(): lax.psum_scatter(grad_attn, ('dp', 'col'), scatter_dimension=0, tiled=True)]
    convert_element_type x3 -> x1, other arithmetic: 31 us -> 1.84 us  [body(): hidden = (swish * up_vals).astype(bf16)]
    another operation x8 -> x0, local copies, waits for them, and re-layouts: 24.5 us -> none  [the longest x6 24 us: body(): jnp.stack([grad_gu[:, :ff], grad_gu[:, ff:], grad_down])]
    reduce_sum x2 -> x0, other arithmetic: 15.2 us -> none  [the longest x1 14.4 us: attend_forward(): row_total = jnp.sum(exp_scores, axis=-1, keepdims=True)]
    unnamed x163 -> x132, local copies, waits for them, and re-layouts: 39 us -> 25.1 us
  transfers between devices with their start and end apart: 66 -> 59, of which waited for: 42 -> 37; matrix products, arithmetic and copies ran while one was open for 49% -> 26% of each run, Pallas kernels for 0% -> 9%
where the time goes in v2:
time: 632 us; the launch traced here: 626 us
  waiting for transfers between devices  270 us (43%)
  matrix products  142 us (22%)
  starting transfers between devices  61.3 us (10%)
  Pallas kernels  56.9 us (9%)
  other arithmetic  40.3 us (6%)
  local copies, waits for them, and re-layouts  38.7 us (6%)
  between operations  16.1 us (3%)
    ppermute x40, waiting for transfers between devices, row_permute(): return lax.ppermute(block, 'row', [(i, i ^ k) for i in range(R)])  193 us
    dot_general x16, matrix products, dot(): lax.dot_general(left, right, (dims, ((), ())), preferred_element_type=f32)  142 us
    ppermute x40, starting transfers between devices, row_permute(): return lax.ppermute(block, 'row', [(i, i ^ k) for i in range(R)])  38.2 us
    reduce_scatter x1, waiting for transfers between devices, body(): lax.psum_scatter(grad_attn, ('dp', 'col'), scatter_dimension=0, tiled=True)  31.5 us
    pallas_call x1, Pallas kernels, attend_backward(): pl.pallas_call(lambda *refs: backward_kernel(blocks, size, *refs), grid_s...  28 us
    unnamed x132, local copies, waits for them, and re-layouts  25.1 us
    ppermute x4, waiting for transfers between devices, spread(): lax.ppermute(packed[k], ('row', 'col'), exchange_pairs(k))  21.7 us
    pallas_call x1, Pallas kernels, attend_forward(): pl.pallas_call(lambda *refs: forward_kernel(blocks, size, *refs), grid_sp...  18.7 us
  transfers between devices with their start and end apart: 59, of which 37 were waited for; matrix products, arithmetic and copies ran while one was open for 26% of the time, Pallas kernels for 9%

profile of v2, /device:TPU:10, one launch (start us, length us, event | category | flops | bytes accessed | tf_op | source)
XLA Modules:
  0.0 625.7 jit_solution(15113319986606815922)
XLA Ops:
  16.2 22.8 %collective-permute-done = bf16[256,2048]{1,0:T(8,128)(2,1)S(1)} collective-permute-done((bf16[256,2048]{1,0:T(8,128)(2,1)S(1)}, bf16[256,2048]{1,0:T(8,128)(2,1)S(1)}, u32[]{:S(2)}, u32[]{:S(2)}) %collective-permute-start) | collective-permute-done | bytes 1048608 | tf_op jit(solution)/shard_map/ppermute | solution.py:362
  60.7 10.5 %collective-permute-done.4.refs_0_ = bf16[128,2176]{1,0:T(8,128)(2,1)S(1)} collective-permute-done((bf16[128,2176]{1,0:T(8,128)(2,1)S(1)}, bf16[128,2176]{1,0:T(8,128)(2,1)S(1)}, u32[]{:S(2)}, u32[]{:S(2)}) %collective-permute-start.4) | collective-permute-done | bytes 557088 | tf_op jit(solution)/shard_map/ppermute | solution.py:413
  73.5 9.0 %collective-permute-done.6.refs_2_ = bf16[128,2176]{1,0:T(8,128)(2,1)S(1)} collective-permute-done((bf16[128,2176]{1,0:T(8,128)(2,1)S(1)}, bf16[128,2176]{1,0:T(8,128)(2,1)S(1)}, u32[]{:S(2)}, u32[]{:S(2)}) %collective-permute-start.6) | collective-permute-done | bytes 557088 | tf_op jit(solution)/shard_map/ppermute | solution.py:413
  92.7 11.9 %fusion.14.refs_1_ = f32[1024,1536]{1,0:T(8,128)} fusion(bf16[1024,2048]{1,0:T(8,128)(2,1)} %constant_dynamic-update-slice_fusion, bf16[2048,2048]{1,0:T(8,128)(2,1)} %all-gather.4.cloned.1.call-done, f32[1536]{0:T(1024)S(1)} %reshape.552), kind=kOutput, calls=%fused_computation.22 | convolution fusion | flops 6444023808 | bytes 16783360 | tf_op jit(solution)/shard_map/dot_general | solution.py:51
  104.6 18.7 %attend_forward.1 = (bf16[1024,1536]{1,0:T(8,128)(2,1)S(1)}, bf16[1024,512]{1,0:T(8,128)(2,1)S(1)}, f32[4,4,16,256]{3,2,1,0:T(8,128)S(1)}) custom-call(s32[4]{0:T(128)S(1)} %pad_add_fusion.info.refs_0_, f32[1024,1536]{1,0:T(8,128)} %fusion.14.refs_1_, f32[3,1024,128]{2,1,0:T(8,128)S(1)} %pad_maximum_fusion.3.refs_2_), custom_call_target="tpu_custom_call" | custom-call | tf_op jit(solution)/shard_map/attend_forward/pallas_call | solution.py:214
  133.2 10.7 %collective-permute-done.12 = bf16[128,2048]{1,0:T(8,128)(2,1)S(1)} collective-permute-done((bf16[128,2048]{1,0:T(8,128)(2,1)S(1)}, bf16[128,2048]{1,0:T(8,128)(2,1)S(1)}, u32[]{:S(2)}, u32[]{:S(2)}) %collective-permute-start.12) | collective-permute-done | bytes 524320 | tf_op jit(solution)/shard_map/ppermute | solution.py:362
  156.7 9.8 %collective-permute-done.10 = bf16[128,2048]{1,0:T(8,128)(2,1)} collective-permute-done((bf16[128,2048]{1,0:T(8,128)(2,1)}, bf16[128,2048]{1,0:T(8,128)(2,1)}, u32[]{:S(2)}, u32[]{:S(2)}) %collective-permute-start.10) | collective-permute-done | bytes 524320 | tf_op jit(solution)/shard_map/ppermute | solution.py:362
  173.2 17.2 %collective-permute-done.14 = bf16[256,2048]{1,0:T(8,128)(2,1)} collective-permute-done((bf16[256,2048]{1,0:T(8,128)(2,1)}, bf16[256,2048]{1,0:T(8,128)(2,1)}, u32[]{:S(2)}, u32[]{:S(2)}) %collective-permute-start.14) | collective-permute-done | bytes 1048608 | tf_op jit(solution)/shard_map/ppermute | solution.py:362
  197.0 9.4 %collective-permute-done.16 = bf16[128,2048]{1,0:T(8,128)(2,1)S(1)} collective-permute-done((bf16[128,2048]{1,0:T(8,128)(2,1)S(1)}, bf16[128,2048]{1,0:T(8,128)(2,1)S(1)}, u32[]{:S(2)}, u32[]{:S(2)}) %collective-permute-start.16) | collective-permute-done | bytes 524320 | tf_op jit(solution)/shard_map/ppermute | solution.py:362
  213.5 9.6 %collective-permute-done.17 = bf16[128,2048]{1,0:T(8,128)(2,1)S(1)} collective-permute-done((bf16[128,2048]{1,0:T(8,128)(2,1)S(1)}, bf16[128,2048]{1,0:T(8,128)(2,1)S(1)}, u32[]{:S(2)}, u32[]{:S(2)}) %collective-permute-start.17) | collective-permute-done | bytes 524320 | tf_op jit(solution)/shard_map/ppermute | solution.py:362
  239.0 17.3 %fusion.103 = f32[1024,2816]{1,0:T(8,128)S(1)} fusion(bf16[1024,2048]{1,0:T(8,128)(2,1)} %constant_dynamic-update-slice_fusion.10, bf16[2048,2816]{1,0:T(8,128)(2,1)} %all-gather.6.cloned.1.call-done), kind=kOutput, calls=%fused_computation.187 | convolution fusion | flops 11811160064 | bytes 27262976 | tf_op jit(solution)/shard_map/dot_general | solution.py:51
  263.2 8.6 %convolution_convert_fusion.2 = bf16[2048,1408]{1,0:T(8,128)(2,1)} fusion(bf16[1024,2048]{1,0:T(8,128)(2,1)S(1)} %copy-done.39, bf16[1024,1408]{1,0:T(8,128)(2,1)S(1)} %multiply_convert_fusion.2), kind=kOutput, calls=%fused_computation.3 | convolution fusion | flops 5908463616 | bytes 12845056 | tf_op jit(solution)/shard_map/dot_general | solution.py:51
  271.9 14.0 %multiply_convert_fusion.1 = (bf16[1024,1408]{1,0:T(8,128)(2,1)S(1)}, bf16[1024,1408]{1,0:T(8,128)(2,1)S(1)}) fusion(f32[1024,2816]{1,0:T(8,128)} %copy-done.26, bf16[1024,2048]{1,0:T(8,128)(2,1)} %copy-done.38, bf16[2048,1408]{1,0:T(8,128)(2,1)} %all-gather.8.cloned.1.call-done), kind=kOutput, calls=%fused_computation.8 | convolution fusion | flops 5924323328 | bytes 27262976 | tf_op jit(solution)/shard_map/dot_general | solution.py:51
  285.9 15.2 %fusion.17 = bf16[768,2048]{1,0:T(8,128)(2,1)} fusion(bf16[2048,2816]{1,0:T(8,128)(2,1)} %all-gather.6.cloned.1.call-done, bf16[1024,1408]{1,0:T(8,128)(2,1)S(1)} %get-tuple-element.100, bf16[1024,1408]{1,0:T(8,128)(2,1)S(1)} %get-tuple-element.99), kind=kOutput, calls=%fused_computation.27 | convolution fusion | flops 8868593664 | bytes 20447232 | tf_op jit(solution)/shard_map/dot_general | solution.py:51
  301.1 18.3 %convolution_convert_fusion = bf16[2048,2816]{1,0:T(8,128)(2,1)} fusion(bf16[1024,2048]{1,0:T(8,128)(2,1)} %constant_dynamic-update-slice_fusion.10, bf16[1024,1408]{1,0:T(8,128)(2,1)S(1)} %get-tuple-element.100, bf16[1024,1408]{1,0:T(8,128)(2,1)S(1)} %get-tuple-element.99), kind=kOutput, calls=%fused_computation | convolution fusion | flops 11828461568 | bytes 21495808 | tf_op jit(solution)/shard_map/dot_general | solution.py:51
  326.1 10.7 %collective-permute-done.23 = bf16[128,2048]{1,0:T(8,128)(2,1)S(1)} collective-permute-done((bf16[128,2048]{1,0:T(8,128)(2,1)S(1)}, bf16[128,2048]{1,0:T(8,128)(2,1)S(1)}, u32[]{:S(2)}, u32[]{:S(2)}) %collective-permute-start.23) | collective-permute-done | bytes 524320 | tf_op jit(solution)/shard_map/ppermute | solution.py:362
  361.5 19.7 %collective-permute-done.28 = bf16[256,2048]{1,0:T(8,128)(2,1)S(1)} collective-permute-done((bf16[256,2048]{1,0:T(8,128)(2,1)S(1)}, bf16[256,2048]{1,0:T(8,128)(2,1)S(1)}, u32[]{:S(2)}, u32[]{:S(2)}) %collective-permute-start.28) | collective-permute-done | bytes 1048608 | tf_op jit(solution)/shard_map/ppermute | solution.py:362
  398.0 28.0 %attend_backward.1 = (bf16[1024,1536]{1,0:T(8,128)(2,1)S(1)}, f32[4,8,384]{2,1,0:T(8,128)S(1)}) custom-call(s32[4]{0:T(128)S(1)} %pad_add_fusion.info.refs_0_, bf16[1024,1536]{1,0:T(8,128)(2,1)} %copy-done, f32[3,1024,128]{2,1,0:T(8,128)S(1)} %pad_maximum_fusion.3.refs_2_, f32[4,4,16,256]{3,2,1,0:T(8,128)S(1)} %get-tuple-element.44.refs_3_, ...), custom_call_target="tpu_custom_call" | custom-call | tf_op jit(solution)/shard_map/attend_backward/pallas_call | solution.py:252
  429.7 8.8 %convolution_convert_fusion.1 = bf16[2048,1536]{1,0:T(8,128)(2,1)} fusion(bf16[1024,2048]{1,0:T(8,128)(2,1)S(1)} %copy-done.40, bf16[1024,1536]{1,0:T(8,128)(2,1)S(1)} %get-tuple-element.46), kind=kOutput, calls=%fused_computation.2 | convolution fusion | flops 6445596672 | bytes 13631488 | tf_op jit(solution)/shard_map/dot_general | solution.py:51
  447.9 8.0 %convolution_convert_fusion.4 = bf16[768,2048]{1,0:T(8,128)(2,1)S(1)} fusion(bf16[2048,1408]{1,0:T(8,128)(2,1)} %all-gather.8.cloned.1.call-done, bf16[1024,1408]{1,0:T(8,128)(2,1)S(1)} %copy-done.31), kind=kOutput, calls=%fused_computation.30 | convolution fusion | flops 4430757888 | bytes 11075584 | tf_op jit(solution)/shard_map/dot_general | solution.py:51
  489.1 12.6 %reduce-scatter.8.cloned.1.call-done.down = bf16[256,1408]{1,0:T(8,128)(2,1)} async-done(((bf16[2048,1408]{1,0:T(8,128)(2,1)}), bf16[256,1408]{1,0:T(8,128)(2,1)}) %reduce-scatter.8.cloned.1.call-update) | async-done | bytes 720912 | tf_op jit(solution)/shard_map/reduce_scatter | solution.py:524
  511.4 8.7 %collective-permute-done.40 = bf16[128,2048]{1,0:T(8,128)(2,1)S(1)} collective-permute-done((bf16[128,2048]{1,0:T(8,128)(2,1)S(1)}, bf16[128,2048]{1,0:T(8,128)(2,1)S(1)}, u32[]{:S(2)}, u32[]{:S(2)}) %collective-permute-start.40) | collective-permute-done | bytes 524320 | tf_op jit(solution)/shard_map/ppermute | solution.py:362
  532.8 16.8 %collective-permute-done.34 = bf16[128,2048]{1,0:T(8,128)(2,1)} collective-permute-done((bf16[128,2048]{1,0:T(8,128)(2,1)}, bf16[128,2048]{1,0:T(8,128)(2,1)}, u32[]{:S(2)}, u32[]{:S(2)}) %collective-permute-start.34) | collective-permute-done | bytes 524320 | tf_op jit(solution)/shard_map/ppermute | solution.py:362
  560.3 31.5 %reduce-scatter.6.cloned.1.call-done.grads = bf16[256,2048]{1,0:T(8,128)(2,1)} async-done(((bf16[2048,2048]{1,0:T(8,128)(2,1)}), bf16[256,2048]{1,0:T(8,128)(2,1)}) %reduce-scatter.6.cloned.1.call-update) | async-done | bytes 1048592 | tf_op jit(solution)/shard_map/reduce_scatter | solution.py:557
  (333 shorter events, 261.8 us)
Async XLA Ops:
  7.2 85.5 %all-gather.4.cloned.1.call-start = ((), (), s32[]{:S(2)}) async-start(), calls=%async_computation.3 | async-start | bytes 9437184 | tf_op jit(solution)/shard_map/all_gather | solution.py:476
  11.8 227.1 %all-gather.6.cloned.1.call-start = ((), (), s32[]{:S(2)}) async-start(), calls=%async_computation.4 | async-start | bytes 12976128 | tf_op jit(solution)/shard_map/all_gather | solution.py:495
  14.7 27.1 %collective-permute-start.1 = (bf16[256,2048]{1,0:T(8,128)(2,1)S(1)}, bf16[256,2048]{1,0:T(8,128)(2,1)S(1)}, u32[]{:S(2)}, u32[]{:S(2)}) collective-permute-start(bf16[256,2048]{1,0:T(8,128)(2,1)S(1)} %get-tuple-element.98), channel_id=1, source_target_pairs={{0,4},{2,6},{4,0},{6,2},{1,5},{3,7},{5,1},{7,3},{8,12},{10,14},{12... | collective-permute-start | bytes 3145736 | tf_op jit(solution)/shard_map/ppermute | solution.py:362
  84.9 187.0 %all-gather.8.cloned.1.call-start = ((), (), s32[]{:S(2)}) async-start(), calls=%async_computation.5 | async-start | bytes 6488064 | tf_op jit(solution)/shard_map/all_gather | solution.py:496
  131.6 25.2 %collective-permute-start.8 = (bf16[128,2048]{1,0:T(8,128)(2,1)}, bf16[128,2048]{1,0:T(8,128)(2,1)}, u32[]{:S(2)}, u32[]{:S(2)}) collective-permute-start(bf16[128,2048]{1,0:T(8,128)(2,1)} %get-tuple-element.119), channel_id=1, source_target_pairs={{0,2},{2,0},{4,6},{6,4},{1,3},{3,1},{5,7},{7,5},{8,10},{10,8},{12,... | collective-permute-start | bytes 1572872 | tf_op jit(solution)/shard_map/ppermute | solution.py:362
  147.7 42.7 %collective-permute-start.14 = (bf16[256,2048]{1,0:T(8,128)(2,1)}, bf16[256,2048]{1,0:T(8,128)(2,1)}, u32[]{:S(2)}, u32[]{:S(2)}) collective-permute-start(bf16[256,2048]{1,0:T(8,128)(2,1)} %bitcast.13), channel_id=1, source_target_pairs={{0,2},{2,0},{4,6},{6,4},{1,3},{3,1},{5,7},{7,5},{8,10},{10,8},{12,... | collective-permute-start | bytes 3145736 | tf_op jit(solution)/shard_map/ppermute | solution.py:362
  149.4 329.7 %reduce-scatter.4.cloned.1.call-start = ((), (), s32[]{:S(2)}) async-start(), calls=%async_computation.6 | async-start | bytes 12976128 | tf_op jit(solution)/shard_map/reduce_scatter | solution.py:536
  155.1 39.8 %collective-permute-start.15 = (bf16[256,2048]{1,0:T(8,128)(2,1)}, bf16[256,2048]{1,0:T(8,128)(2,1)S(1)}, u32[]{:S(2)}, u32[]{:S(2)}) collective-permute-start(bf16[256,2048]{1,0:T(8,128)(2,1)} %bitcast.13), channel_id=1, source_target_pairs={{0,4},{2,6},{4,0},{6,2},{1,5},{3,7},{5,1},{7,3},{8,12},{10,14},{12... | collective-permute-start | bytes 3145736 | tf_op jit(solution)/shard_map/ppermute | solution.py:362
  172.6 40.2 %collective-permute-start.18 = (bf16[256,2048]{1,0:T(8,128)(2,1)S(1)}, bf16[256,2048]{1,0:T(8,128)(2,1)S(1)}, u32[]{:S(2)}, u32[]{:S(2)}) collective-permute-start(bf16[256,2048]{1,0:T(8,128)(2,1)S(1)} %get-tuple-element.94), channel_id=1, source_target_pairs={{0,2},{2,0},{4,6},{6,4},{1,3},{3,1},{5,7},{7,5},{8,10},{10,8},{12,... | collective-permute-start | bytes 3145736 | tf_op jit(solution)/shard_map/ppermute | solution.py:362
  192.1 36.7 %collective-permute-start.19 = (bf16[256,2048]{1,0:T(8,128)(2,1)S(1)}, bf16[256,2048]{1,0:T(8,128)(2,1)S(1)}, u32[]{:S(2)}, u32[]{:S(2)}) collective-permute-start(bf16[256,2048]{1,0:T(8,128)(2,1)S(1)} %get-tuple-element.94), channel_id=1, source_target_pairs={{0,4},{2,6},{4,0},{6,2},{1,5},{3,7},{5,1},{7,3},{8,12},{10,14},{12... | collective-permute-start | bytes 3145736 | tf_op jit(solution)/shard_map/ppermute | solution.py:362
  195.0 28.1 %collective-permute-start.17 = (bf16[128,2048]{1,0:T(8,128)(2,1)S(1)}, bf16[128,2048]{1,0:T(8,128)(2,1)S(1)}, u32[]{:S(2)}, u32[]{:S(2)}) collective-permute-start(bf16[128,2048]{1,0:T(8,128)(2,1)S(1)} %slice.311), channel_id=1, source_target_pairs={{0,2},{2,0},{4,6},{6,4},{1,3},{3,1},{5,7},{7,5},{8,10},{10,8},{12,... | collective-permute-start | bytes 1572872 | tf_op jit(solution)/shard_map/ppermute | solution.py:362
  319.4 182.3 %reduce-scatter.8.cloned.1.call-start = ((), (), s32[]{:S(2)}) async-start(), calls=%async_computation.8 | async-start | bytes 6488064 | tf_op jit(solution)/shard_map/reduce_scatter | solution.py:524
  320.0 271.9 %reduce-scatter.6.cloned.1.call-start = ((), (), s32[]{:S(2)}) async-start(), calls=%async_computation.7 | async-start | bytes 9437184 | tf_op jit(solution)/shard_map/reduce_scatter | solution.py:557
  323.0 25.1 %collective-permute-start.22 = (bf16[128,2048]{1,0:T(8,128)(2,1)S(1)}, bf16[128,2048]{1,0:T(8,128)(2,1)S(1)}, u32[]{:S(2)}, u32[]{:S(2)}) collective-permute-start(bf16[128,2048]{1,0:T(8,128)(2,1)S(1)} %get-tuple-element.113), channel_id=1, source_target_pairs={{0,2},{2,0},{4,6},{6,4},{1,3},{3,1},{5,7},{7,5},{8,10},{10,8},{12,... | collective-permute-start | bytes 1572872 | tf_op jit(solution)/shard_map/ppermute | solution.py:362
  457.4 26.1 %collective-permute-start.33 = (bf16[128,2048]{1,0:T(8,128)(2,1)}, bf16[128,2048]{1,0:T(8,128)(2,1)}, u32[]{:S(2)}, u32[]{:S(2)}) collective-permute-start(bf16[128,2048]{1,0:T(8,128)(2,1)} %get-tuple-element.110), channel_id=1, source_target_pairs={{0,2},{2,0},{4,6},{6,4},{1,3},{3,1},{5,7},{7,5},{8,10},{10,8},{12,... | collective-permute-start | bytes 1572872 | tf_op jit(solution)/shard_map/ppermute | solution.py:362
  457.5 25.9 %collective-permute-start.36 = (bf16[128,2048]{1,0:T(8,128)(2,1)}, bf16[128,2048]{1,0:T(8,128)(2,1)}, u32[]{:S(2)}, u32[]{:S(2)}) collective-permute-start(bf16[128,2048]{1,0:T(8,128)(2,1)} %get-tuple-element.108), channel_id=1, source_target_pairs={{0,4},{2,6},{4,0},{6,2},{1,5},{3,7},{5,1},{7,3},{8,12},{10,14},{12... | collective-permute-start | bytes 1572872 | tf_op jit(solution)/shard_map/ppermute | solution.py:362
  458.2 69.6 %collective-permute-start.32 = (bf16[128,2048]{1,0:T(8,128)(2,1)}, bf16[128,2048]{1,0:T(8,128)(2,1)S(1)}, u32[]{:S(2)}, u32[]{:S(2)}) collective-permute-start(bf16[128,2048]{1,0:T(8,128)(2,1)} %get-tuple-element.107), channel_id=1, source_target_pairs={{0,2},{2,0},{4,6},{6,4},{1,3},{3,1},{5,7},{7,5},{8,10},{10,8},{12,... | collective-permute-start | bytes 1572872 | tf_op jit(solution)/shard_map/ppermute | solution.py:362
  509.9 39.7 %collective-permute-start.34 = (bf16[128,2048]{1,0:T(8,128)(2,1)}, bf16[128,2048]{1,0:T(8,128)(2,1)}, u32[]{:S(2)}, u32[]{:S(2)}) collective-permute-start(bf16[128,2048]{1,0:T(8,128)(2,1)} %get-tuple-element.111), channel_id=1, source_target_pairs={{0,4},{2,6},{4,0},{6,2},{1,5},{3,7},{5,1},{7,3},{8,12},{10,14},{12... | collective-permute-start | bytes 1572872 | tf_op jit(solution)/shard_map/ppermute | solution.py:362
  520.1 31.6 %collective-permute-start.37 = (bf16[128,2048]{1,0:T(8,128)(2,1)}, bf16[128,2048]{1,0:T(8,128)(2,1)}, u32[]{:S(2)}, u32[]{:S(2)}) collective-permute-start(bf16[128,2048]{1,0:T(8,128)(2,1)} %get-tuple-element.112), channel_id=1, source_target_pairs={{0,2},{2,0},{4,6},{6,4},{1,3},{3,1},{5,7},{7,5},{8,10},{10,8},{12,... | collective-permute-start | bytes 1572872 | tf_op jit(solution)/shard_map/ppermute | solution.py:362
  521.9 73.2 %collective-permute-start.49 = (bf16[128,2176]{1,0:T(8,128)(2,1)}, bf16[128,2176]{1,0:T(8,128)(2,1)S(1)}, u32[]{:S(2)}, u32[]{:S(2)}) collective-permute-start(bf16[128,2176]{1,0:T(8,128)(2,1)} %get-tuple-element.128), channel_id=1, source_target_pairs={{0,0},{2,1},{4,2},{6,3},{1,4},{3,5},{5,6},{7,7},{8,8},{10,9},{12,1... | collective-permute-start | bytes 1671176 | tf_op jit(solution)/shard_map/ppermute | solution.py:417
  527.9 67.3 %collective-permute-start.50 = (bf16[128,2176]{1,0:T(8,128)(2,1)}, bf16[128,2176]{1,0:T(8,128)(2,1)S(1)}, u32[]{:S(2)}, u32[]{:S(2)}) collective-permute-start(bf16[128,2176]{1,0:T(8,128)(2,1)} %get-tuple-element.127), channel_id=1, source_target_pairs={{2,0},{0,1},{6,2},{4,3},{3,4},{1,5},{7,6},{5,7},{10,8},{8,9},{14,1... | collective-permute-start | bytes 1671176 | tf_op jit(solution)/shard_map/ppermute | solution.py:417
  531.4 63.7 %collective-permute-start.51 = (bf16[128,2176]{1,0:T(8,128)(2,1)}, bf16[128,2176]{1,0:T(8,128)(2,1)S(1)}, u32[]{:S(2)}, u32[]{:S(2)}) collective-permute-start(bf16[128,2176]{1,0:T(8,128)(2,1)} %get-tuple-element.126), channel_id=1, source_target_pairs={{4,0},{6,1},{0,2},{2,3},{5,4},{7,5},{1,6},{3,7},{12,8},{14,9},{8,1... | collective-permute-start | bytes 1671176 | tf_op jit(solution)/shard_map/ppermute | solution.py:417
  549.6 45.5 %collective-permute-start.52 = (bf16[128,2176]{1,0:T(8,128)(2,1)}, bf16[128,2176]{1,0:T(8,128)(2,1)S(1)}, u32[]{:S(2)}, u32[]{:S(2)}) collective-permute-start(bf16[128,2176]{1,0:T(8,128)(2,1)} %get-tuple-element.125), channel_id=1, source_target_pairs={{6,0},{4,1},{2,2},{0,3},{7,4},{5,5},{3,6},{1,7},{14,8},{12,9},{10,... | collective-permute-start | bytes 1671176 | tf_op jit(solution)/shard_map/ppermute | solution.py:417
  557.1 44.1 %collective-permute-start.45 = (f32[7,2048]{1,0:T(8,128)S(1)}, f32[7,2048]{1,0:T(8,128)S(1)}, u32[]{:S(2)}, u32[]{:S(2)}) collective-permute-start(f32[7,2048]{1,0:T(8,128)S(1)} %add.269), channel_id=1, source_target_pairs={{0,2},{2,0},{4,6},{6,4},{1,3},{3,1},{5,7},{7,5},{8,10},{10,8},{12,... | collective-permute-start | bytes 172040 | tf_op jit(solution)/shard_map/ppermute | solution.py:426
  (93 other events, 1228.8 us)
Sparse Core Ops, SparseCore 0:
  12.0 80.7 all-gather.3
  94.9 106.2 all-gather.5
  203.5 59.4 all-gather.7
  319.5 116.7 reduce-scatter.3
  438.4 63.2 reduce-scatter.7
  503.9 87.9 reduce-scatter.5

commit v3 on v2

--- a/solution.py
+++ b/solution.py
@@ -445,6 +445,7 @@
         r = lax.axis_index("row")
         c = lax.axis_index("col")
         block = tokens.shape[1]
+        length = block * R
         width = tokens.shape[2]
         head_cols = query_key_value_weight.shape[2]
         pairs = head_cols // (2 * HD)
@@ -501,7 +502,8 @@
         dy_rel = jnp.concatenate(gather_rel(grad_out[0], gu_shard), axis=0)
         dy = grad_out[0]
         bias = query_key_value_bias.astype(f32).reshape(3, pairs, 2 * HD).transpose(1, 0, 2)
-        projected = nn(seq_in, w_qkv) + bias.reshape(-1)
+        projected = nn(seq_in, w_qkv)
+        projected = projected + bias.reshape(-1)
 
         qkv, attended, log_sums = attend_forward(info, projected, table, R)
         own = nt(attended[:block], w_out)
@@ -542,19 +544,36 @@
         bias2_grad = jnp.sum(grad_second, axis=0)
 
         branch = jnp.concatenate(gather_rel(grad_middle.astype(bf16)), axis=0)
-        branch, hidden = lax.optimization_barrier((branch, hidden))
         own = nt(hidden[:block], w_down)
         others = nt(hidden[block:], w_down).astype(bf16)
-        mixed = scatter_rel([own] + [others[k * block : (k + 1) * block] for k in range(R - 1)])
+        others, _ = lax.optimization_barrier((others, branch))
+        mixed = scatter_rel(
+            [own] + [others[k * block : (k + 1) * block] for k in range(R - 1)]
+        )
         layer_out = (middle + mixed).astype(bf16)
         grad_heads = nn(branch, w_out).astype(bf16)
         grad_proj, bias_local = attend_backward(info, qkv, table, log_sums, grad_heads, R)
         bias_local = bias_local[:, 0].reshape(pairs, 3, 2 * HD)
         bias_local = bias_local.transpose(1, 0, 2).reshape(3, head_cols)
-        grad_attn = jnp.concatenate(
-            [tn(seq_in, grad_proj).astype(bf16), tn(branch, attended).astype(bf16)], axis=1
-        )
-        grad_attn = lax.psum_scatter(grad_attn, ("dp", "col"), scatter_dimension=0, tiled=True)
+        if C == 2:
+            def columns(array, which):
+                parts = array.reshape(length, -1, C, w_attn.shape[0] // (C * mesh.shape["dp"]))
+                return lax.dynamic_index_in_dim(parts, which, 2, keepdims=False).reshape(length, -1)
+
+            def pair_sum(left, right):
+                away = tn(columns(left, 1 - c), right).astype(bf16)
+                got = lax.ppermute(away, "col", [(0, 1), (1, 0)])
+                return (tn(columns(left, c), right) + got.astype(f32)).astype(bf16)
+
+            grad_attn = jnp.concatenate(
+                [pair_sum(seq_in, grad_proj), pair_sum(branch, attended)], axis=1
+            )
+            grad_attn = lax.psum_scatter(grad_attn, "dp", scatter_dimension=0, tiled=True)
+        else:
+            grad_attn = jnp.concatenate(
+                [tn(seq_in, grad_proj).astype(bf16), tn(branch, attended).astype(bf16)], axis=1
+            )
+            grad_attn = lax.psum_scatter(grad_attn, ("dp", "col"), scatter_dimension=0, tiled=True)
         own = nt(grad_proj[:block], w_qkv)
         others = nt(grad_proj[block:], w_qkv).astype(bf16)
         others, grad_gu = lax.optimization_barrier((others, grad_gu))

time: 632 us -> 680 us (1.076)
  local copies, waits for them, and re-layouts: 38.7 us -> 128 us
  waiting for transfers between devices: 270 us -> 223 us
    unnamed x132 -> x178, local copies, waits for them, and re-layouts: 25.1 us -> 71.6 us
    reduce_scatter x1, waiting for transfers between devices: 31.5 us -> 0.01 us  [body(): lax.psum_scatter(grad_attn, 'dp', scatter_dimension=0, tiled=True)]
    dynamic_slice x0 -> x2, local copies, waits for them, and re-layouts: none -> 22.5 us  [columns(): lax.dynamic_index_in_dim(parts, which, 2, keepdims=False)]
    reshape x0 -> x2, local copies, waits for them, and re-layouts: none -> 15.7 us  [columns(): array.reshape(length, -1, C, w_attn.shape[0] // (C * mesh.shape['dp']))]
    reduce_scatter x1, waiting for transfers between devices: 12.6 us -> 0.01 us  [body(): lax.psum_scatter(grad_down, ('dp', 'col'), scatter_dimension=0, tiled=True)]
    ppermute x40, waiting for transfers between devices: 193 us -> 182 us  [row_permute(): return lax.ppermute(block, 'row', [(i, i ^ k) for i in range(R)])]
    dot_general x16 -> x18, matrix products: 142 us -> 146 us  [dot(): lax.dot_general(left, right, (dims, ((), ())), preferred_element_type=f32)]
  transfers between devices with their start and end apart: 59 -> 61, of which waited for: 37 -> 35; matrix products, arithmetic and copies ran while one was open for 26% -> 37% of each run, Pallas kernels for 9% -> 8%
where the time goes in v3:
time: 680 us; the launch traced here: 671 us
  waiting for transfers between devices  223 us (33%)
  matrix products  146 us (21%)
  local copies, waits for them, and re-layouts  128 us (19%)
  starting transfers between devices  62.2 us (9%)
  Pallas kernels  56.9 us (8%)
  other arithmetic  38.5 us (6%)
  between operations  16.3 us (2%)
    ppermute x40, waiting for transfers between devices, row_permute(): return lax.ppermute(block, 'row', [(i, i ^ k) for i in range(R)])  182 us
    dot_general x18, matrix products, dot(): lax.dot_general(left, right, (dims, ((), ())), preferred_element_type=f32)  146 us
    unnamed x178, local copies, waits for them, and re-layouts  71.6 us
    ppermute x40, starting transfers between devices, row_permute(): return lax.ppermute(block, 'row', [(i, i ^ k) for i in range(R)])  39.5 us
    pallas_call x1, Pallas kernels, attend_backward(): pl.pallas_call(lambda *refs: backward_kernel(blocks, size, *refs), grid_s...  27.9 us
    dynamic_slice x2, local copies, waits for them, and re-layouts, columns(): lax.dynamic_index_in_dim(parts, which, 2, keepdims=False)  22.5 us
    ppermute x4, waiting for transfers between devices, spread(): lax.ppermute(packed[k], ('row', 'col'), exchange_pairs(k))  21.7 us
    pallas_call x1, Pallas kernels, attend_forward(): pl.pallas_call(lambda *refs: forward_kernel(blocks, size, *refs), grid_sp...  18.7 us
  transfers between devices with their start and end apart: 61, of which 35 were waited for; matrix products, arithmetic and copies ran while one was open for 37% of the time, Pallas kernels for 8%

profile of v3, /device:TPU:10, one launch (start us, length us, event | category | flops | bytes accessed | tf_op | source)
XLA Modules:
  0.0 671.2 jit_solution(13516282913389243818)
XLA Ops:
  15.3 22.8 %collective-permute-done = bf16[256,2048]{1,0:T(8,128)(2,1)S(1)} collective-permute-done((bf16[256,2048]{1,0:T(8,128)(2,1)S(1)}, bf16[256,2048]{1,0:T(8,128)(2,1)S(1)}, u32[]{:S(2)}, u32[]{:S(2)}) %collective-permute-start) | collective-permute-done | bytes 1048608 | tf_op jit(solution)/shard_map/ppermute | solution.py:362
  41.7 9.4 %collective-permute-done.2 = bf16[128,2048]{1,0:T(8,128)(2,1)S(1)} collective-permute-done((bf16[128,2048]{1,0:T(8,128)(2,1)S(1)}, bf16[128,2048]{1,0:T(8,128)(2,1)S(1)}, u32[]{:S(2)}, u32[]{:S(2)}) %collective-permute-start.2) | collective-permute-done | bytes 524320 | tf_op jit(solution)/shard_map/ppermute | solution.py:362
  59.0 10.5 %collective-permute-done.4.refs_0_ = bf16[128,2176]{1,0:T(8,128)(2,1)S(1)} collective-permute-done((bf16[128,2176]{1,0:T(8,128)(2,1)S(1)}, bf16[128,2176]{1,0:T(8,128)(2,1)S(1)}, u32[]{:S(2)}, u32[]{:S(2)}) %collective-permute-start.4) | collective-permute-done | bytes 557088 | tf_op jit(solution)/shard_map/ppermute | solution.py:413
  92.7 11.7 %fusion.14.refs_1_ = f32[1024,1536]{1,0:T(8,128)} fusion(bf16[1024,2048]{1,0:T(8,128)(2,1)} %copy-done.32, bf16[2048,2048]{1,0:T(8,128)(2,1)} %all-gather.4.cloned.1.call-done, f32[1536]{0:T(1024)S(1)} %reshape.582), kind=kOutput, calls=%fused_computation.21 | convolution fusion | flops 6444023808 | bytes 16783360 | tf_op jit(solution)/shard_map/dot_general | solution.py:51
  104.4 18.7 %attend_forward.1 = (bf16[1024,1536]{1,0:T(8,128)(2,1)S(1)}, bf16[1024,512]{1,0:T(8,128)(2,1)S(1)}, f32[4,4,16,256]{3,2,1,0:T(8,128)S(1)}) custom-call(s32[4]{0:T(128)S(1)} %pad_add_fusion.info.refs_0_, f32[1024,1536]{1,0:T(8,128)} %fusion.14.refs_1_, f32[3,1024,128]{2,1,0:T(8,128)S(1)} %pad_maximum_fusion.3.refs_2_), custom_call_target="tpu_custom_call" | custom-call | tf_op jit(solution)/shard_map/attend_forward/pallas_call | solution.py:214
  133.4 10.7 %collective-permute-done.12 = bf16[128,2048]{1,0:T(8,128)(2,1)S(1)} collective-permute-done((bf16[128,2048]{1,0:T(8,128)(2,1)S(1)}, bf16[128,2048]{1,0:T(8,128)(2,1)S(1)}, u32[]{:S(2)}, u32[]{:S(2)}) %collective-permute-start.12) | collective-permute-done | bytes 524320 | tf_op jit(solution)/shard_map/ppermute | solution.py:362
  157.0 9.8 %collective-permute-done.10 = bf16[128,2048]{1,0:T(8,128)(2,1)} collective-permute-done((bf16[128,2048]{1,0:T(8,128)(2,1)}, bf16[128,2048]{1,0:T(8,128)(2,1)}, u32[]{:S(2)}, u32[]{:S(2)}) %collective-permute-start.10) | collective-permute-done | bytes 524320 | tf_op jit(solution)/shard_map/ppermute | solution.py:362
  173.5 17.2 %collective-permute-done.18 = bf16[256,2048]{1,0:T(8,128)(2,1)} collective-permute-done((bf16[256,2048]{1,0:T(8,128)(2,1)}, bf16[256,2048]{1,0:T(8,128)(2,1)}, u32[]{:S(2)}, u32[]{:S(2)}) %collective-permute-start.18) | collective-permute-done | bytes 1048608 | tf_op jit(solution)/shard_map/ppermute | solution.py:362
  213.7 9.5 %collective-permute-done.21 = bf16[128,2048]{1,0:T(8,128)(2,1)S(1)} collective-permute-done((bf16[128,2048]{1,0:T(8,128)(2,1)S(1)}, bf16[128,2048]{1,0:T(8,128)(2,1)S(1)}, u32[]{:S(2)}, u32[]{:S(2)}) %collective-permute-start.21) | collective-permute-done | bytes 524320 | tf_op jit(solution)/shard_map/ppermute | solution.py:362
  239.3 17.3 %fusion.103 = f32[1024,2816]{1,0:T(8,128)S(1)} fusion(bf16[1024,2048]{1,0:T(8,128)(2,1)} %constant_dynamic-update-slice_fusion.5, bf16[2048,2816]{1,0:T(8,128)(2,1)} %all-gather.6.cloned.1.call-done), kind=kOutput, calls=%fused_computation.193 | convolution fusion | flops 11811160064 | bytes 27262976 | tf_op jit(solution)/shard_map/dot_general | solution.py:51
  272.2 14.0 %multiply_convert_fusion.1 = (bf16[1024,1408]{1,0:T(8,128)(2,1)S(1)}, bf16[1024,1408]{1,0:T(8,128)(2,1)S(1)}) fusion(f32[1024,2816]{1,0:T(8,128)} %copy-done.27, bf16[1024,2048]{1,0:T(8,128)(2,1)} %copy-done.45, bf16[2048,1408]{1,0:T(8,128)(2,1)} %all-gather.8.cloned.1.call-done), kind=kOutput, calls=%fused_computation.7 | convolution fusion | flops 5924323328 | bytes 27262976 | tf_op jit(solution)/shard_map/dot_general | solution.py:51
  286.2 15.2 %fusion.17 = bf16[768,2048]{1,0:T(8,128)(2,1)} fusion(bf16[2048,2816]{1,0:T(8,128)(2,1)} %all-gather.6.cloned.1.call-done, bf16[1024,1408]{1,0:T(8,128)(2,1)S(1)} %get-tuple-element.98, bf16[1024,1408]{1,0:T(8,128)(2,1)S(1)} %get-tuple-element.97), kind=kOutput, calls=%fused_computation.28 | convolution fusion | flops 8868593664 | bytes 20447232 | tf_op jit(solution)/shard_map/dot_general | solution.py:51
  301.4 18.3 %convolution_convert_fusion = bf16[2048,2816]{1,0:T(8,128)(2,1)} fusion(bf16[1024,2048]{1,0:T(8,128)(2,1)} %constant_dynamic-update-slice_fusion.5, bf16[1024,1408]{1,0:T(8,128)(2,1)S(1)} %get-tuple-element.98, bf16[1024,1408]{1,0:T(8,128)(2,1)S(1)} %get-tuple-element.97), kind=kOutput, calls=%fused_computation | convolution fusion | flops 11828461568 | bytes 21495808 | tf_op jit(solution)/shard_map/dot_general | solution.py:51
  326.7 10.9 %collective-permute-done.23 = bf16[128,2048]{1,0:T(8,128)(2,1)S(1)} collective-permute-done((bf16[128,2048]{1,0:T(8,128)(2,1)}, bf16[128,2048]{1,0:T(8,128)(2,1)S(1)}, u32[]{:S(2)}, u32[]{:S(2)}) %collective-permute-start.23) | collective-permute-done | bytes 524320 | tf_op jit(solution)/shard_map/ppermute | solution.py:362
  372.6 11.3 %collective-permute-done.28 = bf16[256,2048]{1,0:T(8,128)(2,1)} collective-permute-done((bf16[256,2048]{1,0:T(8,128)(2,1)}, bf16[256,2048]{1,0:T(8,128)(2,1)}, u32[]{:S(2)}, u32[]{:S(2)}) %collective-permute-start.28) | collective-permute-done | bytes 1048608 | tf_op jit(solution)/shard_map/ppermute | solution.py:362
  386.7 11.2 %constant_dynamic-slice_fusion.3 = (bf16[1024,4,1,256]{3,2,1,0:T(2,128)(2,1)}, bf16[1024,4,1,256]{3,2,1,0:T(2,128)(2,1)}) fusion(bf16[1024,4,2,256]{3,2,1,0:T(2,128)(2,1)} %reshape.576, s32[]{:T(128)S(6)} %select_n.83, s32[]{:T(128)S(6)} %select_n.82), kind=kLoop, calls=%fused_computation.161 | loop fusion | bytes 8388616 | tf_op jit(solution)/shard_map/jit(dynamic_index_in_dim)/dynamic_slice | solution.py:561
  397.9 10.5 %copy.38 = bf16[1024,4,1,256]{0,3,1,2:T(8,128)(2,1)} copy(bf16[1024,4,1,256]{3,2,1,0:T(2,128)(2,1)} %get-tuple-element.99) | data formatting | bytes 4194304
  424.8 27.9 %attend_backward.1 = (bf16[1024,1536]{1,0:T(8,128)(2,1)S(1)}, f32[4,8,384]{2,1,0:T(8,128)S(1)}) custom-call(s32[4]{0:T(128)S(1)} %pad_add_fusion.info.refs_0_, bf16[1024,1536]{1,0:T(8,128)(2,1)} %copy-done, f32[3,1024,128]{2,1,0:T(8,128)S(1)} %pad_maximum_fusion.3.refs_2_, f32[4,4,16,256]{3,2,1,0:T(8,128)S(1)} %get-tuple-element.43.refs_3_, ...), custom_call_target="tpu_custom_call" | custom-call | tf_op jit(solution)/shard_map/attend_backward/pallas_call | solution.py:252
  465.4 11.3 %constant_dynamic-slice_fusion.1 = (bf16[1024,4,1,256]{3,2,1,0:T(2,128)(2,1)}, bf16[1024,4,1,256]{3,2,1,0:T(2,128)(2,1)}) fusion(bf16[1024,4,2,256]{3,2,1,0:T(2,128)(2,1)} %reshape.579, s32[]{:T(128)S(6)} %select_n.83, s32[]{:T(128)S(6)} %select_n.82), kind=kLoop, calls=%fused_computation.159 | loop fusion | bytes 8388616 | tf_op jit(solution)/shard_map/jit(dynamic_index_in_dim)/dynamic_slice | solution.py:561
  476.7 10.6 %copy.40 = bf16[1024,4,1,256]{0,3,1,2:T(8,128)(2,1)} copy(bf16[1024,4,1,256]{3,2,1,0:T(2,128)(2,1)} %get-tuple-element.101) | data formatting | bytes 4194304
  491.6 10.6 %copy.37 = bf16[1024,4,1,256]{0,3,1,2:T(8,128)(2,1)} copy(bf16[1024,4,1,256]{3,2,1,0:T(2,128)(2,1)} %get-tuple-element.100) | data formatting | bytes 4194304
  502.2 10.5 %copy.39 = bf16[1024,4,1,256]{0,3,1,2:T(8,128)(2,1)} copy(bf16[1024,4,1,256]{3,2,1,0:T(2,128)(2,1)} %get-tuple-element.102) | data formatting | bytes 4194304
  567.0 12.3 %collective-permute-done.39 = bf16[128,2048]{1,0:T(8,128)(2,1)} collective-permute-done((bf16[128,2048]{1,0:T(8,128)(2,1)}, bf16[128,2048]{1,0:T(8,128)(2,1)}, u32[]{:S(2)}, u32[]{:S(2)}) %collective-permute-start.39) | collective-permute-done | bytes 524320 | tf_op jit(solution)/shard_map/ppermute | solution.py:362
  611.1 9.8 %collective-permute-done.34 = bf16[128,2048]{1,0:T(8,128)(2,1)} collective-permute-done((bf16[128,2048]{1,0:T(8,128)(2,1)}, bf16[128,2048]{1,0:T(8,128)(2,1)}, u32[]{:S(2)}, u32[]{:S(2)}) %collective-permute-start.34) | collective-permute-done | bytes 524320 | tf_op jit(solution)/shard_map/ppermute | solution.py:362
  (389 shorter events, 332.9 us)
Async XLA Ops:
  7.2 85.5 %all-gather.4.cloned.1.call-start = ((), (), s32[]{:S(2)}) async-start(), calls=%async_computation.3 | async-start | bytes 9437184 | tf_op jit(solution)/shard_map/all_gather | solution.py:477
  11.8 227.4 %all-gather.6.cloned.1.call-start = ((), (), s32[]{:S(2)}) async-start(), calls=%async_computation.4 | async-start | bytes 12976128 | tf_op jit(solution)/shard_map/all_gather | solution.py:496
  13.7 27.1 %collective-permute-start.1 = (bf16[256,2048]{1,0:T(8,128)(2,1)S(1)}, bf16[256,2048]{1,0:T(8,128)(2,1)S(1)}, u32[]{:S(2)}, u32[]{:S(2)}) collective-permute-start(bf16[256,2048]{1,0:T(8,128)(2,1)S(1)} %get-tuple-element.96), channel_id=1, source_target_pairs={{0,4},{2,6},{4,0},{6,2},{1,5},{3,7},{5,1},{7,3},{8,12},{10,14},{12... | collective-permute-start | bytes 3145736 | tf_op jit(solution)/shard_map/ppermute | solution.py:362
  83.2 189.0 %all-gather.8.cloned.1.call-start = ((), (), s32[]{:S(2)}) async-start(), calls=%async_computation.5 | async-start | bytes 6488064 | tf_op jit(solution)/shard_map/all_gather | solution.py:497
  148.0 42.7 %collective-permute-start.18 = (bf16[256,2048]{1,0:T(8,128)(2,1)}, bf16[256,2048]{1,0:T(8,128)(2,1)}, u32[]{:S(2)}, u32[]{:S(2)}) collective-permute-start(bf16[256,2048]{1,0:T(8,128)(2,1)} %bitcast.13), channel_id=1, source_target_pairs={{0,2},{2,0},{4,6},{6,4},{1,3},{3,1},{5,7},{7,5},{8,10},{10,8},{12,... | collective-permute-start | bytes 3145736 | tf_op jit(solution)/shard_map/ppermute | solution.py:362
  149.7 404.7 %reduce-scatter.4.cloned.1.call-start = ((), (), s32[]{:S(2)}) async-start(), calls=%async_computation.6 | async-start | bytes 12976128 | tf_op jit(solution)/shard_map/reduce_scatter | solution.py:538
  155.4 39.8 %collective-permute-start.19 = (bf16[256,2048]{1,0:T(8,128)(2,1)}, bf16[256,2048]{1,0:T(8,128)(2,1)S(1)}, u32[]{:S(2)}, u32[]{:S(2)}) collective-permute-start(bf16[256,2048]{1,0:T(8,128)(2,1)} %bitcast.13), channel_id=1, source_target_pairs={{0,4},{2,6},{4,0},{6,2},{1,5},{3,7},{5,1},{7,3},{8,12},{10,14},{12... | collective-permute-start | bytes 3145736 | tf_op jit(solution)/shard_map/ppermute | solution.py:362
  173.0 40.1 %collective-permute-start.14 = (bf16[256,2048]{1,0:T(8,128)(2,1)S(1)}, bf16[256,2048]{1,0:T(8,128)(2,1)S(1)}, u32[]{:S(2)}, u32[]{:S(2)}) collective-permute-start(bf16[256,2048]{1,0:T(8,128)(2,1)S(1)} %get-tuple-element.92), channel_id=1, source_target_pairs={{0,2},{2,0},{4,6},{6,4},{1,3},{3,1},{5,7},{7,5},{8,10},{10,8},{12,... | collective-permute-start | bytes 3145736 | tf_op jit(solution)/shard_map/ppermute | solution.py:362
  192.4 36.7 %collective-permute-start.15 = (bf16[256,2048]{1,0:T(8,128)(2,1)S(1)}, bf16[256,2048]{1,0:T(8,128)(2,1)S(1)}, u32[]{:S(2)}, u32[]{:S(2)}) collective-permute-start(bf16[256,2048]{1,0:T(8,128)(2,1)S(1)} %get-tuple-element.92), channel_id=1, source_target_pairs={{0,4},{2,6},{4,0},{6,2},{1,5},{3,7},{5,1},{7,3},{8,12},{10,14},{12... | collective-permute-start | bytes 3145736 | tf_op jit(solution)/shard_map/ppermute | solution.py:362
  195.3 28.0 %collective-permute-start.21 = (bf16[128,2048]{1,0:T(8,128)(2,1)S(1)}, bf16[128,2048]{1,0:T(8,128)(2,1)S(1)}, u32[]{:S(2)}, u32[]{:S(2)}) collective-permute-start(bf16[128,2048]{1,0:T(8,128)(2,1)S(1)} %slice.316), channel_id=1, source_target_pairs={{0,2},{2,0},{4,6},{6,4},{1,3},{3,1},{5,7},{7,5},{8,10},{10,8},{12,... | collective-permute-start | bytes 1572872 | tf_op jit(solution)/shard_map/ppermute | solution.py:362
  319.7 245.2 %reduce-scatter.8.cloned.1.call-start = ((), (), s32[]{:S(2)}) async-start(), calls=%async_computation.8 | async-start | bytes 6488064 | tf_op jit(solution)/shard_map/reduce_scatter | solution.py:526
  323.5 25.4 %collective-permute-start.22 = (bf16[128,2048]{1,0:T(8,128)(2,1)}, bf16[128,2048]{1,0:T(8,128)(2,1)S(1)}, u32[]{:S(2)}, u32[]{:S(2)}) collective-permute-start(bf16[128,2048]{1,0:T(8,128)(2,1)} %get-tuple-element.115), channel_id=1, source_target_pairs={{0,2},{2,0},{4,6},{6,4},{1,3},{3,1},{5,7},{7,5},{8,10},{10,8},{12,... | collective-permute-start | bytes 1572872 | tf_op jit(solution)/shard_map/ppermute | solution.py:362
  326.7 303.9 %reduce-scatter.6.cloned.1.call-start = ((), (), s32[]{:S(2)}) async-start(), calls=%async_computation.7 | async-start | bytes 5242880 | tf_op jit(solution)/shard_map/reduce_scatter | solution.py:571
  364.2 44.2 %collective-permute-start.29 = (bf16[256,2048]{1,0:T(8,128)(2,1)}, bf16[256,2048]{1,0:T(8,128)(2,1)}, u32[]{:S(2)}, u32[]{:S(2)}) collective-permute-start(bf16[256,2048]{1,0:T(8,128)(2,1)} %get-tuple-element.90), channel_id=1, source_target_pairs={{0,4},{2,6},{4,0},{6,2},{1,5},{3,7},{5,1},{7,3},{8,12},{10,14},{12... | collective-permute-start | bytes 3145736 | tf_op jit(solution)/shard_map/ppermute | solution.py:362
  385.8 29.8 %collective-permute-start.30 = (bf16[128,2048]{1,0:T(8,128)(2,1)}, bf16[128,2048]{1,0:T(8,128)(2,1)S(1)}, u32[]{:S(2)}, u32[]{:S(2)}) collective-permute-start(bf16[128,2048]{1,0:T(8,128)(2,1)} %slice.321), channel_id=1, source_target_pairs={{0,4},{2,6},{4,0},{6,2},{1,5},{3,7},{5,1},{7,3},{8,12},{10,14},{12... | collective-permute-start | bytes 1572872 | tf_op jit(solution)/shard_map/ppermute | solution.py:362
  457.6 58.4 %collective-permute-start.49 = (bf16[1024,1536]{1,0:T(8,128)(2,1)}, bf16[1024,1536]{1,0:T(8,128)(2,1)}, u32[]{:S(2)}, u32[]{:S(2)}) collective-permute-start(bf16[1024,1536]{1,0:T(8,128)(2,1)} %convolution_convert_fusion.2), channel_id=1, source_target_pairs={{0,1},{1,0},{2,3},{3,2},{4,5},{5,4},{6,7},{7,6},{8,9},{9,8},{10,11... | collective-permute-start | bytes 9437192 | tf_op jit(solution)/shard_map/ppermute | solution.py:565
  544.1 63.9 %collective-permute-start.32 = (bf16[128,2048]{1,0:T(8,128)(2,1)}, bf16[128,2048]{1,0:T(8,128)(2,1)S(1)}, u32[]{:S(2)}, u32[]{:S(2)}) collective-permute-start(bf16[128,2048]{1,0:T(8,128)(2,1)} %get-tuple-element.109), channel_id=1, source_target_pairs={{0,2},{2,0},{4,6},{6,4},{1,3},{3,1},{5,7},{7,5},{8,10},{10,8},{12,... | collective-permute-start | bytes 1572872 | tf_op jit(solution)/shard_map/ppermute | solution.py:362
  562.9 27.5 %collective-permute-start.38 = (bf16[128,2048]{1,0:T(8,128)(2,1)}, bf16[128,2048]{1,0:T(8,128)(2,1)S(1)}, u32[]{:S(2)}, u32[]{:S(2)}) collective-permute-start(bf16[128,2048]{1,0:T(8,128)(2,1)} %get-tuple-element.103), channel_id=1, source_target_pairs={{0,2},{2,0},{4,6},{6,4},{1,3},{3,1},{5,7},{7,5},{8,10},{10,8},{12,... | collective-permute-start | bytes 1572872 | tf_op jit(solution)/shard_map/ppermute | solution.py:362
  563.7 28.6 %collective-permute-start.41 = (bf16[128,2048]{1,0:T(8,128)(2,1)}, bf16[128,2048]{1,0:T(8,128)(2,1)}, u32[]{:S(2)}, u32[]{:S(2)}) collective-permute-start(bf16[128,2048]{1,0:T(8,128)(2,1)} %get-tuple-element.105), channel_id=1, source_target_pairs={{0,4},{2,6},{4,0},{6,2},{1,5},{3,7},{5,1},{7,3},{8,12},{10,14},{12... | collective-permute-start | bytes 1572872 | tf_op jit(solution)/shard_map/ppermute | solution.py:362
  592.3 28.6 %collective-permute-start.34 = (bf16[128,2048]{1,0:T(8,128)(2,1)}, bf16[128,2048]{1,0:T(8,128)(2,1)}, u32[]{:S(2)}, u32[]{:S(2)}) collective-permute-start(bf16[128,2048]{1,0:T(8,128)(2,1)} %get-tuple-element.113), channel_id=1, source_target_pairs={{0,4},{2,6},{4,0},{6,2},{1,5},{3,7},{5,1},{7,3},{8,12},{10,14},{12... | collective-permute-start | bytes 1572872 | tf_op jit(solution)/shard_map/ppermute | solution.py:362
  596.0 26.9 %collective-permute-start.37 = (bf16[128,2048]{1,0:T(8,128)(2,1)}, bf16[128,2048]{1,0:T(8,128)(2,1)}, u32[]{:S(2)}, u32[]{:S(2)}) collective-permute-start(bf16[128,2048]{1,0:T(8,128)(2,1)} %get-tuple-element.114), channel_id=1, source_target_pairs={{0,2},{2,0},{4,6},{6,4},{1,3},{3,1},{5,7},{7,5},{8,10},{10,8},{12,... | collective-permute-start | bytes 1572872 | tf_op jit(solution)/shard_map/ppermute | solution.py:362
  601.6 32.2 %collective-permute-start.51 = (bf16[128,2176]{1,0:T(8,128)(2,1)}, bf16[128,2176]{1,0:T(8,128)(2,1)S(1)}, u32[]{:S(2)}, u32[]{:S(2)}) collective-permute-start(bf16[128,2176]{1,0:T(8,128)(2,1)} %get-tuple-element.130), channel_id=1, source_target_pairs={{0,0},{2,1},{4,2},{6,3},{1,4},{3,5},{5,6},{7,7},{8,8},{10,9},{12,1... | collective-permute-start | bytes 1671176 | tf_op jit(solution)/shard_map/ppermute | solution.py:417
  608.0 32.6 %collective-permute-start.52 = (bf16[128,2176]{1,0:T(8,128)(2,1)}, bf16[128,2176]{1,0:T(8,128)(2,1)S(1)}, u32[]{:S(2)}, u32[]{:S(2)}) collective-permute-start(bf16[128,2176]{1,0:T(8,128)(2,1)} %get-tuple-element.129), channel_id=1, source_target_pairs={{2,0},{0,1},{6,2},{4,3},{3,4},{1,5},{7,6},{5,7},{10,8},{8,9},{14,1... | collective-permute-start | bytes 1671176 | tf_op jit(solution)/shard_map/ppermute | solution.py:417
  608.9 31.7 %collective-permute-start.53 = (bf16[128,2176]{1,0:T(8,128)(2,1)}, bf16[128,2176]{1,0:T(8,128)(2,1)S(1)}, u32[]{:S(2)}, u32[]{:S(2)}) collective-permute-start(bf16[128,2176]{1,0:T(8,128)(2,1)} %get-tuple-element.128), channel_id=1, source_target_pairs={{4,0},{6,1},{0,2},{2,3},{5,4},{7,5},{1,6},{3,7},{12,8},{14,9},{8,1... | collective-permute-start | bytes 1671176 | tf_op jit(solution)/shard_map/ppermute | solution.py:417
  (116 other events, 1632.5 us)
Sparse Core Ops, SparseCore 0:
  12.0 80.7 all-gather.3
  94.9 106.2 all-gather.5
  202.9 59.4 all-gather.7
  319.8 116.7 reduce-scatter.3
  438.8 63.2 reduce-scatter.7
  524.2 77.9 reduce-scatter.5

commit v4 on v3

--- a/solution.py
+++ b/solution.py
@@ -7,6 +7,7 @@
 from jax.experimental import pallas as pl
 from jax.experimental.pallas import tpu as pltpu
 from jax.sharding import PartitionSpec as P
+
 
 HD = 64
 ROT = 16
@@ -353,6 +354,30 @@
     )(info, *arrays)
 
 
+def split_kernel(info, mine, other, mine_out, other_out):
+    mine_out[...] = mine[...]
+    other_out[...] = other[...]
+
+
+def split_columns(info, array, parts):
+    length, width = array.shape
+    block = width // (2 * parts)
+    shape = jax.ShapeDtypeStruct((length, width // 2), array.dtype)
+    return pl.pallas_call(
+        split_kernel,
+        grid_spec=pltpu.PrefetchScalarGridSpec(
+            num_scalar_prefetch=1,
+            grid=(parts,),
+            in_specs=[
+                pl.BlockSpec((length, block), lambda j, s: (0, 2 * j + s[4])),
+                pl.BlockSpec((length, block), lambda j, s: (0, 2 * j + 1 - s[4])),
+            ],
+            out_specs=[pl.BlockSpec((length, block), lambda j, s: (0, j))] * 2,
+        ),
+        out_shape=[shape, shape],
+    )(info, array, array)
+
+
 def make_body(mesh):
     R = mesh.shape["row"]
     C = mesh.shape["col"]
@@ -445,7 +470,6 @@
         r = lax.axis_index("row")
         c = lax.axis_index("col")
         block = tokens.shape[1]
-        length = block * R
         width = tokens.shape[2]
         head_cols = query_key_value_weight.shape[2]
         pairs = head_cols // (2 * HD)
@@ -457,7 +481,7 @@
         q_rows = max(1, C // R)
         u = source_place(r, c)
         v = r if C <= R else r * q_rows + c % q_rows
-        info = jnp.stack([r, prefix_len[0], u, v]).astype(jnp.int32)
+        info = jnp.stack([r, prefix_len[0], u, v, c]).astype(jnp.int32)
         rows = w_rows // q_rows
         a_rows = N // C * rows
         piece = (3 * ff_slice + 127) // 128 * 128
@@ -556,17 +580,14 @@
         bias_local = bias_local[:, 0].reshape(pairs, 3, 2 * HD)
         bias_local = bias_local.transpose(1, 0, 2).reshape(3, head_cols)
         if C == 2:
-            def columns(array, which):
-                parts = array.reshape(length, -1, C, w_attn.shape[0] // (C * mesh.shape["dp"]))
-                return lax.dynamic_index_in_dim(parts, which, 2, keepdims=False).reshape(length, -1)
-
             def pair_sum(left, right):
-                away = tn(columns(left, 1 - c), right).astype(bf16)
-                got = lax.ppermute(away, "col", [(0, 1), (1, 0)])
-                return (tn(columns(left, c), right) + got.astype(f32)).astype(bf16)
+                mine, other = split_columns(info, left, mesh.shape["dp"])
+                got = lax.ppermute(tn(other, right).astype(bf16), "col", [(0, 1), (1, 0)])
+                return (tn(mine, right) + got.astype(f32)).astype(bf16)
 
             grad_attn = jnp.concatenate(
-                [pair_sum(seq_in, grad_proj), pair_sum(branch, attended)], axis=1
+                [pair_sum(seq_in, grad_proj), pair_sum(branch, attended)],
+                axis=1,
             )
             grad_attn = lax.psum_scatter(grad_attn, "dp", scatter_dimension=0, tiled=True)
         else:
@@ -576,7 +597,6 @@
             grad_attn = lax.psum_scatter(grad_attn, ("dp", "col"), scatter_dimension=0, tiled=True)
         own = nt(grad_proj[:block], w_qkv)
         others = nt(grad_proj[block:], w_qkv).astype(bf16)
-        others, grad_gu = lax.optimization_barrier((others, grad_gu))
         grad_first = scatter_rel(
             [own] + [others[k * block : (k + 1) * block] for k in range(R - 1)]
         )

time: 680 us -> 625 us (0.919)
  local copies, waits for them, and re-layouts: 128 us -> 42.6 us
  waiting for transfers between devices: 223 us -> 252 us
  Pallas kernels: 56.9 us -> 66 us
  other arithmetic: 38.5 us -> 30.6 us
    unnamed x178 -> x132, local copies, waits for them, and re-layouts: 71.6 us -> 30.2 us
    dynamic_slice x2 -> x0, local copies, waits for them, and re-layouts: 22.5 us -> none  [columns(): lax.dynamic_index_in_dim(parts, which, 2, keepdims=False)]
    reshape x2 -> x0, local copies, waits for them, and re-layouts: 15.7 us -> none  [columns(): array.reshape(length, -1, C, w_attn.shape[0] // (C * mesh.shape['dp']))]
    ppermute x5, waiting for transfers between devices: 5.93 us -> 19.1 us  [sum_everywhere(): other = lax.ppermute(array, name, [(i, i ^ step) for i in range(size)])]
    pallas_call x0 -> x2, Pallas kernels: none -> 10.8 us  [split_columns(): pl.pallas_call(split_kernel, grid_spec=pltpu.PrefetchScalarGridSpec(num_s...]
    ppermute x4, waiting for transfers between devices: 6.81 us -> 15.8 us  [bring_back(): lax.ppermute(packed[k], ('row', 'col'), [(b, a) for a, b in exchange_pair...]
  transfers between devices with their start and end apart: 61 -> 61, of which waited for: 35 -> 37; matrix products, arithmetic and copies ran while one was open for 37% -> 33% of each run, Pallas kernels for 8% -> 10%
where the time goes in v4:
time: 625 us; the launch traced here: 613 us
  waiting for transfers between devices  252 us (40%)
  matrix products  146 us (23%)
  Pallas kernels  66 us (11%)
  starting transfers between devices  60.1 us (10%)
  local copies, waits for them, and re-layouts  42.6 us (7%)
  other arithmetic  30.6 us (5%)
  between operations  16.1 us (3%)
    ppermute x40, waiting for transfers between devices, row_permute(): return lax.ppermute(block, 'row', [(i, i ^ k) for i in range(R)])  188 us
    dot_general x18, matrix products, dot(): lax.dot_general(left, right, (dims, ((), ())), preferred_element_type=f32)  146 us
    ppermute x40, starting transfers between devices, row_permute(): return lax.ppermute(block, 'row', [(i, i ^ k) for i in range(R)])  40.6 us
    unnamed x132, local copies, waits for them, and re-layouts  30.2 us
    pallas_call x1, Pallas kernels, attend_backward(): pl.pallas_call(lambda *refs: backward_kernel(blocks, size, *refs), grid_s...  26.7 us
    ppermute x4, waiting for transfers between devices, spread(): lax.ppermute(packed[k], ('row', 'col'), exchange_pairs(k))  21.7 us
    ppermute x5, waiting for transfers between devices, sum_everywhere(): other = lax.ppermute(array, name, [(i, i ^ step) for i in range(size)])  19.1 us
    pallas_call x1, Pallas kernels, attend_forward(): pl.pallas_call(lambda *refs: forward_kernel(blocks, size, *refs), grid_sp...  18.3 us
  transfers between devices with their start and end apart: 61, of which 37 were waited for; matrix products, arithmetic and copies ran while one was open for 33% of the time, Pallas kernels for 10%

profile of v4, /device:TPU:10, one launch (start us, length us, event | category | flops | bytes accessed | tf_op | source)
XLA Modules:
  0.0 613.1 jit_solution(1464506461752201893)
XLA Ops:
  15.3 22.8 %collective-permute-done = bf16[256,2048]{1,0:T(8,128)(2,1)S(1)} collective-permute-done((bf16[256,2048]{1,0:T(8,128)(2,1)S(1)}, bf16[256,2048]{1,0:T(8,128)(2,1)S(1)}, u32[]{:S(2)}, u32[]{:S(2)}) %collective-permute-start) | collective-permute-done | bytes 1048608 | tf_op jit(solution)/shard_map/ppermute | solution.py:387
  41.7 9.5 %collective-permute-done.2 = bf16[128,2048]{1,0:T(8,128)(2,1)S(1)} collective-permute-done((bf16[128,2048]{1,0:T(8,128)(2,1)S(1)}, bf16[128,2048]{1,0:T(8,128)(2,1)S(1)}, u32[]{:S(2)}, u32[]{:S(2)}) %collective-permute-start.2) | collective-permute-done | bytes 524320 | tf_op jit(solution)/shard_map/ppermute | solution.py:387
  59.0 10.5 %collective-permute-done.4.refs_0_ = bf16[128,2176]{1,0:T(8,128)(2,1)S(1)} collective-permute-done((bf16[128,2176]{1,0:T(8,128)(2,1)S(1)}, bf16[128,2176]{1,0:T(8,128)(2,1)S(1)}, u32[]{:S(2)}, u32[]{:S(2)}) %collective-permute-start.4) | collective-permute-done | bytes 557088 | tf_op jit(solution)/shard_map/ppermute | solution.py:438
  71.8 9.0 %collective-permute-done.6.refs_2_ = bf16[128,2176]{1,0:T(8,128)(2,1)S(1)} collective-permute-done((bf16[128,2176]{1,0:T(8,128)(2,1)S(1)}, bf16[128,2176]{1,0:T(8,128)(2,1)S(1)}, u32[]{:S(2)}, u32[]{:S(2)}) %collective-permute-start.6) | collective-permute-done | bytes 557088 | tf_op jit(solution)/shard_map/ppermute | solution.py:438
  92.7 11.7 %fusion.14.refs_1_ = f32[1024,1536]{1,0:T(8,128)} fusion(bf16[1024,2048]{1,0:T(8,128)(2,1)} %copy-done.18, bf16[2048,2048]{1,0:T(8,128)(2,1)} %all-gather.4.cloned.1.call-done, f32[1536]{0:T(1024)S(1)} %reshape.552), kind=kOutput, calls=%fused_computation.21 | convolution fusion | flops 6444023808 | bytes 16783360 | tf_op jit(solution)/shard_map/dot_general | solution.py:52
  104.4 18.3 %attend_forward.1 = (bf16[1024,1536]{1,0:T(8,128)(2,1)S(1)}, bf16[1024,512]{1,0:T(8,128)(2,1)S(1)}, f32[4,4,16,256]{3,2,1,0:T(8,128)S(1)}) custom-call(s32[5]{0:T(128)S(1)} %stack.30.info.refs_0_, f32[1024,1536]{1,0:T(8,128)} %fusion.14.refs_1_, f32[3,1024,128]{2,1,0:T(8,128)S(1)} %pad_maximum_fusion.3.refs_2_), custom_call_target="tpu_custom_call" | custom-call | tf_op jit(solution)/shard_map/attend_forward/pallas_call | solution.py:215
  132.6 10.7 %collective-permute-done.12 = bf16[128,2048]{1,0:T(8,128)(2,1)S(1)} collective-permute-done((bf16[128,2048]{1,0:T(8,128)(2,1)S(1)}, bf16[128,2048]{1,0:T(8,128)(2,1)S(1)}, u32[]{:S(2)}, u32[]{:S(2)}) %collective-permute-start.12) | collective-permute-done | bytes 524320 | tf_op jit(solution)/shard_map/ppermute | solution.py:387
  156.2 9.7 %collective-permute-done.10 = bf16[128,2048]{1,0:T(8,128)(2,1)} collective-permute-done((bf16[128,2048]{1,0:T(8,128)(2,1)}, bf16[128,2048]{1,0:T(8,128)(2,1)}, u32[]{:S(2)}, u32[]{:S(2)}) %collective-permute-start.10) | collective-permute-done | bytes 524320 | tf_op jit(solution)/shard_map/ppermute | solution.py:387
  172.7 17.2 %collective-permute-done.18 = bf16[256,2048]{1,0:T(8,128)(2,1)} collective-permute-done((bf16[256,2048]{1,0:T(8,128)(2,1)}, bf16[256,2048]{1,0:T(8,128)(2,1)}, u32[]{:S(2)}, u32[]{:S(2)}) %collective-permute-start.18) | collective-permute-done | bytes 1048608 | tf_op jit(solution)/shard_map/ppermute | solution.py:387
  196.4 9.4 %collective-permute-done.20 = bf16[128,2048]{1,0:T(8,128)(2,1)S(1)} collective-permute-done((bf16[128,2048]{1,0:T(8,128)(2,1)S(1)}, bf16[128,2048]{1,0:T(8,128)(2,1)S(1)}, u32[]{:S(2)}, u32[]{:S(2)}) %collective-permute-start.20) | collective-permute-done | bytes 524320 | tf_op jit(solution)/shard_map/ppermute | solution.py:387
  212.9 9.5 %collective-permute-done.21 = bf16[128,2048]{1,0:T(8,128)(2,1)S(1)} collective-permute-done((bf16[128,2048]{1,0:T(8,128)(2,1)S(1)}, bf16[128,2048]{1,0:T(8,128)(2,1)S(1)}, u32[]{:S(2)}, u32[]{:S(2)}) %collective-permute-start.21) | collective-permute-done | bytes 524320 | tf_op jit(solution)/shard_map/ppermute | solution.py:387
  238.5 17.3 %fusion.103 = f32[1024,2816]{1,0:T(8,128)S(1)} fusion(bf16[1024,2048]{1,0:T(8,128)(2,1)} %constant_dynamic-update-slice_fusion.5, bf16[2048,2816]{1,0:T(8,128)(2,1)} %all-gather.6.cloned.1.call-done), kind=kOutput, calls=%fused_computation.188 | convolution fusion | flops 11811160064 | bytes 27262976 | tf_op jit(solution)/shard_map/dot_general | solution.py:52
  262.7 8.7 %convolution_convert_fusion.1 = bf16[2048,1408]{1,0:T(8,128)(2,1)} fusion(bf16[1024,2048]{1,0:T(8,128)(2,1)S(1)} %copy-done.37, bf16[1024,1408]{1,0:T(8,128)(2,1)S(1)} %multiply_convert_fusion.2), kind=kOutput, calls=%fused_computation.1 | convolution fusion | flops 5908463616 | bytes 12845056 | tf_op jit(solution)/shard_map/dot_general | solution.py:52
  271.8 14.0 %multiply_convert_fusion.1 = (bf16[1024,1408]{1,0:T(8,128)(2,1)S(1)}, bf16[1024,1408]{1,0:T(8,128)(2,1)S(1)}) fusion(f32[1024,2816]{1,0:T(8,128)} %copy-done.27, bf16[1024,2048]{1,0:T(8,128)(2,1)} %copy-done.36, bf16[2048,1408]{1,0:T(8,128)(2,1)} %all-gather.8.cloned.1.call-done), kind=kOutput, calls=%fused_computation.7 | convolution fusion | flops 5924323328 | bytes 27262976 | tf_op jit(solution)/shard_map/dot_general | solution.py:52
  285.8 15.3 %fusion.17 = bf16[768,2048]{1,0:T(8,128)(2,1)} fusion(bf16[2048,2816]{1,0:T(8,128)(2,1)} %all-gather.6.cloned.1.call-done, bf16[1024,1408]{1,0:T(8,128)(2,1)S(1)} %get-tuple-element.102, bf16[1024,1408]{1,0:T(8,128)(2,1)S(1)} %get-tuple-element.101), kind=kOutput, calls=%fused_computation.28 | convolution fusion | flops 8868593664 | bytes 20447232 | tf_op jit(solution)/shard_map/dot_general | solution.py:52
  301.0 18.2 %convolution_convert_fusion = bf16[2048,2816]{1,0:T(8,128)(2,1)} fusion(bf16[1024,2048]{1,0:T(8,128)(2,1)} %constant_dynamic-update-slice_fusion.5, bf16[1024,1408]{1,0:T(8,128)(2,1)S(1)} %get-tuple-element.102, bf16[1024,1408]{1,0:T(8,128)(2,1)S(1)} %get-tuple-element.101), kind=kOutput, calls=%fused_computation | convolution fusion | flops 11828461568 | bytes 21495808 | tf_op jit(solution)/shard_map/dot_general | solution.py:52
  325.4 10.7 %collective-permute-done.23 = bf16[128,2048]{1,0:T(8,128)(2,1)S(1)} collective-permute-done((bf16[128,2048]{1,0:T(8,128)(2,1)S(1)}, bf16[128,2048]{1,0:T(8,128)(2,1)S(1)}, u32[]{:S(2)}, u32[]{:S(2)}) %collective-permute-start.23) | collective-permute-done | bytes 524320 | tf_op jit(solution)/shard_map/ppermute | solution.py:387
  362.0 18.8 %collective-permute-done.28 = bf16[256,2048]{1,0:T(8,128)(2,1)S(1)} collective-permute-done((bf16[256,2048]{1,0:T(8,128)(2,1)}, bf16[256,2048]{1,0:T(8,128)(2,1)S(1)}, u32[]{:S(2)}, u32[]{:S(2)}) %collective-permute-start.28) | collective-permute-done | bytes 1048608 | tf_op jit(solution)/shard_map/ppermute | solution.py:387
  405.8 26.7 %attend_backward.1 = (bf16[1024,1536]{1,0:T(8,128)(2,1)S(1)}, f32[4,8,384]{2,1,0:T(8,128)S(1)}) custom-call(s32[5]{0:T(128)S(1)} %copy-done.8, bf16[1024,1536]{1,0:T(8,128)(2,1)} %copy-done, f32[3,1024,128]{2,1,0:T(8,128)S(1)} %pad_maximum_fusion.3.refs_2_, f32[4,4,16,256]{3,2,1,0:T(8,128)S(1)} %get-tuple-element.45.refs_3_, ...), custom_call_target="tpu_custom_call" | custom-call | tf_op jit(solution)/shard_map/attend_backward/pallas_call | solution.py:253
  446.7 9.1 %convolution_convert_fusion.4 = bf16[768,2048]{1,0:T(8,128)(2,1)} fusion(bf16[2048,1408]{1,0:T(8,128)(2,1)} %all-gather.8.cloned.1.call-done, bf16[1024,1408]{1,0:T(8,128)(2,1)S(1)} %copy-done.32), kind=kOutput, calls=%fused_computation.31 | convolution fusion | flops 4430757888 | bytes 11075584 | tf_op jit(solution)/shard_map/dot_general | solution.py:52
  472.4 9.2 %fusion.20 = bf16[768,2048]{1,0:T(8,128)(2,1)S(1)} fusion(bf16[2048,2048]{1,0:T(8,128)(2,1)} %all-gather.4.cloned.1.call-done, bf16[1024,1536]{1,0:T(8,128)(2,1)S(1)} %copy-done.12), kind=kOutput, calls=%fused_computation.30 | convolution fusion | flops 4833411072 | bytes 11796480 | tf_op jit(solution)/shard_map/dot_general | solution.py:52
  499.3 8.7 %collective-permute-done.33 = bf16[128,2048]{1,0:T(8,128)(2,1)S(1)} collective-permute-done((bf16[128,2048]{1,0:T(8,128)(2,1)S(1)}, bf16[128,2048]{1,0:T(8,128)(2,1)S(1)}, u32[]{:S(2)}, u32[]{:S(2)}) %collective-permute-start.33) | collective-permute-done | bytes 524320 | tf_op jit(solution)/shard_map/ppermute | solution.py:387
  509.1 11.2 %collective-permute-done.36 = bf16[128,2048]{1,0:T(8,128)(2,1)S(1)} collective-permute-done((bf16[128,2048]{1,0:T(8,128)(2,1)S(1)}, bf16[128,2048]{1,0:T(8,128)(2,1)S(1)}, u32[]{:S(2)}, u32[]{:S(2)}) %collective-permute-start.36) | collective-permute-done | bytes 524320 | tf_op jit(solution)/shard_map/ppermute | solution.py:387
  537.6 16.0 %collective-permute-done.45 = f32[7,2048]{1,0:T(8,128)S(1)} collective-permute-done((f32[7,2048]{1,0:T(8,128)S(1)}, f32[7,2048]{1,0:T(8,128)S(1)}, u32[]{:S(2)}, u32[]{:S(2)}) %collective-permute-start.45) | collective-permute-done | bytes 57376 | tf_op jit(solution)/shard_map/ppermute | solution.py:451
  (341 shorter events, 274.7 us)
Async XLA Ops:
  7.2 85.5 %all-gather.4.cloned.1.call-start = ((), (), s32[]{:S(2)}) async-start(), calls=%async_computation.3 | async-start | bytes 9437184 | tf_op jit(solution)/shard_map/all_gather | solution.py:501
  11.8 226.6 %all-gather.6.cloned.1.call-start = ((), (), s32[]{:S(2)}) async-start(), calls=%async_computation.4 | async-start | bytes 12976128 | tf_op jit(solution)/shard_map/all_gather | solution.py:520
  13.2 24.9 %collective-permute-start = (bf16[256,2048]{1,0:T(8,128)(2,1)S(1)}, bf16[256,2048]{1,0:T(8,128)(2,1)S(1)}, u32[]{:S(2)}, u32[]{:S(2)}) collective-permute-start(bf16[256,2048]{1,0:T(8,128)(2,1)S(1)} %get-tuple-element.100), channel_id=1, source_target_pairs={{0,2},{2,0},{4,6},{6,4},{1,3},{3,1},{5,7},{7,5},{8,10},{10,8},{12,... | collective-permute-start | bytes 3145736 | tf_op jit(solution)/shard_map/ppermute | solution.py:387
  13.8 27.1 %collective-permute-start.1 = (bf16[256,2048]{1,0:T(8,128)(2,1)S(1)}, bf16[256,2048]{1,0:T(8,128)(2,1)S(1)}, u32[]{:S(2)}, u32[]{:S(2)}) collective-permute-start(bf16[256,2048]{1,0:T(8,128)(2,1)S(1)} %get-tuple-element.100), channel_id=1, source_target_pairs={{0,4},{2,6},{4,0},{6,2},{1,5},{3,7},{5,1},{7,3},{8,12},{10,14},{12... | collective-permute-start | bytes 3145736 | tf_op jit(solution)/shard_map/ppermute | solution.py:387
  83.2 188.6 %all-gather.8.cloned.1.call-start = ((), (), s32[]{:S(2)}) async-start(), calls=%async_computation.5 | async-start | bytes 6488064 | tf_op jit(solution)/shard_map/all_gather | solution.py:521
  131.0 25.2 %collective-permute-start.8 = (bf16[128,2048]{1,0:T(8,128)(2,1)}, bf16[128,2048]{1,0:T(8,128)(2,1)}, u32[]{:S(2)}, u32[]{:S(2)}) collective-permute-start(bf16[128,2048]{1,0:T(8,128)(2,1)} %get-tuple-element.121), channel_id=1, source_target_pairs={{0,2},{2,0},{4,6},{6,4},{1,3},{3,1},{5,7},{7,5},{8,10},{10,8},{12,... | collective-permute-start | bytes 1572872 | tf_op jit(solution)/shard_map/ppermute | solution.py:387
  147.2 42.7 %collective-permute-start.18 = (bf16[256,2048]{1,0:T(8,128)(2,1)}, bf16[256,2048]{1,0:T(8,128)(2,1)}, u32[]{:S(2)}, u32[]{:S(2)}) collective-permute-start(bf16[256,2048]{1,0:T(8,128)(2,1)} %bitcast.14), channel_id=1, source_target_pairs={{0,2},{2,0},{4,6},{6,4},{1,3},{3,1},{5,7},{7,5},{8,10},{10,8},{12,... | collective-permute-start | bytes 3145736 | tf_op jit(solution)/shard_map/ppermute | solution.py:387
  148.9 420.4 %reduce-scatter.8.cloned.1.call-start = ((), (), s32[]{:S(2)}) async-start(), calls=%async_computation.8 | async-start | bytes 6488064 | tf_op jit(solution)/shard_map/reduce_scatter | solution.py:550
  154.6 39.8 %collective-permute-start.19 = (bf16[256,2048]{1,0:T(8,128)(2,1)}, bf16[256,2048]{1,0:T(8,128)(2,1)S(1)}, u32[]{:S(2)}, u32[]{:S(2)}) collective-permute-start(bf16[256,2048]{1,0:T(8,128)(2,1)} %bitcast.14), channel_id=1, source_target_pairs={{0,4},{2,6},{4,0},{6,2},{1,5},{3,7},{5,1},{7,3},{8,12},{10,14},{12... | collective-permute-start | bytes 3145736 | tf_op jit(solution)/shard_map/ppermute | solution.py:387
  172.1 40.1 %collective-permute-start.14 = (bf16[256,2048]{1,0:T(8,128)(2,1)S(1)}, bf16[256,2048]{1,0:T(8,128)(2,1)S(1)}, u32[]{:S(2)}, u32[]{:S(2)}) collective-permute-start(bf16[256,2048]{1,0:T(8,128)(2,1)S(1)} %get-tuple-element.96), channel_id=1, source_target_pairs={{0,2},{2,0},{4,6},{6,4},{1,3},{3,1},{5,7},{7,5},{8,10},{10,8},{12,... | collective-permute-start | bytes 3145736 | tf_op jit(solution)/shard_map/ppermute | solution.py:387
  191.6 36.7 %collective-permute-start.15 = (bf16[256,2048]{1,0:T(8,128)(2,1)S(1)}, bf16[256,2048]{1,0:T(8,128)(2,1)S(1)}, u32[]{:S(2)}, u32[]{:S(2)}) collective-permute-start(bf16[256,2048]{1,0:T(8,128)(2,1)S(1)} %get-tuple-element.96), channel_id=1, source_target_pairs={{0,4},{2,6},{4,0},{6,2},{1,5},{3,7},{5,1},{7,3},{8,12},{10,14},{12... | collective-permute-start | bytes 3145736 | tf_op jit(solution)/shard_map/ppermute | solution.py:387
  194.4 28.0 %collective-permute-start.21 = (bf16[128,2048]{1,0:T(8,128)(2,1)S(1)}, bf16[128,2048]{1,0:T(8,128)(2,1)S(1)}, u32[]{:S(2)}, u32[]{:S(2)}) collective-permute-start(bf16[128,2048]{1,0:T(8,128)(2,1)S(1)} %slice.316), channel_id=1, source_target_pairs={{0,2},{2,0},{4,6},{6,4},{1,3},{3,1},{5,7},{7,5},{8,10},{10,8},{12,... | collective-permute-start | bytes 1572872 | tf_op jit(solution)/shard_map/ppermute | solution.py:387
  271.5 297.8 %reduce-scatter.6.cloned.1.call-start = ((), (), s32[]{:S(2)}) async-start(), calls=%async_computation.7 | async-start | bytes 12976128 | tf_op jit(solution)/shard_map/reduce_scatter | solution.py:562
  319.3 261.6 %reduce-scatter.4.cloned.1.call-start = ((), (), s32[]{:S(2)}) async-start(), calls=%async_computation.6 | async-start | bytes 5242880 | tf_op jit(solution)/shard_map/reduce_scatter | solution.py:592
  322.3 25.6 %collective-permute-start.22 = (bf16[128,2048]{1,0:T(8,128)(2,1)S(1)}, bf16[128,2048]{1,0:T(8,128)(2,1)S(1)}, u32[]{:S(2)}, u32[]{:S(2)}) collective-permute-start(bf16[128,2048]{1,0:T(8,128)(2,1)S(1)} %get-tuple-element.115), channel_id=1, source_target_pairs={{0,2},{2,0},{4,6},{6,4},{1,3},{3,1},{5,7},{7,5},{8,10},{10,8},{12,... | collective-permute-start | bytes 1572872 | tf_op jit(solution)/shard_map/ppermute | solution.py:387
  361.1 28.1 %collective-permute-start.29 = (bf16[256,2048]{1,0:T(8,128)(2,1)}, bf16[256,2048]{1,0:T(8,128)(2,1)}, u32[]{:S(2)}, u32[]{:S(2)}) collective-permute-start(bf16[256,2048]{1,0:T(8,128)(2,1)} %get-tuple-element.94), channel_id=1, source_target_pairs={{0,4},{2,6},{4,0},{6,2},{1,5},{3,7},{5,1},{7,3},{8,12},{10,14},{12... | collective-permute-start | bytes 3145736 | tf_op jit(solution)/shard_map/ppermute | solution.py:387
  488.0 34.6 %collective-permute-start.38 = (bf16[128,2048]{1,0:T(8,128)(2,1)S(1)}, bf16[128,2048]{1,0:T(8,128)(2,1)S(1)}, u32[]{:S(2)}, u32[]{:S(2)}) collective-permute-start(bf16[128,2048]{1,0:T(8,128)(2,1)S(1)} %get-tuple-element.103), channel_id=1, source_target_pairs={{0,2},{2,0},{4,6},{6,4},{1,3},{3,1},{5,7},{7,5},{8,10},{10,8},{12,... | collective-permute-start | bytes 1572872 | tf_op jit(solution)/shard_map/ppermute | solution.py:387
  489.3 34.3 %collective-permute-start.41 = (bf16[128,2048]{1,0:T(8,128)(2,1)S(1)}, bf16[128,2048]{1,0:T(8,128)(2,1)S(1)}, u32[]{:S(2)}, u32[]{:S(2)}) collective-permute-start(bf16[128,2048]{1,0:T(8,128)(2,1)S(1)} %get-tuple-element.105), channel_id=1, source_target_pairs={{0,4},{2,6},{4,0},{6,2},{1,5},{3,7},{5,1},{7,3},{8,12},{10,14},{12... | collective-permute-start | bytes 1572872 | tf_op jit(solution)/shard_map/ppermute | solution.py:387
  498.2 33.3 %collective-permute-start.40 = (bf16[128,2048]{1,0:T(8,128)(2,1)S(1)}, bf16[128,2048]{1,0:T(8,128)(2,1)S(1)}, u32[]{:S(2)}, u32[]{:S(2)}) collective-permute-start(bf16[128,2048]{1,0:T(8,128)(2,1)S(1)} %get-tuple-element.107), channel_id=1, source_target_pairs={{0,4},{2,6},{4,0},{6,2},{1,5},{3,7},{5,1},{7,3},{8,12},{10,14},{12... | collective-permute-start | bytes 1572872 | tf_op jit(solution)/shard_map/ppermute | solution.py:387
  508.0 24.6 %collective-permute-start.43 = (bf16[128,2048]{1,0:T(8,128)(2,1)S(1)}, bf16[128,2048]{1,0:T(8,128)(2,1)S(1)}, u32[]{:S(2)}, u32[]{:S(2)}) collective-permute-start(bf16[128,2048]{1,0:T(8,128)(2,1)S(1)} %get-tuple-element.108), channel_id=1, source_target_pairs={{0,2},{2,0},{4,6},{6,4},{1,3},{3,1},{5,7},{7,5},{8,10},{10,8},{12,... | collective-permute-start | bytes 1572872 | tf_op jit(solution)/shard_map/ppermute | solution.py:387
  520.3 41.4 %collective-permute-start.32 = (bf16[128,2048]{1,0:T(8,128)(2,1)}, bf16[128,2048]{1,0:T(8,128)(2,1)}, u32[]{:S(2)}, u32[]{:S(2)}) collective-permute-start(bf16[128,2048]{1,0:T(8,128)(2,1)} %get-tuple-element.109), channel_id=1, source_target_pairs={{0,2},{2,0},{4,6},{6,4},{1,3},{3,1},{5,7},{7,5},{8,10},{10,8},{12,... | collective-permute-start | bytes 1572872 | tf_op jit(solution)/shard_map/ppermute | solution.py:387
  522.6 39.1 %collective-permute-start.35 = (bf16[128,2048]{1,0:T(8,128)(2,1)}, bf16[128,2048]{1,0:T(8,128)(2,1)}, u32[]{:S(2)}, u32[]{:S(2)}) collective-permute-start(bf16[128,2048]{1,0:T(8,128)(2,1)} %get-tuple-element.111), channel_id=1, source_target_pairs={{0,4},{2,6},{4,0},{6,2},{1,5},{3,7},{5,1},{7,3},{8,12},{10,14},{12... | collective-permute-start | bytes 1572872 | tf_op jit(solution)/shard_map/ppermute | solution.py:387
  523.6 38.1 %collective-permute-start.34 = (bf16[128,2048]{1,0:T(8,128)(2,1)}, bf16[128,2048]{1,0:T(8,128)(2,1)}, u32[]{:S(2)}, u32[]{:S(2)}) collective-permute-start(bf16[128,2048]{1,0:T(8,128)(2,1)} %get-tuple-element.113), channel_id=1, source_target_pairs={{0,4},{2,6},{4,0},{6,2},{1,5},{3,7},{5,1},{7,3},{8,12},{10,14},{12... | collective-permute-start | bytes 1572872 | tf_op jit(solution)/shard_map/ppermute | solution.py:387
  531.5 30.2 %collective-permute-start.37 = (bf16[128,2048]{1,0:T(8,128)(2,1)}, bf16[128,2048]{1,0:T(8,128)(2,1)}, u32[]{:S(2)}, u32[]{:S(2)}) collective-permute-start(bf16[128,2048]{1,0:T(8,128)(2,1)} %get-tuple-element.114), channel_id=1, source_target_pairs={{0,2},{2,0},{4,6},{6,4},{1,3},{3,1},{5,7},{7,5},{8,10},{10,8},{12,... | collective-permute-start | bytes 1572872 | tf_op jit(solution)/shard_map/ppermute | solution.py:387
  (95 other events, 1188.1 us)
Sparse Core Ops, SparseCore 0:
  12.0 80.7 all-gather.3
  94.9 106.2 all-gather.5
  202.9 59.4 all-gather.7
  271.6 62.3 reduce-scatter.7
  336.1 117.6 reduce-scatter.5
  466.4 77.6 reduce-scatter.3

commit v5 on v4

--- a/solution.py
+++ b/solution.py
@@ -453,6 +453,11 @@
                 array = array + other
         return array
 
+    def pair_sum(mine, other, right):
+        away = tn(other, right).astype(bf16)
+        got = lax.ppermute(away, "col", [(0, 1), (1, 0)])
+        return (tn(mine, right) + got.astype(f32)).astype(bf16)
+
     def body(
         tokens,
         prefix_len,
@@ -545,9 +550,16 @@
         sig = jax.nn.sigmoid(gate_vals)
         swish = gate_vals * sig
         hidden = (swish * up_vals).astype(bf16)
-        grad_down = tn(dy_rel, hidden).astype(bf16)
-        _, w_down = lax.optimization_barrier((grad_down, w_down))
-        grad_down = lax.psum_scatter(grad_down, ("dp", "col"), scatter_dimension=0, tiled=True)
+        if C == 2:
+            seq_halves = split_columns(info, seq_in, mesh.shape["dp"])
+            halves = split_columns(info, dy_rel, mesh.shape["dp"])
+            grad_down = pair_sum(*halves, hidden)
+            _, w_down = lax.optimization_barrier((grad_down, w_down))
+            grad_down = lax.psum_scatter(grad_down, "dp", scatter_dimension=0, tiled=True)
+        else:
+            grad_down = tn(dy_rel, hidden).astype(bf16)
+            _, w_down = lax.optimization_barrier((grad_down, w_down))
+            grad_down = lax.psum_scatter(grad_down, ("dp", "col"), scatter_dimension=0, tiled=True)
         grad_hidden = nn(dy_rel, w_down)
         grad_gate = grad_hidden * up_vals * sig * (1.0 + gate_vals * (1.0 - sig))
         grad_up = grad_hidden * swish
@@ -580,13 +592,9 @@
         bias_local = bias_local[:, 0].reshape(pairs, 3, 2 * HD)
         bias_local = bias_local.transpose(1, 0, 2).reshape(3, head_cols)
         if C == 2:
-            def pair_sum(left, right):
-                mine, other = split_columns(info, left, mesh.shape["dp"])
-                got = lax.ppermute(tn(other, right).astype(bf16), "col", [(0, 1), (1, 0)])
-                return (tn(mine, right) + got.astype(f32)).astype(bf16)
-
+            halves = split_columns(info, branch, mesh.shape["dp"])
             grad_attn = jnp.concatenate(
-                [pair_sum(seq_in, grad_proj), pair_sum(branch, attended)],
+                [pair_sum(*seq_halves, grad_proj), pair_sum(*halves, attended)],
                 axis=1,
             )
             grad_attn = lax.psum_scatter(grad_attn, "dp", scatter_dimension=0, tiled=True)

time: 625 us -> 641 us (1.026)
  the two profiles are of different devices: /device:TPU:10 before, /device:TPU:0 now
where the time goes in v5:
time: 641 us; the launch traced here: 634 us
  waiting for transfers between devices  261 us (41%)
  matrix products  142 us (22%)
  Pallas kernels  71.6 us (11%)
  starting transfers between devices  62.8 us (10%)
  local copies, waits for them, and re-layouts  52.1 us (8%)
  other arithmetic  28.9 us (5%)
  between operations  16.1 us (3%)
    ppermute x40, waiting for transfers between devices, row_permute(): return lax.ppermute(block, 'row', [(i, i ^ k) for i in range(R)])  186 us
    dot_general x19, matrix products, dot(): lax.dot_general(left, right, (dims, ((), ())), preferred_element_type=f32)  142 us
    ppermute x40, starting transfers between devices, row_permute(): return lax.ppermute(block, 'row', [(i, i ^ k) for i in range(R)])  43.4 us
    unnamed x136, local copies, waits for them, and re-layouts  36.5 us
    pallas_call x1, Pallas kernels, attend_backward(): pl.pallas_call(lambda *refs: backward_kernel(blocks, size, *refs), grid_s...  26.7 us
    ppermute x5, waiting for transfers between devices, sum_everywhere(): other = lax.ppermute(array, name, [(i, i ^ step) for i in range(size)])  23 us
    ppermute x4, waiting for transfers between devices, spread(): lax.ppermute(packed[k], ('row', 'col'), exchange_pairs(k))  20.8 us
    pallas_call x1, Pallas kernels, attend_forward(): pl.pallas_call(lambda *refs: forward_kernel(blocks, size, *refs), grid_sp...  18.2 us
  transfers between devices with their start and end apart: 62, of which 37 were waited for; matrix products, arithmetic and copies ran while one was open for 32% of the time, Pallas kernels for 11%

profile of v5, /device:TPU:0, one launch (start us, length us, event | category | flops | bytes accessed | tf_op | source)
XLA Modules:
  0.0 634.3 jit_solution(12797442134900478777)
XLA Ops:
  17.7 21.6 %collective-permute-done = bf16[256,2048]{1,0:T(8,128)(2,1)S(1)} collective-permute-done((bf16[256,2048]{1,0:T(8,128)(2,1)S(1)}, bf16[256,2048]{1,0:T(8,128)(2,1)S(1)}, u32[]{:S(2)}, u32[]{:S(2)}) %collective-permute-start) | collective-permute-done | bytes 1048608 | tf_op jit(solution)/shard_map/ppermute | solution.py:387
  44.1 8.5 %collective-permute-done.2 = bf16[128,2048]{1,0:T(8,128)(2,1)S(1)} collective-permute-done((bf16[128,2048]{1,0:T(8,128)(2,1)S(1)}, bf16[128,2048]{1,0:T(8,128)(2,1)S(1)}, u32[]{:S(2)}, u32[]{:S(2)}) %collective-permute-start.2) | collective-permute-done | bytes 524320 | tf_op jit(solution)/shard_map/ppermute | solution.py:387
  63.6 8.9 %collective-permute-done.5.refs_1_ = bf16[128,2176]{1,0:T(8,128)(2,1)S(1)} collective-permute-done((bf16[128,2176]{1,0:T(8,128)(2,1)S(1)}, bf16[128,2176]{1,0:T(8,128)(2,1)S(1)}, u32[]{:S(2)}, u32[]{:S(2)}) %collective-permute-start.5) | collective-permute-done | bytes 557088 | tf_op jit(solution)/shard_map/ppermute | solution.py:438
  72.5 11.9 %collective-permute-done.6.refs_2_ = bf16[128,2176]{1,0:T(8,128)(2,1)S(1)} collective-permute-done((bf16[128,2176]{1,0:T(8,128)(2,1)S(1)}, bf16[128,2176]{1,0:T(8,128)(2,1)S(1)}, u32[]{:S(2)}, u32[]{:S(2)}) %collective-permute-start.6) | collective-permute-done | bytes 557088 | tf_op jit(solution)/shard_map/ppermute | solution.py:438
  89.0 7.8 %all-gather.4.cloned.1.call-done = bf16[2048,2048]{1,0:T(8,128)(2,1)} async-done(((bf16[256,2048]{1,0:T(8,128)(2,1)}), bf16[2048,2048]{1,0:T(8,128)(2,1)}) %all-gather.4.cloned.1.call-update) | async-done | bytes 8388624 | tf_op jit(solution)/shard_map/all_gather | solution.py:506
  96.8 12.2 %fusion.14.refs_1_ = f32[1024,1536]{1,0:T(8,128)} fusion(bf16[1024,2048]{1,0:T(8,128)(2,1)} %copy-done.18, bf16[2048,2048]{1,0:T(8,128)(2,1)} %all-gather.4.cloned.1.call-done, f32[1536]{0:T(1024)S(1)} %reshape.552), kind=kOutput, calls=%fused_computation.21 | convolution fusion | flops 6444023808 | bytes 16783360 | tf_op jit(solution)/shard_map/dot_general | solution.py:52
  109.0 18.2 %attend_forward.1 = (bf16[1024,1536]{1,0:T(8,128)(2,1)S(1)}, bf16[1024,512]{1,0:T(8,128)(2,1)S(1)}, f32[4,4,16,256]{3,2,1,0:T(8,128)S(1)}) custom-call(s32[5]{0:T(128)S(1)} %stack.30.info.refs_0_, f32[1024,1536]{1,0:T(8,128)} %fusion.14.refs_1_, f32[3,1024,128]{2,1,0:T(8,128)S(1)} %pad_maximum_fusion.3.refs_2_), custom_call_target="tpu_custom_call" | custom-call | tf_op jit(solution)/shard_map/attend_forward/pallas_call | solution.py:215
  136.1 10.7 %collective-permute-done.12 = bf16[128,2048]{1,0:T(8,128)(2,1)S(1)} collective-permute-done((bf16[128,2048]{1,0:T(8,128)(2,1)S(1)}, bf16[128,2048]{1,0:T(8,128)(2,1)S(1)}, u32[]{:S(2)}, u32[]{:S(2)}) %collective-permute-start.12) | collective-permute-done | bytes 524320 | tf_op jit(solution)/shard_map/ppermute | solution.py:387
  159.7 9.6 %collective-permute-done.10 = bf16[128,2048]{1,0:T(8,128)(2,1)S(1)} collective-permute-done((bf16[128,2048]{1,0:T(8,128)(2,1)S(1)}, bf16[128,2048]{1,0:T(8,128)(2,1)S(1)}, u32[]{:S(2)}, u32[]{:S(2)}) %collective-permute-start.10) | collective-permute-done | bytes 524320 | tf_op jit(solution)/shard_map/ppermute | solution.py:387
  176.1 17.3 %collective-permute-done.18 = bf16[256,2048]{1,0:T(8,128)(2,1)S(1)} collective-permute-done((bf16[256,2048]{1,0:T(8,128)(2,1)}, bf16[256,2048]{1,0:T(8,128)(2,1)S(1)}, u32[]{:S(2)}, u32[]{:S(2)}) %collective-permute-start.18) | collective-permute-done | bytes 1048608 | tf_op jit(solution)/shard_map/ppermute | solution.py:387
  247.5 17.3 %fusion.103 = f32[1024,2816]{1,0:T(8,128)S(1)} fusion(bf16[1024,2048]{1,0:T(8,128)(2,1)} %constant_dynamic-update-slice_fusion.5, bf16[2048,2816]{1,0:T(8,128)(2,1)} %all-gather.6.cloned.1.call-done), kind=kOutput, calls=%fused_computation.189 | convolution fusion | flops 11811160064 | bytes 27262976 | tf_op jit(solution)/shard_map/dot_general | solution.py:52
  283.3 14.7 %multiply_convert_fusion.1 = (bf16[1024,1408]{1,0:T(8,128)(2,1)S(1)}, bf16[1024,1408]{1,0:T(8,128)(2,1)S(1)}) fusion(f32[1024,2816]{1,0:T(8,128)} %copy-done.27, bf16[1024,2048]{1,0:T(8,128)(2,1)} %constant_dynamic-update-slice_fusion.10.mine.other, bf16[2048,1408]{1,0:T(8,128)(2,1)} %all-gather.8.cloned.1.call-done), kind=kOutput, calls=%fused_computation.6 | convolution fusion | flops 5924323328 | bytes 27262976 | tf_op jit(solution)/shard_map/dot_general | solution.py:52
  298.1 15.3 %fusion.17 = bf16[768,2048]{1,0:T(8,128)(2,1)} fusion(bf16[2048,2816]{1,0:T(8,128)(2,1)} %all-gather.6.cloned.1.call-done, bf16[1024,1408]{1,0:T(8,128)(2,1)S(1)} %get-tuple-element.106, bf16[1024,1408]{1,0:T(8,128)(2,1)S(1)} %get-tuple-element.105), kind=kOutput, calls=%fused_computation.29 | convolution fusion | flops 8868593664 | bytes 20447232 | tf_op jit(solution)/shard_map/dot_general | solution.py:52
  313.4 14.5 %convolution_convert_fusion = bf16[2048,2816]{1,0:T(8,128)(2,1)} fusion(bf16[1024,2048]{1,0:T(8,128)(2,1)S(1)} %copy-done.37, bf16[1024,1408]{1,0:T(8,128)(2,1)S(1)} %get-tuple-element.106, bf16[1024,1408]{1,0:T(8,128)(2,1)S(1)} %get-tuple-element.105), kind=kOutput, calls=%fused_computation | convolution fusion | flops 11828461568 | bytes 21495808 | tf_op jit(solution)/shard_map/dot_general | solution.py:52
  334.1 10.7 %collective-permute-done.24 = bf16[128,2048]{1,0:T(8,128)(2,1)S(1)} collective-permute-done((bf16[128,2048]{1,0:T(8,128)(2,1)S(1)}, bf16[128,2048]{1,0:T(8,128)(2,1)S(1)}, u32[]{:S(2)}, u32[]{:S(2)}) %collective-permute-start.24) | collective-permute-done | bytes 524320 | tf_op jit(solution)/shard_map/ppermute | solution.py:387
  357.6 10.2 %collective-permute-done.25 = bf16[128,2048]{1,0:T(8,128)(2,1)S(1)} collective-permute-done((bf16[128,2048]{1,0:T(8,128)(2,1)S(1)}, bf16[128,2048]{1,0:T(8,128)(2,1)S(1)}, u32[]{:S(2)}, u32[]{:S(2)}) %collective-permute-start.25) | collective-permute-done | bytes 524320 | tf_op jit(solution)/shard_map/ppermute | solution.py:387
  373.6 23.6 %collective-permute-done.29 = bf16[256,2048]{1,0:T(8,128)(2,1)S(1)} collective-permute-done((bf16[256,2048]{1,0:T(8,128)(2,1)}, bf16[256,2048]{1,0:T(8,128)(2,1)S(1)}, u32[]{:S(2)}, u32[]{:S(2)}) %collective-permute-start.29) | collective-permute-done | bytes 1048608 | tf_op jit(solution)/shard_map/ppermute | solution.py:387
  424.1 26.7 %attend_backward.1 = (bf16[1024,1536]{1,0:T(8,128)(2,1)S(1)}, f32[4,8,384]{2,1,0:T(8,128)S(1)}) custom-call(s32[5]{0:T(128)S(1)} %copy-done.8, bf16[1024,1536]{1,0:T(8,128)(2,1)} %copy-done, f32[3,1024,128]{2,1,0:T(8,128)S(1)} %pad_maximum_fusion.3.refs_2_, f32[4,4,16,256]{3,2,1,0:T(8,128)S(1)} %get-tuple-element.49.refs_3_, ...), custom_call_target="tpu_custom_call" | custom-call | tf_op jit(solution)/shard_map/attend_backward/pallas_call | solution.py:253
  465.0 9.1 %convolution_convert_fusion.4 = bf16[768,2048]{1,0:T(8,128)(2,1)} fusion(bf16[2048,1408]{1,0:T(8,128)(2,1)} %all-gather.8.cloned.1.call-done, bf16[1024,1408]{1,0:T(8,128)(2,1)S(1)} %copy-done.32), kind=kOutput, calls=%fused_computation.32 | convolution fusion | flops 4430757888 | bytes 11075584 | tf_op jit(solution)/shard_map/dot_general | solution.py:52
  490.8 8.4 %fusion.20 = bf16[768,2048]{1,0:T(8,128)(2,1)S(1)} fusion(bf16[2048,2048]{1,0:T(8,128)(2,1)} %all-gather.4.cloned.1.call-done, bf16[1024,1536]{1,0:T(8,128)(2,1)S(1)} %copy-done.12), kind=kOutput, calls=%fused_computation.31 | convolution fusion | flops 4833411072 | bytes 11796480 | tf_op jit(solution)/shard_map/dot_general | solution.py:52
  517.2 8.4 %collective-permute-done.34 = bf16[128,2048]{1,0:T(8,128)(2,1)S(1)} collective-permute-done((bf16[128,2048]{1,0:T(8,128)(2,1)S(1)}, bf16[128,2048]{1,0:T(8,128)(2,1)S(1)}, u32[]{:S(2)}, u32[]{:S(2)}) %collective-permute-start.34) | collective-permute-done | bytes 524320 | tf_op jit(solution)/shard_map/ppermute | solution.py:387
  526.4 11.2 %collective-permute-done.37 = bf16[128,2048]{1,0:T(8,128)(2,1)S(1)} collective-permute-done((bf16[128,2048]{1,0:T(8,128)(2,1)S(1)}, bf16[128,2048]{1,0:T(8,128)(2,1)S(1)}, u32[]{:S(2)}, u32[]{:S(2)}) %collective-permute-start.37) | collective-permute-done | bytes 524320 | tf_op jit(solution)/shard_map/ppermute | solution.py:387
  554.9 16.2 %collective-permute-done.46 = f32[7,2048]{1,0:T(8,128)S(1)} collective-permute-done((f32[7,2048]{1,0:T(8,128)S(1)}, f32[7,2048]{1,0:T(8,128)S(1)}, u32[]{:S(2)}, u32[]{:S(2)}) %collective-permute-start.46) | collective-permute-done | bytes 57376 | tf_op jit(solution)/shard_map/ppermute | solution.py:451
  603.4 14.0 %collective-permute-done.53.refs_1_ = bf16[128,2176]{1,0:T(8,128)(2,1)S(1)} collective-permute-done((bf16[128,2176]{1,0:T(8,128)(2,1)}, bf16[128,2176]{1,0:T(8,128)(2,1)S(1)}, u32[]{:S(2)}, u32[]{:S(2)}) %collective-permute-start.53) | collective-permute-done | bytes 557088 | tf_op jit(solution)/shard_map/ppermute | solution.py:442
  (349 shorter events, 291.0 us)
Async XLA Ops:
  7.2 89.6 %all-gather.4.cloned.1.call-start = ((), (), s32[]{:S(2)}) async-start(), calls=%async_computation.3 | async-start | bytes 9437184 | tf_op jit(solution)/shard_map/all_gather | solution.py:506
  11.8 235.6 %all-gather.6.cloned.1.call-start = ((), (), s32[]{:S(2)}) async-start(), calls=%async_computation.4 | async-start | bytes 12976128 | tf_op jit(solution)/shard_map/all_gather | solution.py:525
  13.2 26.2 %collective-permute-start = (bf16[256,2048]{1,0:T(8,128)(2,1)S(1)}, bf16[256,2048]{1,0:T(8,128)(2,1)S(1)}, u32[]{:S(2)}, u32[]{:S(2)}) collective-permute-start(bf16[256,2048]{1,0:T(8,128)(2,1)S(1)} %get-tuple-element.104), channel_id=1, source_target_pairs={{0,2},{2,0},{4,6},{6,4},{1,3},{3,1},{5,7},{7,5},{8,10},{10,8},{12,... | collective-permute-start | bytes 3145736 | tf_op jit(solution)/shard_map/ppermute | solution.py:387
  16.2 26.1 %collective-permute-start.1 = (bf16[256,2048]{1,0:T(8,128)(2,1)S(1)}, bf16[256,2048]{1,0:T(8,128)(2,1)S(1)}, u32[]{:S(2)}, u32[]{:S(2)}) collective-permute-start(bf16[256,2048]{1,0:T(8,128)(2,1)S(1)} %get-tuple-element.104), channel_id=1, source_target_pairs={{0,4},{2,6},{4,0},{6,2},{1,5},{3,7},{5,1},{7,3},{8,12},{10,14},{12... | collective-permute-start | bytes 3145736 | tf_op jit(solution)/shard_map/ppermute | solution.py:387
  59.4 24.9 %collective-permute-start.6 = (bf16[128,2176]{1,0:T(8,128)(2,1)S(1)}, bf16[128,2176]{1,0:T(8,128)(2,1)S(1)}, u32[]{:S(2)}, u32[]{:S(2)}) collective-permute-start(bf16[128,2176]{1,0:T(8,128)(2,1)S(1)} %get-tuple-element.136), channel_id=1, source_target_pairs={{0,4},{1,6},{2,0},{3,2},{4,5},{5,7},{6,1},{7,3},{8,12},{9,14},{10,... | collective-permute-start | bytes 1671176 | tf_op jit(solution)/shard_map/ppermute | solution.py:438
  86.7 196.6 %all-gather.8.cloned.1.call-start = ((), (), s32[]{:S(2)}) async-start(), calls=%async_computation.5 | async-start | bytes 6488064 | tf_op jit(solution)/shard_map/all_gather | solution.py:526
  150.9 42.5 %collective-permute-start.18 = (bf16[256,2048]{1,0:T(8,128)(2,1)}, bf16[256,2048]{1,0:T(8,128)(2,1)S(1)}, u32[]{:S(2)}, u32[]{:S(2)}) collective-permute-start(bf16[256,2048]{1,0:T(8,128)(2,1)} %bitcast.14), channel_id=1, source_target_pairs={{0,2},{2,0},{4,6},{6,4},{1,3},{3,1},{5,7},{7,5},{8,10},{10,8},{12,... | collective-permute-start | bytes 3145736 | tf_op jit(solution)/shard_map/ppermute | solution.py:387
  158.1 41.5 %collective-permute-start.19 = (bf16[256,2048]{1,0:T(8,128)(2,1)}, bf16[256,2048]{1,0:T(8,128)(2,1)}, u32[]{:S(2)}, u32[]{:S(2)}) collective-permute-start(bf16[256,2048]{1,0:T(8,128)(2,1)} %bitcast.14), channel_id=1, source_target_pairs={{0,4},{2,6},{4,0},{6,2},{1,5},{3,7},{5,1},{7,3},{8,12},{10,14},{12... | collective-permute-start | bytes 3145736 | tf_op jit(solution)/shard_map/ppermute | solution.py:387
  174.6 41.3 %collective-permute-start.14 = (bf16[256,2048]{1,0:T(8,128)(2,1)}, bf16[256,2048]{1,0:T(8,128)(2,1)}, u32[]{:S(2)}, u32[]{:S(2)}) collective-permute-start(bf16[256,2048]{1,0:T(8,128)(2,1)} %get-tuple-element.100), channel_id=1, source_target_pairs={{0,2},{2,0},{4,6},{6,4},{1,3},{3,1},{5,7},{7,5},{8,10},{10,8},{12,... | collective-permute-start | bytes 3145736 | tf_op jit(solution)/shard_map/ppermute | solution.py:387
  195.6 37.2 %collective-permute-start.15 = (bf16[256,2048]{1,0:T(8,128)(2,1)}, bf16[256,2048]{1,0:T(8,128)(2,1)}, u32[]{:S(2)}, u32[]{:S(2)}) collective-permute-start(bf16[256,2048]{1,0:T(8,128)(2,1)} %get-tuple-element.100), channel_id=1, source_target_pairs={{0,4},{2,6},{4,0},{6,2},{1,5},{3,7},{5,1},{7,3},{8,12},{10,14},{12... | collective-permute-start | bytes 3145736 | tf_op jit(solution)/shard_map/ppermute | solution.py:387
  199.5 387.6 %reduce-scatter.8.cloned.1.call-start = ((), (), s32[]{:S(2)}) async-start(), calls=%async_computation.8 | async-start | bytes 3604480 | tf_op jit(solution)/shard_map/reduce_scatter | solution.py:558
  200.7 25.3 %collective-permute-start.21 = (bf16[128,2048]{1,0:T(8,128)(2,1)S(1)}, bf16[128,2048]{1,0:T(8,128)(2,1)S(1)}, u32[]{:S(2)}, u32[]{:S(2)}) collective-permute-start(bf16[128,2048]{1,0:T(8,128)(2,1)S(1)} %slice.316), channel_id=1, source_target_pairs={{0,2},{2,0},{4,6},{6,4},{1,3},{3,1},{5,7},{7,5},{8,10},{10,8},{12,... | collective-permute-start | bytes 1572872 | tf_op jit(solution)/shard_map/ppermute | solution.py:387
  283.3 303.9 %reduce-scatter.6.cloned.1.call-start = ((), (), s32[]{:S(2)}) async-start(), calls=%async_computation.7 | async-start | bytes 12976128 | tf_op jit(solution)/shard_map/reduce_scatter | solution.py:574
  328.0 272.2 %reduce-scatter.4.cloned.1.call-start = ((), (), s32[]{:S(2)}) async-start(), calls=%async_computation.6 | async-start | bytes 5242880 | tf_op jit(solution)/shard_map/reduce_scatter | solution.py:600
  332.6 25.0 %collective-permute-start.26 = (bf16[128,2048]{1,0:T(8,128)(2,1)S(1)}, bf16[128,2048]{1,0:T(8,128)(2,1)S(1)}, u32[]{:S(2)}, u32[]{:S(2)}) collective-permute-start(bf16[128,2048]{1,0:T(8,128)(2,1)S(1)} %get-tuple-element.121), channel_id=1, source_target_pairs={{0,4},{2,6},{4,0},{6,2},{1,5},{3,7},{5,1},{7,3},{8,12},{10,14},{12... | collective-permute-start | bytes 1572872 | tf_op jit(solution)/shard_map/ppermute | solution.py:387
  373.2 31.6 %collective-permute-start.30 = (bf16[256,2048]{1,0:T(8,128)(2,1)}, bf16[256,2048]{1,0:T(8,128)(2,1)}, u32[]{:S(2)}, u32[]{:S(2)}) collective-permute-start(bf16[256,2048]{1,0:T(8,128)(2,1)} %get-tuple-element.98), channel_id=1, source_target_pairs={{0,4},{2,6},{4,0},{6,2},{1,5},{3,7},{5,1},{7,3},{8,12},{10,14},{12... | collective-permute-start | bytes 3145736 | tf_op jit(solution)/shard_map/ppermute | solution.py:387
  506.3 33.9 %collective-permute-start.39 = (bf16[128,2048]{1,0:T(8,128)(2,1)S(1)}, bf16[128,2048]{1,0:T(8,128)(2,1)S(1)}, u32[]{:S(2)}, u32[]{:S(2)}) collective-permute-start(bf16[128,2048]{1,0:T(8,128)(2,1)S(1)} %get-tuple-element.107), channel_id=1, source_target_pairs={{0,2},{2,0},{4,6},{6,4},{1,3},{3,1},{5,7},{7,5},{8,10},{10,8},{12,... | collective-permute-start | bytes 1572872 | tf_op jit(solution)/shard_map/ppermute | solution.py:387
  507.0 34.9 %collective-permute-start.42 = (bf16[128,2048]{1,0:T(8,128)(2,1)S(1)}, bf16[128,2048]{1,0:T(8,128)(2,1)S(1)}, u32[]{:S(2)}, u32[]{:S(2)}) collective-permute-start(bf16[128,2048]{1,0:T(8,128)(2,1)S(1)} %get-tuple-element.109), channel_id=1, source_target_pairs={{0,4},{2,6},{4,0},{6,2},{1,5},{3,7},{5,1},{7,3},{8,12},{10,14},{12... | collective-permute-start | bytes 1572872 | tf_op jit(solution)/shard_map/ppermute | solution.py:387
  516.4 32.4 %collective-permute-start.41 = (bf16[128,2048]{1,0:T(8,128)(2,1)S(1)}, bf16[128,2048]{1,0:T(8,128)(2,1)S(1)}, u32[]{:S(2)}, u32[]{:S(2)}) collective-permute-start(bf16[128,2048]{1,0:T(8,128)(2,1)S(1)} %get-tuple-element.111), channel_id=1, source_target_pairs={{0,4},{2,6},{4,0},{6,2},{1,5},{3,7},{5,1},{7,3},{8,12},{10,14},{12... | collective-permute-start | bytes 1572872 | tf_op jit(solution)/shard_map/ppermute | solution.py:387
  537.6 39.8 %collective-permute-start.33 = (bf16[128,2048]{1,0:T(8,128)(2,1)}, bf16[128,2048]{1,0:T(8,128)(2,1)}, u32[]{:S(2)}, u32[]{:S(2)}) collective-permute-start(bf16[128,2048]{1,0:T(8,128)(2,1)} %get-tuple-element.113), channel_id=1, source_target_pairs={{0,2},{2,0},{4,6},{6,4},{1,3},{3,1},{5,7},{7,5},{8,10},{10,8},{12,... | collective-permute-start | bytes 1572872 | tf_op jit(solution)/shard_map/ppermute | solution.py:387
  540.2 37.2 %collective-permute-start.36 = (bf16[128,2048]{1,0:T(8,128)(2,1)}, bf16[128,2048]{1,0:T(8,128)(2,1)}, u32[]{:S(2)}, u32[]{:S(2)}) collective-permute-start(bf16[128,2048]{1,0:T(8,128)(2,1)} %get-tuple-element.115), channel_id=1, source_target_pairs={{0,4},{2,6},{4,0},{6,2},{1,5},{3,7},{5,1},{7,3},{8,12},{10,14},{12... | collective-permute-start | bytes 1572872 | tf_op jit(solution)/shard_map/ppermute | solution.py:387
  541.9 35.5 %collective-permute-start.35 = (bf16[128,2048]{1,0:T(8,128)(2,1)}, bf16[128,2048]{1,0:T(8,128)(2,1)}, u32[]{:S(2)}, u32[]{:S(2)}) collective-permute-start(bf16[128,2048]{1,0:T(8,128)(2,1)} %get-tuple-element.117), channel_id=1, source_target_pairs={{0,4},{2,6},{4,0},{6,2},{1,5},{3,7},{5,1},{7,3},{8,12},{10,14},{12... | collective-permute-start | bytes 1572872 | tf_op jit(solution)/shard_map/ppermute | solution.py:387
  548.9 28.6 %collective-permute-start.38 = (bf16[128,2048]{1,0:T(8,128)(2,1)}, bf16[128,2048]{1,0:T(8,128)(2,1)}, u32[]{:S(2)}, u32[]{:S(2)}) collective-permute-start(bf16[128,2048]{1,0:T(8,128)(2,1)} %get-tuple-element.118), channel_id=1, source_target_pairs={{0,2},{2,0},{4,6},{6,4},{1,3},{3,1},{5,7},{7,5},{8,10},{10,8},{12,... | collective-permute-start | bytes 1572872 | tf_op jit(solution)/shard_map/ppermute | solution.py:387
  595.5 25.8 %collective-permute-start.55 = (bf16[128,2176]{1,0:T(8,128)(2,1)S(1)}, bf16[128,2176]{1,0:T(8,128)(2,1)S(1)}, u32[]{:S(2)}, u32[]{:S(2)}) collective-permute-start(bf16[128,2176]{1,0:T(8,128)(2,1)S(1)} %get-tuple-element.131), channel_id=1, source_target_pairs={{6,0},{4,1},{2,2},{0,3},{7,4},{5,5},{3,6},{1,7},{14,8},{12,9},{10,... | collective-permute-start | bytes 1671176 | tf_op jit(solution)/shard_map/ppermute | solution.py:442
  (98 other events, 1226.8 us)
Sparse Core Ops, SparseCore 0:
  12.0 84.7 all-gather.3
  99.0 106.5 all-gather.5
  207.2 58.6 all-gather.7
  283.4 54.1 reduce-scatter.7
  339.7 118.9 reduce-scatter.5
  484.7 74.3 reduce-scatter.3

commit v6 on v5

--- a/solution.py
+++ b/solution.py
@@ -15,6 +15,8 @@
 norm_eps = 1e-05
 rope_base = 10000.0
 masked_fill = -1e30
+
+DP, ROW, COL = "dp", "row", "col"
 
 bf16 = jnp.bfloat16
 f32 = jnp.float32
@@ -220,7 +222,7 @@
             jax.ShapeDtypeStruct((length, w * pairs), bf16),
             jax.ShapeDtypeStruct((pairs, blocks, 16, size), f32),
         ],
-        name="attend_forward",
+        name="attn_f",
         compiler_params=pltpu.CompilerParams(vmem_limit_bytes=48 << 20),
     )(info, projected, table)
 
@@ -257,7 +259,7 @@
             jax.ShapeDtypeStruct((length, 3 * w * pairs), bf16),
             jax.ShapeDtypeStruct((pairs, 8, 3 * w), f32),
         ],
-        name="attend_backward",
+        name="attn_b",
         compiler_params=pltpu.CompilerParams(vmem_limit_bytes=48 << 20),
     )(info, qkv, table, sums, grads)
 
@@ -379,12 +381,12 @@
 
 
 def make_body(mesh):
-    R = mesh.shape["row"]
-    C = mesh.shape["col"]
+    R = mesh.shape[ROW]
+    C = mesh.shape[COL]
     N = max(R, C)
 
     def row_permute(block, k):
-        return lax.ppermute(block, "row", [(i, i ^ k) for i in range(R)])
+        return lax.ppermute(block, ROW, [(i, i ^ k) for i in range(R)])
 
     def gather_rel(block, after=None):
         if R != 4:
@@ -435,16 +437,16 @@
         return pairs
 
     def spread(packed):
-        return [lax.ppermute(packed[k], ("row", "col"), exchange_pairs(k)) for k in range(N)]
+        return [lax.ppermute(packed[k], (ROW, COL), exchange_pairs(k)) for k in range(N)]
 
     def bring_back(packed):
         return [
-            lax.ppermute(packed[k], ("row", "col"), [(b, a) for a, b in exchange_pairs(k)])
+            lax.ppermute(packed[k], (ROW, COL), [(b, a) for a, b in exchange_pairs(k)])
             for k in range(N)
         ]
 
     def sum_everywhere(array):
-        for name in ("col", "row", "dp"):
+        for name in (COL, DP, ROW):
             size = mesh.shape[name]
             step = 1
             while step < size:
@@ -455,7 +457,7 @@
 
     def pair_sum(mine, other, right):
         away = tn(other, right).astype(bf16)
-        got = lax.ppermute(away, "col", [(0, 1), (1, 0)])
+        got = lax.ppermute(away, COL, [(0, 1), (1, 0)])
         return (tn(mine, right) + got.astype(f32)).astype(bf16)
 
     def body(
@@ -472,8 +474,8 @@
         down_projection_weight,
         grad_out,
     ):
-        r = lax.axis_index("row")
-        c = lax.axis_index("col")
+        r = lax.axis_index(ROW)
+        c = lax.axis_index(COL)
         block = tokens.shape[1]
         width = tokens.shape[2]
         head_cols = query_key_value_weight.shape[2]
@@ -503,7 +505,7 @@
             [query_key_value_weight.transpose(1, 0, 2), attention_output_weight],
             [jax.ShapeDtypeStruct((attention_output_weight.shape[0], 4 * head_cols), bf16)],
         )
-        w_attn = lax.all_gather(attn_shard, ("dp", "col"), axis=0, tiled=True)
+        w_attn = lax.all_gather(attn_shard, (DP, COL), axis=0, tiled=True)
         (packed,) = whole_call(
             functools.partial(pack_kernel, R, q_rows),
             info,
@@ -522,8 +524,8 @@
             ],
             [held],
         )
-        w_gu = lax.all_gather(gu_shard, ("dp", "col"), axis=0, tiled=True)
-        w_down = lax.all_gather(down_shard, ("dp", "col"), axis=0, tiled=True)
+        w_gu = lax.all_gather(gu_shard, (DP, COL), axis=0, tiled=True)
+        w_down = lax.all_gather(down_shard, (DP, COL), axis=0, tiled=True)
 
         w_attn, _ = lax.optimization_barrier((w_attn, gu_shard))
         w_qkv = w_attn[:, : 3 * head_cols]
@@ -551,15 +553,17 @@
         swish = gate_vals * sig
         hidden = (swish * up_vals).astype(bf16)
         if C == 2:
-            seq_halves = split_columns(info, seq_in, mesh.shape["dp"])
-            halves = split_columns(info, dy_rel, mesh.shape["dp"])
+            seq_halves = split_columns(info, seq_in, mesh.shape[DP])
+            halves = split_columns(info, dy_rel, mesh.shape[DP])
             grad_down = pair_sum(*halves, hidden)
             _, w_down = lax.optimization_barrier((grad_down, w_down))
-            grad_down = lax.psum_scatter(grad_down, "dp", scatter_dimension=0, tiled=True)
+            grad_down = lax.psum_scatter(grad_down, DP, scatter_dimension=0, tiled=True)
         else:
             grad_down = tn(dy_rel, hidden).astype(bf16)
             _, w_down = lax.optimization_barrier((grad_down, w_down))
-            grad_down = lax.psum_scatter(grad_down, ("dp", "col"), scatter_dimension=0, tiled=True)
+            grad_down = lax.psum_scatter(
+                grad_down, (DP, COL), scatter_dimension=0, tiled=True
+            )
         grad_hidden = nn(dy_rel, w_down)
         grad_gate = grad_hidden * up_vals * sig * (1.0 + gate_vals * (1.0 - sig))
         grad_up = grad_hidden * swish
@@ -571,7 +575,7 @@
             [own] + [others[k * block : (k + 1) * block] for k in range(R - 1)]
         )
         grad_gu = tn(second_in, grad_gu_vals).astype(bf16)
-        grad_gu = lax.psum_scatter(grad_gu, ("dp", "col"), scatter_dimension=0, tiled=True)
+        grad_gu = lax.psum_scatter(grad_gu, (DP, COL), scatter_dimension=0, tiled=True)
 
         grad_middle = dy.astype(f32) + layer_norm_backward(
             grad_second, second_std, second_inv, gain2
@@ -592,17 +596,23 @@
         bias_local = bias_local[:, 0].reshape(pairs, 3, 2 * HD)
         bias_local = bias_local.transpose(1, 0, 2).reshape(3, head_cols)
         if C == 2:
-            halves = split_columns(info, branch, mesh.shape["dp"])
+            outer = tn(branch, attended).astype(bf16).reshape(mesh.shape[DP], C, -1, head_cols)
+            away = lax.dynamic_index_in_dim(outer, 1 - c, 1, keepdims=False)
+            mine = lax.dynamic_index_in_dim(outer, c, 1, keepdims=False)
+            got = lax.ppermute(away.reshape(-1, head_cols), COL, [(0, 1), (1, 0)])
+            outer = mine.reshape(-1, head_cols).astype(f32) + got.astype(f32)
             grad_attn = jnp.concatenate(
-                [pair_sum(*seq_halves, grad_proj), pair_sum(*halves, attended)],
-                axis=1,
+                [pair_sum(*seq_halves, grad_proj), outer.astype(bf16)], axis=1
             )
-            grad_attn = lax.psum_scatter(grad_attn, "dp", scatter_dimension=0, tiled=True)
+            grad_proj, _ = lax.optimization_barrier((grad_proj, grad_attn))
+            grad_attn = lax.psum_scatter(grad_attn, DP, scatter_dimension=0, tiled=True)
         else:
             grad_attn = jnp.concatenate(
                 [tn(seq_in, grad_proj).astype(bf16), tn(branch, attended).astype(bf16)], axis=1
             )
-            grad_attn = lax.psum_scatter(grad_attn, ("dp", "col"), scatter_dimension=0, tiled=True)
+            grad_attn = lax.psum_scatter(
+                grad_attn, (DP, COL), scatter_dimension=0, tiled=True
+            )
         own = nt(grad_proj[:block], w_qkv)
         others = nt(grad_proj[block:], w_qkv).astype(bf16)
         grad_first = scatter_rel(
@@ -664,31 +674,31 @@
 
 def solution(mesh):
     in_specs = (
-        P(("dp", "col"), "row", None),
-        P(("dp", "col")),
+        P((DP, COL), ROW, None),
+        P((DP, COL)),
         P(),
         P(),
-        P(("dp", "col"), None, "row"),
-        P(None, "row"),
-        P(("dp", "col"), "row"),
+        P((DP, COL), None, ROW),
+        P(None, ROW),
+        P((DP, COL), ROW),
         P(),
         P(),
-        P(("dp", "row"), None, "col"),
-        P(("dp", "row"), "col"),
-        P(("dp", "col"), "row", None),
+        P((DP, ROW), None, COL),
+        P((DP, ROW), COL),
+        P((DP, COL), ROW, None),
     )
     out_specs = (
-        P(("dp", "col"), "row", None),
-        P(("dp", "col"), "row", None),
+        P((DP, COL), ROW, None),
+        P((DP, COL), ROW, None),
         P(),
         P(),
-        P(("dp", "col"), None, "row"),
-        P(None, "row"),
-        P(("dp", "col"), "row"),
+        P((DP, COL), None, ROW),
+        P(None, ROW),
+        P((DP, COL), ROW),
         P(),
         P(),
-        P(("dp", "row"), None, "col"),
-        P(("dp", "row"), "col"),
+        P((DP, ROW), None, COL),
+        P((DP, ROW), COL),
     )
     body = make_body(mesh)
 

time: 641 us -> 638 us (level)
    ppermute x5, waiting for transfers between devices: 23 us -> 11 us  [sum_everywhere(): other = lax.ppermute(array, name, [(i, i ^ step) for i in range(size)])]
    ppermute x51, waiting for transfers between devices: 230 us -> 241 us  [the longest x40 198 us: row_permute(): return lax.ppermute(block, ROW, [(i, i ^ k) for i in range(R)])]
    pallas_call x3 -> x2, Pallas kernels: 16.5 us -> 11.1 us  [split_columns(): pl.pallas_call(split_kernel, grid_spec=pltpu.PrefetchScalarGridSpec(num_s...]
    unnamed x136 -> x134, local copies, waits for them, and re-layouts: 36.5 us -> 37.7 us
    dot_general x19 -> x18, matrix products: 142 us -> 142 us  [dot(): lax.dot_general(left, right, (dims, ((), ())), preferred_element_type=f32)]
  transfers between devices with their start and end apart: 62 -> 62, of which waited for: 37 -> 40; matrix products, arithmetic and copies ran while one was open for 32% -> 33% of each run, Pallas kernels for 11% -> 10%
where the time goes in v6:
time: 638 us; the launch traced here: 632 us
  waiting for transfers between devices  260 us (41%)
  matrix products  142 us (22%)
  Pallas kernels  66.2 us (10%)
  starting transfers between devices  64.5 us (10%)
  local copies, waits for them, and re-layouts  53.5 us (8%)
  other arithmetic  29.5 us (5%)
  between operations  16.1 us (3%)
    ppermute x40, waiting for transfers between devices, row_permute(): return lax.ppermute(block, ROW, [(i, i ^ k) for i in range(R)])  198 us
    dot_general x18, matrix products, dot(): lax.dot_general(left, right, (dims, ((), ())), preferred_element_type=f32)  142 us
    ppermute x40, starting transfers between devices, row_permute(): return lax.ppermute(block, ROW, [(i, i ^ k) for i in range(R)])  44.5 us
    unnamed x134, local copies, waits for them, and re-layouts  37.7 us
    pallas_call x1, Pallas kernels, attend_backward(): pl.pallas_call(lambda *refs: backward_kernel(blocks, size, *refs), grid_s...  26.7 us
    ppermute x4, waiting for transfers between devices, spread(): lax.ppermute(packed[k], (ROW, COL), exchange_pairs(k))  20.8 us
    pallas_call x1, Pallas kernels, attend_forward(): pl.pallas_call(lambda *refs: forward_kernel(blocks, size, *refs), grid_sp...  18.2 us
    ppermute x4, waiting for transfers between devices, bring_back(): lax.ppermute(packed[k], (ROW, COL), [(b, a) for a, b in exchange_pairs(k)])  17.3 us
  transfers between devices with their start and end apart: 62, of which 40 were waited for; matrix products, arithmetic and copies ran while one was open for 33% of the time, Pallas kernels for 10%

profile of v6, /device:TPU:0, one launch (start us, length us, event | category | flops | bytes accessed | tf_op | source)
XLA Modules:
  0.0 631.8 jit_solution(7765296407524071006)
XLA Ops:
  17.7 21.6 %collective-permute-done = bf16[256,2048]{1,0:T(8,128)(2,1)S(1)} collective-permute-done((bf16[256,2048]{1,0:T(8,128)(2,1)S(1)}, bf16[256,2048]{1,0:T(8,128)(2,1)S(1)}, u32[]{:S(2)}, u32[]{:S(2)}) %collective-permute-start) | collective-permute-done | bytes 1048608 | tf_op jit(solution)/shard_map/ppermute | solution.py:389
  44.1 8.5 %collective-permute-done.2 = bf16[128,2048]{1,0:T(8,128)(2,1)S(1)} collective-permute-done((bf16[128,2048]{1,0:T(8,128)(2,1)S(1)}, bf16[128,2048]{1,0:T(8,128)(2,1)S(1)}, u32[]{:S(2)}, u32[]{:S(2)}) %collective-permute-start.2) | collective-permute-done | bytes 524320 | tf_op jit(solution)/shard_map/ppermute | solution.py:389
  63.6 8.9 %collective-permute-done.5.refs_1_ = bf16[128,2176]{1,0:T(8,128)(2,1)S(1)} collective-permute-done((bf16[128,2176]{1,0:T(8,128)(2,1)S(1)}, bf16[128,2176]{1,0:T(8,128)(2,1)S(1)}, u32[]{:S(2)}, u32[]{:S(2)}) %collective-permute-start.5) | collective-permute-done | bytes 557088 | tf_op jit(solution)/shard_map/ppermute | solution.py:440
  72.5 11.9 %collective-permute-done.6.refs_2_ = bf16[128,2176]{1,0:T(8,128)(2,1)S(1)} collective-permute-done((bf16[128,2176]{1,0:T(8,128)(2,1)S(1)}, bf16[128,2176]{1,0:T(8,128)(2,1)S(1)}, u32[]{:S(2)}, u32[]{:S(2)}) %collective-permute-start.6) | collective-permute-done | bytes 557088 | tf_op jit(solution)/shard_map/ppermute | solution.py:440
  89.0 7.7 %all-gather.4.cloned.1.call-done = bf16[2048,2048]{1,0:T(8,128)(2,1)} async-done(((bf16[256,2048]{1,0:T(8,128)(2,1)}), bf16[2048,2048]{1,0:T(8,128)(2,1)}) %all-gather.4.cloned.1.call-update) | async-done | bytes 8388624 | tf_op jit(solution)/shard_map/all_gather | solution.py:508
  96.8 12.2 %fusion.14.refs_1_ = f32[1024,1536]{1,0:T(8,128)} fusion(bf16[1024,2048]{1,0:T(8,128)(2,1)} %copy-done.17, bf16[2048,2048]{1,0:T(8,128)(2,1)} %all-gather.4.cloned.1.call-done, f32[1536]{0:T(1024)S(1)} %reshape.565), kind=kOutput, calls=%fused_computation.21 | convolution fusion | flops 6444023808 | bytes 16783360 | tf_op jit(solution)/shard_map/dot_general | solution.py:54
  109.0 18.2 %attn_f.1 = (bf16[1024,1536]{1,0:T(8,128)(2,1)S(1)}, bf16[1024,512]{1,0:T(8,128)(2,1)S(1)}, f32[4,4,16,256]{3,2,1,0:T(8,128)S(1)}) custom-call(s32[5]{0:T(128)S(1)} %stack.30.info.refs_0_, f32[1024,1536]{1,0:T(8,128)} %fusion.14.refs_1_, f32[3,1024,128]{2,1,0:T(8,128)S(1)} %pad_maximum_fusion.3.refs_2_), custom_call_target="tpu_custom_call" | custom-call | tf_op jit(solution)/shard_map/attn_f/pallas_call | solution.py:217
  136.0 10.7 %collective-permute-done.12 = bf16[128,2048]{1,0:T(8,128)(2,1)S(1)} collective-permute-done((bf16[128,2048]{1,0:T(8,128)(2,1)S(1)}, bf16[128,2048]{1,0:T(8,128)(2,1)S(1)}, u32[]{:S(2)}, u32[]{:S(2)}) %collective-permute-start.12) | collective-permute-done | bytes 524320 | tf_op jit(solution)/shard_map/ppermute | solution.py:389
  159.7 9.5 %collective-permute-done.10 = bf16[128,2048]{1,0:T(8,128)(2,1)S(1)} collective-permute-done((bf16[128,2048]{1,0:T(8,128)(2,1)S(1)}, bf16[128,2048]{1,0:T(8,128)(2,1)S(1)}, u32[]{:S(2)}, u32[]{:S(2)}) %collective-permute-start.10) | collective-permute-done | bytes 524320 | tf_op jit(solution)/shard_map/ppermute | solution.py:389
  176.1 17.3 %collective-permute-done.18 = bf16[256,2048]{1,0:T(8,128)(2,1)S(1)} collective-permute-done((bf16[256,2048]{1,0:T(8,128)(2,1)}, bf16[256,2048]{1,0:T(8,128)(2,1)S(1)}, u32[]{:S(2)}, u32[]{:S(2)}) %collective-permute-start.18) | collective-permute-done | bytes 1048608 | tf_op jit(solution)/shard_map/ppermute | solution.py:389
  218.3 7.8 %collective-permute-done.21 = bf16[128,2048]{1,0:T(8,128)(2,1)S(1)} collective-permute-done((bf16[128,2048]{1,0:T(8,128)(2,1)S(1)}, bf16[128,2048]{1,0:T(8,128)(2,1)S(1)}, u32[]{:S(2)}, u32[]{:S(2)}) %collective-permute-start.21) | collective-permute-done | bytes 524320 | tf_op jit(solution)/shard_map/ppermute | solution.py:389
  247.5 17.3 %fusion.104 = f32[1024,2816]{1,0:T(8,128)S(1)} fusion(bf16[1024,2048]{1,0:T(8,128)(2,1)} %constant_dynamic-update-slice_fusion.5, bf16[2048,2816]{1,0:T(8,128)(2,1)} %all-gather.6.cloned.1.call-done), kind=kOutput, calls=%fused_computation.192 | convolution fusion | flops 11811160064 | bytes 27262976 | tf_op jit(solution)/shard_map/dot_general | solution.py:54
  283.4 14.7 %multiply_convert_fusion.1 = (bf16[1024,1408]{1,0:T(8,128)(2,1)S(1)}, bf16[1024,1408]{1,0:T(8,128)(2,1)S(1)}) fusion(f32[1024,2816]{1,0:T(8,128)} %copy-done.26, bf16[1024,2048]{1,0:T(8,128)(2,1)} %constant_dynamic-update-slice_fusion.10.mine.other, bf16[2048,1408]{1,0:T(8,128)(2,1)} %all-gather.8.cloned.1.call-done), kind=kOutput, calls=%fused_computation.6 | convolution fusion | flops 5924323328 | bytes 27262976 | tf_op jit(solution)/shard_map/dot_general | solution.py:54
  298.1 15.3 %fusion.17 = bf16[768,2048]{1,0:T(8,128)(2,1)} fusion(bf16[2048,2816]{1,0:T(8,128)(2,1)} %all-gather.6.cloned.1.call-done, bf16[1024,1408]{1,0:T(8,128)(2,1)S(1)} %get-tuple-element.104, bf16[1024,1408]{1,0:T(8,128)(2,1)S(1)} %get-tuple-element.103), kind=kOutput, calls=%fused_computation.29 | convolution fusion | flops 8868593664 | bytes 20447232 | tf_op jit(solution)/shard_map/dot_general | solution.py:54
  313.4 14.6 %convolution_convert_fusion = bf16[2048,2816]{1,0:T(8,128)(2,1)} fusion(bf16[1024,2048]{1,0:T(8,128)(2,1)S(1)} %copy-done.37, bf16[1024,1408]{1,0:T(8,128)(2,1)S(1)} %get-tuple-element.104, bf16[1024,1408]{1,0:T(8,128)(2,1)S(1)} %get-tuple-element.103), kind=kOutput, calls=%fused_computation | convolution fusion | flops 11828461568 | bytes 21495808 | tf_op jit(solution)/shard_map/dot_general | solution.py:54
  334.2 10.7 %collective-permute-done.24 = bf16[128,2048]{1,0:T(8,128)(2,1)S(1)} collective-permute-done((bf16[128,2048]{1,0:T(8,128)(2,1)S(1)}, bf16[128,2048]{1,0:T(8,128)(2,1)S(1)}, u32[]{:S(2)}, u32[]{:S(2)}) %collective-permute-start.24) | collective-permute-done | bytes 524320 | tf_op jit(solution)/shard_map/ppermute | solution.py:389
  357.7 10.2 %collective-permute-done.25 = bf16[128,2048]{1,0:T(8,128)(2,1)S(1)} collective-permute-done((bf16[128,2048]{1,0:T(8,128)(2,1)S(1)}, bf16[128,2048]{1,0:T(8,128)(2,1)S(1)}, u32[]{:S(2)}, u32[]{:S(2)}) %collective-permute-start.25) | collective-permute-done | bytes 524320 | tf_op jit(solution)/shard_map/ppermute | solution.py:389
  373.7 23.5 %collective-permute-done.29 = bf16[256,2048]{1,0:T(8,128)(2,1)S(1)} collective-permute-done((bf16[256,2048]{1,0:T(8,128)(2,1)}, bf16[256,2048]{1,0:T(8,128)(2,1)S(1)}, u32[]{:S(2)}, u32[]{:S(2)}) %collective-permute-start.29) | collective-permute-done | bytes 1048608 | tf_op jit(solution)/shard_map/ppermute | solution.py:389
  424.1 26.7 %attn_b.1 = (bf16[1024,1536]{1,0:T(8,128)(2,1)S(1)}, f32[4,8,384]{2,1,0:T(8,128)S(1)}) custom-call(s32[5]{0:T(128)S(1)} %copy-done.8, bf16[1024,1536]{1,0:T(8,128)(2,1)} %copy-done, f32[3,1024,128]{2,1,0:T(8,128)S(1)} %pad_maximum_fusion.3.refs_2_, f32[4,4,16,256]{3,2,1,0:T(8,128)S(1)} %get-tuple-element.48.refs_3_, bf16[1024,512]{1,0:T(8,128)(2,1)S(1)} %fusion.54.refs_4_), custom_call_target="tpu_custom_call" | custom-call | tf_op jit(solution)/shard_map/attn_b/pallas_call | solution.py:255
  462.4 9.2 %convolution_convert_fusion.4 = bf16[768,2048]{1,0:T(8,128)(2,1)} fusion(bf16[2048,1408]{1,0:T(8,128)(2,1)} %all-gather.8.cloned.1.call-done, bf16[1024,1408]{1,0:T(8,128)(2,1)S(1)} %copy-done.33), kind=kOutput, calls=%fused_computation.32 | convolution fusion | flops 4430757888 | bytes 11075584 | tf_op jit(solution)/shard_map/dot_general | solution.py:54
  492.2 8.3 %fusion.20 = bf16[768,2048]{1,0:T(8,128)(2,1)S(1)} fusion(bf16[2048,2048]{1,0:T(8,128)(2,1)} %all-gather.4.cloned.1.call-done, bf16[1024,1536]{1,0:T(8,128)(2,1)S(1)} %copy-done.11), kind=kOutput, calls=%fused_computation.31 | convolution fusion | flops 4833411072 | bytes 11796480 | tf_op jit(solution)/shard_map/dot_general | solution.py:54
  508.4 17.3 %collective-permute-done.42 = bf16[128,2048]{1,0:T(8,128)(2,1)S(1)} collective-permute-done((bf16[128,2048]{1,0:T(8,128)(2,1)S(1)}, bf16[128,2048]{1,0:T(8,128)(2,1)S(1)}, u32[]{:S(2)}, u32[]{:S(2)}) %collective-permute-start.42) | collective-permute-done | bytes 524320 | tf_op jit(solution)/shard_map/ppermute | solution.py:389
  552.0 9.9 %collective-permute-done.35 = bf16[128,2048]{1,0:T(8,128)(2,1)} collective-permute-done((bf16[128,2048]{1,0:T(8,128)(2,1)}, bf16[128,2048]{1,0:T(8,128)(2,1)}, u32[]{:S(2)}, u32[]{:S(2)}) %collective-permute-start.35) | collective-permute-done | bytes 524320 | tf_op jit(solution)/shard_map/ppermute | solution.py:389
  601.4 11.7 %collective-permute-done.53.refs_1_ = bf16[128,2176]{1,0:T(8,128)(2,1)S(1)} collective-permute-done((bf16[128,2176]{1,0:T(8,128)(2,1)}, bf16[128,2176]{1,0:T(8,128)(2,1)S(1)}, u32[]{:S(2)}, u32[]{:S(2)}) %collective-permute-start.53) | collective-permute-done | bytes 557088 | tf_op jit(solution)/shard_map/ppermute | solution.py:444
  (347 shorter events, 291.7 us)
Async XLA Ops:
  7.2 89.6 %all-gather.4.cloned.1.call-start = ((), (), s32[]{:S(2)}) async-start(), calls=%async_computation.3 | async-start | bytes 9437184 | tf_op jit(solution)/shard_map/all_gather | solution.py:508
  11.8 235.6 %all-gather.6.cloned.1.call-start = ((), (), s32[]{:S(2)}) async-start(), calls=%async_computation.4 | async-start | bytes 12976128 | tf_op jit(solution)/shard_map/all_gather | solution.py:527
  13.2 26.2 %collective-permute-start = (bf16[256,2048]{1,0:T(8,128)(2,1)S(1)}, bf16[256,2048]{1,0:T(8,128)(2,1)S(1)}, u32[]{:S(2)}, u32[]{:S(2)}) collective-permute-start(bf16[256,2048]{1,0:T(8,128)(2,1)S(1)} %get-tuple-element.102), channel_id=1, source_target_pairs={{0,2},{2,0},{4,6},{6,4},{1,3},{3,1},{5,7},{7,5},{8,10},{10,8},{12,... | collective-permute-start | bytes 3145736 | tf_op jit(solution)/shard_map/ppermute | solution.py:389
  16.2 26.1 %collective-permute-start.1 = (bf16[256,2048]{1,0:T(8,128)(2,1)S(1)}, bf16[256,2048]{1,0:T(8,128)(2,1)S(1)}, u32[]{:S(2)}, u32[]{:S(2)}) collective-permute-start(bf16[256,2048]{1,0:T(8,128)(2,1)S(1)} %get-tuple-element.102), channel_id=1, source_target_pairs={{0,4},{2,6},{4,0},{6,2},{1,5},{3,7},{5,1},{7,3},{8,12},{10,14},{12... | collective-permute-start | bytes 3145736 | tf_op jit(solution)/shard_map/ppermute | solution.py:389
  59.4 24.9 %collective-permute-start.6 = (bf16[128,2176]{1,0:T(8,128)(2,1)S(1)}, bf16[128,2176]{1,0:T(8,128)(2,1)S(1)}, u32[]{:S(2)}, u32[]{:S(2)}) collective-permute-start(bf16[128,2176]{1,0:T(8,128)(2,1)S(1)} %get-tuple-element.134), channel_id=1, source_target_pairs={{0,4},{1,6},{2,0},{3,2},{4,5},{5,7},{6,1},{7,3},{8,12},{9,14},{10,... | collective-permute-start | bytes 1671176 | tf_op jit(solution)/shard_map/ppermute | solution.py:440
  86.7 196.6 %all-gather.8.cloned.1.call-start = ((), (), s32[]{:S(2)}) async-start(), calls=%async_computation.5 | async-start | bytes 6488064 | tf_op jit(solution)/shard_map/all_gather | solution.py:528
  135.7 24.0 %collective-permute-start.8 = (bf16[128,2048]{1,0:T(8,128)(2,1)S(1)}, bf16[128,2048]{1,0:T(8,128)(2,1)S(1)}, u32[]{:S(2)}, u32[]{:S(2)}) collective-permute-start(bf16[128,2048]{1,0:T(8,128)(2,1)S(1)} %get-tuple-element.123), channel_id=1, source_target_pairs={{0,2},{2,0},{4,6},{6,4},{1,3},{3,1},{5,7},{7,5},{8,10},{10,8},{12,... | collective-permute-start | bytes 1572872 | tf_op jit(solution)/shard_map/ppermute | solution.py:389
  151.0 42.4 %collective-permute-start.18 = (bf16[256,2048]{1,0:T(8,128)(2,1)}, bf16[256,2048]{1,0:T(8,128)(2,1)S(1)}, u32[]{:S(2)}, u32[]{:S(2)}) collective-permute-start(bf16[256,2048]{1,0:T(8,128)(2,1)} %bitcast.14), channel_id=1, source_target_pairs={{0,2},{2,0},{4,6},{6,4},{1,3},{3,1},{5,7},{7,5},{8,10},{10,8},{12,... | collective-permute-start | bytes 3145736 | tf_op jit(solution)/shard_map/ppermute | solution.py:389
  158.0 41.6 %collective-permute-start.19 = (bf16[256,2048]{1,0:T(8,128)(2,1)}, bf16[256,2048]{1,0:T(8,128)(2,1)}, u32[]{:S(2)}, u32[]{:S(2)}) collective-permute-start(bf16[256,2048]{1,0:T(8,128)(2,1)} %bitcast.14), channel_id=1, source_target_pairs={{0,4},{2,6},{4,0},{6,2},{1,5},{3,7},{5,1},{7,3},{8,12},{10,14},{12... | collective-permute-start | bytes 3145736 | tf_op jit(solution)/shard_map/ppermute | solution.py:389
  174.6 41.4 %collective-permute-start.14 = (bf16[256,2048]{1,0:T(8,128)(2,1)}, bf16[256,2048]{1,0:T(8,128)(2,1)}, u32[]{:S(2)}, u32[]{:S(2)}) collective-permute-start(bf16[256,2048]{1,0:T(8,128)(2,1)} %get-tuple-element.98), channel_id=1, source_target_pairs={{0,2},{2,0},{4,6},{6,4},{1,3},{3,1},{5,7},{7,5},{8,10},{10,8},{12,... | collective-permute-start | bytes 3145736 | tf_op jit(solution)/shard_map/ppermute | solution.py:389
  195.6 37.2 %collective-permute-start.15 = (bf16[256,2048]{1,0:T(8,128)(2,1)}, bf16[256,2048]{1,0:T(8,128)(2,1)}, u32[]{:S(2)}, u32[]{:S(2)}) collective-permute-start(bf16[256,2048]{1,0:T(8,128)(2,1)} %get-tuple-element.98), channel_id=1, source_target_pairs={{0,4},{2,6},{4,0},{6,2},{1,5},{3,7},{5,1},{7,3},{8,12},{10,14},{12... | collective-permute-start | bytes 3145736 | tf_op jit(solution)/shard_map/ppermute | solution.py:389
  199.6 385.1 %reduce-scatter.8.cloned.1.call-start = ((), (), s32[]{:S(2)}) async-start(), calls=%async_computation.8 | async-start | bytes 3604480 | tf_op jit(solution)/shard_map/reduce_scatter | solution.py:560
  200.7 25.3 %collective-permute-start.21 = (bf16[128,2048]{1,0:T(8,128)(2,1)S(1)}, bf16[128,2048]{1,0:T(8,128)(2,1)S(1)}, u32[]{:S(2)}, u32[]{:S(2)}) collective-permute-start(bf16[128,2048]{1,0:T(8,128)(2,1)S(1)} %slice.316), channel_id=1, source_target_pairs={{0,2},{2,0},{4,6},{6,4},{1,3},{3,1},{5,7},{7,5},{8,10},{10,8},{12,... | collective-permute-start | bytes 1572872 | tf_op jit(solution)/shard_map/ppermute | solution.py:389
  283.3 301.4 %reduce-scatter.6.cloned.1.call-start = ((), (), s32[]{:S(2)}) async-start(), calls=%async_computation.7 | async-start | bytes 12976128 | tf_op jit(solution)/shard_map/reduce_scatter | solution.py:578
  328.1 270.0 %reduce-scatter.4.cloned.1.call-start = ((), (), s32[]{:S(2)}) async-start(), calls=%async_computation.6 | async-start | bytes 5242880 | tf_op jit(solution)/shard_map/reduce_scatter | solution.py:608
  332.2 24.0 %collective-permute-start.23 = (bf16[128,2048]{1,0:T(8,128)(2,1)S(1)}, bf16[128,2048]{1,0:T(8,128)(2,1)S(1)}, u32[]{:S(2)}, u32[]{:S(2)}) collective-permute-start(bf16[128,2048]{1,0:T(8,128)(2,1)S(1)} %get-tuple-element.117), channel_id=1, source_target_pairs={{0,2},{2,0},{4,6},{6,4},{1,3},{3,1},{5,7},{7,5},{8,10},{10,8},{12,... | collective-permute-start | bytes 1572872 | tf_op jit(solution)/shard_map/ppermute | solution.py:389
  332.7 25.0 %collective-permute-start.26 = (bf16[128,2048]{1,0:T(8,128)(2,1)S(1)}, bf16[128,2048]{1,0:T(8,128)(2,1)S(1)}, u32[]{:S(2)}, u32[]{:S(2)}) collective-permute-start(bf16[128,2048]{1,0:T(8,128)(2,1)S(1)} %get-tuple-element.119), channel_id=1, source_target_pairs={{0,4},{2,6},{4,0},{6,2},{1,5},{3,7},{5,1},{7,3},{8,12},{10,14},{12... | collective-permute-start | bytes 1572872 | tf_op jit(solution)/shard_map/ppermute | solution.py:389
  372.7 24.4 %collective-permute-start.29 = (bf16[256,2048]{1,0:T(8,128)(2,1)}, bf16[256,2048]{1,0:T(8,128)(2,1)S(1)}, u32[]{:S(2)}, u32[]{:S(2)}) collective-permute-start(bf16[256,2048]{1,0:T(8,128)(2,1)} %get-tuple-element.96), channel_id=1, source_target_pairs={{0,2},{2,0},{4,6},{6,4},{1,3},{3,1},{5,7},{7,5},{8,10},{10,8},{12,... | collective-permute-start | bytes 3145736 | tf_op jit(solution)/shard_map/ppermute | solution.py:389
  373.2 31.6 %collective-permute-start.30 = (bf16[256,2048]{1,0:T(8,128)(2,1)}, bf16[256,2048]{1,0:T(8,128)(2,1)}, u32[]{:S(2)}, u32[]{:S(2)}) collective-permute-start(bf16[256,2048]{1,0:T(8,128)(2,1)} %get-tuple-element.96), channel_id=1, source_target_pairs={{0,4},{2,6},{4,0},{6,2},{1,5},{3,7},{5,1},{7,3},{8,12},{10,14},{12... | collective-permute-start | bytes 3145736 | tf_op jit(solution)/shard_map/ppermute | solution.py:389
  490.8 60.0 %collective-permute-start.33 = (bf16[128,2048]{1,0:T(8,128)(2,1)}, bf16[128,2048]{1,0:T(8,128)(2,1)S(1)}, u32[]{:S(2)}, u32[]{:S(2)}) collective-permute-start(bf16[128,2048]{1,0:T(8,128)(2,1)} %get-tuple-element.111), channel_id=1, source_target_pairs={{0,2},{2,0},{4,6},{6,4},{1,3},{3,1},{5,7},{7,5},{8,10},{10,8},{12,... | collective-permute-start | bytes 1572872 | tf_op jit(solution)/shard_map/ppermute | solution.py:389
  500.7 25.0 %collective-permute-start.42 = (bf16[128,2048]{1,0:T(8,128)(2,1)S(1)}, bf16[128,2048]{1,0:T(8,128)(2,1)S(1)}, u32[]{:S(2)}, u32[]{:S(2)}) collective-permute-start(bf16[128,2048]{1,0:T(8,128)(2,1)S(1)} %get-tuple-element.108), channel_id=1, source_target_pairs={{0,2},{2,0},{4,6},{6,4},{1,3},{3,1},{5,7},{7,5},{8,10},{10,8},{12,... | collective-permute-start | bytes 1572872 | tf_op jit(solution)/shard_map/ppermute | solution.py:389
  504.8 32.2 %collective-permute-start.41 = (bf16[128,2048]{1,0:T(8,128)(2,1)S(1)}, bf16[128,2048]{1,0:T(8,128)(2,1)S(1)}, u32[]{:S(2)}, u32[]{:S(2)}) collective-permute-start(bf16[128,2048]{1,0:T(8,128)(2,1)S(1)} %get-tuple-element.105), channel_id=1, source_target_pairs={{0,2},{2,0},{4,6},{6,4},{1,3},{3,1},{5,7},{7,5},{8,10},{10,8},{12,... | collective-permute-start | bytes 1572872 | tf_op jit(solution)/shard_map/ppermute | solution.py:389
  506.0 32.7 %collective-permute-start.44 = (bf16[128,2048]{1,0:T(8,128)(2,1)S(1)}, bf16[128,2048]{1,0:T(8,128)(2,1)S(1)}, u32[]{:S(2)}, u32[]{:S(2)}) collective-permute-start(bf16[128,2048]{1,0:T(8,128)(2,1)S(1)} %get-tuple-element.107), channel_id=1, source_target_pairs={{0,4},{2,6},{4,0},{6,2},{1,5},{3,7},{5,1},{7,3},{8,12},{10,14},{12... | collective-permute-start | bytes 1572872 | tf_op jit(solution)/shard_map/ppermute | solution.py:389
  593.0 25.7 %collective-permute-start.55 = (bf16[128,2176]{1,0:T(8,128)(2,1)S(1)}, bf16[128,2176]{1,0:T(8,128)(2,1)S(1)}, u32[]{:S(2)}, u32[]{:S(2)}) collective-permute-start(bf16[128,2176]{1,0:T(8,128)(2,1)S(1)} %get-tuple-element.129), channel_id=1, source_target_pairs={{6,0},{4,1},{2,2},{0,3},{7,4},{5,5},{3,6},{1,7},{14,8},{12,9},{10,... | collective-permute-start | bytes 1671176 | tf_op jit(solution)/shard_map/ppermute | solution.py:444
  (97 other events, 1305.2 us)
Sparse Core Ops, SparseCore 0:
  12.0 84.7 all-gather.3
  99.0 106.5 all-gather.5
  207.2 58.6 all-gather.7
  283.4 54.1 reduce-scatter.7
  339.7 118.9 reduce-scatter.5
  481.5 74.5 reduce-scatter.3

commit v7 on v6

--- a/solution.py
+++ b/solution.py
@@ -408,14 +408,12 @@
             return total
         half = blocks[0].shape[0] // 2
         b = [(x[:half], x[half:]) for x in blocks]
-        top2 = row_permute(b[3][0].astype(bf16), 1)
-        low1 = row_permute(b[3][1].astype(bf16), 2)
-        top0 = row_permute(b[1][0].astype(bf16), 1)
-        low0 = row_permute(b[2][1].astype(bf16), 2)
-        top2 = row_permute((b[2][0].astype(f32) + top2.astype(f32)).astype(bf16), 2)
-        low1 = row_permute((b[1][1].astype(f32) + low1.astype(f32)).astype(bf16), 1)
-        top = b[0][0].astype(f32) + top0.astype(f32) + top2.astype(f32)
-        low = b[0][1].astype(f32) + low0.astype(f32) + low1.astype(f32)
+        top = row_permute(jnp.concatenate([b[1][0], b[3][0]]).astype(bf16), 1).astype(f32)
+        low = row_permute(jnp.concatenate([b[2][1], b[3][1]]).astype(bf16), 2).astype(f32)
+        top2 = row_permute((b[2][0].astype(f32) + top[half:]).astype(bf16), 2)
+        low1 = row_permute((b[1][1].astype(f32) + low[half:]).astype(bf16), 1)
+        top = b[0][0].astype(f32) + top[:half] + top2.astype(f32)
+        low = b[0][1].astype(f32) + low[:half] + low1.astype(f32)
         return jnp.concatenate([top, low], axis=0)
 
     def source_place(s, c):
@@ -568,14 +566,25 @@
         grad_gate = grad_hidden * up_vals * sig * (1.0 + gate_vals * (1.0 - sig))
         grad_up = grad_hidden * swish
         grad_gu_vals = jnp.concatenate([grad_gate.astype(bf16), grad_up.astype(bf16)], axis=1)
-        own = nt(grad_gu_vals[:block], w_gu)
-        others = nt(grad_gu_vals[block:], w_gu).astype(bf16)
-        others, second_in = lax.optimization_barrier((others, second_in))
+        if C == 2:
+            halves = split_columns(info, second_in, mesh.shape[DP])
+            away = tn(halves[1], grad_gu_vals).astype(bf16)
+            got = lax.ppermute(away, COL, [(0, 1), (1, 0)])
+            second_vals, _ = lax.optimization_barrier((grad_gu_vals, away))
+        else:
+            second_vals = grad_gu_vals
+        own = nt(second_vals[:block], w_gu)
+        others = nt(second_vals[block:], w_gu).astype(bf16)
+        others, grad_gu_vals = lax.optimization_barrier((others, grad_gu_vals))
         grad_second = scatter_rel(
             [own] + [others[k * block : (k + 1) * block] for k in range(R - 1)]
         )
-        grad_gu = tn(second_in, grad_gu_vals).astype(bf16)
-        grad_gu = lax.psum_scatter(grad_gu, (DP, COL), scatter_dimension=0, tiled=True)
+        if C == 2:
+            grad_gu = (tn(halves[0], grad_gu_vals) + got.astype(f32)).astype(bf16)
+            grad_gu = lax.psum_scatter(grad_gu, DP, scatter_dimension=0, tiled=True)
+        else:
+            grad_gu = tn(second_in, grad_gu_vals).astype(bf16)
+            grad_gu = lax.psum_scatter(grad_gu, (DP, COL), scatter_dimension=0, tiled=True)
 
         grad_middle = dy.astype(f32) + layer_norm_backward(
             grad_second, second_std, second_inv, gain2

time: 638 us -> 629 us (0.986)
  waiting for transfers between devices: 260 us -> 235 us
  other arithmetic: 29.5 us -> 47.4 us
    ppermute x40 -> x32, waiting for transfers between devices: 198 us -> 175 us  [row_permute(): return lax.ppermute(block, ROW, [(i, i ^ k) for i in range(R)])]
    convert_element_type x4 -> x12, other arithmetic: 3.85 us -> 12.9 us  [the longest x4 5.44 us: scatter_rel(): top2 = row_permute((b[2][0].astype(f32) + top[half:]).astype(bf16), 2)]
    concatenate x0 -> x9, other arithmetic: none -> 8.07 us  [the longest x1 3.09 us: body(): jnp.concatenate([grad_gate.astype(bf16), grad_up.astype(bf16)], axis=1)]
    pallas_call x2 -> x3, Pallas kernels: 11.1 us -> 16.4 us  [split_columns(): pl.pallas_call(split_kernel, grid_spec=pltpu.PrefetchScalarGridSpec(num_s...]
    ppermute x40 -> x32, starting transfers between devices: 44.5 us -> 41.2 us  [row_permute(): return lax.ppermute(block, ROW, [(i, i ^ k) for i in range(R)])]
    dot_general x18 -> x19, matrix products: 142 us -> 139 us  [dot(): lax.dot_general(left, right, (dims, ((), ())), preferred_element_type=f32)]
    unnamed x134 -> x138, local copies, waits for them, and re-layouts: 37.7 us -> 37.5 us
  transfers between devices with their start and end apart: 62 -> 55, of which waited for: 40 -> 32; matrix products, arithmetic and copies ran while one was open for 33% -> 32% of each run, Pallas kernels for 10% -> 11%
where the time goes in v7:
time: 629 us; the launch traced here: 622 us
  waiting for transfers between devices  235 us (37%)
  matrix products  139 us (22%)
  Pallas kernels  71.5 us (11%)
  starting transfers between devices  62.5 us (10%)
  local copies, waits for them, and re-layouts  50.8 us (8%)
  other arithmetic  47.4 us (8%)
  between operations  16.4 us (3%)
    ppermute x32, waiting for transfers between devices, row_permute(): return lax.ppermute(block, ROW, [(i, i ^ k) for i in range(R)])  175 us
    dot_general x19, matrix products, dot(): lax.dot_general(left, right, (dims, ((), ())), preferred_element_type=f32)  139 us
    ppermute x32, starting transfers between devices, row_permute(): return lax.ppermute(block, ROW, [(i, i ^ k) for i in range(R)])  41.2 us
    unnamed x138, local copies, waits for them, and re-layouts  37.5 us
    pallas_call x1, Pallas kernels, attend_backward(): pl.pallas_call(lambda *refs: backward_kernel(blocks, size, *refs), grid_s...  26.7 us
    ppermute x4, waiting for transfers between devices, spread(): lax.ppermute(packed[k], (ROW, COL), exchange_pairs(k))  20.8 us
    pallas_call x1, Pallas kernels, attend_forward(): pl.pallas_call(lambda *refs: forward_kernel(blocks, size, *refs), grid_sp...  18.2 us
    ppermute x4, waiting for transfers between devices, bring_back(): lax.ppermute(packed[k], (ROW, COL), [(b, a) for a, b in exchange_pairs(k)])  17.5 us
  transfers between devices with their start and end apart: 55, of which 32 were waited for; matrix products, arithmetic and copies ran while one was open for 32% of the time, Pallas kernels for 11%

profile of v7, /device:TPU:0, one launch (start us, length us, event | category | flops | bytes accessed | tf_op | source)
XLA Modules:
  0.0 622.5 jit_solution(7339737738567366960)
XLA Ops:
  17.7 21.6 %collective-permute-done = bf16[256,2048]{1,0:T(8,128)(2,1)S(1)} collective-permute-done((bf16[256,2048]{1,0:T(8,128)(2,1)S(1)}, bf16[256,2048]{1,0:T(8,128)(2,1)S(1)}, u32[]{:S(2)}, u32[]{:S(2)}) %collective-permute-start) | collective-permute-done | bytes 1048608 | tf_op jit(solution)/shard_map/ppermute | solution.py:389
  44.1 8.5 %collective-permute-done.2 = bf16[128,2048]{1,0:T(8,128)(2,1)S(1)} collective-permute-done((bf16[128,2048]{1,0:T(8,128)(2,1)S(1)}, bf16[128,2048]{1,0:T(8,128)(2,1)S(1)}, u32[]{:S(2)}, u32[]{:S(2)}) %collective-permute-start.2) | collective-permute-done | bytes 524320 | tf_op jit(solution)/shard_map/ppermute | solution.py:389
  63.6 8.9 %collective-permute-done.5.refs_1_ = bf16[128,2176]{1,0:T(8,128)(2,1)S(1)} collective-permute-done((bf16[128,2176]{1,0:T(8,128)(2,1)S(1)}, bf16[128,2176]{1,0:T(8,128)(2,1)S(1)}, u32[]{:S(2)}, u32[]{:S(2)}) %collective-permute-start.5) | collective-permute-done | bytes 557088 | tf_op jit(solution)/shard_map/ppermute | solution.py:438
  72.5 11.9 %collective-permute-done.6.refs_2_ = bf16[128,2176]{1,0:T(8,128)(2,1)S(1)} collective-permute-done((bf16[128,2176]{1,0:T(8,128)(2,1)S(1)}, bf16[128,2176]{1,0:T(8,128)(2,1)S(1)}, u32[]{:S(2)}, u32[]{:S(2)}) %collective-permute-start.6) | collective-permute-done | bytes 557088 | tf_op jit(solution)/shard_map/ppermute | solution.py:438
  89.0 7.7 %all-gather.4.cloned.1.call-done = bf16[2048,2048]{1,0:T(8,128)(2,1)} async-done(((bf16[256,2048]{1,0:T(8,128)(2,1)}), bf16[2048,2048]{1,0:T(8,128)(2,1)}) %all-gather.4.cloned.1.call-update) | async-done | bytes 8388624 | tf_op jit(solution)/shard_map/all_gather | solution.py:506
  96.8 12.0 %fusion.9.refs_1_ = f32[1024,1536]{1,0:T(8,128)} fusion(bf16[1024,2048]{1,0:T(8,128)(2,1)} %copy-done.15, bf16[2048,2048]{1,0:T(8,128)(2,1)} %all-gather.4.cloned.1.call-done, f32[1536]{0:T(1024)S(1)} %reshape.565), kind=kOutput, calls=%fused_computation.18 | convolution fusion | flops 6444023808 | bytes 16783360 | tf_op jit(solution)/shard_map/dot_general | solution.py:54
  108.8 18.2 %attn_f.1 = (bf16[1024,1536]{1,0:T(8,128)(2,1)S(1)}, bf16[1024,512]{1,0:T(8,128)(2,1)S(1)}, f32[4,4,16,256]{3,2,1,0:T(8,128)S(1)}) custom-call(s32[5]{0:T(128)S(1)} %stack.30.info.refs_0_, f32[1024,1536]{1,0:T(8,128)} %fusion.9.refs_1_, f32[3,1024,128]{2,1,0:T(8,128)S(1)} %pad_maximum_fusion.4.refs_2_), custom_call_target="tpu_custom_call" | custom-call | tf_op jit(solution)/shard_map/attn_f/pallas_call | solution.py:217
  132.5 22.1 %collective-permute-done.10 = bf16[256,2048]{1,0:T(8,128)(2,1)S(1)} collective-permute-done((bf16[256,2048]{1,0:T(8,128)(2,1)S(1)}, bf16[256,2048]{1,0:T(8,128)(2,1)S(1)}, u32[]{:S(2)}, u32[]{:S(2)}) %collective-permute-start.10) | collective-permute-done | bytes 1048608 | tf_op jit(solution)/shard_map/ppermute | solution.py:389
  161.7 9.9 %collective-permute-done.11 = bf16[128,2048]{1,0:T(8,128)(2,1)S(1)} collective-permute-done((bf16[128,2048]{1,0:T(8,128)(2,1)S(1)}, bf16[128,2048]{1,0:T(8,128)(2,1)S(1)}, u32[]{:S(2)}, u32[]{:S(2)}) %collective-permute-start.11) | collective-permute-done | bytes 524320 | tf_op jit(solution)/shard_map/ppermute | solution.py:389
  177.3 16.7 %collective-permute-done.16 = bf16[256,2048]{1,0:T(8,128)(2,1)S(1)} collective-permute-done((bf16[256,2048]{1,0:T(8,128)(2,1)}, bf16[256,2048]{1,0:T(8,128)(2,1)S(1)}, u32[]{:S(2)}, u32[]{:S(2)}) %collective-permute-start.16) | collective-permute-done | bytes 1048608 | tf_op jit(solution)/shard_map/ppermute | solution.py:389
  246.8 17.3 %fusion.102 = f32[1024,2816]{1,0:T(8,128)S(1)} fusion(bf16[1024,2048]{1,0:T(8,128)(2,1)} %constant_dynamic-update-slice_fusion.5.mine.other, bf16[2048,2816]{1,0:T(8,128)(2,1)} %all-gather.6.cloned.1.call-done), kind=kOutput, calls=%fused_computation.200 | convolution fusion | flops 11811160064 | bytes 27262976 | tf_op jit(solution)/shard_map/dot_general | solution.py:54
  279.1 8.4 %add_convert_fusion.2 = bf16[1024,1408]{1,0:T(8,128)(2,1)} fusion(bf16[1024,1408]{1,0:T(8,128)(2,1)} %collective-permute-done.20, bf16[1024,1024]{1,0:T(8,128)(2,1)} %get-tuple-element.44, bf16[1024,1408]{1,0:T(8,128)(2,1)} %copy-done.34), kind=kOutput, calls=%fused_computation.5 | convolution fusion | flops 2957115392 | bytes 10747904 | tf_op jit(solution)/shard_map/dot_general | solution.py:54
  287.5 14.2 %multiply_convert_fusion.1 = (bf16[1024,1408]{1,0:T(8,128)(2,1)S(1)}, bf16[1024,1408]{1,0:T(8,128)(2,1)S(1)}) fusion(f32[1024,2816]{1,0:T(8,128)} %copy-done.24, bf16[1024,2048]{1,0:T(8,128)(2,1)} %constant_dynamic-update-slice_fusion.10.mine.other, bf16[2048,1408]{1,0:T(8,128)(2,1)} %all-gather.8.cloned.1.call-done), kind=kOutput, calls=%fused_computation.4 | convolution fusion | flops 5924323328 | bytes 27262976 | tf_op jit(solution)/shard_map/dot_general | solution.py:54
  301.7 8.3 %convolution_convert_fusion = bf16[1024,2816]{1,0:T(8,128)(2,1)} fusion(bf16[1024,1024]{1,0:T(8,128)(2,1)S(1)} %copy-done.58, bf16[1024,1408]{1,0:T(8,128)(2,1)S(1)} %get-tuple-element.110, bf16[1024,1408]{1,0:T(8,128)(2,1)S(1)} %get-tuple-element.109), kind=kOutput, calls=%fused_computation.9 | convolution fusion | flops 5919997952 | bytes 13631488 | tf_op jit(solution)/shard_map/dot_general | solution.py:54
  313.6 14.1 %fusion.12 = bf16[768,2048]{1,0:T(8,128)(2,1)S(1)} fusion(bf16[2048,2816]{1,0:T(8,128)(2,1)} %all-gather.6.cloned.1.call-done, bf16[1024,2816]{1,0:T(8,128)(2,1)S(1)} %pad_maximum_fusion), kind=kOutput, calls=%fused_computation.27 | convolution fusion | flops 8859942912 | bytes 19005440 | tf_op jit(solution)/shard_map/dot_general | solution.py:54
  333.1 10.2 %add_convert_fusion = bf16[1024,2816]{1,0:T(8,128)(2,1)} fusion(bf16[1024,2816]{1,0:T(8,128)(2,1)} %collective-permute-done.44, bf16[1024,1024]{1,0:T(8,128)(2,1)S(1)} %copy-done.55, bf16[1024,2816]{1,0:T(8,128)(2,1)S(1)} %pad_maximum_fusion), kind=kOutput, calls=%fused_computation | convolution fusion | flops 5914230784 | bytes 19398656 | tf_op jit(solution)/shard_map/dot_general | solution.py:54
  343.4 12.0 %collective-permute-done.23 = bf16[256,2048]{1,0:T(8,128)(2,1)} collective-permute-done((bf16[256,2048]{1,0:T(8,128)(2,1)}, bf16[256,2048]{1,0:T(8,128)(2,1)}, u32[]{:S(2)}, u32[]{:S(2)}) %collective-permute-start.23) | collective-permute-done | bytes 1048608 | tf_op jit(solution)/shard_map/ppermute | solution.py:389
  381.1 21.1 %collective-permute-done.25 = bf16[256,2048]{1,0:T(8,128)(2,1)S(1)} collective-permute-done((bf16[256,2048]{1,0:T(8,128)(2,1)}, bf16[256,2048]{1,0:T(8,128)(2,1)S(1)}, u32[]{:S(2)}, u32[]{:S(2)}) %collective-permute-start.25) | collective-permute-done | bytes 1048608 | tf_op jit(solution)/shard_map/ppermute | solution.py:389
  429.0 26.7 %attn_b.1 = (bf16[1024,1536]{1,0:T(8,128)(2,1)S(1)}, f32[4,8,384]{2,1,0:T(8,128)S(1)}) custom-call(s32[5]{0:T(128)S(1)} %copy-done.8, bf16[1024,1536]{1,0:T(8,128)(2,1)} %copy-done, f32[3,1024,128]{2,1,0:T(8,128)S(1)} %pad_maximum_fusion.4.refs_2_, f32[4,4,16,256]{3,2,1,0:T(8,128)S(1)} %get-tuple-element.53.refs_3_, bf16[1024,512]{1,0:T(8,128)(2,1)S(1)} %fusion.49.refs_4_), custom_call_target="tpu_custom_call" | custom-call | tf_op jit(solution)/shard_map/attn_b/pallas_call | solution.py:255
  464.0 7.9 %convolution_convert_fusion.4 = bf16[768,2048]{1,0:T(8,128)(2,1)S(1)} fusion(bf16[2048,1408]{1,0:T(8,128)(2,1)} %all-gather.8.cloned.1.call-done, bf16[1024,1408]{1,0:T(8,128)(2,1)S(1)} %copy-done.35), kind=kOutput, calls=%fused_computation.29 | convolution fusion | flops 4430757888 | bytes 11075584 | tf_op jit(solution)/shard_map/dot_general | solution.py:54
  484.2 8.1 %fusion.15 = bf16[768,2048]{1,0:T(8,128)(2,1)S(1)} fusion(bf16[2048,2048]{1,0:T(8,128)(2,1)} %all-gather.4.cloned.1.call-done, bf16[1024,1536]{1,0:T(8,128)(2,1)} %copy-done.9), kind=kOutput, calls=%fused_computation.28 | convolution fusion | flops 4833411072 | bytes 11796480 | tf_op jit(solution)/shard_map/dot_general | solution.py:54
  510.0 12.6 %collective-permute-done.37 = bf16[256,2048]{1,0:T(8,128)(2,1)S(1)} collective-permute-done((bf16[256,2048]{1,0:T(8,128)(2,1)S(1)}, bf16[256,2048]{1,0:T(8,128)(2,1)S(1)}, u32[]{:S(2)}, u32[]{:S(2)}) %collective-permute-start.37) | collective-permute-done | bytes 1048608 | tf_op jit(solution)/shard_map/ppermute | solution.py:389
  531.1 13.5 %collective-permute-done.36 = bf16[128,2048]{1,0:T(8,128)(2,1)S(1)} collective-permute-done((bf16[128,2048]{1,0:T(8,128)(2,1)S(1)}, bf16[128,2048]{1,0:T(8,128)(2,1)S(1)}, u32[]{:S(2)}, u32[]{:S(2)}) %collective-permute-start.36) | collective-permute-done | bytes 524320 | tf_op jit(solution)/shard_map/ppermute | solution.py:389
  591.8 14.4 %collective-permute-done.46.refs_1_ = bf16[128,2176]{1,0:T(8,128)(2,1)S(1)} collective-permute-done((bf16[128,2176]{1,0:T(8,128)(2,1)}, bf16[128,2176]{1,0:T(8,128)(2,1)S(1)}, u32[]{:S(2)}, u32[]{:S(2)}) %collective-permute-start.46) | collective-permute-done | bytes 557088 | tf_op jit(solution)/shard_map/ppermute | solution.py:442
  (356 shorter events, 279.6 us)
Async XLA Ops:
  7.2 89.6 %all-gather.4.cloned.1.call-start = ((), (), s32[]{:S(2)}) async-start(), calls=%async_computation.3 | async-start | bytes 9437184 | tf_op jit(solution)/shard_map/all_gather | solution.py:506
  11.8 234.9 %all-gather.6.cloned.1.call-start = ((), (), s32[]{:S(2)}) async-start(), calls=%async_computation.4 | async-start | bytes 12976128 | tf_op jit(solution)/shard_map/all_gather | solution.py:525
  13.2 26.2 %collective-permute-start = (bf16[256,2048]{1,0:T(8,128)(2,1)S(1)}, bf16[256,2048]{1,0:T(8,128)(2,1)S(1)}, u32[]{:S(2)}, u32[]{:S(2)}) collective-permute-start(bf16[256,2048]{1,0:T(8,128)(2,1)S(1)} %get-tuple-element.108), channel_id=1, source_target_pairs={{0,2},{2,0},{4,6},{6,4},{1,3},{3,1},{5,7},{7,5},{8,10},{10,8},{12,... | collective-permute-start | bytes 3145736 | tf_op jit(solution)/shard_map/ppermute | solution.py:389
  16.2 26.1 %collective-permute-start.1 = (bf16[256,2048]{1,0:T(8,128)(2,1)S(1)}, bf16[256,2048]{1,0:T(8,128)(2,1)S(1)}, u32[]{:S(2)}, u32[]{:S(2)}) collective-permute-start(bf16[256,2048]{1,0:T(8,128)(2,1)S(1)} %get-tuple-element.108), channel_id=1, source_target_pairs={{0,4},{2,6},{4,0},{6,2},{1,5},{3,7},{5,1},{7,3},{8,12},{10,14},{12... | collective-permute-start | bytes 3145736 | tf_op jit(solution)/shard_map/ppermute | solution.py:389
  86.7 200.7 %all-gather.8.cloned.1.call-start = ((), (), s32[]{:S(2)}) async-start(), calls=%async_computation.5 | async-start | bytes 6488064 | tf_op jit(solution)/shard_map/all_gather | solution.py:526
  129.2 25.5 %collective-permute-start.10 = (bf16[256,2048]{1,0:T(8,128)(2,1)S(1)}, bf16[256,2048]{1,0:T(8,128)(2,1)S(1)}, u32[]{:S(2)}, u32[]{:S(2)}) collective-permute-start(bf16[256,2048]{1,0:T(8,128)(2,1)S(1)} %pad_maximum_fusion.6), channel_id=1, source_target_pairs={{0,4},{2,6},{4,0},{6,2},{1,5},{3,7},{5,1},{7,3},{8,12},{10,14},{12... | collective-permute-start | bytes 3145736 | tf_op jit(solution)/shard_map/ppermute | solution.py:389
  158.8 35.2 %collective-permute-start.16 = (bf16[256,2048]{1,0:T(8,128)(2,1)}, bf16[256,2048]{1,0:T(8,128)(2,1)S(1)}, u32[]{:S(2)}, u32[]{:S(2)}) collective-permute-start(bf16[256,2048]{1,0:T(8,128)(2,1)} %bitcast.14), channel_id=1, source_target_pairs={{0,2},{2,0},{4,6},{6,4},{1,3},{3,1},{5,7},{7,5},{8,10},{10,8},{12,... | collective-permute-start | bytes 3145736 | tf_op jit(solution)/shard_map/ppermute | solution.py:389
  159.3 41.3 %collective-permute-start.17 = (bf16[256,2048]{1,0:T(8,128)(2,1)}, bf16[256,2048]{1,0:T(8,128)(2,1)}, u32[]{:S(2)}, u32[]{:S(2)}) collective-permute-start(bf16[256,2048]{1,0:T(8,128)(2,1)} %bitcast.14), channel_id=1, source_target_pairs={{0,4},{2,6},{4,0},{6,2},{1,5},{3,7},{5,1},{7,3},{8,12},{10,14},{12... | collective-permute-start | bytes 3145736 | tf_op jit(solution)/shard_map/ppermute | solution.py:389
  176.8 39.8 %collective-permute-start.12 = (bf16[256,2048]{1,0:T(8,128)(2,1)}, bf16[256,2048]{1,0:T(8,128)(2,1)}, u32[]{:S(2)}, u32[]{:S(2)}) collective-permute-start(bf16[256,2048]{1,0:T(8,128)(2,1)} %get-tuple-element.104), channel_id=1, source_target_pairs={{0,2},{2,0},{4,6},{6,4},{1,3},{3,1},{5,7},{7,5},{8,10},{10,8},{12,... | collective-permute-start | bytes 3145736 | tf_op jit(solution)/shard_map/ppermute | solution.py:389
  196.3 37.1 %collective-permute-start.13 = (bf16[256,2048]{1,0:T(8,128)(2,1)}, bf16[256,2048]{1,0:T(8,128)(2,1)}, u32[]{:S(2)}, u32[]{:S(2)}) collective-permute-start(bf16[256,2048]{1,0:T(8,128)(2,1)} %get-tuple-element.104), channel_id=1, source_target_pairs={{0,4},{2,6},{4,0},{6,2},{1,5},{3,7},{5,1},{7,3},{8,12},{10,14},{12... | collective-permute-start | bytes 3145736 | tf_op jit(solution)/shard_map/ppermute | solution.py:389
  200.2 374.2 %reduce-scatter.8.cloned.1.call-start = ((), (), s32[]{:S(2)}) async-start(), calls=%async_computation.8 | async-start | bytes 3604480 | tf_op jit(solution)/shard_map/reduce_scatter | solution.py:558
  310.5 263.9 %reduce-scatter.6.cloned.1.call-start = ((), (), s32[]{:S(2)}) async-start(), calls=%async_computation.7 | async-start | bytes 7208960 | tf_op jit(solution)/shard_map/reduce_scatter | solution.py:584
  329.8 25.5 %collective-permute-start.23 = (bf16[256,2048]{1,0:T(8,128)(2,1)}, bf16[256,2048]{1,0:T(8,128)(2,1)}, u32[]{:S(2)}, u32[]{:S(2)}) collective-permute-start(bf16[256,2048]{1,0:T(8,128)(2,1)} %pad_maximum_fusion.8), channel_id=1, source_target_pairs={{0,4},{2,6},{4,0},{6,2},{1,5},{3,7},{5,1},{7,3},{8,12},{10,14},{12... | collective-permute-start | bytes 3145736 | tf_op jit(solution)/shard_map/ppermute | solution.py:389
  331.7 25.3 %collective-permute-start.21 = (bf16[256,2048]{1,0:T(8,128)(2,1)}, bf16[256,2048]{1,0:T(8,128)(2,1)}, u32[]{:S(2)}, u32[]{:S(2)}) collective-permute-start(bf16[256,2048]{1,0:T(8,128)(2,1)} %pad_maximum_fusion.7), channel_id=1, source_target_pairs={{0,2},{2,0},{4,6},{6,4},{1,3},{3,1},{5,7},{7,5},{8,10},{10,8},{12,... | collective-permute-start | bytes 3145736 | tf_op jit(solution)/shard_map/ppermute | solution.py:389
  343.3 245.2 %reduce-scatter.4.cloned.1.call-start = ((), (), s32[]{:S(2)}) async-start(), calls=%async_computation.6 | async-start | bytes 5242880 | tf_op jit(solution)/shard_map/reduce_scatter | solution.py:617
  380.2 30.4 %collective-permute-start.26 = (bf16[256,2048]{1,0:T(8,128)(2,1)}, bf16[256,2048]{1,0:T(8,128)(2,1)}, u32[]{:S(2)}, u32[]{:S(2)}) collective-permute-start(bf16[256,2048]{1,0:T(8,128)(2,1)} %get-tuple-element.102), channel_id=1, source_target_pairs={{0,4},{2,6},{4,0},{6,2},{1,5},{3,7},{5,1},{7,3},{8,12},{10,14},{12... | collective-permute-start | bytes 3145736 | tf_op jit(solution)/shard_map/ppermute | solution.py:389
  473.9 26.6 %collective-permute-start.31 = (bf16[256,2048]{1,0:T(8,128)(2,1)}, bf16[256,2048]{1,0:T(8,128)(2,1)}, u32[]{:S(2)}, u32[]{:S(2)}) collective-permute-start(bf16[256,2048]{1,0:T(8,128)(2,1)} %pad_maximum_fusion.10), channel_id=1, source_target_pairs={{0,4},{2,6},{4,0},{6,2},{1,5},{3,7},{5,1},{7,3},{8,12},{10,14},{12... | collective-permute-start | bytes 3145736 | tf_op jit(solution)/shard_map/ppermute | solution.py:389
  475.7 26.3 %collective-permute-start.29 = (bf16[256,2048]{1,0:T(8,128)(2,1)}, bf16[256,2048]{1,0:T(8,128)(2,1)}, u32[]{:S(2)}, u32[]{:S(2)}) collective-permute-start(bf16[256,2048]{1,0:T(8,128)(2,1)} %pad_maximum_fusion.9), channel_id=1, source_target_pairs={{0,2},{2,0},{4,6},{6,4},{1,3},{3,1},{5,7},{7,5},{8,10},{10,8},{12,... | collective-permute-start | bytes 3145736 | tf_op jit(solution)/shard_map/ppermute | solution.py:389
  492.7 29.9 %collective-permute-start.37 = (bf16[256,2048]{1,0:T(8,128)(2,1)S(1)}, bf16[256,2048]{1,0:T(8,128)(2,1)S(1)}, u32[]{:S(2)}, u32[]{:S(2)}) collective-permute-start(bf16[256,2048]{1,0:T(8,128)(2,1)S(1)} %pad_maximum_fusion.12), channel_id=1, source_target_pairs={{0,4},{2,6},{4,0},{6,2},{1,5},{3,7},{5,1},{7,3},{8,12},{10,14},{12... | collective-permute-start | bytes 3145736 | tf_op jit(solution)/shard_map/ppermute | solution.py:389
  494.3 30.1 %collective-permute-start.35 = (bf16[256,2048]{1,0:T(8,128)(2,1)S(1)}, bf16[256,2048]{1,0:T(8,128)(2,1)S(1)}, u32[]{:S(2)}, u32[]{:S(2)}) collective-permute-start(bf16[256,2048]{1,0:T(8,128)(2,1)S(1)} %pad_maximum_fusion.11), channel_id=1, source_target_pairs={{0,2},{2,0},{4,6},{6,4},{1,3},{3,1},{5,7},{7,5},{8,10},{10,8},{12,... | collective-permute-start | bytes 3145736 | tf_op jit(solution)/shard_map/ppermute | solution.py:389
  507.6 41.1 %collective-permute-start.30 = (bf16[128,2048]{1,0:T(8,128)(2,1)}, bf16[128,2048]{1,0:T(8,128)(2,1)S(1)}, u32[]{:S(2)}, u32[]{:S(2)}) collective-permute-start(bf16[128,2048]{1,0:T(8,128)(2,1)} %get-tuple-element.117), channel_id=1, source_target_pairs={{0,4},{2,6},{4,0},{6,2},{1,5},{3,7},{5,1},{7,3},{8,12},{10,14},{12... | collective-permute-start | bytes 1572872 | tf_op jit(solution)/shard_map/ppermute | solution.py:389
  508.3 40.4 %collective-permute-start.32 = (bf16[128,2048]{1,0:T(8,128)(2,1)}, bf16[128,2048]{1,0:T(8,128)(2,1)S(1)}, u32[]{:S(2)}, u32[]{:S(2)}) collective-permute-start(bf16[128,2048]{1,0:T(8,128)(2,1)} %get-tuple-element.118), channel_id=1, source_target_pairs={{0,2},{2,0},{4,6},{6,4},{1,3},{3,1},{5,7},{7,5},{8,10},{10,8},{12,... | collective-permute-start | bytes 1572872 | tf_op jit(solution)/shard_map/ppermute | solution.py:389
  580.7 25.5 %collective-permute-start.46 = (bf16[128,2176]{1,0:T(8,128)(2,1)}, bf16[128,2176]{1,0:T(8,128)(2,1)S(1)}, u32[]{:S(2)}, u32[]{:S(2)}) collective-permute-start(bf16[128,2176]{1,0:T(8,128)(2,1)} %get-tuple-element.137), channel_id=1, source_target_pairs={{2,0},{0,1},{6,2},{4,3},{3,4},{1,5},{7,6},{5,7},{10,8},{8,9},{14,1... | collective-permute-start | bytes 1671176 | tf_op jit(solution)/shard_map/ppermute | solution.py:442
  582.7 26.6 %collective-permute-start.48 = (bf16[128,2176]{1,0:T(8,128)(2,1)S(1)}, bf16[128,2176]{1,0:T(8,128)(2,1)S(1)}, u32[]{:S(2)}, u32[]{:S(2)}) collective-permute-start(bf16[128,2176]{1,0:T(8,128)(2,1)S(1)} %get-tuple-element.135), channel_id=1, source_target_pairs={{6,0},{4,1},{2,2},{0,3},{7,4},{5,5},{3,6},{1,7},{14,8},{12,9},{10,... | collective-permute-start | bytes 1671176 | tf_op jit(solution)/shard_map/ppermute | solution.py:442
  (92 other events, 1131.2 us)
Sparse Core Ops, SparseCore 0:
  12.0 84.7 all-gather.3
  99.0 106.5 all-gather.5
  207.2 58.5 all-gather.7
  310.6 53.8 reduce-scatter.7
  366.7 102.0 reduce-scatter.5
  484.3 75.2 reduce-scatter.3

commit v8 on v6

--- a/solution.py
+++ b/solution.py
@@ -313,8 +313,8 @@
     for slot in range(len(pieces)):
         span = pl.ds((slot % q) * rows, rows)
         lo = (slot // q) * fs
-        gate_up[0, span, lo : lo + fs] = held[slot, :, 0:fs].astype(f32)
-        gate_up[1, span, lo : lo + fs] = held[slot, :, fs : 2 * fs].astype(f32)
+        gate_up[span, 0, lo : lo + fs] = held[slot, :, 0:fs].astype(f32)
+        gate_up[span, 1, lo : lo + fs] = held[slot, :, fs : 2 * fs].astype(f32)
         down[span, lo : lo + fs] = held[slot, :, 2 * fs : 3 * fs].astype(f32)
 
 
@@ -641,7 +641,7 @@
             info,
             bring_back(packed),
             [
-                jax.ShapeDtypeStruct((2, w_rows, ff_local), f32),
+                jax.ShapeDtypeStruct((w_rows, 2, ff_local), f32),
                 jax.ShapeDtypeStruct((w_rows, ff_local), f32),
             ],
             [held],
@@ -665,7 +665,7 @@
             home_out,
             sums[2],
             sums[3],
-            home_gu.transpose(1, 0, 2),
+            home_gu,
             home_down,
         )
 

time: 638 us -> 636 us (level)
    unnamed x134 -> x133, local copies, waits for them, and re-layouts: 37.7 us -> 33.9 us
where the time goes in v8:
time: 636 us; the launch traced here: 630 us
  waiting for transfers between devices  262 us (41%)
  matrix products  142 us (22%)
  Pallas kernels  67.6 us (11%)
  starting transfers between devices  63.4 us (10%)
  local copies, waits for them, and re-layouts  49.7 us (8%)
  other arithmetic  29.5 us (5%)
  between operations  16.1 us (3%)
    ppermute x40, waiting for transfers between devices, row_permute(): return lax.ppermute(block, ROW, [(i, i ^ k) for i in range(R)])  199 us
    dot_general x18, matrix products, dot(): lax.dot_general(left, right, (dims, ((), ())), preferred_element_type=f32)  142 us
    ppermute x40, starting transfers between devices, row_permute(): return lax.ppermute(block, ROW, [(i, i ^ k) for i in range(R)])  44 us
    unnamed x133, local copies, waits for them, and re-layouts  33.9 us
    pallas_call x1, Pallas kernels, attend_backward(): pl.pallas_call(lambda *refs: backward_kernel(blocks, size, *refs), grid_s...  26.7 us
    ppermute x4, waiting for transfers between devices, spread(): lax.ppermute(packed[k], (ROW, COL), exchange_pairs(k))  20.8 us
    pallas_call x1, Pallas kernels, attend_forward(): pl.pallas_call(lambda *refs: forward_kernel(blocks, size, *refs), grid_sp...  18.2 us
    ppermute x4, waiting for transfers between devices, bring_back(): lax.ppermute(packed[k], (ROW, COL), [(b, a) for a, b in exchange_pairs(k)])  17.8 us
  transfers between devices with their start and end apart: 62, of which 40 were waited for; matrix products, arithmetic and copies ran while one was open for 33% of the time, Pallas kernels for 10%

profile of v8, /device:TPU:0, one launch (start us, length us, event | category | flops | bytes accessed | tf_op | source)
XLA Modules:
  0.0 629.5 jit_solution(2010330663491293910)
XLA Ops:
  17.7 21.6 %collective-permute-done = bf16[256,2048]{1,0:T(8,128)(2,1)S(1)} collective-permute-done((bf16[256,2048]{1,0:T(8,128)(2,1)S(1)}, bf16[256,2048]{1,0:T(8,128)(2,1)S(1)}, u32[]{:S(2)}, u32[]{:S(2)}) %collective-permute-start) | collective-permute-done | bytes 1048608 | tf_op jit(solution)/shard_map/ppermute | solution.py:389
  44.1 8.5 %collective-permute-done.2 = bf16[128,2048]{1,0:T(8,128)(2,1)S(1)} collective-permute-done((bf16[128,2048]{1,0:T(8,128)(2,1)S(1)}, bf16[128,2048]{1,0:T(8,128)(2,1)S(1)}, u32[]{:S(2)}, u32[]{:S(2)}) %collective-permute-start.2) | collective-permute-done | bytes 524320 | tf_op jit(solution)/shard_map/ppermute | solution.py:389
  63.6 8.9 %collective-permute-done.5.refs_1_ = bf16[128,2176]{1,0:T(8,128)(2,1)S(1)} collective-permute-done((bf16[128,2176]{1,0:T(8,128)(2,1)S(1)}, bf16[128,2176]{1,0:T(8,128)(2,1)S(1)}, u32[]{:S(2)}, u32[]{:S(2)}) %collective-permute-start.5) | collective-permute-done | bytes 557088 | tf_op jit(solution)/shard_map/ppermute | solution.py:440
  72.5 11.9 %collective-permute-done.6.refs_2_ = bf16[128,2176]{1,0:T(8,128)(2,1)S(1)} collective-permute-done((bf16[128,2176]{1,0:T(8,128)(2,1)S(1)}, bf16[128,2176]{1,0:T(8,128)(2,1)S(1)}, u32[]{:S(2)}, u32[]{:S(2)}) %collective-permute-start.6) | collective-permute-done | bytes 557088 | tf_op jit(solution)/shard_map/ppermute | solution.py:440
  89.0 7.7 %all-gather.4.cloned.1.call-done = bf16[2048,2048]{1,0:T(8,128)(2,1)} async-done(((bf16[256,2048]{1,0:T(8,128)(2,1)}), bf16[2048,2048]{1,0:T(8,128)(2,1)}) %all-gather.4.cloned.1.call-update) | async-done | bytes 8388624 | tf_op jit(solution)/shard_map/all_gather | solution.py:508
  96.8 12.1 %fusion.14.refs_1_ = f32[1024,1536]{1,0:T(8,128)} fusion(bf16[1024,2048]{1,0:T(8,128)(2,1)} %copy-done.17, bf16[2048,2048]{1,0:T(8,128)(2,1)} %all-gather.4.cloned.1.call-done, f32[1536]{0:T(1024)S(1)} %reshape.565), kind=kOutput, calls=%fused_computation.21 | convolution fusion | flops 6444023808 | bytes 16783360 | tf_op jit(solution)/shard_map/dot_general | solution.py:54
  108.9 18.2 %attn_f.1 = (bf16[1024,1536]{1,0:T(8,128)(2,1)S(1)}, bf16[1024,512]{1,0:T(8,128)(2,1)S(1)}, f32[4,4,16,256]{3,2,1,0:T(8,128)S(1)}) custom-call(s32[5]{0:T(128)S(1)} %stack.30.info.refs_0_, f32[1024,1536]{1,0:T(8,128)} %fusion.14.refs_1_, f32[3,1024,128]{2,1,0:T(8,128)S(1)} %pad_maximum_fusion.3.refs_2_), custom_call_target="tpu_custom_call" | custom-call | tf_op jit(solution)/shard_map/attn_f/pallas_call | solution.py:217
  136.0 10.7 %collective-permute-done.12 = bf16[128,2048]{1,0:T(8,128)(2,1)S(1)} collective-permute-done((bf16[128,2048]{1,0:T(8,128)(2,1)S(1)}, bf16[128,2048]{1,0:T(8,128)(2,1)S(1)}, u32[]{:S(2)}, u32[]{:S(2)}) %collective-permute-start.12) | collective-permute-done | bytes 524320 | tf_op jit(solution)/shard_map/ppermute | solution.py:389
  159.7 9.5 %collective-permute-done.10 = bf16[128,2048]{1,0:T(8,128)(2,1)S(1)} collective-permute-done((bf16[128,2048]{1,0:T(8,128)(2,1)S(1)}, bf16[128,2048]{1,0:T(8,128)(2,1)S(1)}, u32[]{:S(2)}, u32[]{:S(2)}) %collective-permute-start.10) | collective-permute-done | bytes 524320 | tf_op jit(solution)/shard_map/ppermute | solution.py:389
  176.0 17.3 %collective-permute-done.18 = bf16[256,2048]{1,0:T(8,128)(2,1)S(1)} collective-permute-done((bf16[256,2048]{1,0:T(8,128)(2,1)}, bf16[256,2048]{1,0:T(8,128)(2,1)S(1)}, u32[]{:S(2)}, u32[]{:S(2)}) %collective-permute-start.18) | collective-permute-done | bytes 1048608 | tf_op jit(solution)/shard_map/ppermute | solution.py:389
  218.2 7.9 %collective-permute-done.21 = bf16[128,2048]{1,0:T(8,128)(2,1)S(1)} collective-permute-done((bf16[128,2048]{1,0:T(8,128)(2,1)S(1)}, bf16[128,2048]{1,0:T(8,128)(2,1)S(1)}, u32[]{:S(2)}, u32[]{:S(2)}) %collective-permute-start.21) | collective-permute-done | bytes 524320 | tf_op jit(solution)/shard_map/ppermute | solution.py:389
  247.5 17.3 %fusion.104 = f32[1024,2816]{1,0:T(8,128)S(1)} fusion(bf16[1024,2048]{1,0:T(8,128)(2,1)} %constant_dynamic-update-slice_fusion.5, bf16[2048,2816]{1,0:T(8,128)(2,1)} %all-gather.6.cloned.1.call-done), kind=kOutput, calls=%fused_computation.192 | convolution fusion | flops 11811160064 | bytes 27262976 | tf_op jit(solution)/shard_map/dot_general | solution.py:54
  283.4 14.7 %multiply_convert_fusion.1 = (bf16[1024,1408]{1,0:T(8,128)(2,1)S(1)}, bf16[1024,1408]{1,0:T(8,128)(2,1)S(1)}) fusion(f32[1024,2816]{1,0:T(8,128)} %copy-done.26, bf16[1024,2048]{1,0:T(8,128)(2,1)} %constant_dynamic-update-slice_fusion.10.mine.other, bf16[2048,1408]{1,0:T(8,128)(2,1)} %all-gather.8.cloned.1.call-done), kind=kOutput, calls=%fused_computation.6 | convolution fusion | flops 5924323328 | bytes 27262976 | tf_op jit(solution)/shard_map/dot_general | solution.py:54
  298.2 15.3 %fusion.17 = bf16[768,2048]{1,0:T(8,128)(2,1)} fusion(bf16[2048,2816]{1,0:T(8,128)(2,1)} %all-gather.6.cloned.1.call-done, bf16[1024,1408]{1,0:T(8,128)(2,1)S(1)} %get-tuple-element.82, bf16[1024,1408]{1,0:T(8,128)(2,1)S(1)} %get-tuple-element.81), kind=kOutput, calls=%fused_computation.29 | convolution fusion | flops 8868593664 | bytes 20447232 | tf_op jit(solution)/shard_map/dot_general | solution.py:54
  313.5 14.6 %convolution_convert_fusion = bf16[2048,2816]{1,0:T(8,128)(2,1)} fusion(bf16[1024,2048]{1,0:T(8,128)(2,1)S(1)} %copy-done.37, bf16[1024,1408]{1,0:T(8,128)(2,1)S(1)} %get-tuple-element.82, bf16[1024,1408]{1,0:T(8,128)(2,1)S(1)} %get-tuple-element.81), kind=kOutput, calls=%fused_computation | convolution fusion | flops 11828461568 | bytes 21495808 | tf_op jit(solution)/shard_map/dot_general | solution.py:54
  334.3 10.7 %collective-permute-done.24 = bf16[128,2048]{1,0:T(8,128)(2,1)S(1)} collective-permute-done((bf16[128,2048]{1,0:T(8,128)(2,1)S(1)}, bf16[128,2048]{1,0:T(8,128)(2,1)S(1)}, u32[]{:S(2)}, u32[]{:S(2)}) %collective-permute-start.24) | collective-permute-done | bytes 524320 | tf_op jit(solution)/shard_map/ppermute | solution.py:389
  357.7 10.2 %collective-permute-done.25 = bf16[128,2048]{1,0:T(8,128)(2,1)S(1)} collective-permute-done((bf16[128,2048]{1,0:T(8,128)(2,1)S(1)}, bf16[128,2048]{1,0:T(8,128)(2,1)S(1)}, u32[]{:S(2)}, u32[]{:S(2)}) %collective-permute-start.25) | collective-permute-done | bytes 524320 | tf_op jit(solution)/shard_map/ppermute | solution.py:389
  373.6 23.5 %collective-permute-done.29 = bf16[256,2048]{1,0:T(8,128)(2,1)S(1)} collective-permute-done((bf16[256,2048]{1,0:T(8,128)(2,1)}, bf16[256,2048]{1,0:T(8,128)(2,1)S(1)}, u32[]{:S(2)}, u32[]{:S(2)}) %collective-permute-start.29) | collective-permute-done | bytes 1048608 | tf_op jit(solution)/shard_map/ppermute | solution.py:389
  424.2 26.7 %attn_b.1 = (bf16[1024,1536]{1,0:T(8,128)(2,1)S(1)}, f32[4,8,384]{2,1,0:T(8,128)S(1)}) custom-call(s32[5]{0:T(128)S(1)} %copy-done.8, bf16[1024,1536]{1,0:T(8,128)(2,1)} %copy-done, f32[3,1024,128]{2,1,0:T(8,128)S(1)} %pad_maximum_fusion.3.refs_2_, f32[4,4,16,256]{3,2,1,0:T(8,128)S(1)} %get-tuple-element.48.refs_3_, bf16[1024,512]{1,0:T(8,128)(2,1)S(1)} %fusion.54.refs_4_), custom_call_target="tpu_custom_call" | custom-call | tf_op jit(solution)/shard_map/attn_b/pallas_call | solution.py:255
  462.5 9.2 %convolution_convert_fusion.4 = bf16[768,2048]{1,0:T(8,128)(2,1)} fusion(bf16[2048,1408]{1,0:T(8,128)(2,1)} %all-gather.8.cloned.1.call-done, bf16[1024,1408]{1,0:T(8,128)(2,1)S(1)} %copy-done.33), kind=kOutput, calls=%fused_computation.32 | convolution fusion | flops 4430757888 | bytes 11075584 | tf_op jit(solution)/shard_map/dot_general | solution.py:54
  492.2 8.3 %fusion.20 = bf16[768,2048]{1,0:T(8,128)(2,1)S(1)} fusion(bf16[2048,2048]{1,0:T(8,128)(2,1)} %all-gather.4.cloned.1.call-done, bf16[1024,1536]{1,0:T(8,128)(2,1)S(1)} %copy-done.11), kind=kOutput, calls=%fused_computation.31 | convolution fusion | flops 4833411072 | bytes 11796480 | tf_op jit(solution)/shard_map/dot_general | solution.py:54
  508.4 17.5 %collective-permute-done.42 = bf16[128,2048]{1,0:T(8,128)(2,1)S(1)} collective-permute-done((bf16[128,2048]{1,0:T(8,128)(2,1)S(1)}, bf16[128,2048]{1,0:T(8,128)(2,1)S(1)}, u32[]{:S(2)}, u32[]{:S(2)}) %collective-permute-start.42) | collective-permute-done | bytes 524320 | tf_op jit(solution)/shard_map/ppermute | solution.py:389
  552.1 9.9 %collective-permute-done.35 = bf16[128,2048]{1,0:T(8,128)(2,1)} collective-permute-done((bf16[128,2048]{1,0:T(8,128)(2,1)}, bf16[128,2048]{1,0:T(8,128)(2,1)}, u32[]{:S(2)}, u32[]{:S(2)}) %collective-permute-start.35) | collective-permute-done | bytes 524320 | tf_op jit(solution)/shard_map/ppermute | solution.py:389
  601.0 12.2 %collective-permute-done.53.refs_1_ = bf16[128,2176]{1,0:T(8,128)(2,1)S(1)} collective-permute-done((bf16[128,2176]{1,0:T(8,128)(2,1)}, bf16[128,2176]{1,0:T(8,128)(2,1)S(1)}, u32[]{:S(2)}, u32[]{:S(2)}) %collective-permute-start.53) | collective-permute-done | bytes 557088 | tf_op jit(solution)/shard_map/ppermute | solution.py:444
  (346 shorter events, 288.7 us)
Async XLA Ops:
  7.2 89.6 %all-gather.4.cloned.1.call-start = ((), (), s32[]{:S(2)}) async-start(), calls=%async_computation.3 | async-start | bytes 9437184 | tf_op jit(solution)/shard_map/all_gather | solution.py:508
  11.8 235.7 %all-gather.6.cloned.1.call-start = ((), (), s32[]{:S(2)}) async-start(), calls=%async_computation.4 | async-start | bytes 12976128 | tf_op jit(solution)/shard_map/all_gather | solution.py:527
  13.2 26.2 %collective-permute-start = (bf16[256,2048]{1,0:T(8,128)(2,1)S(1)}, bf16[256,2048]{1,0:T(8,128)(2,1)S(1)}, u32[]{:S(2)}, u32[]{:S(2)}) collective-permute-start(bf16[256,2048]{1,0:T(8,128)(2,1)S(1)} %get-tuple-element.80), channel_id=1, source_target_pairs={{0,2},{2,0},{4,6},{6,4},{1,3},{3,1},{5,7},{7,5},{8,10},{10,8},{12,... | collective-permute-start | bytes 3145736 | tf_op jit(solution)/shard_map/ppermute | solution.py:389
  16.2 26.1 %collective-permute-start.1 = (bf16[256,2048]{1,0:T(8,128)(2,1)S(1)}, bf16[256,2048]{1,0:T(8,128)(2,1)S(1)}, u32[]{:S(2)}, u32[]{:S(2)}) collective-permute-start(bf16[256,2048]{1,0:T(8,128)(2,1)S(1)} %get-tuple-element.80), channel_id=1, source_target_pairs={{0,4},{2,6},{4,0},{6,2},{1,5},{3,7},{5,1},{7,3},{8,12},{10,14},{12... | collective-permute-start | bytes 3145736 | tf_op jit(solution)/shard_map/ppermute | solution.py:389
  59.4 24.9 %collective-permute-start.6 = (bf16[128,2176]{1,0:T(8,128)(2,1)S(1)}, bf16[128,2176]{1,0:T(8,128)(2,1)S(1)}, u32[]{:S(2)}, u32[]{:S(2)}) collective-permute-start(bf16[128,2176]{1,0:T(8,128)(2,1)S(1)} %get-tuple-element.112), channel_id=1, source_target_pairs={{0,4},{1,6},{2,0},{3,2},{4,5},{5,7},{6,1},{7,3},{8,12},{9,14},{10,... | collective-permute-start | bytes 1671176 | tf_op jit(solution)/shard_map/ppermute | solution.py:440
  86.7 196.7 %all-gather.8.cloned.1.call-start = ((), (), s32[]{:S(2)}) async-start(), calls=%async_computation.5 | async-start | bytes 6488064 | tf_op jit(solution)/shard_map/all_gather | solution.py:528
  150.9 42.5 %collective-permute-start.18 = (bf16[256,2048]{1,0:T(8,128)(2,1)}, bf16[256,2048]{1,0:T(8,128)(2,1)S(1)}, u32[]{:S(2)}, u32[]{:S(2)}) collective-permute-start(bf16[256,2048]{1,0:T(8,128)(2,1)} %bitcast.14), channel_id=1, source_target_pairs={{0,2},{2,0},{4,6},{6,4},{1,3},{3,1},{5,7},{7,5},{8,10},{10,8},{12,... | collective-permute-start | bytes 3145736 | tf_op jit(solution)/shard_map/ppermute | solution.py:389
  158.0 41.6 %collective-permute-start.19 = (bf16[256,2048]{1,0:T(8,128)(2,1)}, bf16[256,2048]{1,0:T(8,128)(2,1)}, u32[]{:S(2)}, u32[]{:S(2)}) collective-permute-start(bf16[256,2048]{1,0:T(8,128)(2,1)} %bitcast.14), channel_id=1, source_target_pairs={{0,4},{2,6},{4,0},{6,2},{1,5},{3,7},{5,1},{7,3},{8,12},{10,14},{12... | collective-permute-start | bytes 3145736 | tf_op jit(solution)/shard_map/ppermute | solution.py:389
  174.6 41.4 %collective-permute-start.14 = (bf16[256,2048]{1,0:T(8,128)(2,1)}, bf16[256,2048]{1,0:T(8,128)(2,1)}, u32[]{:S(2)}, u32[]{:S(2)}) collective-permute-start(bf16[256,2048]{1,0:T(8,128)(2,1)} %get-tuple-element.76), channel_id=1, source_target_pairs={{0,2},{2,0},{4,6},{6,4},{1,3},{3,1},{5,7},{7,5},{8,10},{10,8},{12,... | collective-permute-start | bytes 3145736 | tf_op jit(solution)/shard_map/ppermute | solution.py:389
  195.5 37.3 %collective-permute-start.15 = (bf16[256,2048]{1,0:T(8,128)(2,1)}, bf16[256,2048]{1,0:T(8,128)(2,1)}, u32[]{:S(2)}, u32[]{:S(2)}) collective-permute-start(bf16[256,2048]{1,0:T(8,128)(2,1)} %get-tuple-element.76), channel_id=1, source_target_pairs={{0,4},{2,6},{4,0},{6,2},{1,5},{3,7},{5,1},{7,3},{8,12},{10,14},{12... | collective-permute-start | bytes 3145736 | tf_op jit(solution)/shard_map/ppermute | solution.py:389
  199.5 385.1 %reduce-scatter.8.cloned.1.call-start = ((), (), s32[]{:S(2)}) async-start(), calls=%async_computation.8 | async-start | bytes 3604480 | tf_op jit(solution)/shard_map/reduce_scatter | solution.py:560
  200.7 25.4 %collective-permute-start.21 = (bf16[128,2048]{1,0:T(8,128)(2,1)S(1)}, bf16[128,2048]{1,0:T(8,128)(2,1)S(1)}, u32[]{:S(2)}, u32[]{:S(2)}) collective-permute-start(bf16[128,2048]{1,0:T(8,128)(2,1)S(1)} %slice.316), channel_id=1, source_target_pairs={{0,2},{2,0},{4,6},{6,4},{1,3},{3,1},{5,7},{7,5},{8,10},{10,8},{12,... | collective-permute-start | bytes 1572872 | tf_op jit(solution)/shard_map/ppermute | solution.py:389
  283.3 301.4 %reduce-scatter.6.cloned.1.call-start = ((), (), s32[]{:S(2)}) async-start(), calls=%async_computation.7 | async-start | bytes 12976128 | tf_op jit(solution)/shard_map/reduce_scatter | solution.py:578
  328.2 269.6 %reduce-scatter.4.cloned.1.call-start = ((), (), s32[]{:S(2)}) async-start(), calls=%async_computation.6 | async-start | bytes 5242880 | tf_op jit(solution)/shard_map/reduce_scatter | solution.py:608
  332.2 24.0 %collective-permute-start.23 = (bf16[128,2048]{1,0:T(8,128)(2,1)S(1)}, bf16[128,2048]{1,0:T(8,128)(2,1)S(1)}, u32[]{:S(2)}, u32[]{:S(2)}) collective-permute-start(bf16[128,2048]{1,0:T(8,128)(2,1)S(1)} %get-tuple-element.95), channel_id=1, source_target_pairs={{0,2},{2,0},{4,6},{6,4},{1,3},{3,1},{5,7},{7,5},{8,10},{10,8},{12,... | collective-permute-start | bytes 1572872 | tf_op jit(solution)/shard_map/ppermute | solution.py:389
  332.6 25.1 %collective-permute-start.26 = (bf16[128,2048]{1,0:T(8,128)(2,1)S(1)}, bf16[128,2048]{1,0:T(8,128)(2,1)S(1)}, u32[]{:S(2)}, u32[]{:S(2)}) collective-permute-start(bf16[128,2048]{1,0:T(8,128)(2,1)S(1)} %get-tuple-element.97), channel_id=1, source_target_pairs={{0,4},{2,6},{4,0},{6,2},{1,5},{3,7},{5,1},{7,3},{8,12},{10,14},{12... | collective-permute-start | bytes 1572872 | tf_op jit(solution)/shard_map/ppermute | solution.py:389
  372.7 24.4 %collective-permute-start.29 = (bf16[256,2048]{1,0:T(8,128)(2,1)}, bf16[256,2048]{1,0:T(8,128)(2,1)S(1)}, u32[]{:S(2)}, u32[]{:S(2)}) collective-permute-start(bf16[256,2048]{1,0:T(8,128)(2,1)} %get-tuple-element.74), channel_id=1, source_target_pairs={{0,2},{2,0},{4,6},{6,4},{1,3},{3,1},{5,7},{7,5},{8,10},{10,8},{12,... | collective-permute-start | bytes 3145736 | tf_op jit(solution)/shard_map/ppermute | solution.py:389
  373.3 31.7 %collective-permute-start.30 = (bf16[256,2048]{1,0:T(8,128)(2,1)}, bf16[256,2048]{1,0:T(8,128)(2,1)}, u32[]{:S(2)}, u32[]{:S(2)}) collective-permute-start(bf16[256,2048]{1,0:T(8,128)(2,1)} %get-tuple-element.74), channel_id=1, source_target_pairs={{0,4},{2,6},{4,0},{6,2},{1,5},{3,7},{5,1},{7,3},{8,12},{10,14},{12... | collective-permute-start | bytes 3145736 | tf_op jit(solution)/shard_map/ppermute | solution.py:389
  490.7 60.2 %collective-permute-start.33 = (bf16[128,2048]{1,0:T(8,128)(2,1)}, bf16[128,2048]{1,0:T(8,128)(2,1)S(1)}, u32[]{:S(2)}, u32[]{:S(2)}) collective-permute-start(bf16[128,2048]{1,0:T(8,128)(2,1)} %get-tuple-element.89), channel_id=1, source_target_pairs={{0,2},{2,0},{4,6},{6,4},{1,3},{3,1},{5,7},{7,5},{8,10},{10,8},{12,... | collective-permute-start | bytes 1572872 | tf_op jit(solution)/shard_map/ppermute | solution.py:389
  500.8 25.1 %collective-permute-start.42 = (bf16[128,2048]{1,0:T(8,128)(2,1)S(1)}, bf16[128,2048]{1,0:T(8,128)(2,1)S(1)}, u32[]{:S(2)}, u32[]{:S(2)}) collective-permute-start(bf16[128,2048]{1,0:T(8,128)(2,1)S(1)} %get-tuple-element.86), channel_id=1, source_target_pairs={{0,2},{2,0},{4,6},{6,4},{1,3},{3,1},{5,7},{7,5},{8,10},{10,8},{12,... | collective-permute-start | bytes 1572872 | tf_op jit(solution)/shard_map/ppermute | solution.py:389
  501.7 24.2 %collective-permute-start.45 = (bf16[128,2048]{1,0:T(8,128)(2,1)S(1)}, bf16[128,2048]{1,0:T(8,128)(2,1)S(1)}, u32[]{:S(2)}, u32[]{:S(2)}) collective-permute-start(bf16[128,2048]{1,0:T(8,128)(2,1)S(1)} %get-tuple-element.84), channel_id=1, source_target_pairs={{0,4},{2,6},{4,0},{6,2},{1,5},{3,7},{5,1},{7,3},{8,12},{10,14},{12... | collective-permute-start | bytes 1572872 | tf_op jit(solution)/shard_map/ppermute | solution.py:389
  505.0 32.2 %collective-permute-start.41 = (bf16[128,2048]{1,0:T(8,128)(2,1)S(1)}, bf16[128,2048]{1,0:T(8,128)(2,1)S(1)}, u32[]{:S(2)}, u32[]{:S(2)}) collective-permute-start(bf16[128,2048]{1,0:T(8,128)(2,1)S(1)} %get-tuple-element.83), channel_id=1, source_target_pairs={{0,2},{2,0},{4,6},{6,4},{1,3},{3,1},{5,7},{7,5},{8,10},{10,8},{12,... | collective-permute-start | bytes 1572872 | tf_op jit(solution)/shard_map/ppermute | solution.py:389
  506.1 32.5 %collective-permute-start.44 = (bf16[128,2048]{1,0:T(8,128)(2,1)S(1)}, bf16[128,2048]{1,0:T(8,128)(2,1)S(1)}, u32[]{:S(2)}, u32[]{:S(2)}) collective-permute-start(bf16[128,2048]{1,0:T(8,128)(2,1)S(1)} %get-tuple-element.85), channel_id=1, source_target_pairs={{0,4},{2,6},{4,0},{6,2},{1,5},{3,7},{5,1},{7,3},{8,12},{10,14},{12... | collective-permute-start | bytes 1572872 | tf_op jit(solution)/shard_map/ppermute | solution.py:389
  593.0 25.9 %collective-permute-start.55 = (bf16[128,2176]{1,0:T(8,128)(2,1)S(1)}, bf16[128,2176]{1,0:T(8,128)(2,1)S(1)}, u32[]{:S(2)}, u32[]{:S(2)}) collective-permute-start(bf16[128,2176]{1,0:T(8,128)(2,1)S(1)} %get-tuple-element.107), channel_id=1, source_target_pairs={{6,0},{4,1},{2,2},{0,3},{7,4},{5,5},{3,6},{1,7},{14,8},{12,9},{10,... | collective-permute-start | bytes 1671176 | tf_op jit(solution)/shard_map/ppermute | solution.py:444
  (97 other events, 1304.1 us)
Sparse Core Ops, SparseCore 0:
  12.0 84.7 all-gather.3
  99.0 106.5 all-gather.5
  207.2 58.6 all-gather.7
  283.4 53.9 reduce-scatter.7
  339.6 118.9 reduce-scatter.5
  481.6 74.2 reduce-scatter.3

commit v9 on v8

--- a/solution.py
+++ b/solution.py
@@ -568,14 +568,28 @@
         grad_gate = grad_hidden * up_vals * sig * (1.0 + gate_vals * (1.0 - sig))
         grad_up = grad_hidden * swish
         grad_gu_vals = jnp.concatenate([grad_gate.astype(bf16), grad_up.astype(bf16)], axis=1)
-        own = nt(grad_gu_vals[:block], w_gu)
-        others = nt(grad_gu_vals[block:], w_gu).astype(bf16)
-        others, second_in = lax.optimization_barrier((others, second_in))
+        if C == 2:
+            halves = split_columns(info, second_in, mesh.shape[DP])
+            away = tn(halves[1], grad_gu_vals).astype(bf16)
+            got = lax.ppermute(away, COL, [(0, 1), (1, 0)])
+            second_vals, _ = lax.optimization_barrier((grad_gu_vals, away))
+        else:
+            second_vals = grad_gu_vals
+        own = nt(second_vals[:block], w_gu)
+        last = (R - 1) * block
+        far = nt(second_vals[last:], w_gu).astype(bf16)
+        second_vals, _ = lax.optimization_barrier((second_vals, far))
+        others = nt(second_vals[block:last], w_gu).astype(bf16)
+        _, grad_gu_vals = lax.optimization_barrier((others, grad_gu_vals))
         grad_second = scatter_rel(
-            [own] + [others[k * block : (k + 1) * block] for k in range(R - 1)]
-        )
-        grad_gu = tn(second_in, grad_gu_vals).astype(bf16)
-        grad_gu = lax.psum_scatter(grad_gu, (DP, COL), scatter_dimension=0, tiled=True)
+            [own] + [others[k * block : (k + 1) * block] for k in range(R - 2)] + [far]
+        )
+        if C == 2:
+            grad_gu = (tn(halves[0], grad_gu_vals) + got.astype(f32)).astype(bf16)
+            grad_gu = lax.psum_scatter(grad_gu, DP, scatter_dimension=0, tiled=True)
+        else:
+            grad_gu = tn(second_in, grad_gu_vals).astype(bf16)
+            grad_gu = lax.psum_scatter(grad_gu, (DP, COL), scatter_dimension=0, tiled=True)
 
         grad_middle = dy.astype(f32) + layer_norm_backward(
             grad_second, second_std, second_inv, gain2

time: 636 us -> 643 us (1.011)
  the two profiles are of different devices: /device:TPU:0 before, /device:TPU:10 now
where the time goes in v9:
time: 643 us; the launch traced here: 630 us
  waiting for transfers between devices  248 us (39%)
  matrix products  155 us (24%)
  Pallas kernels  73.2 us (11%)
  starting transfers between devices  55.2 us (9%)
  local copies, waits for them, and re-layouts  50.2 us (8%)
  other arithmetic  33 us (5%)
  between operations  16.1 us (3%)
    ppermute x40, waiting for transfers between devices, row_permute(): return lax.ppermute(block, ROW, [(i, i ^ k) for i in range(R)])  192 us
    dot_general x20, matrix products, dot(): lax.dot_general(left, right, (dims, ((), ())), preferred_element_type=f32)  155 us
    ppermute x40, starting transfers between devices, row_permute(): return lax.ppermute(block, ROW, [(i, i ^ k) for i in range(R)])  37.4 us
    unnamed x131, local copies, waits for them, and re-layouts  33.9 us
    pallas_call x1, Pallas kernels, attend_backward(): pl.pallas_call(lambda *refs: backward_kernel(blocks, size, *refs), grid_s...  26.7 us
    ppermute x4, waiting for transfers between devices, spread(): lax.ppermute(packed[k], (ROW, COL), exchange_pairs(k))  21.7 us
    pallas_call x1, Pallas kernels, attend_forward(): pl.pallas_call(lambda *refs: forward_kernel(blocks, size, *refs), grid_sp...  18.3 us
    ppermute x4, waiting for transfers between devices, bring_back(): lax.ppermute(packed[k], (ROW, COL), [(b, a) for a, b in exchange_pairs(k)])  17.9 us
  transfers between devices with their start and end apart: 63, of which 37 were waited for; matrix products, arithmetic and copies ran while one was open for 32% of the time, Pallas kernels for 11%

profile of v9, /device:TPU:10, one launch (start us, length us, event | category | flops | bytes accessed | tf_op | source)
XLA Modules:
  0.0 630.5 jit_solution(14302862089549922617)
XLA Ops:
  15.3 22.8 %collective-permute-done = bf16[256,2048]{1,0:T(8,128)(2,1)S(1)} collective-permute-done((bf16[256,2048]{1,0:T(8,128)(2,1)S(1)}, bf16[256,2048]{1,0:T(8,128)(2,1)S(1)}, u32[]{:S(2)}, u32[]{:S(2)}) %collective-permute-start) | collective-permute-done | bytes 1048608 | tf_op jit(solution)/shard_map/ppermute | solution.py:389
  41.7 9.5 %collective-permute-done.2 = bf16[128,2048]{1,0:T(8,128)(2,1)S(1)} collective-permute-done((bf16[128,2048]{1,0:T(8,128)(2,1)S(1)}, bf16[128,2048]{1,0:T(8,128)(2,1)S(1)}, u32[]{:S(2)}, u32[]{:S(2)}) %collective-permute-start.2) | collective-permute-done | bytes 524320 | tf_op jit(solution)/shard_map/ppermute | solution.py:389
  59.0 10.5 %collective-permute-done.4.refs_0_ = bf16[128,2176]{1,0:T(8,128)(2,1)S(1)} collective-permute-done((bf16[128,2176]{1,0:T(8,128)(2,1)S(1)}, bf16[128,2176]{1,0:T(8,128)(2,1)S(1)}, u32[]{:S(2)}, u32[]{:S(2)}) %collective-permute-start.4) | collective-permute-done | bytes 557088 | tf_op jit(solution)/shard_map/ppermute | solution.py:440
  71.8 9.0 %collective-permute-done.6.refs_2_ = bf16[128,2176]{1,0:T(8,128)(2,1)S(1)} collective-permute-done((bf16[128,2176]{1,0:T(8,128)(2,1)S(1)}, bf16[128,2176]{1,0:T(8,128)(2,1)S(1)}, u32[]{:S(2)}, u32[]{:S(2)}) %collective-permute-start.6) | collective-permute-done | bytes 557088 | tf_op jit(solution)/shard_map/ppermute | solution.py:440
  92.7 11.9 %fusion.7.refs_1_ = f32[1024,1536]{1,0:T(8,128)} fusion(bf16[1024,2048]{1,0:T(8,128)(2,1)} %copy-done.17, bf16[2048,2048]{1,0:T(8,128)(2,1)} %all-gather.4.cloned.1.call-done, f32[1536]{0:T(1024)S(1)} %reshape.565), kind=kOutput, calls=%fused_computation.16 | convolution fusion | flops 6444023808 | bytes 16783360 | tf_op jit(solution)/shard_map/dot_general | solution.py:54
  104.6 18.3 %attn_f.1 = (bf16[1024,1536]{1,0:T(8,128)(2,1)S(1)}, bf16[1024,512]{1,0:T(8,128)(2,1)S(1)}, f32[4,4,16,256]{3,2,1,0:T(8,128)S(1)}) custom-call(s32[5]{0:T(128)S(1)} %stack.30.info.refs_0_, f32[1024,1536]{1,0:T(8,128)} %fusion.7.refs_1_, f32[3,1024,128]{2,1,0:T(8,128)S(1)} %pad_maximum_fusion.4.refs_2_), custom_call_target="tpu_custom_call" | custom-call | tf_op jit(solution)/shard_map/attn_f/pallas_call | solution.py:217
  131.7 10.7 %collective-permute-done.12 = bf16[128,2048]{1,0:T(8,128)(2,1)S(1)} collective-permute-done((bf16[128,2048]{1,0:T(8,128)(2,1)S(1)}, bf16[128,2048]{1,0:T(8,128)(2,1)S(1)}, u32[]{:S(2)}, u32[]{:S(2)}) %collective-permute-start.12) | collective-permute-done | bytes 524320 | tf_op jit(solution)/shard_map/ppermute | solution.py:389
  155.2 9.8 %collective-permute-done.10 = bf16[128,2048]{1,0:T(8,128)(2,1)S(1)} collective-permute-done((bf16[128,2048]{1,0:T(8,128)(2,1)S(1)}, bf16[128,2048]{1,0:T(8,128)(2,1)S(1)}, u32[]{:S(2)}, u32[]{:S(2)}) %collective-permute-start.10) | collective-permute-done | bytes 524320 | tf_op jit(solution)/shard_map/ppermute | solution.py:389
  170.6 18.3 %collective-permute-done.18 = bf16[256,2048]{1,0:T(8,128)(2,1)S(1)} collective-permute-done((bf16[256,2048]{1,0:T(8,128)(2,1)}, bf16[256,2048]{1,0:T(8,128)(2,1)S(1)}, u32[]{:S(2)}, u32[]{:S(2)}) %collective-permute-start.18) | collective-permute-done | bytes 1048608 | tf_op jit(solution)/shard_map/ppermute | solution.py:389
  243.4 17.3 %fusion.92 = f32[1024,2816]{1,0:T(8,128)S(1)} fusion(bf16[1024,2048]{1,0:T(8,128)(2,1)} %constant_dynamic-update-slice_fusion.5.mine.other, bf16[2048,2816]{1,0:T(8,128)(2,1)} %all-gather.6.cloned.1.call-done), kind=kOutput, calls=%fused_computation.186 | convolution fusion | flops 11811160064 | bytes 27262976 | tf_op jit(solution)/shard_map/dot_general | solution.py:54
  275.7 8.4 %add_convert_fusion.2 = bf16[1024,1408]{1,0:T(8,128)(2,1)} fusion(bf16[1024,1408]{1,0:T(8,128)(2,1)} %collective-permute-done.22, bf16[1024,1024]{1,0:T(8,128)(2,1)} %get-tuple-element.44, bf16[1024,1408]{1,0:T(8,128)(2,1)} %copy-done.33), kind=kOutput, calls=%fused_computation.5 | convolution fusion | flops 2957115392 | bytes 10747904 | tf_op jit(solution)/shard_map/dot_general | solution.py:54
  284.1 14.2 %multiply_convert_fusion.1 = (bf16[1024,1408]{1,0:T(8,128)(2,1)S(1)}, bf16[1024,1408]{1,0:T(8,128)(2,1)S(1)}) fusion(f32[1024,2816]{1,0:T(8,128)} %copy-done.26, bf16[1024,2048]{1,0:T(8,128)(2,1)} %constant_dynamic-update-slice_fusion.10.mine.other, bf16[2048,1408]{1,0:T(8,128)(2,1)} %all-gather.8.cloned.1.call-done), kind=kOutput, calls=%fused_computation.4 | convolution fusion | flops 5924323328 | bytes 27262976 | tf_op jit(solution)/shard_map/dot_general | solution.py:54
  298.4 8.5 %convolution_convert_fusion = bf16[1024,2816]{1,0:T(8,128)(2,1)} fusion(bf16[1024,1024]{1,0:T(8,128)(2,1)S(1)} %copy-done.55, bf16[1024,1408]{1,0:T(8,128)(2,1)S(1)} %get-tuple-element.88, bf16[1024,1408]{1,0:T(8,128)(2,1)S(1)} %get-tuple-element.87), kind=kOutput, calls=%fused_computation.9 | convolution fusion | flops 5919997952 | bytes 13631488 | tf_op jit(solution)/shard_map/dot_general | solution.py:54
  310.3 9.9 %convolution_convert_fusion.7 = bf16[256,2048]{1,0:T(8,128)(2,1)S(1)} fusion(bf16[2048,2816]{1,0:T(8,128)(2,1)} %all-gather.6.cloned.1.call-done, bf16[1024,2816]{1,0:T(8,128)(2,1)S(1)} %pad_maximum_fusion), kind=kOutput, calls=%fused_computation.32 | convolution fusion | flops 2953314304 | bytes 14024704 | tf_op jit(solution)/shard_map/dot_general | solution.py:54
  320.2 10.2 %convolution_convert_fusion.6 = bf16[512,2048]{1,0:T(8,128)(2,1)} fusion(bf16[2048,2816]{1,0:T(8,128)(2,1)} %all-gather.6.cloned.1.call-done, bf16[1024,2816]{1,0:T(8,128)(2,1)S(1)} %pad_maximum_fusion), kind=kOutput, calls=%fused_computation.28 | convolution fusion | flops 5906628608 | bytes 16515072 | tf_op jit(solution)/shard_map/dot_general | solution.py:54
  332.5 10.3 %add_convert_fusion = bf16[1024,2816]{1,0:T(8,128)(2,1)} fusion(bf16[1024,2816]{1,0:T(8,128)(2,1)} %collective-permute-done.52, bf16[1024,1024]{1,0:T(8,128)(2,1)S(1)} %copy-done.52, bf16[1024,2816]{1,0:T(8,128)(2,1)S(1)} %pad_maximum_fusion), kind=kOutput, calls=%fused_computation | convolution fusion | flops 5914230784 | bytes 19398656 | tf_op jit(solution)/shard_map/dot_general | solution.py:54
  360.7 9.6 %collective-permute-done.25 = bf16[128,2048]{1,0:T(8,128)(2,1)S(1)} collective-permute-done((bf16[128,2048]{1,0:T(8,128)(2,1)S(1)}, bf16[128,2048]{1,0:T(8,128)(2,1)S(1)}, u32[]{:S(2)}, u32[]{:S(2)}) %collective-permute-start.25) | collective-permute-done | bytes 524320 | tf_op jit(solution)/shard_map/ppermute | solution.py:389
  377.4 21.6 %collective-permute-done.29 = bf16[256,2048]{1,0:T(8,128)(2,1)S(1)} collective-permute-done((bf16[256,2048]{1,0:T(8,128)(2,1)}, bf16[256,2048]{1,0:T(8,128)(2,1)S(1)}, u32[]{:S(2)}, u32[]{:S(2)}) %collective-permute-start.29) | collective-permute-done | bytes 1048608 | tf_op jit(solution)/shard_map/ppermute | solution.py:389
  425.5 26.7 %attn_b.1 = (bf16[1024,1536]{1,0:T(8,128)(2,1)S(1)}, f32[4,8,384]{2,1,0:T(8,128)S(1)}) custom-call(s32[5]{0:T(128)S(1)} %copy-done.8, bf16[1024,1536]{1,0:T(8,128)(2,1)} %copy-done, f32[3,1024,128]{2,1,0:T(8,128)S(1)} %pad_maximum_fusion.4.refs_2_, f32[4,4,16,256]{3,2,1,0:T(8,128)S(1)} %get-tuple-element.53.refs_3_, bf16[1024,512]{1,0:T(8,128)(2,1)S(1)} %fusion.45.refs_4_), custom_call_target="tpu_custom_call" | custom-call | tf_op jit(solution)/shard_map/attn_b/pallas_call | solution.py:255
  463.9 9.2 %convolution_convert_fusion.4 = bf16[768,2048]{1,0:T(8,128)(2,1)} fusion(bf16[2048,1408]{1,0:T(8,128)(2,1)} %all-gather.8.cloned.1.call-done, bf16[1024,1408]{1,0:T(8,128)(2,1)S(1)} %copy-done.34), kind=kOutput, calls=%fused_computation.26 | convolution fusion | flops 4430757888 | bytes 11075584 | tf_op jit(solution)/shard_map/dot_general | solution.py:54
  508.3 18.9 %collective-permute-done.42 = bf16[128,2048]{1,0:T(8,128)(2,1)S(1)} collective-permute-done((bf16[128,2048]{1,0:T(8,128)(2,1)S(1)}, bf16[128,2048]{1,0:T(8,128)(2,1)S(1)}, u32[]{:S(2)}, u32[]{:S(2)}) %collective-permute-start.42) | collective-permute-done | bytes 524320 | tf_op jit(solution)/shard_map/ppermute | solution.py:389
  553.5 10.1 %collective-permute-done.35 = bf16[128,2048]{1,0:T(8,128)(2,1)} collective-permute-done((bf16[128,2048]{1,0:T(8,128)(2,1)}, bf16[128,2048]{1,0:T(8,128)(2,1)}, u32[]{:S(2)}, u32[]{:S(2)}) %collective-permute-start.35) | collective-permute-done | bytes 524320 | tf_op jit(solution)/shard_map/ppermute | solution.py:389
  601.9 8.3 %collective-permute-done.53.refs_0_ = bf16[128,2176]{1,0:T(8,128)(2,1)S(1)} collective-permute-done((bf16[128,2176]{1,0:T(8,128)(2,1)}, bf16[128,2176]{1,0:T(8,128)(2,1)S(1)}, u32[]{:S(2)}, u32[]{:S(2)}) %collective-permute-start.53) | collective-permute-done | bytes 557088 | tf_op jit(solution)/shard_map/ppermute | solution.py:444
  610.1 9.6 %collective-permute-done.54.refs_1_ = bf16[128,2176]{1,0:T(8,128)(2,1)S(1)} collective-permute-done((bf16[128,2176]{1,0:T(8,128)(2,1)}, bf16[128,2176]{1,0:T(8,128)(2,1)S(1)}, u32[]{:S(2)}, u32[]{:S(2)}) %collective-permute-start.54) | collective-permute-done | bytes 557088 | tf_op jit(solution)/shard_map/ppermute | solution.py:444
  (351 shorter events, 301.0 us)
Async XLA Ops:
  7.2 85.5 %all-gather.4.cloned.1.call-start = ((), (), s32[]{:S(2)}) async-start(), calls=%async_computation.3 | async-start | bytes 9437184 | tf_op jit(solution)/shard_map/all_gather | solution.py:508
  11.8 231.6 %all-gather.6.cloned.1.call-start = ((), (), s32[]{:S(2)}) async-start(), calls=%async_computation.4 | async-start | bytes 12976128 | tf_op jit(solution)/shard_map/all_gather | solution.py:527
  13.2 24.9 %collective-permute-start = (bf16[256,2048]{1,0:T(8,128)(2,1)S(1)}, bf16[256,2048]{1,0:T(8,128)(2,1)S(1)}, u32[]{:S(2)}, u32[]{:S(2)}) collective-permute-start(bf16[256,2048]{1,0:T(8,128)(2,1)S(1)} %get-tuple-element.86), channel_id=1, source_target_pairs={{0,2},{2,0},{4,6},{6,4},{1,3},{3,1},{5,7},{7,5},{8,10},{10,8},{12,... | collective-permute-start | bytes 3145736 | tf_op jit(solution)/shard_map/ppermute | solution.py:389
  13.8 27.1 %collective-permute-start.1 = (bf16[256,2048]{1,0:T(8,128)(2,1)S(1)}, bf16[256,2048]{1,0:T(8,128)(2,1)S(1)}, u32[]{:S(2)}, u32[]{:S(2)}) collective-permute-start(bf16[256,2048]{1,0:T(8,128)(2,1)S(1)} %get-tuple-element.86), channel_id=1, source_target_pairs={{0,4},{2,6},{4,0},{6,2},{1,5},{3,7},{5,1},{7,3},{8,12},{10,14},{12... | collective-permute-start | bytes 3145736 | tf_op jit(solution)/shard_map/ppermute | solution.py:389
  56.4 24.4 %collective-permute-start.6 = (bf16[128,2176]{1,0:T(8,128)(2,1)S(1)}, bf16[128,2176]{1,0:T(8,128)(2,1)S(1)}, u32[]{:S(2)}, u32[]{:S(2)}) collective-permute-start(bf16[128,2176]{1,0:T(8,128)(2,1)S(1)} %get-tuple-element.112), channel_id=1, source_target_pairs={{0,4},{1,6},{2,0},{3,2},{4,5},{5,7},{6,1},{7,3},{8,12},{9,14},{10,... | collective-permute-start | bytes 1671176 | tf_op jit(solution)/shard_map/ppermute | solution.py:440
  83.2 201.0 %all-gather.8.cloned.1.call-start = ((), (), s32[]{:S(2)}) async-start(), calls=%async_computation.5 | async-start | bytes 6488064 | tf_op jit(solution)/shard_map/all_gather | solution.py:528
  130.1 25.1 %collective-permute-start.8 = (bf16[128,2048]{1,0:T(8,128)(2,1)S(1)}, bf16[128,2048]{1,0:T(8,128)(2,1)S(1)}, u32[]{:S(2)}, u32[]{:S(2)}) collective-permute-start(bf16[128,2048]{1,0:T(8,128)(2,1)S(1)} %get-tuple-element.101), channel_id=1, source_target_pairs={{0,2},{2,0},{4,6},{6,4},{1,3},{3,1},{5,7},{7,5},{8,10},{10,8},{12,... | collective-permute-start | bytes 1572872 | tf_op jit(solution)/shard_map/ppermute | solution.py:389
  145.4 43.5 %collective-permute-start.18 = (bf16[256,2048]{1,0:T(8,128)(2,1)}, bf16[256,2048]{1,0:T(8,128)(2,1)S(1)}, u32[]{:S(2)}, u32[]{:S(2)}) collective-permute-start(bf16[256,2048]{1,0:T(8,128)(2,1)} %bitcast.14), channel_id=1, source_target_pairs={{0,2},{2,0},{4,6},{6,4},{1,3},{3,1},{5,7},{7,5},{8,10},{10,8},{12,... | collective-permute-start | bytes 3145736 | tf_op jit(solution)/shard_map/ppermute | solution.py:389
  153.7 41.4 %collective-permute-start.19 = (bf16[256,2048]{1,0:T(8,128)(2,1)}, bf16[256,2048]{1,0:T(8,128)(2,1)}, u32[]{:S(2)}, u32[]{:S(2)}) collective-permute-start(bf16[256,2048]{1,0:T(8,128)(2,1)} %bitcast.14), channel_id=1, source_target_pairs={{0,4},{2,6},{4,0},{6,2},{1,5},{3,7},{5,1},{7,3},{8,12},{10,14},{12... | collective-permute-start | bytes 3145736 | tf_op jit(solution)/shard_map/ppermute | solution.py:389
  170.0 41.4 %collective-permute-start.14 = (bf16[256,2048]{1,0:T(8,128)(2,1)}, bf16[256,2048]{1,0:T(8,128)(2,1)}, u32[]{:S(2)}, u32[]{:S(2)}) collective-permute-start(bf16[256,2048]{1,0:T(8,128)(2,1)} %get-tuple-element.82), channel_id=1, source_target_pairs={{0,2},{2,0},{4,6},{6,4},{1,3},{3,1},{5,7},{7,5},{8,10},{10,8},{12,... | collective-permute-start | bytes 3145736 | tf_op jit(solution)/shard_map/ppermute | solution.py:389
  191.2 37.1 %collective-permute-start.15 = (bf16[256,2048]{1,0:T(8,128)(2,1)}, bf16[256,2048]{1,0:T(8,128)(2,1)}, u32[]{:S(2)}, u32[]{:S(2)}) collective-permute-start(bf16[256,2048]{1,0:T(8,128)(2,1)} %get-tuple-element.82), channel_id=1, source_target_pairs={{0,4},{2,6},{4,0},{6,2},{1,5},{3,7},{5,1},{7,3},{8,12},{10,14},{12... | collective-permute-start | bytes 3145736 | tf_op jit(solution)/shard_map/ppermute | solution.py:389
  195.1 392.0 %reduce-scatter.8.cloned.1.call-start = ((), (), s32[]{:S(2)}) async-start(), calls=%async_computation.8 | async-start | bytes 3604480 | tf_op jit(solution)/shard_map/reduce_scatter | solution.py:560
  196.2 25.4 %collective-permute-start.21 = (bf16[128,2048]{1,0:T(8,128)(2,1)S(1)}, bf16[128,2048]{1,0:T(8,128)(2,1)S(1)}, u32[]{:S(2)}, u32[]{:S(2)}) collective-permute-start(bf16[128,2048]{1,0:T(8,128)(2,1)S(1)} %slice.317), channel_id=1, source_target_pairs={{0,2},{2,0},{4,6},{6,4},{1,3},{3,1},{5,7},{7,5},{8,10},{10,8},{12,... | collective-permute-start | bytes 1572872 | tf_op jit(solution)/shard_map/ppermute | solution.py:389
  306.9 25.6 %collective-permute-start.52 = (bf16[1024,2816]{1,0:T(8,128)(2,1)}, bf16[1024,2816]{1,0:T(8,128)(2,1)}, u32[]{:S(2)}, u32[]{:S(2)}) collective-permute-start(bf16[1024,2816]{1,0:T(8,128)(2,1)} %convolution_convert_fusion), channel_id=1, source_target_pairs={{0,1},{1,0},{2,3},{3,2},{4,5},{5,4},{6,7},{7,6},{8,9},{9,8},{10,11... | collective-permute-start | bytes 17301512 | tf_op jit(solution)/shard_map/ppermute | solution.py:574
  307.1 279.9 %reduce-scatter.6.cloned.1.call-start = ((), (), s32[]{:S(2)}) async-start(), calls=%async_computation.7 | async-start | bytes 7208960 | tf_op jit(solution)/shard_map/reduce_scatter | solution.py:589
  342.8 255.8 %reduce-scatter.4.cloned.1.call-start = ((), (), s32[]{:S(2)}) async-start(), calls=%async_computation.6 | async-start | bytes 5242880 | tf_op jit(solution)/shard_map/reduce_scatter | solution.py:622
  375.9 31.5 %collective-permute-start.30 = (bf16[256,2048]{1,0:T(8,128)(2,1)}, bf16[256,2048]{1,0:T(8,128)(2,1)}, u32[]{:S(2)}, u32[]{:S(2)}) collective-permute-start(bf16[256,2048]{1,0:T(8,128)(2,1)} %get-tuple-element.80), channel_id=1, source_target_pairs={{0,4},{2,6},{4,0},{6,2},{1,5},{3,7},{5,1},{7,3},{8,12},{10,14},{12... | collective-permute-start | bytes 3145736 | tf_op jit(solution)/shard_map/ppermute | solution.py:389
  491.6 60.7 %collective-permute-start.33 = (bf16[128,2048]{1,0:T(8,128)(2,1)}, bf16[128,2048]{1,0:T(8,128)(2,1)S(1)}, u32[]{:S(2)}, u32[]{:S(2)}) collective-permute-start(bf16[128,2048]{1,0:T(8,128)(2,1)} %get-tuple-element.95), channel_id=1, source_target_pairs={{0,2},{2,0},{4,6},{6,4},{1,3},{3,1},{5,7},{7,5},{8,10},{10,8},{12,... | collective-permute-start | bytes 1572872 | tf_op jit(solution)/shard_map/ppermute | solution.py:389
  501.3 25.9 %collective-permute-start.42 = (bf16[128,2048]{1,0:T(8,128)(2,1)S(1)}, bf16[128,2048]{1,0:T(8,128)(2,1)S(1)}, u32[]{:S(2)}, u32[]{:S(2)}) collective-permute-start(bf16[128,2048]{1,0:T(8,128)(2,1)S(1)} %get-tuple-element.92), channel_id=1, source_target_pairs={{0,2},{2,0},{4,6},{6,4},{1,3},{3,1},{5,7},{7,5},{8,10},{10,8},{12,... | collective-permute-start | bytes 1572872 | tf_op jit(solution)/shard_map/ppermute | solution.py:389
  502.4 24.8 %collective-permute-start.45 = (bf16[128,2048]{1,0:T(8,128)(2,1)S(1)}, bf16[128,2048]{1,0:T(8,128)(2,1)S(1)}, u32[]{:S(2)}, u32[]{:S(2)}) collective-permute-start(bf16[128,2048]{1,0:T(8,128)(2,1)S(1)} %get-tuple-element.90), channel_id=1, source_target_pairs={{0,4},{2,6},{4,0},{6,2},{1,5},{3,7},{5,1},{7,3},{8,12},{10,14},{12... | collective-permute-start | bytes 1572872 | tf_op jit(solution)/shard_map/ppermute | solution.py:389
  506.3 32.1 %collective-permute-start.41 = (bf16[128,2048]{1,0:T(8,128)(2,1)S(1)}, bf16[128,2048]{1,0:T(8,128)(2,1)S(1)}, u32[]{:S(2)}, u32[]{:S(2)}) collective-permute-start(bf16[128,2048]{1,0:T(8,128)(2,1)S(1)} %get-tuple-element.89), channel_id=1, source_target_pairs={{0,2},{2,0},{4,6},{6,4},{1,3},{3,1},{5,7},{7,5},{8,10},{10,8},{12,... | collective-permute-start | bytes 1572872 | tf_op jit(solution)/shard_map/ppermute | solution.py:389
  508.1 31.2 %collective-permute-start.44 = (bf16[128,2048]{1,0:T(8,128)(2,1)S(1)}, bf16[128,2048]{1,0:T(8,128)(2,1)S(1)}, u32[]{:S(2)}, u32[]{:S(2)}) collective-permute-start(bf16[128,2048]{1,0:T(8,128)(2,1)S(1)} %get-tuple-element.91), channel_id=1, source_target_pairs={{0,4},{2,6},{4,0},{6,2},{1,5},{3,7},{5,1},{7,3},{8,12},{10,14},{12... | collective-permute-start | bytes 1572872 | tf_op jit(solution)/shard_map/ppermute | solution.py:389
  593.6 26.2 %collective-permute-start.54 = (bf16[128,2176]{1,0:T(8,128)(2,1)}, bf16[128,2176]{1,0:T(8,128)(2,1)S(1)}, u32[]{:S(2)}, u32[]{:S(2)}) collective-permute-start(bf16[128,2176]{1,0:T(8,128)(2,1)} %get-tuple-element.109), channel_id=1, source_target_pairs={{2,0},{0,1},{6,2},{4,3},{3,4},{1,5},{7,6},{5,7},{10,8},{8,9},{14,1... | collective-permute-start | bytes 1671176 | tf_op jit(solution)/shard_map/ppermute | solution.py:444
  593.9 25.8 %collective-permute-start.55 = (bf16[128,2176]{1,0:T(8,128)(2,1)S(1)}, bf16[128,2176]{1,0:T(8,128)(2,1)S(1)}, u32[]{:S(2)}, u32[]{:S(2)}) collective-permute-start(bf16[128,2176]{1,0:T(8,128)(2,1)S(1)} %get-tuple-element.108), channel_id=1, source_target_pairs={{4,0},{6,1},{0,2},{2,3},{5,4},{7,5},{1,6},{3,7},{12,8},{14,9},{8,1... | collective-permute-start | bytes 1671176 | tf_op jit(solution)/shard_map/ppermute | solution.py:444
  (97 other events, 1279.2 us)
Sparse Core Ops, SparseCore 0:
  12.0 80.7 all-gather.3
  94.9 106.2 all-gather.5
  202.9 59.4 all-gather.7
  307.3 55.6 reduce-scatter.7
  365.1 102.8 reduce-scatter.5
  483.0 77.9 reduce-scatter.3

commit v10 on v9

--- a/solution.py
+++ b/solution.py
@@ -328,14 +328,14 @@
     out[:, 3 * cols :] = outer[...]
 
 
-def finish_kernel(info, grads, qkv, outer):
+def finish_kernel(info, grads, part_out, qkv, outer):
     w = 2 * HD
     cols = outer.shape[1]
     for pair in range(cols // w):
         for part in range(3):
             lo = (3 * pair + part) * w
             qkv[part, :, pair * w : (pair + 1) * w] = grads[:, lo : lo + w].astype(f32)
-    outer[...] = grads[:, 3 * cols :].astype(f32)
+    outer[...] = part_out[...].astype(f32)
 
 
 def whole_call(kernel, info, arrays, shapes, scratch=()):
@@ -615,18 +615,16 @@
             mine = lax.dynamic_index_in_dim(outer, c, 1, keepdims=False)
             got = lax.ppermute(away.reshape(-1, head_cols), COL, [(0, 1), (1, 0)])
             outer = mine.reshape(-1, head_cols).astype(f32) + got.astype(f32)
-            grad_attn = jnp.concatenate(
-                [pair_sum(*seq_halves, grad_proj), outer.astype(bf16)], axis=1
-            )
+            outer = outer.astype(bf16)
+            grad_attn = pair_sum(*seq_halves, grad_proj)
             grad_proj, _ = lax.optimization_barrier((grad_proj, grad_attn))
+            grad_outer = lax.psum_scatter(outer, DP, scatter_dimension=0, tiled=True)
             grad_attn = lax.psum_scatter(grad_attn, DP, scatter_dimension=0, tiled=True)
         else:
-            grad_attn = jnp.concatenate(
-                [tn(seq_in, grad_proj).astype(bf16), tn(branch, attended).astype(bf16)], axis=1
-            )
-            grad_attn = lax.psum_scatter(
-                grad_attn, (DP, COL), scatter_dimension=0, tiled=True
-            )
+            outer = tn(branch, attended).astype(bf16)
+            grad_attn = tn(seq_in, grad_proj).astype(bf16)
+            grad_outer = lax.psum_scatter(outer, (DP, COL), scatter_dimension=0, tiled=True)
+            grad_attn = lax.psum_scatter(grad_attn, (DP, COL), scatter_dimension=0, tiled=True)
         own = nt(grad_proj[:block], w_qkv)
         others = nt(grad_proj[block:], w_qkv).astype(bf16)
         grad_first = scatter_rel(
@@ -663,7 +661,7 @@
         home_qkv, home_out = whole_call(
             finish_kernel,
             info,
-            [grad_attn],
+            [grad_attn, grad_outer],
             [
                 jax.ShapeDtypeStruct((3, grad_attn.shape[0], head_cols), f32),
                 jax.ShapeDtypeStruct((grad_attn.shape[0], head_cols), f32),

time: 643 us -> 650 us (1.011)
  the two profiles are of different devices: /device:TPU:10 before, /device:TPU:0 now
where the time goes in v10:
time: 650 us; the launch traced here: 643 us
  waiting for transfers between devices  247 us (38%)
  matrix products  159 us (24%)
  Pallas kernels  72.9 us (11%)
  starting transfers between devices  65.3 us (10%)
  local copies, waits for them, and re-layouts  51.3 us (8%)
  other arithmetic  31.9 us (5%)
  between operations  16.1 us (2%)
    ppermute x40, waiting for transfers between devices, row_permute(): return lax.ppermute(block, ROW, [(i, i ^ k) for i in range(R)])  192 us
    dot_general x20, matrix products, dot(): lax.dot_general(left, right, (dims, ((), ())), preferred_element_type=f32)  159 us
    ppermute x40, starting transfers between devices, row_permute(): return lax.ppermute(block, ROW, [(i, i ^ k) for i in range(R)])  43.9 us
    unnamed x125, local copies, waits for them, and re-layouts  33.8 us
    pallas_call x1, Pallas kernels, attend_backward(): pl.pallas_call(lambda *refs: backward_kernel(blocks, size, *refs), grid_s...  26.8 us
    ppermute x4, waiting for transfers between devices, spread(): lax.ppermute(packed[k], (ROW, COL), exchange_pairs(k))  20.8 us
    pallas_call x1, Pallas kernels, attend_forward(): pl.pallas_call(lambda *refs: forward_kernel(blocks, size, *refs), grid_sp...  18.2 us
    ppermute x4, waiting for transfers between devices, bring_back(): lax.ppermute(packed[k], (ROW, COL), [(b, a) for a, b in exchange_pairs(k)])  17.2 us
  transfers between devices with their start and end apart: 64, of which 37 were waited for; matrix products, arithmetic and copies ran while one was open for 32% of the time, Pallas kernels for 11%

profile of v10, /device:TPU:0, one launch (start us, length us, event | category | flops | bytes accessed | tf_op | source)
XLA Modules:
  0.0 643.2 jit_solution(15864596636592511397)
XLA Ops:
  17.7 21.6 %collective-permute-done = bf16[256,2048]{1,0:T(8,128)(2,1)S(1)} collective-permute-done((bf16[256,2048]{1,0:T(8,128)(2,1)S(1)}, bf16[256,2048]{1,0:T(8,128)(2,1)S(1)}, u32[]{:S(2)}, u32[]{:S(2)}) %collective-permute-start) | collective-permute-done | bytes 1048608 | tf_op jit(solution)/shard_map/ppermute | solution.py:389
  44.1 8.5 %collective-permute-done.2 = bf16[128,2048]{1,0:T(8,128)(2,1)S(1)} collective-permute-done((bf16[128,2048]{1,0:T(8,128)(2,1)S(1)}, bf16[128,2048]{1,0:T(8,128)(2,1)S(1)}, u32[]{:S(2)}, u32[]{:S(2)}) %collective-permute-start.2) | collective-permute-done | bytes 524320 | tf_op jit(solution)/shard_map/ppermute | solution.py:389
  63.6 8.9 %collective-permute-done.5.refs_1_ = bf16[128,2176]{1,0:T(8,128)(2,1)S(1)} collective-permute-done((bf16[128,2176]{1,0:T(8,128)(2,1)S(1)}, bf16[128,2176]{1,0:T(8,128)(2,1)S(1)}, u32[]{:S(2)}, u32[]{:S(2)}) %collective-permute-start.5) | collective-permute-done | bytes 557088 | tf_op jit(solution)/shard_map/ppermute | solution.py:440
  72.5 11.9 %collective-permute-done.6.refs_2_ = bf16[128,2176]{1,0:T(8,128)(2,1)S(1)} collective-permute-done((bf16[128,2176]{1,0:T(8,128)(2,1)S(1)}, bf16[128,2176]{1,0:T(8,128)(2,1)S(1)}, u32[]{:S(2)}, u32[]{:S(2)}) %collective-permute-start.6) | collective-permute-done | bytes 557088 | tf_op jit(solution)/shard_map/ppermute | solution.py:440
  96.8 12.3 %fusion.7.refs_1_ = f32[1024,1536]{1,0:T(8,128)} fusion(bf16[1024,2048]{1,0:T(8,128)(2,1)} %copy-done.17, bf16[2048,2048]{1,0:T(8,128)(2,1)} %all-gather.4.cloned.1.call-done, f32[1536]{0:T(1024)S(1)} %reshape.565), kind=kOutput, calls=%fused_computation.16 | convolution fusion | flops 6444023808 | bytes 16783360 | tf_op jit(solution)/shard_map/dot_general | solution.py:54
  109.1 18.2 %attn_f.1 = (bf16[1024,1536]{1,0:T(8,128)(2,1)S(1)}, bf16[1024,512]{1,0:T(8,128)(2,1)S(1)}, f32[4,4,16,256]{3,2,1,0:T(8,128)S(1)}) custom-call(s32[5]{0:T(128)S(1)} %stack.30.info.refs_0_, f32[1024,1536]{1,0:T(8,128)} %fusion.7.refs_1_, f32[3,1024,128]{2,1,0:T(8,128)S(1)} %pad_maximum_fusion.3.refs_2_), custom_call_target="tpu_custom_call" | custom-call | tf_op jit(solution)/shard_map/attn_f/pallas_call | solution.py:217
  136.2 10.7 %collective-permute-done.12 = bf16[128,2048]{1,0:T(8,128)(2,1)S(1)} collective-permute-done((bf16[128,2048]{1,0:T(8,128)(2,1)S(1)}, bf16[128,2048]{1,0:T(8,128)(2,1)S(1)}, u32[]{:S(2)}, u32[]{:S(2)}) %collective-permute-start.12) | collective-permute-done | bytes 524320 | tf_op jit(solution)/shard_map/ppermute | solution.py:389
  159.7 9.7 %collective-permute-done.10 = bf16[128,2048]{1,0:T(8,128)(2,1)S(1)} collective-permute-done((bf16[128,2048]{1,0:T(8,128)(2,1)S(1)}, bf16[128,2048]{1,0:T(8,128)(2,1)S(1)}, u32[]{:S(2)}, u32[]{:S(2)}) %collective-permute-start.10) | collective-permute-done | bytes 524320 | tf_op jit(solution)/shard_map/ppermute | solution.py:389
  176.1 17.4 %collective-permute-done.18 = bf16[256,2048]{1,0:T(8,128)(2,1)S(1)} collective-permute-done((bf16[256,2048]{1,0:T(8,128)(2,1)}, bf16[256,2048]{1,0:T(8,128)(2,1)S(1)}, u32[]{:S(2)}, u32[]{:S(2)}) %collective-permute-start.18) | collective-permute-done | bytes 1048608 | tf_op jit(solution)/shard_map/ppermute | solution.py:389
  247.4 17.3 %fusion.92 = f32[1024,2816]{1,0:T(8,128)S(1)} fusion(bf16[1024,2048]{1,0:T(8,128)(2,1)} %constant_dynamic-update-slice_fusion.5.mine.other, bf16[2048,2816]{1,0:T(8,128)(2,1)} %all-gather.6.cloned.1.call-done), kind=kOutput, calls=%fused_computation.185 | convolution fusion | flops 11811160064 | bytes 27262976 | tf_op jit(solution)/shard_map/dot_general | solution.py:54
  279.8 8.4 %add_convert_fusion.2 = bf16[1024,1408]{1,0:T(8,128)(2,1)} fusion(bf16[1024,1408]{1,0:T(8,128)(2,1)} %collective-permute-done.22, bf16[1024,1024]{1,0:T(8,128)(2,1)} %get-tuple-element.44, bf16[1024,1408]{1,0:T(8,128)(2,1)} %copy-done.31), kind=kOutput, calls=%fused_computation.5 | convolution fusion | flops 2957115392 | bytes 10747904 | tf_op jit(solution)/shard_map/dot_general | solution.py:54
  288.2 14.3 %multiply_convert_fusion.1 = (bf16[1024,1408]{1,0:T(8,128)(2,1)S(1)}, bf16[1024,1408]{1,0:T(8,128)(2,1)S(1)}) fusion(f32[1024,2816]{1,0:T(8,128)} %copy-done.26, bf16[1024,2048]{1,0:T(8,128)(2,1)} %constant_dynamic-update-slice_fusion.10.mine.other, bf16[2048,1408]{1,0:T(8,128)(2,1)} %all-gather.8.cloned.1.call-done), kind=kOutput, calls=%fused_computation.4 | convolution fusion | flops 5924323328 | bytes 27262976 | tf_op jit(solution)/shard_map/dot_general | solution.py:54
  302.4 8.5 %convolution_convert_fusion = bf16[1024,2816]{1,0:T(8,128)(2,1)} fusion(bf16[1024,1024]{1,0:T(8,128)(2,1)S(1)} %copy-done.54, bf16[1024,1408]{1,0:T(8,128)(2,1)S(1)} %get-tuple-element.88, bf16[1024,1408]{1,0:T(8,128)(2,1)S(1)} %get-tuple-element.87), kind=kOutput, calls=%fused_computation.9 | convolution fusion | flops 5919997952 | bytes 13631488 | tf_op jit(solution)/shard_map/dot_general | solution.py:54
  314.3 10.6 %convolution_convert_fusion.7 = bf16[256,2048]{1,0:T(8,128)(2,1)} fusion(bf16[2048,2816]{1,0:T(8,128)(2,1)} %all-gather.6.cloned.1.call-done, bf16[1024,2816]{1,0:T(8,128)(2,1)S(1)} %pad_maximum_fusion), kind=kOutput, calls=%fused_computation.31 | convolution fusion | flops 2953314304 | bytes 14024704 | tf_op jit(solution)/shard_map/dot_general | solution.py:54
  324.9 10.4 %convolution_convert_fusion.6 = bf16[512,2048]{1,0:T(8,128)(2,1)} fusion(bf16[2048,2816]{1,0:T(8,128)(2,1)} %all-gather.6.cloned.1.call-done, bf16[1024,2816]{1,0:T(8,128)(2,1)S(1)} %pad_maximum_fusion), kind=kOutput, calls=%fused_computation.27 | convolution fusion | flops 5906628608 | bytes 16515072 | tf_op jit(solution)/shard_map/dot_general | solution.py:54
  335.3 10.3 %add_convert_fusion = bf16[1024,2816]{1,0:T(8,128)(2,1)} fusion(bf16[1024,2816]{1,0:T(8,128)(2,1)} %collective-permute-done.52, bf16[1024,1024]{1,0:T(8,128)(2,1)S(1)} %copy-done.52, bf16[1024,2816]{1,0:T(8,128)(2,1)S(1)} %pad_maximum_fusion), kind=kOutput, calls=%fused_computation | convolution fusion | flops 5914230784 | bytes 19398656 | tf_op jit(solution)/shard_map/dot_general | solution.py:54
  352.6 9.4 %collective-permute-done.24 = bf16[128,2048]{1,0:T(8,128)(2,1)S(1)} collective-permute-done((bf16[128,2048]{1,0:T(8,128)(2,1)S(1)}, bf16[128,2048]{1,0:T(8,128)(2,1)S(1)}, u32[]{:S(2)}, u32[]{:S(2)}) %collective-permute-start.24) | collective-permute-done | bytes 524320 | tf_op jit(solution)/shard_map/ppermute | solution.py:389
  374.7 10.2 %collective-permute-done.25 = bf16[128,2048]{1,0:T(8,128)(2,1)S(1)} collective-permute-done((bf16[128,2048]{1,0:T(8,128)(2,1)S(1)}, bf16[128,2048]{1,0:T(8,128)(2,1)S(1)}, u32[]{:S(2)}, u32[]{:S(2)}) %collective-permute-start.25) | collective-permute-done | bytes 524320 | tf_op jit(solution)/shard_map/ppermute | solution.py:389
  391.1 23.1 %collective-permute-done.29 = bf16[256,2048]{1,0:T(8,128)(2,1)S(1)} collective-permute-done((bf16[256,2048]{1,0:T(8,128)(2,1)}, bf16[256,2048]{1,0:T(8,128)(2,1)S(1)}, u32[]{:S(2)}, u32[]{:S(2)}) %collective-permute-start.29) | collective-permute-done | bytes 1048608 | tf_op jit(solution)/shard_map/ppermute | solution.py:389
  447.5 26.8 %attn_b.1 = (bf16[1024,1536]{1,0:T(8,128)(2,1)S(1)}, f32[4,8,384]{2,1,0:T(8,128)S(1)}) custom-call(s32[5]{0:T(128)S(1)} %copy-done.9, bf16[1024,1536]{1,0:T(8,128)(2,1)} %copy-done, f32[3,1024,128]{2,1,0:T(8,128)S(1)} %pad_maximum_fusion.3.refs_2_, f32[4,4,16,256]{3,2,1,0:T(8,128)S(1)} %get-tuple-element.53.refs_3_, bf16[1024,512]{1,0:T(8,128)(2,1)S(1)} %fusion.45.refs_4_), custom_call_target="tpu_custom_call" | custom-call | tf_op jit(solution)/shard_map/attn_b/pallas_call | solution.py:255
  507.9 8.2 %fusion.10 = bf16[768,2048]{1,0:T(8,128)(2,1)S(1)} fusion(bf16[2048,2048]{1,0:T(8,128)(2,1)} %all-gather.4.cloned.1.call-done, bf16[1024,1536]{1,0:T(8,128)(2,1)} %copy-done.10), kind=kOutput, calls=%fused_computation.24 | convolution fusion | flops 4833411072 | bytes 11796480 | tf_op jit(solution)/shard_map/dot_general | solution.py:54
  523.0 12.6 %collective-permute-done.41 = bf16[128,2048]{1,0:T(8,128)(2,1)S(1)} collective-permute-done((bf16[128,2048]{1,0:T(8,128)(2,1)S(1)}, bf16[128,2048]{1,0:T(8,128)(2,1)S(1)}, u32[]{:S(2)}, u32[]{:S(2)}) %collective-permute-start.41) | collective-permute-done | bytes 524320 | tf_op jit(solution)/shard_map/ppermute | solution.py:389
  565.5 9.8 %collective-permute-done.35 = bf16[128,2048]{1,0:T(8,128)(2,1)} collective-permute-done((bf16[128,2048]{1,0:T(8,128)(2,1)}, bf16[128,2048]{1,0:T(8,128)(2,1)}, u32[]{:S(2)}, u32[]{:S(2)}) %collective-permute-start.35) | collective-permute-done | bytes 524320 | tf_op jit(solution)/shard_map/ppermute | solution.py:389
  615.3 11.1 %collective-permute-done.54.refs_1_ = bf16[128,2176]{1,0:T(8,128)(2,1)S(1)} collective-permute-done((bf16[128,2176]{1,0:T(8,128)(2,1)}, bf16[128,2176]{1,0:T(8,128)(2,1)S(1)}, u32[]{:S(2)}, u32[]{:S(2)}) %collective-permute-start.54) | collective-permute-done | bytes 557088 | tf_op jit(solution)/shard_map/ppermute | solution.py:444
  (346 shorter events, 317.1 us)
Async XLA Ops:
  7.2 89.6 %all-gather.4.cloned.1.call-start = ((), (), s32[]{:S(2)}) async-start(), calls=%async_computation.4 | async-start | bytes 9437184 | tf_op jit(solution)/shard_map/all_gather | solution.py:508
  11.8 235.6 %all-gather.6.cloned.1.call-start = ((), (), s32[]{:S(2)}) async-start(), calls=%async_computation.5 | async-start | bytes 12976128 | tf_op jit(solution)/shard_map/all_gather | solution.py:527
  13.2 26.2 %collective-permute-start = (bf16[256,2048]{1,0:T(8,128)(2,1)S(1)}, bf16[256,2048]{1,0:T(8,128)(2,1)S(1)}, u32[]{:S(2)}, u32[]{:S(2)}) collective-permute-start(bf16[256,2048]{1,0:T(8,128)(2,1)S(1)} %get-tuple-element.86), channel_id=1, source_target_pairs={{0,2},{2,0},{4,6},{6,4},{1,3},{3,1},{5,7},{7,5},{8,10},{10,8},{12,... | collective-permute-start | bytes 3145736 | tf_op jit(solution)/shard_map/ppermute | solution.py:389
  16.2 26.1 %collective-permute-start.1 = (bf16[256,2048]{1,0:T(8,128)(2,1)S(1)}, bf16[256,2048]{1,0:T(8,128)(2,1)S(1)}, u32[]{:S(2)}, u32[]{:S(2)}) collective-permute-start(bf16[256,2048]{1,0:T(8,128)(2,1)S(1)} %get-tuple-element.86), channel_id=1, source_target_pairs={{0,4},{2,6},{4,0},{6,2},{1,5},{3,7},{5,1},{7,3},{8,12},{10,14},{12... | collective-permute-start | bytes 3145736 | tf_op jit(solution)/shard_map/ppermute | solution.py:389
  59.4 24.9 %collective-permute-start.6 = (bf16[128,2176]{1,0:T(8,128)(2,1)S(1)}, bf16[128,2176]{1,0:T(8,128)(2,1)S(1)}, u32[]{:S(2)}, u32[]{:S(2)}) collective-permute-start(bf16[128,2176]{1,0:T(8,128)(2,1)S(1)} %get-tuple-element.112), channel_id=1, source_target_pairs={{0,4},{1,6},{2,0},{3,2},{4,5},{5,7},{6,1},{7,3},{8,12},{9,14},{10,... | collective-permute-start | bytes 1671176 | tf_op jit(solution)/shard_map/ppermute | solution.py:440
  86.7 201.4 %all-gather.8.cloned.1.call-start = ((), (), s32[]{:S(2)}) async-start(), calls=%async_computation.6 | async-start | bytes 6488064 | tf_op jit(solution)/shard_map/all_gather | solution.py:528
  151.0 42.4 %collective-permute-start.18 = (bf16[256,2048]{1,0:T(8,128)(2,1)}, bf16[256,2048]{1,0:T(8,128)(2,1)S(1)}, u32[]{:S(2)}, u32[]{:S(2)}) collective-permute-start(bf16[256,2048]{1,0:T(8,128)(2,1)} %bitcast.14), channel_id=1, source_target_pairs={{0,2},{2,0},{4,6},{6,4},{1,3},{3,1},{5,7},{7,5},{8,10},{10,8},{12,... | collective-permute-start | bytes 3145736 | tf_op jit(solution)/shard_map/ppermute | solution.py:389
  158.1 41.5 %collective-permute-start.19 = (bf16[256,2048]{1,0:T(8,128)(2,1)}, bf16[256,2048]{1,0:T(8,128)(2,1)}, u32[]{:S(2)}, u32[]{:S(2)}) collective-permute-start(bf16[256,2048]{1,0:T(8,128)(2,1)} %bitcast.14), channel_id=1, source_target_pairs={{0,4},{2,6},{4,0},{6,2},{1,5},{3,7},{5,1},{7,3},{8,12},{10,14},{12... | collective-permute-start | bytes 3145736 | tf_op jit(solution)/shard_map/ppermute | solution.py:389
  174.6 41.4 %collective-permute-start.14 = (bf16[256,2048]{1,0:T(8,128)(2,1)}, bf16[256,2048]{1,0:T(8,128)(2,1)}, u32[]{:S(2)}, u32[]{:S(2)}) collective-permute-start(bf16[256,2048]{1,0:T(8,128)(2,1)} %get-tuple-element.82), channel_id=1, source_target_pairs={{0,2},{2,0},{4,6},{6,4},{1,3},{3,1},{5,7},{7,5},{8,10},{10,8},{12,... | collective-permute-start | bytes 3145736 | tf_op jit(solution)/shard_map/ppermute | solution.py:389
  195.7 37.1 %collective-permute-start.15 = (bf16[256,2048]{1,0:T(8,128)(2,1)}, bf16[256,2048]{1,0:T(8,128)(2,1)}, u32[]{:S(2)}, u32[]{:S(2)}) collective-permute-start(bf16[256,2048]{1,0:T(8,128)(2,1)} %get-tuple-element.82), channel_id=1, source_target_pairs={{0,4},{2,6},{4,0},{6,2},{1,5},{3,7},{5,1},{7,3},{8,12},{10,14},{12... | collective-permute-start | bytes 3145736 | tf_op jit(solution)/shard_map/ppermute | solution.py:389
  199.6 397.8 %reduce-scatter.11.cloned.1.call-start = ((), (), s32[]{:S(2)}) async-start(), calls=%async_computation.10 | async-start | bytes 3604480 | tf_op jit(solution)/shard_map/reduce_scatter | solution.py:560
  200.7 25.3 %collective-permute-start.21 = (bf16[128,2048]{1,0:T(8,128)(2,1)S(1)}, bf16[128,2048]{1,0:T(8,128)(2,1)S(1)}, u32[]{:S(2)}, u32[]{:S(2)}) collective-permute-start(bf16[128,2048]{1,0:T(8,128)(2,1)S(1)} %slice.317), channel_id=1, source_target_pairs={{0,2},{2,0},{4,6},{6,4},{1,3},{3,1},{5,7},{7,5},{8,10},{10,8},{12,... | collective-permute-start | bytes 1572872 | tf_op jit(solution)/shard_map/ppermute | solution.py:389
  310.9 24.4 %collective-permute-start.52 = (bf16[1024,2816]{1,0:T(8,128)(2,1)}, bf16[1024,2816]{1,0:T(8,128)(2,1)}, u32[]{:S(2)}, u32[]{:S(2)}) collective-permute-start(bf16[1024,2816]{1,0:T(8,128)(2,1)} %convolution_convert_fusion), channel_id=1, source_target_pairs={{0,1},{1,0},{2,3},{3,2},{4,5},{5,4},{6,7},{7,6},{8,9},{9,8},{10,11... | collective-permute-start | bytes 17301512 | tf_op jit(solution)/shard_map/ppermute | solution.py:574
  311.2 286.2 %reduce-scatter.9.cloned.1.call-start = ((), (), s32[]{:S(2)}) async-start(), calls=%async_computation.9 | async-start | bytes 7208960 | tf_op jit(solution)/shard_map/reduce_scatter | solution.py:589
  345.7 265.5 %reduce-scatter.7.cloned.1.call-start = ((), (), s32[]{:S(2)}) async-start(), calls=%async_computation.8 | async-start | bytes 1310720 | tf_op jit(solution)/shard_map/reduce_scatter | solution.py:621
  389.7 24.4 %collective-permute-start.29 = (bf16[256,2048]{1,0:T(8,128)(2,1)}, bf16[256,2048]{1,0:T(8,128)(2,1)S(1)}, u32[]{:S(2)}, u32[]{:S(2)}) collective-permute-start(bf16[256,2048]{1,0:T(8,128)(2,1)} %get-tuple-element.80), channel_id=1, source_target_pairs={{0,2},{2,0},{4,6},{6,4},{1,3},{3,1},{5,7},{7,5},{8,10},{10,8},{12,... | collective-permute-start | bytes 3145736 | tf_op jit(solution)/shard_map/ppermute | solution.py:389
  390.3 31.9 %collective-permute-start.30 = (bf16[256,2048]{1,0:T(8,128)(2,1)}, bf16[256,2048]{1,0:T(8,128)(2,1)}, u32[]{:S(2)}, u32[]{:S(2)}) collective-permute-start(bf16[256,2048]{1,0:T(8,128)(2,1)} %get-tuple-element.80), channel_id=1, source_target_pairs={{0,4},{2,6},{4,0},{6,2},{1,5},{3,7},{5,1},{7,3},{8,12},{10,14},{12... | collective-permute-start | bytes 3145736 | tf_op jit(solution)/shard_map/ppermute | solution.py:389
  442.2 37.2 %collective-permute-start.51 = (bf16[1024,512]{1,0:T(8,128)(2,1)}, bf16[1024,512]{1,0:T(8,128)(2,1)}, u32[]{:S(2)}, u32[]{:S(2)}) collective-permute-start(bf16[1024,512]{1,0:T(8,128)(2,1)} %bitcast.31), channel_id=1, source_target_pairs={{0,1},{1,0},{2,3},{3,2},{4,5},{5,4},{6,7},{7,6},{8,9},{9,8},{10,11... | collective-permute-start | bytes 3145736 | tf_op jit(solution)/shard_map/ppermute | solution.py:616
  481.9 129.2 %reduce-scatter.5.cloned.1.call-start = ((), (), s32[]{:S(2)}) async-start(), calls=%async_computation.7 | async-start | bytes 3932160 | tf_op jit(solution)/shard_map/reduce_scatter | solution.py:622
  499.9 60.8 %collective-permute-start.33 = (bf16[128,2048]{1,0:T(8,128)(2,1)}, bf16[128,2048]{1,0:T(8,128)(2,1)S(1)}, u32[]{:S(2)}, u32[]{:S(2)}) collective-permute-start(bf16[128,2048]{1,0:T(8,128)(2,1)} %get-tuple-element.95), channel_id=1, source_target_pairs={{0,2},{2,0},{4,6},{6,4},{1,3},{3,1},{5,7},{7,5},{8,10},{10,8},{12,... | collective-permute-start | bytes 1572872 | tf_op jit(solution)/shard_map/ppermute | solution.py:389
  520.7 26.1 %collective-permute-start.40 = (bf16[128,2048]{1,0:T(8,128)(2,1)S(1)}, bf16[128,2048]{1,0:T(8,128)(2,1)S(1)}, u32[]{:S(2)}, u32[]{:S(2)}) collective-permute-start(bf16[128,2048]{1,0:T(8,128)(2,1)S(1)} %get-tuple-element.89), channel_id=1, source_target_pairs={{0,2},{2,0},{4,6},{6,4},{1,3},{3,1},{5,7},{7,5},{8,10},{10,8},{12,... | collective-permute-start | bytes 1572872 | tf_op jit(solution)/shard_map/ppermute | solution.py:389
  522.0 25.8 %collective-permute-start.43 = (bf16[128,2048]{1,0:T(8,128)(2,1)S(1)}, bf16[128,2048]{1,0:T(8,128)(2,1)S(1)}, u32[]{:S(2)}, u32[]{:S(2)}) collective-permute-start(bf16[128,2048]{1,0:T(8,128)(2,1)S(1)} %get-tuple-element.91), channel_id=1, source_target_pairs={{0,4},{2,6},{4,0},{6,2},{1,5},{3,7},{5,1},{7,3},{8,12},{10,14},{12... | collective-permute-start | bytes 1572872 | tf_op jit(solution)/shard_map/ppermute | solution.py:389
  547.8 27.4 %collective-permute-start.35 = (bf16[128,2048]{1,0:T(8,128)(2,1)}, bf16[128,2048]{1,0:T(8,128)(2,1)}, u32[]{:S(2)}, u32[]{:S(2)}) collective-permute-start(bf16[128,2048]{1,0:T(8,128)(2,1)} %get-tuple-element.99), channel_id=1, source_target_pairs={{0,4},{2,6},{4,0},{6,2},{1,5},{3,7},{5,1},{7,3},{8,12},{10,14},{12... | collective-permute-start | bytes 1572872 | tf_op jit(solution)/shard_map/ppermute | solution.py:389
  605.7 26.7 %collective-permute-start.56 = (bf16[128,2176]{1,0:T(8,128)(2,1)S(1)}, bf16[128,2176]{1,0:T(8,128)(2,1)S(1)}, u32[]{:S(2)}, u32[]{:S(2)}) collective-permute-start(bf16[128,2176]{1,0:T(8,128)(2,1)S(1)} %get-tuple-element.107), channel_id=1, source_target_pairs={{6,0},{4,1},{2,2},{0,3},{7,4},{5,5},{3,6},{1,7},{14,8},{12,9},{10,... | collective-permute-start | bytes 1671176 | tf_op jit(solution)/shard_map/ppermute | solution.py:444
  (95 other events, 1252.1 us)
Sparse Core Ops, SparseCore 0:
  12.0 84.7 all-gather.3
  99.0 106.5 all-gather.5
  207.2 58.6 all-gather.7
  311.3 54.3 reduce-scatter.10
  367.9 102.0 reduce-scatter.8
  482.0 25.3 reduce-scatter.6
  509.8 58.8 reduce-scatter.4

commit v11 on v9

--- a/solution.py
+++ b/solution.py
@@ -448,6 +448,13 @@
     def sum_everywhere(array):
         for name in (COL, DP, ROW):
             size = mesh.shape[name]
+            if size == 4:
+                other = []
+                for k in range(1, 4):
+                    pairs = [(i, i ^ k) for i in range(4)]
+                    other.append(lax.ppermute(array, name, pairs))
+                array = (array + other[0]) + (other[1] + other[2])
+                continue
             step = 1
             while step < size:
                 other = lax.ppermute(array, name, [(i, i ^ step) for i in range(size)])

time: 643 us -> 627 us (0.975)
  waiting for transfers between devices: 248 us -> 238 us
    ppermute x40, waiting for transfers between devices: 192 us -> 179 us  [row_permute(): return lax.ppermute(block, ROW, [(i, i ^ k) for i in range(R)])]
    ppermute x0 -> x6, waiting for transfers between devices: none -> 12.2 us  [sum_everywhere(): other.append(lax.ppermute(array, name, pairs))]
    ppermute x0 -> x6, starting transfers between devices: none -> 9.29 us  [sum_everywhere(): other.append(lax.ppermute(array, name, pairs))]
    ppermute x5 -> x1, waiting for transfers between devices: 9.28 us -> 1.23 us  [sum_everywhere(): other = lax.ppermute(array, name, [(i, i ^ step) for i in range(size)])]
    unnamed x131 -> x127, local copies, waits for them, and re-layouts: 33.9 us -> 32.5 us
  transfers between devices with their start and end apart: 63 -> 65, of which waited for: 37 -> 38; matrix products, arithmetic and copies ran while one was open for 32% -> 31% of each run, Pallas kernels for 11% -> 11%
where the time goes in v11:
time: 627 us; the launch traced here: 617 us
  waiting for transfers between devices  238 us (38%)
  matrix products  149 us (24%)
  Pallas kernels  73.2 us (12%)
  starting transfers between devices  59.7 us (10%)
  local copies, waits for them, and re-layouts  48.8 us (8%)
  other arithmetic  31.5 us (5%)
  between operations  16.2 us (3%)
    ppermute x40, waiting for transfers between devices, row_permute(): return lax.ppermute(block, ROW, [(i, i ^ k) for i in range(R)])  179 us
    dot_general x20, matrix products, dot(): lax.dot_general(left, right, (dims, ((), ())), preferred_element_type=f32)  149 us
    ppermute x40, starting transfers between devices, row_permute(): return lax.ppermute(block, ROW, [(i, i ^ k) for i in range(R)])  38.4 us
    unnamed x127, local copies, waits for them, and re-layouts  32.5 us
    pallas_call x1, Pallas kernels, attend_backward(): pl.pallas_call(lambda *refs: backward_kernel(blocks, size, *refs), grid_s...  26.7 us
    ppermute x4, waiting for transfers between devices, spread(): lax.ppermute(packed[k], (ROW, COL), exchange_pairs(k))  21.7 us
    pallas_call x1, Pallas kernels, attend_forward(): pl.pallas_call(lambda *refs: forward_kernel(blocks, size, *refs), grid_sp...  18.2 us
    pallas_call x3, Pallas kernels, split_columns(): pl.pallas_call(split_kernel, grid_spec=pltpu.PrefetchScalarGridSpec(num_s...  16.6 us
  transfers between devices with their start and end apart: 65, of which 38 were waited for; matrix products, arithmetic and copies ran while one was open for 31% of the time, Pallas kernels for 11%

profile of v11, /device:TPU:10, one launch (start us, length us, event | category | flops | bytes accessed | tf_op | source)
XLA Modules:
  0.0 616.7 jit_solution(8037743602301994085)
XLA Ops:
  15.3 22.8 %collective-permute-done = bf16[256,2048]{1,0:T(8,128)(2,1)S(1)} collective-permute-done((bf16[256,2048]{1,0:T(8,128)(2,1)S(1)}, bf16[256,2048]{1,0:T(8,128)(2,1)S(1)}, u32[]{:S(2)}, u32[]{:S(2)}) %collective-permute-start) | collective-permute-done | bytes 1048608 | tf_op jit(solution)/shard_map/ppermute | solution.py:389
  41.7 9.5 %collective-permute-done.2 = bf16[128,2048]{1,0:T(8,128)(2,1)S(1)} collective-permute-done((bf16[128,2048]{1,0:T(8,128)(2,1)S(1)}, bf16[128,2048]{1,0:T(8,128)(2,1)S(1)}, u32[]{:S(2)}, u32[]{:S(2)}) %collective-permute-start.2) | collective-permute-done | bytes 524320 | tf_op jit(solution)/shard_map/ppermute | solution.py:389
  59.0 10.5 %collective-permute-done.4.refs_0_ = bf16[128,2176]{1,0:T(8,128)(2,1)S(1)} collective-permute-done((bf16[128,2176]{1,0:T(8,128)(2,1)S(1)}, bf16[128,2176]{1,0:T(8,128)(2,1)S(1)}, u32[]{:S(2)}, u32[]{:S(2)}) %collective-permute-start.4) | collective-permute-done | bytes 557088 | tf_op jit(solution)/shard_map/ppermute | solution.py:440
  71.8 9.0 %collective-permute-done.6.refs_2_ = bf16[128,2176]{1,0:T(8,128)(2,1)S(1)} collective-permute-done((bf16[128,2176]{1,0:T(8,128)(2,1)S(1)}, bf16[128,2176]{1,0:T(8,128)(2,1)S(1)}, u32[]{:S(2)}, u32[]{:S(2)}) %collective-permute-start.6) | collective-permute-done | bytes 557088 | tf_op jit(solution)/shard_map/ppermute | solution.py:440
  92.7 11.9 %fusion.7.refs_1_ = f32[1024,1536]{1,0:T(8,128)} fusion(bf16[1024,2048]{1,0:T(8,128)(2,1)} %copy-done.16, bf16[2048,2048]{1,0:T(8,128)(2,1)} %all-gather.4.cloned.1.call-done, f32[1536]{0:T(1024)S(1)} %reshape.565), kind=kOutput, calls=%fused_computation.16 | convolution fusion | flops 6444023808 | bytes 16783360 | tf_op jit(solution)/shard_map/dot_general | solution.py:54
  104.6 18.2 %attn_f.1 = (bf16[1024,1536]{1,0:T(8,128)(2,1)S(1)}, bf16[1024,512]{1,0:T(8,128)(2,1)S(1)}, f32[4,4,16,256]{3,2,1,0:T(8,128)S(1)}) custom-call(s32[5]{0:T(128)S(1)} %stack.30.info.refs_0_, f32[1024,1536]{1,0:T(8,128)} %fusion.7.refs_1_, f32[3,1024,128]{2,1,0:T(8,128)S(1)} %pad_maximum_fusion.4.refs_2_), custom_call_target="tpu_custom_call" | custom-call | tf_op jit(solution)/shard_map/attn_f/pallas_call | solution.py:217
  131.7 10.7 %collective-permute-done.12 = bf16[128,2048]{1,0:T(8,128)(2,1)S(1)} collective-permute-done((bf16[128,2048]{1,0:T(8,128)(2,1)S(1)}, bf16[128,2048]{1,0:T(8,128)(2,1)S(1)}, u32[]{:S(2)}, u32[]{:S(2)}) %collective-permute-start.12) | collective-permute-done | bytes 524320 | tf_op jit(solution)/shard_map/ppermute | solution.py:389
  155.2 9.7 %collective-permute-done.10 = bf16[128,2048]{1,0:T(8,128)(2,1)S(1)} collective-permute-done((bf16[128,2048]{1,0:T(8,128)(2,1)S(1)}, bf16[128,2048]{1,0:T(8,128)(2,1)S(1)}, u32[]{:S(2)}, u32[]{:S(2)}) %collective-permute-start.10) | collective-permute-done | bytes 524320 | tf_op jit(solution)/shard_map/ppermute | solution.py:389
  170.6 18.3 %collective-permute-done.18 = bf16[256,2048]{1,0:T(8,128)(2,1)S(1)} collective-permute-done((bf16[256,2048]{1,0:T(8,128)(2,1)}, bf16[256,2048]{1,0:T(8,128)(2,1)S(1)}, u32[]{:S(2)}, u32[]{:S(2)}) %collective-permute-start.18) | collective-permute-done | bytes 1048608 | tf_op jit(solution)/shard_map/ppermute | solution.py:389
  243.4 17.3 %fusion.92 = f32[1024,2816]{1,0:T(8,128)S(1)} fusion(bf16[1024,2048]{1,0:T(8,128)(2,1)} %constant_dynamic-update-slice_fusion.5.mine.other, bf16[2048,2816]{1,0:T(8,128)(2,1)} %all-gather.6.cloned.1.call-done), kind=kOutput, calls=%fused_computation.188 | convolution fusion | flops 11811160064 | bytes 27262976 | tf_op jit(solution)/shard_map/dot_general | solution.py:54
  275.7 8.4 %add_convert_fusion.2 = bf16[1024,1408]{1,0:T(8,128)(2,1)} fusion(bf16[1024,1408]{1,0:T(8,128)(2,1)} %collective-permute-done.22, bf16[1024,1024]{1,0:T(8,128)(2,1)} %get-tuple-element.44, bf16[1024,1408]{1,0:T(8,128)(2,1)} %copy-done.29), kind=kOutput, calls=%fused_computation.5 | convolution fusion | flops 2957115392 | bytes 10747904 | tf_op jit(solution)/shard_map/dot_general | solution.py:54
  284.1 14.2 %multiply_convert_fusion.1 = (bf16[1024,1408]{1,0:T(8,128)(2,1)S(1)}, bf16[1024,1408]{1,0:T(8,128)(2,1)S(1)}) fusion(f32[1024,2816]{1,0:T(8,128)} %copy-done.24, bf16[1024,2048]{1,0:T(8,128)(2,1)} %constant_dynamic-update-slice_fusion.10.mine.other, bf16[2048,1408]{1,0:T(8,128)(2,1)} %all-gather.8.cloned.1.call-done), kind=kOutput, calls=%fused_computation.4 | convolution fusion | flops 5924323328 | bytes 27262976 | tf_op jit(solution)/shard_map/dot_general | solution.py:54
  298.4 8.4 %convolution_convert_fusion = bf16[1024,2816]{1,0:T(8,128)(2,1)} fusion(bf16[1024,1024]{1,0:T(8,128)(2,1)S(1)} %copy-done.53, bf16[1024,1408]{1,0:T(8,128)(2,1)S(1)} %get-tuple-element.88, bf16[1024,1408]{1,0:T(8,128)(2,1)S(1)} %get-tuple-element.87), kind=kOutput, calls=%fused_computation.9 | convolution fusion | flops 5919997952 | bytes 13631488 | tf_op jit(solution)/shard_map/dot_general | solution.py:54
  310.3 9.9 %convolution_convert_fusion.7 = bf16[256,2048]{1,0:T(8,128)(2,1)S(1)} fusion(bf16[2048,2816]{1,0:T(8,128)(2,1)} %all-gather.6.cloned.1.call-done, bf16[1024,2816]{1,0:T(8,128)(2,1)S(1)} %pad_maximum_fusion), kind=kOutput, calls=%fused_computation.32 | convolution fusion | flops 2953314304 | bytes 14024704 | tf_op jit(solution)/shard_map/dot_general | solution.py:54
  320.2 10.2 %convolution_convert_fusion.6 = bf16[512,2048]{1,0:T(8,128)(2,1)} fusion(bf16[2048,2816]{1,0:T(8,128)(2,1)} %all-gather.6.cloned.1.call-done, bf16[1024,2816]{1,0:T(8,128)(2,1)S(1)} %pad_maximum_fusion), kind=kOutput, calls=%fused_computation.28 | convolution fusion | flops 5906628608 | bytes 16515072 | tf_op jit(solution)/shard_map/dot_general | solution.py:54
  332.5 10.3 %add_convert_fusion = bf16[1024,2816]{1,0:T(8,128)(2,1)} fusion(bf16[1024,2816]{1,0:T(8,128)(2,1)} %collective-permute-done.54, bf16[1024,1024]{1,0:T(8,128)(2,1)S(1)} %copy-done.50, bf16[1024,2816]{1,0:T(8,128)(2,1)S(1)} %pad_maximum_fusion), kind=kOutput, calls=%fused_computation | convolution fusion | flops 5914230784 | bytes 19398656 | tf_op jit(solution)/shard_map/dot_general | solution.py:54
  360.7 9.6 %collective-permute-done.25 = bf16[128,2048]{1,0:T(8,128)(2,1)S(1)} collective-permute-done((bf16[128,2048]{1,0:T(8,128)(2,1)S(1)}, bf16[128,2048]{1,0:T(8,128)(2,1)S(1)}, u32[]{:S(2)}, u32[]{:S(2)}) %collective-permute-start.25) | collective-permute-done | bytes 524320 | tf_op jit(solution)/shard_map/ppermute | solution.py:389
  377.5 21.6 %collective-permute-done.29 = bf16[256,2048]{1,0:T(8,128)(2,1)S(1)} collective-permute-done((bf16[256,2048]{1,0:T(8,128)(2,1)}, bf16[256,2048]{1,0:T(8,128)(2,1)S(1)}, u32[]{:S(2)}, u32[]{:S(2)}) %collective-permute-start.29) | collective-permute-done | bytes 1048608 | tf_op jit(solution)/shard_map/ppermute | solution.py:389
  425.6 26.7 %attn_b.1 = (bf16[1024,1536]{1,0:T(8,128)(2,1)S(1)}, f32[4,8,384]{2,1,0:T(8,128)S(1)}) custom-call(s32[5]{0:T(128)S(1)} %copy-done.8, bf16[1024,1536]{1,0:T(8,128)(2,1)} %copy-done, f32[3,1024,128]{2,1,0:T(8,128)S(1)} %pad_maximum_fusion.4.refs_2_, f32[4,4,16,256]{3,2,1,0:T(8,128)S(1)} %get-tuple-element.53.refs_3_, bf16[1024,512]{1,0:T(8,128)(2,1)S(1)} %fusion.45.refs_4_), custom_call_target="tpu_custom_call" | custom-call | tf_op jit(solution)/shard_map/attn_b/pallas_call | solution.py:255
  460.6 8.7 %convolution_convert_fusion.4 = bf16[768,2048]{1,0:T(8,128)(2,1)S(1)} fusion(bf16[2048,1408]{1,0:T(8,128)(2,1)} %all-gather.8.cloned.1.call-done, bf16[1024,1408]{1,0:T(8,128)(2,1)S(1)} %copy-done.30), kind=kOutput, calls=%fused_computation.26 | convolution fusion | flops 4430757888 | bytes 11075584 | tf_op jit(solution)/shard_map/dot_general | solution.py:54
  493.2 8.3 %fusion.10 = bf16[768,2048]{1,0:T(8,128)(2,1)S(1)} fusion(bf16[2048,2048]{1,0:T(8,128)(2,1)} %all-gather.4.cloned.1.call-done, bf16[1024,1536]{1,0:T(8,128)(2,1)S(1)} %copy-done.10), kind=kOutput, calls=%fused_computation.25 | convolution fusion | flops 4833411072 | bytes 11796480 | tf_op jit(solution)/shard_map/dot_general | solution.py:54
  503.8 8.1 %collective-permute-done.35 = bf16[128,2048]{1,0:T(8,128)(2,1)S(1)} collective-permute-done((bf16[128,2048]{1,0:T(8,128)(2,1)S(1)}, bf16[128,2048]{1,0:T(8,128)(2,1)S(1)}, u32[]{:S(2)}, u32[]{:S(2)}) %collective-permute-start.35) | collective-permute-done | bytes 524320 | tf_op jit(solution)/shard_map/ppermute | solution.py:389
  534.3 10.4 %collective-permute-done.43 = bf16[128,2048]{1,0:T(8,128)(2,1)S(1)} collective-permute-done((bf16[128,2048]{1,0:T(8,128)(2,1)S(1)}, bf16[128,2048]{1,0:T(8,128)(2,1)S(1)}, u32[]{:S(2)}, u32[]{:S(2)}) %collective-permute-start.43) | collective-permute-done | bytes 524320 | tf_op jit(solution)/shard_map/ppermute | solution.py:389
  589.7 8.3 %collective-permute-done.55.refs_0_ = bf16[128,2176]{1,0:T(8,128)(2,1)S(1)} collective-permute-done((bf16[128,2176]{1,0:T(8,128)(2,1)}, bf16[128,2176]{1,0:T(8,128)(2,1)S(1)}, u32[]{:S(2)}, u32[]{:S(2)}) %collective-permute-start.55) | collective-permute-done | bytes 557088 | tf_op jit(solution)/shard_map/ppermute | solution.py:444
  (349 shorter events, 299.4 us)
Async XLA Ops:
  7.2 85.5 %all-gather.4.cloned.1.call-start = ((), (), s32[]{:S(2)}) async-start(), calls=%async_computation.3 | async-start | bytes 9437184 | tf_op jit(solution)/shard_map/all_gather | solution.py:515
  11.9 231.5 %all-gather.6.cloned.1.call-start = ((), (), s32[]{:S(2)}) async-start(), calls=%async_computation.4 | async-start | bytes 12976128 | tf_op jit(solution)/shard_map/all_gather | solution.py:534
  13.2 24.9 %collective-permute-start = (bf16[256,2048]{1,0:T(8,128)(2,1)S(1)}, bf16[256,2048]{1,0:T(8,128)(2,1)S(1)}, u32[]{:S(2)}, u32[]{:S(2)}) collective-permute-start(bf16[256,2048]{1,0:T(8,128)(2,1)S(1)} %get-tuple-element.86), channel_id=1, source_target_pairs={{0,2},{2,0},{4,6},{6,4},{1,3},{3,1},{5,7},{7,5},{8,10},{10,8},{12,... | collective-permute-start | bytes 3145736 | tf_op jit(solution)/shard_map/ppermute | solution.py:389
  13.8 27.1 %collective-permute-start.1 = (bf16[256,2048]{1,0:T(8,128)(2,1)S(1)}, bf16[256,2048]{1,0:T(8,128)(2,1)S(1)}, u32[]{:S(2)}, u32[]{:S(2)}) collective-permute-start(bf16[256,2048]{1,0:T(8,128)(2,1)S(1)} %get-tuple-element.86), channel_id=1, source_target_pairs={{0,4},{2,6},{4,0},{6,2},{1,5},{3,7},{5,1},{7,3},{8,12},{10,14},{12... | collective-permute-start | bytes 3145736 | tf_op jit(solution)/shard_map/ppermute | solution.py:389
  56.4 24.4 %collective-permute-start.6 = (bf16[128,2176]{1,0:T(8,128)(2,1)S(1)}, bf16[128,2176]{1,0:T(8,128)(2,1)S(1)}, u32[]{:S(2)}, u32[]{:S(2)}) collective-permute-start(bf16[128,2176]{1,0:T(8,128)(2,1)S(1)} %get-tuple-element.112), channel_id=1, source_target_pairs={{0,4},{1,6},{2,0},{3,2},{4,5},{5,7},{6,1},{7,3},{8,12},{9,14},{10,... | collective-permute-start | bytes 1671176 | tf_op jit(solution)/shard_map/ppermute | solution.py:440
  83.2 200.9 %all-gather.8.cloned.1.call-start = ((), (), s32[]{:S(2)}) async-start(), calls=%async_computation.5 | async-start | bytes 6488064 | tf_op jit(solution)/shard_map/all_gather | solution.py:535
  129.7 24.0 %collective-permute-start.11 = (bf16[128,2048]{1,0:T(8,128)(2,1)S(1)}, bf16[128,2048]{1,0:T(8,128)(2,1)S(1)}, u32[]{:S(2)}, u32[]{:S(2)}) collective-permute-start(bf16[128,2048]{1,0:T(8,128)(2,1)S(1)} %get-tuple-element.103), channel_id=1, source_target_pairs={{0,4},{2,6},{4,0},{6,2},{1,5},{3,7},{5,1},{7,3},{8,12},{10,14},{12... | collective-permute-start | bytes 1572872 | tf_op jit(solution)/shard_map/ppermute | solution.py:389
  130.1 25.1 %collective-permute-start.8 = (bf16[128,2048]{1,0:T(8,128)(2,1)S(1)}, bf16[128,2048]{1,0:T(8,128)(2,1)S(1)}, u32[]{:S(2)}, u32[]{:S(2)}) collective-permute-start(bf16[128,2048]{1,0:T(8,128)(2,1)S(1)} %get-tuple-element.101), channel_id=1, source_target_pairs={{0,2},{2,0},{4,6},{6,4},{1,3},{3,1},{5,7},{7,5},{8,10},{10,8},{12,... | collective-permute-start | bytes 1572872 | tf_op jit(solution)/shard_map/ppermute | solution.py:389
  145.4 43.5 %collective-permute-start.18 = (bf16[256,2048]{1,0:T(8,128)(2,1)}, bf16[256,2048]{1,0:T(8,128)(2,1)S(1)}, u32[]{:S(2)}, u32[]{:S(2)}) collective-permute-start(bf16[256,2048]{1,0:T(8,128)(2,1)} %bitcast.14), channel_id=1, source_target_pairs={{0,2},{2,0},{4,6},{6,4},{1,3},{3,1},{5,7},{7,5},{8,10},{10,8},{12,... | collective-permute-start | bytes 3145736 | tf_op jit(solution)/shard_map/ppermute | solution.py:389
  153.7 41.4 %collective-permute-start.19 = (bf16[256,2048]{1,0:T(8,128)(2,1)}, bf16[256,2048]{1,0:T(8,128)(2,1)}, u32[]{:S(2)}, u32[]{:S(2)}) collective-permute-start(bf16[256,2048]{1,0:T(8,128)(2,1)} %bitcast.14), channel_id=1, source_target_pairs={{0,4},{2,6},{4,0},{6,2},{1,5},{3,7},{5,1},{7,3},{8,12},{10,14},{12... | collective-permute-start | bytes 3145736 | tf_op jit(solution)/shard_map/ppermute | solution.py:389
  170.1 41.4 %collective-permute-start.14 = (bf16[256,2048]{1,0:T(8,128)(2,1)}, bf16[256,2048]{1,0:T(8,128)(2,1)}, u32[]{:S(2)}, u32[]{:S(2)}) collective-permute-start(bf16[256,2048]{1,0:T(8,128)(2,1)} %get-tuple-element.82), channel_id=1, source_target_pairs={{0,2},{2,0},{4,6},{6,4},{1,3},{3,1},{5,7},{7,5},{8,10},{10,8},{12,... | collective-permute-start | bytes 3145736 | tf_op jit(solution)/shard_map/ppermute | solution.py:389
  191.2 37.1 %collective-permute-start.15 = (bf16[256,2048]{1,0:T(8,128)(2,1)}, bf16[256,2048]{1,0:T(8,128)(2,1)}, u32[]{:S(2)}, u32[]{:S(2)}) collective-permute-start(bf16[256,2048]{1,0:T(8,128)(2,1)} %get-tuple-element.82), channel_id=1, source_target_pairs={{0,4},{2,6},{4,0},{6,2},{1,5},{3,7},{5,1},{7,3},{8,12},{10,14},{12... | collective-permute-start | bytes 3145736 | tf_op jit(solution)/shard_map/ppermute | solution.py:389
  195.1 379.8 %reduce-scatter.8.cloned.1.call-start = ((), (), s32[]{:S(2)}) async-start(), calls=%async_computation.8 | async-start | bytes 3604480 | tf_op jit(solution)/shard_map/reduce_scatter | solution.py:567
  196.2 25.4 %collective-permute-start.21 = (bf16[128,2048]{1,0:T(8,128)(2,1)S(1)}, bf16[128,2048]{1,0:T(8,128)(2,1)S(1)}, u32[]{:S(2)}, u32[]{:S(2)}) collective-permute-start(bf16[128,2048]{1,0:T(8,128)(2,1)S(1)} %slice.317), channel_id=1, source_target_pairs={{0,2},{2,0},{4,6},{6,4},{1,3},{3,1},{5,7},{7,5},{8,10},{10,8},{12,... | collective-permute-start | bytes 1572872 | tf_op jit(solution)/shard_map/ppermute | solution.py:389
  213.4 23.3 %collective-permute-start.16 = (bf16[128,2048]{1,0:T(8,128)(2,1)}, bf16[128,2048]{1,0:T(8,128)(2,1)S(1)}, u32[]{:S(2)}, u32[]{:S(2)}) collective-permute-start(bf16[128,2048]{1,0:T(8,128)(2,1)} %slice.311), channel_id=1, source_target_pairs={{0,4},{2,6},{4,0},{6,2},{1,5},{3,7},{5,1},{7,3},{8,12},{10,14},{12... | collective-permute-start | bytes 1572872 | tf_op jit(solution)/shard_map/ppermute | solution.py:389
  306.8 25.7 %collective-permute-start.54 = (bf16[1024,2816]{1,0:T(8,128)(2,1)}, bf16[1024,2816]{1,0:T(8,128)(2,1)}, u32[]{:S(2)}, u32[]{:S(2)}) collective-permute-start(bf16[1024,2816]{1,0:T(8,128)(2,1)} %convolution_convert_fusion), channel_id=1, source_target_pairs={{0,1},{1,0},{2,3},{3,2},{4,5},{5,4},{6,7},{7,6},{8,9},{9,8},{10,11... | collective-permute-start | bytes 17301512 | tf_op jit(solution)/shard_map/ppermute | solution.py:581
  307.1 267.8 %reduce-scatter.6.cloned.1.call-start = ((), (), s32[]{:S(2)}) async-start(), calls=%async_computation.7 | async-start | bytes 7208960 | tf_op jit(solution)/shard_map/reduce_scatter | solution.py:596
  342.8 243.5 %reduce-scatter.4.cloned.1.call-start = ((), (), s32[]{:S(2)}) async-start(), calls=%async_computation.6 | async-start | bytes 5242880 | tf_op jit(solution)/shard_map/reduce_scatter | solution.py:629
  375.7 23.4 %collective-permute-start.29 = (bf16[256,2048]{1,0:T(8,128)(2,1)}, bf16[256,2048]{1,0:T(8,128)(2,1)S(1)}, u32[]{:S(2)}, u32[]{:S(2)}) collective-permute-start(bf16[256,2048]{1,0:T(8,128)(2,1)} %get-tuple-element.80), channel_id=1, source_target_pairs={{0,2},{2,0},{4,6},{6,4},{1,3},{3,1},{5,7},{7,5},{8,10},{10,8},{12,... | collective-permute-start | bytes 3145736 | tf_op jit(solution)/shard_map/ppermute | solution.py:389
  376.0 31.4 %collective-permute-start.30 = (bf16[256,2048]{1,0:T(8,128)(2,1)}, bf16[256,2048]{1,0:T(8,128)(2,1)}, u32[]{:S(2)}, u32[]{:S(2)}) collective-permute-start(bf16[256,2048]{1,0:T(8,128)(2,1)} %get-tuple-element.80), channel_id=1, source_target_pairs={{0,4},{2,6},{4,0},{6,2},{1,5},{3,7},{5,1},{7,3},{8,12},{10,14},{12... | collective-permute-start | bytes 3145736 | tf_op jit(solution)/shard_map/ppermute | solution.py:389
  475.3 27.3 %collective-permute-start.33 = (bf16[128,2048]{1,0:T(8,128)(2,1)S(1)}, bf16[128,2048]{1,0:T(8,128)(2,1)S(1)}, u32[]{:S(2)}, u32[]{:S(2)}) collective-permute-start(bf16[128,2048]{1,0:T(8,128)(2,1)S(1)} %get-tuple-element.95), channel_id=1, source_target_pairs={{0,2},{2,0},{4,6},{6,4},{1,3},{3,1},{5,7},{7,5},{8,10},{10,8},{12,... | collective-permute-start | bytes 1572872 | tf_op jit(solution)/shard_map/ppermute | solution.py:389
  476.5 27.2 %collective-permute-start.36 = (bf16[128,2048]{1,0:T(8,128)(2,1)}, bf16[128,2048]{1,0:T(8,128)(2,1)S(1)}, u32[]{:S(2)}, u32[]{:S(2)}) collective-permute-start(bf16[128,2048]{1,0:T(8,128)(2,1)} %get-tuple-element.97), channel_id=1, source_target_pairs={{0,4},{2,6},{4,0},{6,2},{1,5},{3,7},{5,1},{7,3},{8,12},{10,14},{12... | collective-permute-start | bytes 1572872 | tf_op jit(solution)/shard_map/ppermute | solution.py:389
  581.4 24.6 %collective-permute-start.56 = (bf16[128,2176]{1,0:T(8,128)(2,1)}, bf16[128,2176]{1,0:T(8,128)(2,1)S(1)}, u32[]{:S(2)}, u32[]{:S(2)}) collective-permute-start(bf16[128,2176]{1,0:T(8,128)(2,1)} %get-tuple-element.109), channel_id=1, source_target_pairs={{2,0},{0,1},{6,2},{4,3},{3,4},{1,5},{7,6},{5,7},{10,8},{8,9},{14,1... | collective-permute-start | bytes 1671176 | tf_op jit(solution)/shard_map/ppermute | solution.py:444
  581.7 24.2 %collective-permute-start.57 = (bf16[128,2176]{1,0:T(8,128)(2,1)S(1)}, bf16[128,2176]{1,0:T(8,128)(2,1)S(1)}, u32[]{:S(2)}, u32[]{:S(2)}) collective-permute-start(bf16[128,2176]{1,0:T(8,128)(2,1)S(1)} %get-tuple-element.108), channel_id=1, source_target_pairs={{4,0},{6,1},{0,2},{2,3},{5,4},{7,5},{1,6},{3,7},{12,8},{14,9},{8,1... | collective-permute-start | bytes 1671176 | tf_op jit(solution)/shard_map/ppermute | solution.py:444
  (97 other events, 1249.7 us)
Sparse Core Ops, SparseCore 0:
  12.0 80.7 all-gather.3
  94.9 106.2 all-gather.5
  202.9 59.4 all-gather.7
  307.2 55.6 reduce-scatter.7
  365.1 102.7 reduce-scatter.5
  484.8 83.2 reduce-scatter.3
